TPU v7x, 256 devices: a whole 4x4x8 slice. The times are simulated.
256 devices in a mesh: rows: 8 (over y, core), cols: 32 (over z, x).
Axes of the slice: x: 4, y: 4, z: 8, core: 2. Of those that a mesh axis runs over, the one named last changes fastest.
Arguments:
- band_input: bfloat16 [512, 1024, 512], P('rows', 'cols'), may hold values from -1000 to 1000
- column_taps: float32 [21, 512], replicated, may hold values from -1 to 1
- row_taps: float32 [21, 512], replicated, may hold values from -1 to 1
- w_squeeze: bfloat16 [512, 512], replicated, may hold values from -0.25 to 0.25
- bases_init: float32 [512, 64], replicated, may hold values from 0.004 to 0.12
- w_ham: bfloat16 [512, 512], replicated, may hold values from -0.25 to 0.25
- w_align: bfloat16 [512, 512], replicated, may hold values from -0.25 to 0.25
Outputs:
- head_out: bfloat16 [512, 1024, 512], P('rows', 'cols')
All inputs are finite; a program needn't handle non-finite values.
Results may differ from a plain program's by a relative error of at most 0.0071.
The roundings to bfloat16 on the way count: a program that leaves them out, or rounds other values in their place, can miss the bound.
Values may be sent and summed in bfloat16 or wider, within the bound.
No kernel may reach another device: no remote copies, remote signals or barrier semaphores. Data moves between devices by JAX's collectives and lax.ppermute only.
A program may use at most 64 MiB of HBM per device.

v0:
```python
import jax
import jax.numpy as jnp
from jax import lax
from jax.sharding import Mesh
from jax.sharding import PartitionSpec as P

STEPS = 3
ROWS = ("rows_0", "rows_1")
COLS = ("cols_0", "cols_1")


EPS = 1e-06


def padded(x, sides, width, wrap):
    for axis, dim in sides:
        count, length = (lax.axis_size(axis), x.shape[dim])
        up = [(i, (i + 1) % count) for i in range(count if wrap else count - 1)]
        down = [(j, i) for i, j in up]
        last = lax.slice_in_dim(x, length - width, length, axis=dim)
        initial = lax.slice_in_dim(x, 0, width, axis=dim)
        before = lax.ppermute(last, axis, up)
        after = lax.ppermute(initial, axis, down)
        x = jnp.concatenate([before, x, after], axis=dim)
    return x


def padded_to(lines, count):
    spare = -lines.shape[0] % count
    if not spare:
        return lines
    return jnp.concatenate([lines, jnp.zeros((spare, *lines.shape[1:]), lines.dtype)])


def sent_to_all(x, axis):
    copies = jnp.broadcast_to(x, (lax.axis_size(axis), *x.shape))
    return lax.all_to_all(copies, axis, split_axis=0, concat_axis=0, tiled=True)


def joined_along(tiles, dim):
    tiles = jnp.moveaxis(tiles, 0, dim)
    dims = tiles.shape
    return tiles.reshape(*dims[:dim], dims[dim] * dims[dim + 1], *dims[dim + 2 :])


def gathered_by_axis(x, axes, dim):
    far, near = axes
    initial = sent_to_all(x, far)
    tiles = jnp.swapaxes(sent_to_all(initial, near), 0, 1)
    return joined_along(tiles.reshape(-1, *x.shape), dim)


def cut_along(x, dim, count):
    dims = x.shape
    tiles = x.reshape(*dims[:dim], count, dims[dim] // count, *dims[dim + 1 :])
    return jnp.moveaxis(tiles, dim, 0)


def sent_and_summed(x, axis, dim):
    tiles = cut_along(x, dim, lax.axis_size(axis))
    arrived = lax.all_to_all(tiles, axis, split_axis=0, concat_axis=0, tiled=True)
    return arrived.sum(axis=0)


def sum_in_two_steps(x, axes, dim):
    far, near = axes
    tiles = cut_along(x, dim, lax.axis_size(far))
    nearer = sent_and_summed(tiles, near, dim + 1)
    arrived = lax.all_to_all(nearer, far, split_axis=0, concat_axis=0, tiled=True)
    return arrived.sum(axis=0)


def total_of(x, axes):
    padded = padded_to(x, lax.axis_size(axes[0]) * lax.axis_size(axes[1]))
    whole = gathered_by_axis(sum_in_two_steps(padded, axes, 0), axes, 0)
    return lax.slice_in_dim(whole, 0, len(x)).reshape(x.shape)


def together(arrays, axis):
    line, at, gathered = (jnp.concatenate([a.reshape(-1) for a in arrays]), 0, [])
    so_far = total_of(line, axis)
    for a in arrays:
        gathered.append(so_far[at : at + a.size].reshape(a.shape))
        at += a.size
    return tuple(gathered)


def filter_columns(widened, column_taps, extent):
    summed = jnp.zeros((widened.shape[0], extent, widened.shape[2]), jnp.float32)
    for offset in range(column_taps.shape[0]):
        summed = summed + column_taps[offset] * widened[:, offset : offset + extent, :].astype(
            jnp.float32
        )
    return summed


def filter_rows(extended, row_taps, extent):
    summed = jnp.zeros((extent, extended.shape[1], extended.shape[2]), jnp.float32)
    for offset in range(row_taps.shape[0]):
        summed = summed + row_taps[offset] * extended[offset : offset + extent].astype(jnp.float32)
    return summed


def update_coeffs(feature, basis_now, coeffs):
    numerator = lax.dot_general(
        basis_now.astype(jnp.bfloat16),
        feature,
        (((0,), (1,)), ((), ())),
        preferred_element_type=jnp.float32,
    )
    gram_local = jnp.dot(basis_now.T, basis_now, precision=lax.Precision.HIGHEST)
    denominator = jnp.dot(gram_local, coeffs, precision=lax.Precision.HIGHEST)
    return coeffs * numerator / (denominator + EPS)


def on_device(band_input, column_taps, row_taps, w_squeeze, bases_init, w_ham, w_align):
    tile_rows, tile_cols, channels = band_input.shape
    margin = column_taps.shape[0] // 2
    framed = padded(band_input, ((ROWS, 0), (COLS, 1)), margin, False)
    col_filtered = filter_columns(framed, column_taps, tile_cols).astype(jnp.bfloat16)
    strip_sum = filter_rows(col_filtered, row_taps, tile_rows)
    mixed_tile = (
        (band_input.astype(jnp.float32) + strip_sum)
        .astype(jnp.bfloat16)
        .reshape(tile_rows * tile_cols, channels)
    )
    feature = jax.nn.relu(
        jnp.dot(mixed_tile, w_squeeze, preferred_element_type=jnp.float32)
    ).astype(jnp.bfloat16)
    basis_now = bases_init
    scores = lax.dot_general(
        basis_now.astype(jnp.bfloat16),
        feature,
        (((0,), (1,)), ((), ())),
        preferred_element_type=jnp.float32,
    )
    coeffs = jax.nn.softmax(scores, axis=0)
    for iteration in range(STEPS):
        coeffs = update_coeffs(feature, basis_now, coeffs)
        coeff_low = coeffs.astype(jnp.bfloat16)
        numerator = lax.dot_general(
            feature, coeff_low, (((0,), (1,)), ((), ())), preferred_element_type=jnp.float32
        )
        gram_part = jnp.dot(coeffs, coeffs.T, precision=lax.Precision.HIGHEST)
        numerator, gram_sum = together(
            (numerator, gram_part), (("rows_0", "rows_1", "cols_0"), "cols_1")
        )
        basis_now = (
            basis_now
            * numerator
            / (jnp.dot(basis_now, gram_sum, precision=lax.Precision.HIGHEST) + EPS)
        )
    coeffs = update_coeffs(feature, basis_now, coeffs)
    rebuilt = lax.dot_general(
        coeffs.astype(jnp.bfloat16),
        basis_now.astype(jnp.bfloat16),
        (((0,), (1,)), ((), ())),
        preferred_element_type=jnp.float32,
    ).astype(jnp.bfloat16)
    ham_term = jnp.dot(rebuilt, w_ham, preferred_element_type=jnp.float32)
    hammed = jax.nn.relu(feature.astype(jnp.float32) + ham_term).astype(jnp.bfloat16)
    head_out = jnp.dot(hammed, w_align, preferred_element_type=jnp.float32).astype(jnp.bfloat16)
    return head_out.reshape(tile_rows, tile_cols, channels)


def solution(mesh):
    split = Mesh(mesh.devices.reshape(4, 2, 8, 4), ("rows_0", "rows_1", "cols_0", "cols_1"))
    in_specs = (P(ROWS, COLS, None), P(), P(), P(), P(), P(), P())
    out_specs = P(ROWS, COLS, None)
    return jax.shard_map(
        on_device, mesh=split, in_specs=in_specs, out_specs=out_specs, check_vma=False
    )
```

profile of v0, /device:TPU:1, one launch (start us, length us, event | category | flops | bytes accessed | tf_op | source)
XLA Modules:
  0.0 277.8 jit_solution(5840414815344603280)
XLA Ops:
  0.0 1.2 fusion.50
  1.2 4.6 %collective-permute-start = (bf16[10,32,512]{2,1,0:T(8,128)(2,1)S(1)}, bf16[10,32,512]{2,1,0:T(8,128)(2,1)S(1)}, u32[]{:S(2)}, u32[]{:S(2)}) collective-permute-start(bf16[10,32,512]{2,1,0:T(8,128)(2,1)S(1)} %get-tuple-element.8), channel_id=1, source_target_pairs={{0,32},{32,64},{64,96},{96,128},{128,160},{160,192},{192,224},{1,3... | collective-permute-start | bytes 983048 | tf_op jit(solution)/shard_map/ppermute | solution.py:22
  5.8 1.9 collective-permute-start.1
  8.5 1.3 collective-permute-done
  9.8 1.7 constant_dynamic-update-slice_fusion.1
  11.5 2.6 collective-permute-done.1
  15.4 3.2 %collective-permute-start.2 = (bf16[84,10,512]{2,0,1:T(8,128)(2,1)S(1)}, bf16[84,10,512]{2,0,1:T(8,128)(2,1)S(1)}, u32[]{:S(2)}, u32[]{:S(2)}) collective-permute-start(bf16[84,10,512]{2,0,1:T(8,128)(2,1)S(1)} %copy.27), channel_id=1, source_target_pairs={{0,1},{1,2},{2,3},{3,4},{4,5},{5,6},{6,7},{7,8},{8,9},{9,10},{10,1... | collective-permute-start | bytes 2580488 | tf_op jit(solution)/shard_map/ppermute | solution.py:22
  19.0 1.3 collective-permute-start.3
  20.7 13.2 %collective-permute-done.2 = bf16[84,10,512]{2,0,1:T(8,128)(2,1)S(1)} collective-permute-done((bf16[84,10,512]{2,0,1:T(8,128)(2,1)S(1)}, bf16[84,10,512]{2,0,1:T(8,128)(2,1)S(1)}, u32[]{:S(2)}, u32[]{:S(2)}) %collective-permute-start.2) | collective-permute-done | bytes 860192 | tf_op jit(solution)/shard_map/ppermute | solution.py:22
  34.2 4.3 %collective-permute-done.3 = bf16[84,10,512]{2,0,1:T(8,128)(2,1)S(1)} collective-permute-done((bf16[84,10,512]{2,0,1:T(8,128)(2,1)S(1)}, bf16[84,10,512]{2,0,1:T(8,128)(2,1)S(1)}, u32[]{:S(2)}, u32[]{:S(2)}) %collective-permute-start.3) | collective-permute-done | bytes 860192 | tf_op jit(solution)/shard_map/ppermute | solution.py:23
  38.9 20.2 %add_convert_fusion = bf16[84,32,512]{2,1,0:T(8,128)(2,1)S(1)} fusion(bf16[84,32,512]{2,1,0:T(8,128)(2,1)S(1)} %constant_dynamic-update-slice_fusion, bf16[84,10,512]{2,1,0:T(8,128)(2,1)S(1)} %copy.30, bf16[84,10,512]{2,1,0:T(8,128)(2,1)S(1)} %copy.28, f32[512]{0:T(512)S(1)} %bitcast.166, f32[512]{0:T(512)S(1)} %bitcast.165, f32[512]{0:T(512)S(1)} %bitcast.147, ...), kind=kLoop, calls=%fused_computation.36 | loop fusion | flops 169279488 | bytes 7268352 | tf_op jit(solution)/shard_map/convert_element_type | solution.py:120
  59.1 13.2 %add_convert_fusion.1 = bf16[64,32,512]{2,1,0:T(8,128)(2,1)S(1)} fusion(bf16[64,32,512]{2,1,0:T(8,128)(2,1)S(1)} %copy-done.1, bf16[84,32,512]{2,1,0:T(8,128)(2,1)S(1)} %add_convert_fusion, f32[512]{0:T(512)S(1)} %bitcast.145, f32[512]{0:T(512)S(1)} %bitcast.144, f32[512]{0:T(512)S(1)} %bitcast.126, f32[512]{0:T(512)S(1)} %bitcast.127, f32[512]{0:T(512)S(1)} %bitcast.128, ...), kind=kLoop, calls=%fused_computation.39 | loop fusion | flops 68157440 | bytes 48277504 | tf_op jit(solution)/shard_map/convert_element_type | solution.py:124
  72.3 1.3 maximum_convert_fusion.1
  75.9 1.2 fusion.57
  78.7 1.6 pad_maximum_fusion.2
  80.2 1.3 reshape_reshape.12
  81.6 11.5 %all_to_all.84 = f32[4,64,144]{2,1,0:T(8,128)S(1)} all-to-all(f32[4,64,144]{2,1,0:T(8,128)S(1)} %copy.32), channel_id=1, replica_groups=mesh['rows_0'=4,'rows_1'=2,'cols_0'=8,'cols_1'=4] {'cols_1'}, dimensions={0} | all-to-all | bytes 294912 | tf_op jit(solution)/shard_map/all_to_all | solution.py:61
  94.6 26.4 %all_to_all.85 = f32[64,1,144]{2,1,0:T(1,128)S(1)} all-to-all(f32[64,1,144]{2,1,0:T(1,128)S(1)} %all_to_all.55), channel_id=1, replica_groups=mesh['rows_0'=4,'rows_1'=2,'cols_0'=8,'cols_1'=4] {'rows_0','rows_1','co..., dimensions={0} | all-to-all | bytes 73728 | tf_op jit(solution)/shard_map/all_to_all | solution.py:69
  121.2 13.9 %all_to_all.86 = f32[64,1,144]{2,1,0:T(1,128)S(1)} all-to-all(f32[64,1,144]{2,1,0:T(1,128)S(1)} %broadcast_in_dim.20), channel_id=1, replica_groups=mesh['rows_0'=4,'rows_1'=2,'cols_0'=8,'cols_1'=4] {'rows_0','rows_1','co..., dimensions={0} | all-to-all | bytes 73728 | tf_op jit(solution)/shard_map/all_to_all | solution.py:37
  135.1 7.9 %all_to_all.87 = f32[4,64,144]{2,1,0:T(8,128)S(1)} all-to-all(f32[4,64,144]{2,1,0:T(8,128)S(1)} %broadcast_in_dim.21), channel_id=1, replica_groups=mesh['rows_0'=4,'rows_1'=2,'cols_0'=8,'cols_1'=4] {'cols_1'}, dimensions={0} | all-to-all | bytes 294912 | tf_op jit(solution)/shard_map/all_to_all | solution.py:37
  143.2 1.0 slice.398
  144.2 1.0 slice.466
  145.9 1.2 fusion.24
  150.4 1.1 reshape_reshape.13
  151.5 1.1 copy.36
  152.5 8.6 %all_to_all.88 = f32[4,64,144]{2,1,0:T(8,128)} all-to-all(f32[4,64,144]{2,1,0:T(8,128)S(1)} %copy.36), channel_id=1, replica_groups=mesh['rows_0'=4,'rows_1'=2,'cols_0'=8,'cols_1'=4] {'cols_1'}, dimensions={0} | all-to-all | bytes 294912 | tf_op jit(solution)/shard_map/all_to_all | solution.py:61
  161.1 1.0 reduce_sum.66
  162.1 16.2 %all_to_all.89 = f32[64,1,144]{2,1,0:T(1,128)S(1)} all-to-all(f32[64,1,144]{2,1,0:T(1,128)S(1)} %all_to_all.61), channel_id=1, replica_groups=mesh['rows_0'=4,'rows_1'=2,'cols_0'=8,'cols_1'=4] {'rows_0','rows_1','co..., dimensions={0} | all-to-all | bytes 73728 | tf_op jit(solution)/shard_map/all_to_all | solution.py:69
  178.5 13.7 %all_to_all.90 = f32[64,1,144]{2,1,0:T(1,128)S(1)} all-to-all(f32[64,1,144]{2,1,0:T(1,128)S(1)} %broadcast_in_dim.22), channel_id=1, replica_groups=mesh['rows_0'=4,'rows_1'=2,'cols_0'=8,'cols_1'=4] {'rows_0','rows_1','co..., dimensions={0} | all-to-all | bytes 73728 | tf_op jit(solution)/shard_map/all_to_all | solution.py:37
  192.3 7.9 %all_to_all.91 = f32[4,64,144]{2,1,0:T(8,128)S(1)} all-to-all(f32[4,64,144]{2,1,0:T(8,128)S(1)} %broadcast_in_dim.23), channel_id=1, replica_groups=mesh['rows_0'=4,'rows_1'=2,'cols_0'=8,'cols_1'=4] {'cols_1'}, dimensions={0} | all-to-all | bytes 294912 | tf_op jit(solution)/shard_map/all_to_all | solution.py:37
  201.1 1.9 slice.401
  203.0 1.7 slice.468
  204.7 1.1 copy.50
  205.8 1.1 fusion.25
  209.3 1.2 fusion.61
  212.1 1.6 pad_maximum_fusion.4
  213.6 1.3 reshape_reshape.14
  215.0 7.9 %all_to_all.92 = f32[4,64,144]{2,1,0:T(8,128)S(1)} all-to-all(f32[4,64,144]{2,1,0:T(8,128)S(1)} %copy.40), channel_id=1, replica_groups=mesh['rows_0'=4,'rows_1'=2,'cols_0'=8,'cols_1'=4] {'cols_1'}, dimensions={0} | all-to-all | bytes 294912 | tf_op jit(solution)/shard_map/all_to_all | solution.py:61
  223.6 0.9 all_to_all.67
  224.5 16.2 %all_to_all.93 = f32[64,1,144]{2,1,0:T(1,128)S(1)} all-to-all(f32[64,1,144]{2,1,0:T(1,128)S(1)} %all_to_all.67), channel_id=1, replica_groups=mesh['rows_0'=4,'rows_1'=2,'cols_0'=8,'cols_1'=4] {'rows_0','rows_1','co..., dimensions={0} | all-to-all | bytes 73728 | tf_op jit(solution)/shard_map/all_to_all | solution.py:69
  240.8 14.0 %all_to_all.94 = f32[64,1,144]{2,1,0:T(1,128)S(1)} all-to-all(f32[64,1,144]{2,1,0:T(1,128)S(1)} %broadcast_in_dim.24), channel_id=1, replica_groups=mesh['rows_0'=4,'rows_1'=2,'cols_0'=8,'cols_1'=4] {'rows_0','rows_1','co..., dimensions={0} | all-to-all | bytes 73728 | tf_op jit(solution)/shard_map/all_to_all | solution.py:37
  254.8 7.9 %all_to_all.95 = f32[4,64,144]{2,1,0:T(8,128)S(1)} all-to-all(f32[4,64,144]{2,1,0:T(8,128)S(1)} %broadcast_in_dim.25), channel_id=1, replica_groups=mesh['rows_0'=4,'rows_1'=2,'cols_0'=8,'cols_1'=4] {'cols_1'}, dimensions={0} | all-to-all | bytes 294912 | tf_op jit(solution)/shard_map/all_to_all | solution.py:37
  263.0 1.0 slice.404
  263.9 1.0 slice.470
  265.7 1.2 fusion.26
  267.9 1.3 fusion.22
  269.2 4.4 %maximum_convert_fusion = bf16[2048,512]{1,0:T(8,128)(2,1)} fusion(bf16[2048,512]{1,0:T(8,128)(2,1)S(1)} %maximum_convert_fusion.1, bf16[512,512]{1,0:T(8,128)(2,1)} %param.12, bf16[64,2048]{1,0:T(8,128)(2,1)} %fusion.22, f32[512,64]{0,1:T(8,128)S(1)} %fusion.26), kind=kOutput, calls=%fused_computation.37 | convolution fusion | flops 1213235200 | bytes 5111808 | tf_op jit(solution)/shard_map/dot_general | solution.py:160
  273.6 4.2 %convolution_convert_fusion = bf16[2048,512]{1,0:T(8,128)(2,1)} fusion(bf16[2048,512]{1,0:T(8,128)(2,1)} %maximum_convert_fusion, bf16[512,512]{1,0:T(8,128)(2,1)S(1)} %copy-done.8), kind=kOutput, calls=%fused_computation.40 | convolution fusion | flops 1074790400 | bytes 4718592 | tf_op jit(solution)/shard_map/dot_general | solution.py:162
  (75 shorter events, 20.9 us)
Async XLA Ops:
  0.0 72.3 %copy-start = (bf16[512,512]{1,0:T(8,128)(2,1)S(1)}, bf16[512,512]{1,0:T(8,128)(2,1)}, u32[]{:S(2)}) copy-start(bf16[512,512]{1,0:T(8,128)(2,1)} %param.10) | copy-start | bytes 1572868
  1.2 8.6 %collective-permute-start = (bf16[10,32,512]{2,1,0:T(8,128)(2,1)S(1)}, bf16[10,32,512]{2,1,0:T(8,128)(2,1)S(1)}, u32[]{:S(2)}, u32[]{:S(2)}) collective-permute-start(bf16[10,32,512]{2,1,0:T(8,128)(2,1)S(1)} %get-tuple-element.8), channel_id=1, source_target_pairs={{0,32},{32,64},{64,96},{96,128},{128,160},{160,192},{192,224},{1,3... | collective-permute-start | bytes 983048 | tf_op jit(solution)/shard_map/ppermute | solution.py:22
  5.8 8.4 %collective-permute-start.1 = (bf16[10,32,512]{2,1,0:T(8,128)(2,1)S(1)}, bf16[10,32,512]{2,1,0:T(8,128)(2,1)S(1)}, u32[]{:S(2)}, u32[]{:S(2)}) collective-permute-start(bf16[10,32,512]{2,1,0:T(8,128)(2,1)S(1)} %get-tuple-element.7), channel_id=1, source_target_pairs={{32,0},{64,32},{96,64},{128,96},{160,128},{192,160},{224,192},{33,... | collective-permute-start | bytes 983048 | tf_op jit(solution)/shard_map/ppermute | solution.py:23
  14.9 5.5 %copy-start.7 = (f32[21,512]{1,0:T(8,128)S(1)}, f32[21,512]{1,0:T(8,128)}, u32[]{:S(2)}) copy-start(f32[21,512]{1,0:T(8,128)} %param.9) | copy-start | bytes 129028
  14.9 5.5 %copy-start.6 = (f32[21,512]{1,0:T(8,128)S(1)}, f32[21,512]{1,0:T(8,128)}, u32[]{:S(2)}) copy-start(f32[21,512]{1,0:T(8,128)} %param.8) | copy-start | bytes 129028
  14.9 5.6 %copy-start.5 = (f32[512,64]{0,1:T(8,128)S(1)}, f32[512,64]{0,1:T(8,128)}, u32[]{:S(2)}) copy-start(f32[512,64]{0,1:T(8,128)} %param.11) | copy-start | bytes 393220
  15.4 18.5 %collective-permute-start.2 = (bf16[84,10,512]{2,0,1:T(8,128)(2,1)S(1)}, bf16[84,10,512]{2,0,1:T(8,128)(2,1)S(1)}, u32[]{:S(2)}, u32[]{:S(2)}) collective-permute-start(bf16[84,10,512]{2,0,1:T(8,128)(2,1)S(1)} %copy.27), channel_id=1, source_target_pairs={{0,1},{1,2},{2,3},{3,4},{4,5},{5,6},{6,7},{7,8},{8,9},{9,10},{10,1... | collective-permute-start | bytes 2580488 | tf_op jit(solution)/shard_map/ppermute | solution.py:22
  19.0 19.5 %collective-permute-start.3 = (bf16[84,10,512]{2,0,1:T(8,128)(2,1)S(1)}, bf16[84,10,512]{2,0,1:T(8,128)(2,1)S(1)}, u32[]{:S(2)}, u32[]{:S(2)}) collective-permute-start(bf16[84,10,512]{2,0,1:T(8,128)(2,1)S(1)} %copy.29), channel_id=1, source_target_pairs={{1,0},{2,1},{3,2},{4,3},{5,4},{6,5},{7,6},{8,7},{9,8},{10,9},{11,1... | collective-permute-start | bytes 2580488 | tf_op jit(solution)/shard_map/ppermute | solution.py:23
  38.9 20.2 %copy-start.1 = (bf16[64,32,512]{2,1,0:T(8,128)(2,1)S(1)}, bf16[64,32,512]{2,1,0:T(8,128)(2,1)}, u32[]{:S(2)}) copy-start(bf16[64,32,512]{2,1,0:T(8,128)(2,1)} %param.7) | copy-start | bytes 6291460
  148.8 0.8 copy-start.2
  151.5 55.5 %copy-start.3 = (f32[64,2048]{1,0:T(8,128)S(1)}, f32[64,2048]{1,0:T(8,128)}, u32[]{:S(2)}) copy-start(f32[64,2048]{1,0:T(8,128)} %copy-done.2) | copy-start | bytes 1572868
  205.8 2.2 copy-start.4
  269.2 4.4 %copy-start.8 = (bf16[512,512]{1,0:T(8,128)(2,1)S(1)}, bf16[512,512]{1,0:T(8,128)(2,1)}, u32[]{:S(2)}) copy-start(bf16[512,512]{1,0:T(8,128)(2,1)} %param.13) | copy-start | bytes 1572868
where the time goes:
time: 279 us; the launch traced here: 278 us
  blocking collectives  152 us (54%)
  other arithmetic  39.2 us (14%)
  local copies, waits for them, and re-layouts  27.6 us (10%)
  matrix products  25.8 us (9%)
  waiting for transfers between devices  21.4 us (8%)
  starting transfers between devices  11 us (4%)
    all_to_all x6, blocking collectives, sent_to_all(): return lax.all_to_all(copies, axis, split_axis=0, concat_axis=0, tiled=True)  65.5 us
    all_to_all x3, blocking collectives, sum_in_two_steps(): lax.all_to_all(nearer, far, split_axis=0, concat_axis=0, tiled=True)  58.9 us
    all_to_all x3, blocking collectives, sent_and_summed(): lax.all_to_all(tiles, axis, split_axis=0, concat_axis=0, tiled=True)  28 us
    convert_element_type x1, other arithmetic, on_device(): filter_columns(framed, column_taps, tile_cols).astype(jnp.bfloat16)  20.2 us
    ppermute x2, waiting for transfers between devices, padded(): before = lax.ppermute(last, axis, up)  14.4 us
    convert_element_type x1, other arithmetic, on_device(): mixed_tile = (band_input.astype(jnp.float32) + strip_sum).astype(jnp.bflo...  13.2 us
    ppermute x2, starting transfers between devices, padded(): before = lax.ppermute(last, axis, up)  7.76 us
    slice x6, local copies, waits for them, and re-layouts, together(): gathered.append(so_far[at:at + a.size].reshape(a.shape))  7.48 us
  transfers between devices with their start and end apart: 4, of which 4 were waited for; matrix products, arithmetic and copies ran while one was open for 1% of the time, Pallas kernels for 0%

commit v1 on v0

v1 whole, which is shorter than its diff:
```python
import jax
import jax.numpy as jnp
from jax import lax
from jax.experimental import pallas as pl
from jax.experimental.pallas import tpu as pltpu
from jax.sharding import Mesh
from jax.sharding import PartitionSpec as P

STEPS = 3
Y, CORE, Z, X = 4, 2, 8, 4
ROWS = ("y", "core")
COLS = ("z", "x")
ALL = ("y", "core", "z", "x")
EPS = 1e-06
BF = jnp.bfloat16
F32 = jnp.float32


def padded(x, sides, width, wrap):
    for axis, dim in sides:
        count, length = (lax.axis_size(axis), x.shape[dim])
        up = [(i, (i + 1) % count) for i in range(count if wrap else count - 1)]
        down = [(j, i) for i, j in up]
        last = lax.slice_in_dim(x, length - width, length, axis=dim)
        initial = lax.slice_in_dim(x, 0, width, axis=dim)
        before = lax.ppermute(last, axis, up)
        after = lax.ppermute(initial, axis, down)
        x = jnp.concatenate([before, x, after], axis=dim)
    return x


def filter_columns(widened, column_taps, extent):
    summed = jnp.zeros((widened.shape[0], extent, widened.shape[2]), jnp.float32)
    for offset in range(column_taps.shape[0]):
        summed = summed + column_taps[offset] * widened[:, offset : offset + extent, :].astype(
            jnp.float32
        )
    return summed


def filter_rows(extended, row_taps, extent):
    summed = jnp.zeros((extent, extended.shape[1], extended.shape[2]), jnp.float32)
    for offset in range(row_taps.shape[0]):
        summed = summed + row_taps[offset] * extended[offset : offset + extent].astype(jnp.float32)
    return summed


def pair_4a(i):
    return i ^ 1


def pair_4b(i):
    return 3 - i


def pair_8a(i):
    return i ^ 1


def pair_8b(i):
    return (i + 1) % 8 if i % 2 else (i - 1) % 8


def pair_8c(i):
    return (3, 6, 5, 0, 7, 2, 1, 4)[i]


X_ROUNDS = [("x", pair_4a), ("x", pair_4b)]
Y_ROUNDS = [("y", pair_4a), ("y", pair_4b)]
Z_ROUNDS = [("z", pair_8a), ("z", pair_8b)]
LAST = [("z", pair_8c)]
ROUNDS = list(
    zip(
        X_ROUNDS + Z_ROUNDS + Y_ROUNDS + LAST,
        Z_ROUNDS + Y_ROUNDS + X_ROUNDS + LAST,
        strict=True,
    )
)


def round_pairs(by_core):
    pairs = []
    for y in range(Y):
        for c in range(CORE):
            for z in range(Z):
                for x in range(X):
                    at = {"y": y, "core": c, "z": z, "x": x}
                    axis, rule = by_core[c]
                    to = dict(at)
                    to[axis] = rule(at[axis])

                    def flat(p):
                        return ((p["y"] * CORE + p["core"]) * Z + p["z"]) * X + p["x"]

                    pairs.append((flat(at), flat(to)))
    return pairs


def summed_over_all(mine, theirs):
    swap = [(0, 1), (1, 0)]
    total = mine + lax.ppermute(theirs, "core", swap).astype(F32)
    for by_core in ROUNDS:
        got = lax.ppermute(total.astype(BF), ALL, round_pairs(by_core))
        total = total + got.astype(F32)
    return total, lax.ppermute(total, "core", swap)


def split3(a):
    hi = a.astype(BF)
    return hi, (a - hi.astype(F32)).astype(BF)


def dot(a, b, dims):
    return lax.dot_general(a, b, (dims, ((), ())), preferred_element_type=F32)


def dot3(a, b, dims):
    ah, al = split3(a)
    bh, bl = split3(b)
    return dot(ah, bh, dims) + (dot(ah, bl, dims) + dot(al, bh, dims))


NN = ((1,), (0,))
NT = ((1,), (1,))
TN = ((0,), (0,))


def coeffs_of(basis, coeffs, numerator):
    gram = dot3(basis, basis, NT)
    return coeffs * numerator / (dot3(gram, coeffs, NN) + EPS)


def emit_sums(core, coeffs, feature, mine_ref, theirs_ref):
    num = dot(coeffs.astype(BF), feature, NN)
    gram = dot3(coeffs, coeffs, NT)
    half = num.shape[0] // 2
    c = num.shape[1]
    mine_num = jnp.where(core == 0, num[:half], num[half:])
    theirs_num = jnp.where(core == 0, num[half:], num[:half])
    mine_gram = jnp.where(core == 0, gram[:half], gram[half:])
    theirs_gram = jnp.where(core == 0, gram[half:], gram[:half])
    pad = jnp.zeros((half, mine_ref.shape[1] - c - gram.shape[1]), F32)
    mine_ref[:, :c] = mine_num
    mine_ref[:, c:] = jnp.concatenate([mine_gram, pad], axis=1)
    theirs_ref[:, :c] = theirs_num.astype(BF)
    theirs_ref[:, c:] = jnp.concatenate([theirs_gram, pad], axis=1).astype(BF)


def first_kernel(core_ref, mixed_ref, w_ref, basis_ref, feature_ref, coeffs_ref, mine_ref, theirs_ref):
    feature = jnp.maximum(dot(mixed_ref[...], w_ref[...], NN), 0.0).astype(BF)
    feature_ref[...] = feature
    basis = basis_ref[...]
    scores = dot(basis.astype(BF), feature, NT)
    e = jnp.exp(scores - jnp.max(scores, axis=0, keepdims=True))
    soft = e / jnp.sum(e, axis=0, keepdims=True)
    coeffs = coeffs_of(basis, soft, scores)
    coeffs_ref[...] = coeffs
    emit_sums(core_ref[0], coeffs, feature, mine_ref, theirs_ref)


def updated_basis(core, mine_ref, other_ref, basis):
    mine, other = mine_ref[...], other_ref[...]
    both = jnp.concatenate(
        [jnp.where(core == 0, mine, other), jnp.where(core == 0, other, mine)], axis=0
    )
    r, c = basis.shape
    gram = both[:, c : c + r]
    return basis * both[:, :c] / (dot3(gram, basis, TN) + EPS)


def step_kernel(
    core_ref, smine_ref, sother_ref, basis_ref, feature_ref, coeffs_ref,
    newbasis_ref, newcoeffs_ref, mine_ref, theirs_ref,
):
    basis = updated_basis(core_ref[0], smine_ref, sother_ref, basis_ref[...])
    newbasis_ref[...] = basis
    feature = feature_ref[...]
    coeffs = coeffs_of(basis, coeffs_ref[...], dot(basis.astype(BF), feature, NT))
    newcoeffs_ref[...] = coeffs
    emit_sums(core_ref[0], coeffs, feature, mine_ref, theirs_ref)


def last_kernel(
    core_ref, smine_ref, sother_ref, basis_ref, feature_ref, coeffs_ref, wham_ref, walign_ref, out_ref
):
    basis = updated_basis(core_ref[0], smine_ref, sother_ref, basis_ref[...])
    feature = feature_ref[...]
    low = basis.astype(BF)
    coeffs = coeffs_of(basis, coeffs_ref[...], dot(low, feature, NT))
    rebuilt = dot(coeffs.astype(BF), low, TN).astype(BF)
    hammed = jnp.maximum(feature.astype(F32) + dot(rebuilt, wham_ref[...], NN), 0.0).astype(BF)
    out_ref[...] = dot(hammed, walign_ref[...], NN).astype(BF)


def call(kernel, outs, *args):
    specs = [pl.BlockSpec(memory_space=pltpu.SMEM)]
    specs += [pl.BlockSpec(memory_space=pltpu.VMEM)] * (len(args) - 1)
    return pl.pallas_call(
        kernel,
        out_shape=outs,
        in_specs=specs,
        out_specs=jax.tree.map(lambda _: pl.BlockSpec(memory_space=pltpu.VMEM), outs),
        compiler_params=pltpu.CompilerParams(vmem_limit_bytes=56 * 2**20),
    )(*args)


def on_device(band_input, column_taps, row_taps, w_squeeze, bases_init, w_ham, w_align):
    tile_rows, tile_cols, channels = band_input.shape
    margin = column_taps.shape[0] // 2
    core = lax.axis_index("core").astype(jnp.int32).reshape(1)
    framed = padded(band_input, ((ROWS, 0), (COLS, 1)), margin, False)
    col_filtered = filter_columns(framed, column_taps, tile_cols).astype(jnp.bfloat16)
    strip_sum = filter_rows(col_filtered, row_taps, tile_rows)
    mixed_tile = (
        (band_input.astype(jnp.float32) + strip_sum)
        .astype(jnp.bfloat16)
        .reshape(tile_rows * tile_cols, channels)
    )
    n, r = tile_rows * tile_cols, bases_init.shape[1]
    width = channels + 128
    sds = jax.ShapeDtypeStruct
    sums = [sds((r // 2, width), F32), sds((r // 2, width), BF)]
    basis = bases_init.T
    feature, coeffs, mine, theirs = call(
        first_kernel,
        [sds((n, channels), BF), sds((r, n), F32)] + sums,
        core, mixed_tile, w_squeeze, basis,
    )
    for _ in range(STEPS - 1):
        smine, sother = summed_over_all(mine, theirs)
        basis, coeffs, mine, theirs = call(
            step_kernel,
            [sds((r, channels), F32), sds((r, n), F32)] + sums,
            core, smine, sother, basis, feature, coeffs,
        )
    smine, sother = summed_over_all(mine, theirs)
    head_out = call(
        last_kernel,
        sds((n, channels), BF),
        core, smine, sother, basis, feature, coeffs, w_ham, w_align,
    )
    return head_out.reshape(tile_rows, tile_cols, channels)


def solution(mesh):
    split = Mesh(mesh.devices.reshape(Y, CORE, Z, X), ALL)
    in_specs = (P(ROWS, COLS, None), P(), P(), P(), P(), P(), P())
    out_specs = P(ROWS, COLS, None)
    return jax.shard_map(
        on_device, mesh=split, in_specs=in_specs, out_specs=out_specs, check_vma=False
    )
```

time: 279 us -> 232 us (0.83)
  blocking collectives: 152 us -> 0 us
  starting transfers between devices: 11 us -> 82 us
  waiting for transfers between devices: 21.4 us -> 74.7 us
  matrix products: 25.8 us -> 0 us
  Pallas kernels: 0 us -> 22.5 us
  local copies, waits for them, and re-layouts: 27.6 us -> 8.47 us
  other arithmetic: 39.2 us -> 43.4 us
    all_to_all x12 -> x0, blocking collectives: 152 us -> none  [the longest x6 65.5 us: sent_to_all(): return lax.all_to_all(copies, axis, split_axis=0, concat_axis=0, tiled=True)]
    ppermute x0 -> x27, starting transfers between devices: none -> 70.8 us  [the longest x21 46.5 us: summed_over_all(): got = lax.ppermute(total.astype(BF), ALL, round_pairs(by_core))]
    ppermute x0 -> x27, waiting for transfers between devices: none -> 50 us  [the longest x21 43.6 us: summed_over_all(): got = lax.ppermute(total.astype(BF), ALL, round_pairs(by_core))]
    dot_general x24 -> x0, matrix products: 25.8 us -> none  [the longest x1 4.38 us: on_device(): ham_term = jnp.dot(rebuilt, w_ham, preferred_element_type=jnp.float32)]
    pallas_call x0 -> x4, Pallas kernels: none -> 22.5 us  [call(): pl.pallas_call(kernel, out_shape=outs, in_specs=specs, out_specs=jax.tree...]
    convert_element_type x0 -> x21, other arithmetic: none -> 11.1 us  [summed_over_all(): got = lax.ppermute(total.astype(BF), ALL, round_pairs(by_core))]
    slice x8 -> x0, local copies, waits for them, and re-layouts: 9.14 us -> none  [the longest x6 7.48 us: together(): gathered.append(so_far[at:at + a.size].reshape(a.shape))]
    convert_element_type x1, other arithmetic: 20.2 us -> 13.4 us  [on_device(): filter_columns(framed, column_taps, tile_cols).astype(jnp.bfloat16)]
  transfers between devices with their start and end apart: 4 -> 31, of which waited for: 4 -> 31; matrix products, arithmetic and copies ran while one was open for 1% -> 0% of each run, Pallas kernels for 0% -> 0%
where the time goes in v1:
time: 232 us; the launch traced here: 231 us
  starting transfers between devices  82 us (35%)
  waiting for transfers between devices  74.7 us (32%)
  other arithmetic  43.4 us (19%)
  Pallas kernels  22.5 us (10%)
  local copies, waits for them, and re-layouts  8.47 us (4%)
    ppermute x21, starting transfers between devices, summed_over_all(): got = lax.ppermute(total.astype(BF), ALL, round_pairs(by_core))  46.5 us
    ppermute x21, waiting for transfers between devices, summed_over_all(): got = lax.ppermute(total.astype(BF), ALL, round_pairs(by_core))  43.6 us
    ppermute x3, starting transfers between devices, summed_over_all(): return (total, lax.ppermute(total, 'core', swap))  23.6 us
    pallas_call x4, Pallas kernels, call(): pl.pallas_call(kernel, out_shape=outs, in_specs=specs, out_specs=jax.tree...  22.5 us
    ppermute x2, waiting for transfers between devices, padded(): before = lax.ppermute(last, axis, up)  16.3 us
    convert_element_type x1, other arithmetic, on_device(): mixed_tile = (band_input.astype(jnp.float32) + strip_sum).astype(jnp.bflo...  14.4 us
    convert_element_type x1, other arithmetic, on_device(): filter_columns(framed, column_taps, tile_cols).astype(jnp.bfloat16)  13.4 us
    convert_element_type x21, other arithmetic, summed_over_all(): got = lax.ppermute(total.astype(BF), ALL, round_pairs(by_core))  11.1 us
  transfers between devices with their start and end apart: 31, of which 31 were waited for; matrix products, arithmetic and copies ran while one was open for 0% of the time, Pallas kernels for 0%

profile of v1, /device:TPU:1, one launch (start us, length us, event | category | flops | bytes accessed | tf_op | source)
XLA Modules:
  0.0 231.4 jit_solution(15227763944467400644)
XLA Ops:
  0.0 2.8 %copy.8 = bf16[64,32,512]{2,0,1:T(8,128)(2,1)S(1)} copy(bf16[64,32,512]{2,1,0:T(8,128)(2,1)} %param.7) | data formatting | bytes 4194304 | tf_op args[0]
  3.9 4.6 %collective-permute-start = (bf16[10,32,512]{2,0,1:T(8,128)(2,1)}, bf16[10,32,512]{2,0,1:T(8,128)(2,1)S(1)}, u32[]{:S(2)}, u32[]{:S(2)}) collective-permute-start(bf16[10,32,512]{2,0,1:T(8,128)(2,1)} %get-tuple-element.39), channel_id=1, source_target_pairs={{0,32},{32,64},{64,96},{96,128},{128,160},{160,192},{192,224},{1,3... | collective-permute-start | bytes 983048 | tf_op jit(solution)/shard_map/ppermute | solution.py:26
  8.4 1.9 collective-permute-start.1
  10.4 4.5 %collective-permute-done = bf16[10,32,512]{2,0,1:T(8,128)(2,1)S(1)} collective-permute-done((bf16[10,32,512]{2,0,1:T(8,128)(2,1)}, bf16[10,32,512]{2,0,1:T(8,128)(2,1)S(1)}, u32[]{:S(2)}, u32[]{:S(2)}) %collective-permute-start) | collective-permute-done | bytes 327712 | tf_op jit(solution)/shard_map/ppermute | solution.py:26
  14.9 4.3 %collective-permute-done.1 = bf16[10,32,512]{2,0,1:T(8,128)(2,1)S(1)} collective-permute-done((bf16[10,32,512]{2,0,1:T(8,128)(2,1)}, bf16[10,32,512]{2,0,1:T(8,128)(2,1)S(1)}, u32[]{:S(2)}, u32[]{:S(2)}) %collective-permute-start.1) | collective-permute-done | bytes 327712 | tf_op jit(solution)/shard_map/ppermute | solution.py:27
  19.2 1.5 pad_maximum_fusion.1
  20.9 3.5 %collective-permute-start.2 = (bf16[84,10,512]{2,0,1:T(8,128)(2,1)S(1)}, bf16[84,10,512]{2,0,1:T(8,128)(2,1)S(1)}, u32[]{:S(2)}, u32[]{:S(2)}) collective-permute-start(bf16[84,10,512]{2,0,1:T(8,128)(2,1)S(1)} %get-tuple-element.37), channel_id=1, source_target_pairs={{0,1},{1,2},{2,3},{3,4},{4,5},{5,6},{6,7},{7,8},{8,9},{9,10},{10,1... | collective-permute-start | bytes 2580488 | tf_op jit(solution)/shard_map/ppermute | solution.py:26
  25.8 11.8 %collective-permute-done.2 = bf16[84,10,512]{2,0,1:T(8,128)(2,1)S(1)} collective-permute-done((bf16[84,10,512]{2,0,1:T(8,128)(2,1)S(1)}, bf16[84,10,512]{2,0,1:T(8,128)(2,1)S(1)}, u32[]{:S(2)}, u32[]{:S(2)}) %collective-permute-start.2) | collective-permute-done | bytes 860192 | tf_op jit(solution)/shard_map/ppermute | solution.py:26
  37.6 4.2 %collective-permute-done.3 = bf16[84,10,512]{2,0,1:T(8,128)(2,1)S(1)} collective-permute-done((bf16[84,10,512]{2,0,1:T(8,128)(2,1)S(1)}, bf16[84,10,512]{2,0,1:T(8,128)(2,1)S(1)}, u32[]{:S(2)}, u32[]{:S(2)}) %collective-permute-start.3) | collective-permute-done | bytes 860192 | tf_op jit(solution)/shard_map/ppermute | solution.py:27
  41.7 2.9 %maximum_maximum_fusion = (bf16[84,42,512]{2,0,1:T(8,128)(2,1)S(1)}, bf16[84,42,512]{2,0,1:T(8,128)(2,1)S(1)}) fusion(bf16[10,32,512]{2,0,1:T(8,128)(2,1)S(1)} %collective-permute-done.1, bf16[64,32,512]{2,0,1:T(8,128)(2,1)S(1)} %copy.8, bf16[10,32,512]{2,0,1:T(8,128)(2,1)S(1)} %collective-permute-done, bf16[84,10,512]{2,0,1:T(8,128)(2,1)S(1)} %collective-permute-done.2, ...), kind=kLoop, calls=%fused_computation.2 | loop fusion | flops 28901376 | bytes 11698176 | tf_op jit(solution)/shard_map/concatenate | solution.py:28
  44.6 13.4 %add_convert_fusion = bf16[84,32,512]{2,0,1:T(8,128)(2,1)S(1)} fusion(bf16[84,42,512]{2,0,1:T(8,128)(2,1)S(1)} %get-tuple-element.36, bf16[84,42,512]{2,0,1:T(8,128)(2,1)S(1)} %get-tuple-element.35, f32[512]{0:T(512)S(1)} %bitcast.69, f32[512]{0:T(512)S(1)} %bitcast.68, f32[512]{0:T(512)S(1)} %bitcast.50, f32[512]{0:T(512)S(1)} %bitcast.51, ...), kind=kLoop, calls=%fused_computation | loop fusion | flops 93585408 | bytes 60598272 | tf_op jit(solution)/shard_map/convert_element_type | solution.py:212
  58.0 14.4 %add_convert_fusion.1 = bf16[64,32,512]{2,0,1:T(8,128)(2,1)S(1)} fusion(bf16[84,32,512]{2,0,1:T(8,128)(2,1)S(1)} %add_convert_fusion, f32[512]{0:T(512)S(1)} %bitcast.90, f32[512]{0:T(512)S(1)} %bitcast.89, f32[512]{0:T(512)S(1)} %bitcast.71, f32[512]{0:T(512)S(1)} %bitcast.72, f32[512]{0:T(512)S(1)} %bitcast.73, f32[512]{0:T(512)S(1)} %bitcast.74, ...), kind=kLoop, calls=%fused_computation.1 | loop fusion | flops 68157440 | bytes 48277504 | tf_op jit(solution)/shard_map/convert_element_type | solution.py:216
  72.5 2.5 %copy.12 = bf16[64,32,512]{2,1,0:T(8,128)(2,1)} copy(bf16[64,32,512]{2,0,1:T(8,128)(2,1)S(1)} %add_convert_fusion.1) | data formatting | bytes 4194304 | tf_op jit(solution)/shard_map/convert_element_type | solution.py:216
  74.9 5.4 %shard_map.73 = (bf16[2048,512]{1,0:T(8,128)(2,1)}, f32[64,2048]{1,0:T(8,128)}, f32[32,640]{1,0:T(8,128)}, bf16[32,640]{1,0:T(8,128)(2,1)}) custom-call(s32[1]{0:T(128)} %bitcast.core_ref, bf16[2048,512]{1,0:T(8,128)(2,1)} %bitcast.46, bf16[512,512]{1,0:T(8,128)(2,1)} %w_ref.1, f32[64,512]{1,0:T(8,128)} %bitcast.47), custom_call_target="tpu_custom_call" | custom-call | tf_op jit(solution)/shard_map/pallas_call | solution.py:198
  80.4 1.4 collective-permute-done.4
  82.7 2.1 collective-permute-start.5
  84.8 1.7 collective-permute-done.5
  87.4 5.2 %collective-permute-start.6 = (bf16[32,640]{1,0:T(8,128)(2,1)S(1)}, bf16[32,640]{1,0:T(8,128)(2,1)S(1)}, u32[]{:S(2)}, u32[]{:S(2)}) collective-permute-start(bf16[32,640]{1,0:T(8,128)(2,1)S(1)} %fusion.12), channel_id=1, source_target_pairs={{0,3},{1,2},{2,1},{3,0},{4,7},{5,6},{6,5},{7,4},{8,11},{9,10},{10,... | collective-permute-start | bytes 122888 | tf_op jit(solution)/shard_map/ppermute | solution.py:103
  92.6 1.7 collective-permute-done.6
  95.2 6.8 %collective-permute-start.7 = (bf16[32,640]{1,0:T(8,128)(2,1)S(1)}, bf16[32,640]{1,0:T(8,128)(2,1)S(1)}, u32[]{:S(2)}, u32[]{:S(2)}) collective-permute-start(bf16[32,640]{1,0:T(8,128)(2,1)S(1)} %fusion.1), channel_id=1, source_target_pairs={{0,4},{1,5},{2,6},{3,7},{4,0},{5,1},{6,2},{7,3},{8,12},{9,13},{10,... | collective-permute-start | bytes 122888 | tf_op jit(solution)/shard_map/ppermute | solution.py:103
  104.4 1.7 collective-permute-start.8
  106.1 2.5 %collective-permute-done.8 = bf16[32,640]{1,0:T(8,128)(2,1)S(1)} collective-permute-done((bf16[32,640]{1,0:T(8,128)(2,1)S(1)}, bf16[32,640]{1,0:T(8,128)(2,1)S(1)}, u32[]{:S(2)}, u32[]{:S(2)}) %collective-permute-start.8) | collective-permute-done | bytes 40992 | tf_op jit(solution)/shard_map/ppermute | solution.py:103
  109.1 2.4 %collective-permute-done.9 = bf16[32,640]{1,0:T(8,128)(2,1)S(1)} collective-permute-done((bf16[32,640]{1,0:T(8,128)(2,1)S(1)}, bf16[32,640]{1,0:T(8,128)(2,1)S(1)}, u32[]{:S(2)}, u32[]{:S(2)}) %collective-permute-start.9) | collective-permute-done | bytes 40992 | tf_op jit(solution)/shard_map/ppermute | solution.py:103
  111.5 2.6 %collective-permute-start.10 = (bf16[32,640]{1,0:T(8,128)(2,1)S(1)}, bf16[32,640]{1,0:T(8,128)(2,1)S(1)}, u32[]{:S(2)}, u32[]{:S(2)}) collective-permute-start(bf16[32,640]{1,0:T(8,128)(2,1)S(1)} %fusion.13), channel_id=1, source_target_pairs={{0,192},{1,193},{2,194},{3,195},{4,196},{5,197},{6,198},{7,199},{8... | collective-permute-start | bytes 122888 | tf_op jit(solution)/shard_map/ppermute | solution.py:103
  114.1 1.5 collective-permute-done.10
  115.7 5.4 %collective-permute-start.11 = (bf16[32,640]{1,0:T(8,128)(2,1)S(1)}, bf16[32,640]{1,0:T(8,128)(2,1)S(1)}, u32[]{:S(2)}, u32[]{:S(2)}) collective-permute-start(bf16[32,640]{1,0:T(8,128)(2,1)S(1)} %fusion.3), channel_id=1, source_target_pairs={{0,12},{1,13},{2,14},{3,15},{4,24},{5,25},{6,26},{7,27},{8,20},{9,... | collective-permute-start | bytes 122888 | tf_op jit(solution)/shard_map/ppermute | solution.py:103
  122.6 7.5 %collective-permute-start.12 = (f32[32,640]{1,0:T(8,128)S(1)}, f32[32,640]{1,0:T(8,128)S(1)}, u32[]{:S(2)}, u32[]{:S(2)}) collective-permute-start(f32[32,640]{1,0:T(8,128)S(1)} %convert_add_fusion.16.smine_ref), channel_id=1, source_target_pairs={{0,32},{32,0},{1,33},{33,1},{2,34},{34,2},{3,35},{35,3},{4,36},{36... | collective-permute-start | bytes 245768 | tf_op jit(solution)/shard_map/ppermute | solution.py:105
  131.6 4.6 %shard_map.74 = (f32[64,512]{1,0:T(8,128)}, f32[64,2048]{1,0:T(8,128)}, f32[32,640]{1,0:T(8,128)}, bf16[32,640]{1,0:T(8,128)(2,1)}) custom-call(s32[1]{0:T(128)} %bitcast.core_ref, f32[32,640]{1,0:T(8,128)} %copy-done.2, f32[32,640]{1,0:T(8,128)} %copy-done.5, f32[64,512]{1,0:T(8,128)} %bitcast.48, bf16[2048,512]{1,0:T(8,128)(2,1)} %get-tuple-element.19.feature_ref, ...), custom_call_target="tpu_custom_call" | custom-call | tf_op jit(solution)/shard_map/pallas_call | solution.py:198
  139.3 2.2 collective-permute-done.14
  143.3 3.3 %collective-permute-done.15 = bf16[32,640]{1,0:T(8,128)(2,1)S(1)} collective-permute-done((bf16[32,640]{1,0:T(8,128)(2,1)S(1)}, bf16[32,640]{1,0:T(8,128)(2,1)S(1)}, u32[]{:S(2)}, u32[]{:S(2)}) %collective-permute-start.15) | collective-permute-done | bytes 40992 | tf_op jit(solution)/shard_map/ppermute | solution.py:103
  148.1 2.3 %collective-permute-done.16 = bf16[32,640]{1,0:T(8,128)(2,1)S(1)} collective-permute-done((bf16[32,640]{1,0:T(8,128)(2,1)S(1)}, bf16[32,640]{1,0:T(8,128)(2,1)S(1)}, u32[]{:S(2)}, u32[]{:S(2)}) %collective-permute-start.16) | collective-permute-done | bytes 40992 | tf_op jit(solution)/shard_map/ppermute | solution.py:103
  151.3 2.3 collective-permute-start.17
  153.6 1.9 collective-permute-done.17
  155.6 2.8 %collective-permute-done.18 = bf16[32,640]{1,0:T(8,128)(2,1)S(1)} collective-permute-done((bf16[32,640]{1,0:T(8,128)(2,1)S(1)}, bf16[32,640]{1,0:T(8,128)(2,1)S(1)}, u32[]{:S(2)}, u32[]{:S(2)}) %collective-permute-start.18) | collective-permute-done | bytes 40992 | tf_op jit(solution)/shard_map/ppermute | solution.py:103
  158.4 3.0 %collective-permute-start.19 = (bf16[32,640]{1,0:T(8,128)(2,1)S(1)}, bf16[32,640]{1,0:T(8,128)(2,1)S(1)}, u32[]{:S(2)}, u32[]{:S(2)}) collective-permute-start(bf16[32,640]{1,0:T(8,128)(2,1)S(1)} %fusion.15), channel_id=1, source_target_pairs={{0,192},{1,193},{2,194},{3,195},{4,196},{5,197},{6,198},{7,199},{8... | collective-permute-start | bytes 122888 | tf_op jit(solution)/shard_map/ppermute | solution.py:103
  162.9 3.6 %collective-permute-start.20 = (bf16[32,640]{1,0:T(8,128)(2,1)S(1)}, bf16[32,640]{1,0:T(8,128)(2,1)S(1)}, u32[]{:S(2)}, u32[]{:S(2)}) collective-permute-start(bf16[32,640]{1,0:T(8,128)(2,1)S(1)} %fusion.7), channel_id=1, source_target_pairs={{0,12},{1,13},{2,14},{3,15},{4,24},{5,25},{6,26},{7,27},{8,20},{9,... | collective-permute-start | bytes 122888 | tf_op jit(solution)/shard_map/ppermute | solution.py:103
  168.0 8.1 %collective-permute-start.21 = (f32[32,640]{1,0:T(8,128)S(1)}, f32[32,640]{1,0:T(8,128)S(1)}, u32[]{:S(2)}, u32[]{:S(2)}) collective-permute-start(f32[32,640]{1,0:T(8,128)S(1)} %convert_add_fusion.8.smine_ref), channel_id=1, source_target_pairs={{0,32},{32,0},{1,33},{33,1},{2,34},{34,2},{3,35},{35,3},{4,36},{36... | collective-permute-start | bytes 245768 | tf_op jit(solution)/shard_map/ppermute | solution.py:105
  177.7 4.6 %shard_map.75 = (f32[64,512]{1,0:T(8,128)}, f32[64,2048]{1,0:T(8,128)}, f32[32,640]{1,0:T(8,128)}, bf16[32,640]{1,0:T(8,128)(2,1)}) custom-call(s32[1]{0:T(128)} %bitcast.core_ref, f32[32,640]{1,0:T(8,128)} %copy-done.1, f32[32,640]{1,0:T(8,128)} %copy-done.4, f32[64,512]{1,0:T(8,128)} %get-tuple-element.23.basis_ref, ...), custom_call_target="tpu_custom_call" | custom-call | tf_op jit(solution)/shard_map/pallas_call | solution.py:198
  185.3 2.2 collective-permute-done.23
  189.4 3.2 %collective-permute-done.24 = bf16[32,640]{1,0:T(8,128)(2,1)S(1)} collective-permute-done((bf16[32,640]{1,0:T(8,128)(2,1)S(1)}, bf16[32,640]{1,0:T(8,128)(2,1)S(1)}, u32[]{:S(2)}, u32[]{:S(2)}) %collective-permute-start.24) | collective-permute-done | bytes 40992 | tf_op jit(solution)/shard_map/ppermute | solution.py:103
  193.6 2.8 %collective-permute-done.25 = bf16[32,640]{1,0:T(8,128)(2,1)S(1)} collective-permute-done((bf16[32,640]{1,0:T(8,128)(2,1)S(1)}, bf16[32,640]{1,0:T(8,128)(2,1)S(1)}, u32[]{:S(2)}, u32[]{:S(2)}) %collective-permute-start.25) | collective-permute-done | bytes 40992 | tf_op jit(solution)/shard_map/ppermute | solution.py:103
  197.4 2.3 collective-permute-start.26
  199.7 1.9 collective-permute-done.26
  201.6 2.8 %collective-permute-done.27 = bf16[32,640]{1,0:T(8,128)(2,1)S(1)} collective-permute-done((bf16[32,640]{1,0:T(8,128)(2,1)S(1)}, bf16[32,640]{1,0:T(8,128)(2,1)S(1)}, u32[]{:S(2)}, u32[]{:S(2)}) %collective-permute-start.27) | collective-permute-done | bytes 40992 | tf_op jit(solution)/shard_map/ppermute | solution.py:103
  204.5 3.0 %collective-permute-start.28 = (bf16[32,640]{1,0:T(8,128)(2,1)S(1)}, bf16[32,640]{1,0:T(8,128)(2,1)S(1)}, u32[]{:S(2)}, u32[]{:S(2)}) collective-permute-start(bf16[32,640]{1,0:T(8,128)(2,1)S(1)} %fusion.17), channel_id=1, source_target_pairs={{0,192},{1,193},{2,194},{3,195},{4,196},{5,197},{6,198},{7,199},{8... | collective-permute-start | bytes 122888 | tf_op jit(solution)/shard_map/ppermute | solution.py:103
  209.0 3.6 %collective-permute-start.29 = (bf16[32,640]{1,0:T(8,128)(2,1)S(1)}, bf16[32,640]{1,0:T(8,128)(2,1)S(1)}, u32[]{:S(2)}, u32[]{:S(2)}) collective-permute-start(bf16[32,640]{1,0:T(8,128)(2,1)S(1)} %fusion.11), channel_id=1, source_target_pairs={{0,12},{1,13},{2,14},{3,15},{4,24},{5,25},{6,26},{7,27},{8,20},{9,... | collective-permute-start | bytes 122888 | tf_op jit(solution)/shard_map/ppermute | solution.py:103
  214.0 7.9 %collective-permute-start.30 = (f32[32,640]{1,0:T(8,128)S(1)}, f32[32,640]{1,0:T(8,128)S(1)}, u32[]{:S(2)}, u32[]{:S(2)}) collective-permute-start(f32[32,640]{1,0:T(8,128)S(1)} %convert_add_fusion.smine_ref), channel_id=1, source_target_pairs={{0,32},{32,0},{1,33},{33,1},{2,34},{34,2},{3,35},{35,3},{4,36},{36... | collective-permute-start | bytes 245768 | tf_op jit(solution)/shard_map/ppermute | solution.py:105
  223.5 7.9 %shard_map.76 = bf16[2048,512]{1,0:T(8,128)(2,1)} custom-call(s32[1]{0:T(128)} %bitcast.core_ref, f32[32,640]{1,0:T(8,128)} %copy-done.3, f32[32,640]{1,0:T(8,128)} %copy-done.6, f32[64,512]{1,0:T(8,128)} %get-tuple-element.27.basis_ref, bf16[2048,512]{1,0:T(8,128)(2,1)} %get-tuple-element.19.feature_ref, f32[64,2048]{1,0:T(8,128)} %get-tuple-element.28.coeffs_ref, ...), custom_call_target="tpu_custom_call" | custom-call | tf_op jit(solution)/shard_map/pallas_call | solution.py:198
  (72 shorter events, 34.4 us)
Async XLA Ops:
  3.9 11.0 %collective-permute-start = (bf16[10,32,512]{2,0,1:T(8,128)(2,1)}, bf16[10,32,512]{2,0,1:T(8,128)(2,1)S(1)}, u32[]{:S(2)}, u32[]{:S(2)}) collective-permute-start(bf16[10,32,512]{2,0,1:T(8,128)(2,1)} %get-tuple-element.39), channel_id=1, source_target_pairs={{0,32},{32,64},{64,96},{96,128},{128,160},{160,192},{192,224},{1,3... | collective-permute-start | bytes 983048 | tf_op jit(solution)/shard_map/ppermute | solution.py:26
  8.4 10.7 %collective-permute-start.1 = (bf16[10,32,512]{2,0,1:T(8,128)(2,1)}, bf16[10,32,512]{2,0,1:T(8,128)(2,1)S(1)}, u32[]{:S(2)}, u32[]{:S(2)}) collective-permute-start(bf16[10,32,512]{2,0,1:T(8,128)(2,1)} %get-tuple-element.40), channel_id=1, source_target_pairs={{32,0},{64,32},{96,64},{128,96},{160,128},{192,160},{224,192},{33,... | collective-permute-start | bytes 983048 | tf_op jit(solution)/shard_map/ppermute | solution.py:27
  10.4 15.3 %copy-start.7 = (f32[21,512]{1,0:T(8,128)S(1)}, f32[21,512]{1,0:T(8,128)}, u32[]{:S(2)}) copy-start(f32[21,512]{1,0:T(8,128)} %param.8) | copy-start | bytes 129028
  10.4 15.3 %copy-start.8 = (f32[21,512]{1,0:T(8,128)S(1)}, f32[21,512]{1,0:T(8,128)}, u32[]{:S(2)}) copy-start(f32[21,512]{1,0:T(8,128)} %param.9) | copy-start | bytes 129028
  20.9 16.7 %collective-permute-start.2 = (bf16[84,10,512]{2,0,1:T(8,128)(2,1)S(1)}, bf16[84,10,512]{2,0,1:T(8,128)(2,1)S(1)}, u32[]{:S(2)}, u32[]{:S(2)}) collective-permute-start(bf16[84,10,512]{2,0,1:T(8,128)(2,1)S(1)} %get-tuple-element.37), channel_id=1, source_target_pairs={{0,1},{1,2},{2,3},{3,4},{4,5},{5,6},{6,7},{7,8},{8,9},{9,10},{10,1... | collective-permute-start | bytes 2580488 | tf_op jit(solution)/shard_map/ppermute | solution.py:26
  24.3 17.4 %collective-permute-start.3 = (bf16[84,10,512]{2,0,1:T(8,128)(2,1)S(1)}, bf16[84,10,512]{2,0,1:T(8,128)(2,1)S(1)}, u32[]{:S(2)}, u32[]{:S(2)}) collective-permute-start(bf16[84,10,512]{2,0,1:T(8,128)(2,1)S(1)} %get-tuple-element.38), channel_id=1, source_target_pairs={{1,0},{2,1},{3,2},{4,3},{5,4},{6,5},{7,6},{8,7},{9,8},{10,9},{11,1... | collective-permute-start | bytes 2580488 | tf_op jit(solution)/shard_map/ppermute | solution.py:27
  44.6 13.4 %copy-start = (bf16[64,32,512]{2,1,0:T(8,128)(2,1)S(1)}, bf16[64,32,512]{2,1,0:T(8,128)(2,1)}, u32[]{:S(2)}) copy-start(bf16[64,32,512]{2,1,0:T(8,128)(2,1)} %param.7) | copy-start | bytes 6291460
  80.4 1.4 collective-permute-start.4
  82.7 3.8 %collective-permute-start.5 = (bf16[32,640]{1,0:T(8,128)(2,1)S(1)}, bf16[32,640]{1,0:T(8,128)(2,1)S(1)}, u32[]{:S(2)}, u32[]{:S(2)}) collective-permute-start(bf16[32,640]{1,0:T(8,128)(2,1)S(1)} %fusion), channel_id=1, source_target_pairs={{0,1},{1,0},{2,3},{3,2},{4,5},{5,4},{6,7},{7,6},{8,9},{9,8},{10,11... | collective-permute-start | bytes 122888 | tf_op jit(solution)/shard_map/ppermute | solution.py:103
  87.4 6.9 %collective-permute-start.6 = (bf16[32,640]{1,0:T(8,128)(2,1)S(1)}, bf16[32,640]{1,0:T(8,128)(2,1)S(1)}, u32[]{:S(2)}, u32[]{:S(2)}) collective-permute-start(bf16[32,640]{1,0:T(8,128)(2,1)S(1)} %fusion.12), channel_id=1, source_target_pairs={{0,3},{1,2},{2,1},{3,0},{4,7},{5,6},{6,5},{7,4},{8,11},{9,10},{10,... | collective-permute-start | bytes 122888 | tf_op jit(solution)/shard_map/ppermute | solution.py:103
  95.2 8.2 %collective-permute-start.7 = (bf16[32,640]{1,0:T(8,128)(2,1)S(1)}, bf16[32,640]{1,0:T(8,128)(2,1)S(1)}, u32[]{:S(2)}, u32[]{:S(2)}) collective-permute-start(bf16[32,640]{1,0:T(8,128)(2,1)S(1)} %fusion.1), channel_id=1, source_target_pairs={{0,4},{1,5},{2,6},{3,7},{4,0},{5,1},{6,2},{7,3},{8,12},{9,13},{10,... | collective-permute-start | bytes 122888 | tf_op jit(solution)/shard_map/ppermute | solution.py:103
  104.4 4.2 %collective-permute-start.8 = (bf16[32,640]{1,0:T(8,128)(2,1)S(1)}, bf16[32,640]{1,0:T(8,128)(2,1)S(1)}, u32[]{:S(2)}, u32[]{:S(2)}) collective-permute-start(bf16[32,640]{1,0:T(8,128)(2,1)S(1)} %get-tuple-element.33), channel_id=1, source_target_pairs={{0,28},{1,29},{2,30},{3,31},{4,8},{5,9},{6,10},{7,11},{8,4},{9,5},... | collective-permute-start | bytes 122888 | tf_op jit(solution)/shard_map/ppermute | solution.py:103
  108.5 2.9 %collective-permute-start.9 = (bf16[32,640]{1,0:T(8,128)(2,1)S(1)}, bf16[32,640]{1,0:T(8,128)(2,1)S(1)}, u32[]{:S(2)}, u32[]{:S(2)}) collective-permute-start(bf16[32,640]{1,0:T(8,128)(2,1)S(1)} %fusion.2), channel_id=1, source_target_pairs={{0,64},{1,65},{2,66},{3,67},{4,68},{5,69},{6,70},{7,71},{8,72},{9,... | collective-permute-start | bytes 122888 | tf_op jit(solution)/shard_map/ppermute | solution.py:103
  111.5 4.2 %collective-permute-start.10 = (bf16[32,640]{1,0:T(8,128)(2,1)S(1)}, bf16[32,640]{1,0:T(8,128)(2,1)S(1)}, u32[]{:S(2)}, u32[]{:S(2)}) collective-permute-start(bf16[32,640]{1,0:T(8,128)(2,1)S(1)} %fusion.13), channel_id=1, source_target_pairs={{0,192},{1,193},{2,194},{3,195},{4,196},{5,197},{6,198},{7,199},{8... | collective-permute-start | bytes 122888 | tf_op jit(solution)/shard_map/ppermute | solution.py:103
  115.7 6.8 %collective-permute-start.11 = (bf16[32,640]{1,0:T(8,128)(2,1)S(1)}, bf16[32,640]{1,0:T(8,128)(2,1)S(1)}, u32[]{:S(2)}, u32[]{:S(2)}) collective-permute-start(bf16[32,640]{1,0:T(8,128)(2,1)S(1)} %fusion.3), channel_id=1, source_target_pairs={{0,12},{1,13},{2,14},{3,15},{4,24},{5,25},{6,26},{7,27},{8,20},{9,... | collective-permute-start | bytes 122888 | tf_op jit(solution)/shard_map/ppermute | solution.py:103
  122.6 8.4 %copy-start.2 = (f32[32,640]{1,0:T(8,128)}, f32[32,640]{1,0:T(8,128)S(1)}, u32[]{:S(2)}) copy-start(f32[32,640]{1,0:T(8,128)S(1)} %convert_add_fusion.16.smine_ref) | copy-start | bytes 245764
  122.6 8.4 %collective-permute-start.12 = (f32[32,640]{1,0:T(8,128)S(1)}, f32[32,640]{1,0:T(8,128)S(1)}, u32[]{:S(2)}, u32[]{:S(2)}) collective-permute-start(f32[32,640]{1,0:T(8,128)S(1)} %convert_add_fusion.16.smine_ref), channel_id=1, source_target_pairs={{0,32},{32,0},{1,33},{33,1},{2,34},{34,2},{3,35},{35,3},{4,36},{36... | collective-permute-start | bytes 245768 | tf_op jit(solution)/shard_map/ppermute | solution.py:105
  131.0 0.6 copy-start.5
  136.2 1.4 collective-permute-start.13
  138.5 2.9 %collective-permute-start.14 = (bf16[32,640]{1,0:T(8,128)(2,1)S(1)}, bf16[32,640]{1,0:T(8,128)(2,1)S(1)}, u32[]{:S(2)}, u32[]{:S(2)}) collective-permute-start(bf16[32,640]{1,0:T(8,128)(2,1)S(1)} %fusion.4), channel_id=1, source_target_pairs={{0,1},{1,0},{2,3},{3,2},{4,5},{5,4},{6,7},{7,6},{8,9},{9,8},{10,11... | collective-permute-start | bytes 122888 | tf_op jit(solution)/shard_map/ppermute | solution.py:103
  142.4 4.2 %collective-permute-start.15 = (bf16[32,640]{1,0:T(8,128)(2,1)S(1)}, bf16[32,640]{1,0:T(8,128)(2,1)S(1)}, u32[]{:S(2)}, u32[]{:S(2)}) collective-permute-start(bf16[32,640]{1,0:T(8,128)(2,1)S(1)} %fusion.14), channel_id=1, source_target_pairs={{0,3},{1,2},{2,1},{3,0},{4,7},{5,6},{6,5},{7,4},{8,11},{9,10},{10,... | collective-permute-start | bytes 122888 | tf_op jit(solution)/shard_map/ppermute | solution.py:103
  147.5 2.9 %collective-permute-start.16 = (bf16[32,640]{1,0:T(8,128)(2,1)S(1)}, bf16[32,640]{1,0:T(8,128)(2,1)S(1)}, u32[]{:S(2)}, u32[]{:S(2)}) collective-permute-start(bf16[32,640]{1,0:T(8,128)(2,1)S(1)} %fusion.5), channel_id=1, source_target_pairs={{0,4},{1,5},{2,6},{3,7},{4,0},{5,1},{6,2},{7,3},{8,12},{9,13},{10,... | collective-permute-start | bytes 122888 | tf_op jit(solution)/shard_map/ppermute | solution.py:103
  151.3 4.2 %collective-permute-start.17 = (bf16[32,640]{1,0:T(8,128)(2,1)S(1)}, bf16[32,640]{1,0:T(8,128)(2,1)S(1)}, u32[]{:S(2)}, u32[]{:S(2)}) collective-permute-start(bf16[32,640]{1,0:T(8,128)(2,1)S(1)} %get-tuple-element.31), channel_id=1, source_target_pairs={{0,28},{1,29},{2,30},{3,31},{4,8},{5,9},{6,10},{7,11},{8,4},{9,5},... | collective-permute-start | bytes 122888 | tf_op jit(solution)/shard_map/ppermute | solution.py:103
  155.5 2.9 %collective-permute-start.18 = (bf16[32,640]{1,0:T(8,128)(2,1)S(1)}, bf16[32,640]{1,0:T(8,128)(2,1)S(1)}, u32[]{:S(2)}, u32[]{:S(2)}) collective-permute-start(bf16[32,640]{1,0:T(8,128)(2,1)S(1)} %fusion.6), channel_id=1, source_target_pairs={{0,64},{1,65},{2,66},{3,67},{4,68},{5,69},{6,70},{7,71},{8,72},{9,... | collective-permute-start | bytes 122888 | tf_op jit(solution)/shard_map/ppermute | solution.py:103
  158.4 4.4 %collective-permute-start.19 = (bf16[32,640]{1,0:T(8,128)(2,1)S(1)}, bf16[32,640]{1,0:T(8,128)(2,1)S(1)}, u32[]{:S(2)}, u32[]{:S(2)}) collective-permute-start(bf16[32,640]{1,0:T(8,128)(2,1)S(1)} %fusion.15), channel_id=1, source_target_pairs={{0,192},{1,193},{2,194},{3,195},{4,196},{5,197},{6,198},{7,199},{8... | collective-permute-start | bytes 122888 | tf_op jit(solution)/shard_map/ppermute | solution.py:103
  162.9 5.0 %collective-permute-start.20 = (bf16[32,640]{1,0:T(8,128)(2,1)S(1)}, bf16[32,640]{1,0:T(8,128)(2,1)S(1)}, u32[]{:S(2)}, u32[]{:S(2)}) collective-permute-start(bf16[32,640]{1,0:T(8,128)(2,1)S(1)} %fusion.7), channel_id=1, source_target_pairs={{0,12},{1,13},{2,14},{3,15},{4,24},{5,25},{6,26},{7,27},{8,20},{9,... | collective-permute-start | bytes 122888 | tf_op jit(solution)/shard_map/ppermute | solution.py:103
  168.0 9.1 %copy-start.1 = (f32[32,640]{1,0:T(8,128)}, f32[32,640]{1,0:T(8,128)S(1)}, u32[]{:S(2)}) copy-start(f32[32,640]{1,0:T(8,128)S(1)} %convert_add_fusion.8.smine_ref) | copy-start | bytes 245764
  168.0 9.1 %collective-permute-start.21 = (f32[32,640]{1,0:T(8,128)S(1)}, f32[32,640]{1,0:T(8,128)S(1)}, u32[]{:S(2)}, u32[]{:S(2)}) collective-permute-start(f32[32,640]{1,0:T(8,128)S(1)} %convert_add_fusion.8.smine_ref), channel_id=1, source_target_pairs={{0,32},{32,0},{1,33},{33,1},{2,34},{34,2},{3,35},{35,3},{4,36},{36... | collective-permute-start | bytes 245768 | tf_op jit(solution)/shard_map/ppermute | solution.py:105
  177.0 0.6 copy-start.4
  182.3 1.4 collective-permute-start.22
  184.6 2.9 %collective-permute-start.23 = (bf16[32,640]{1,0:T(8,128)(2,1)S(1)}, bf16[32,640]{1,0:T(8,128)(2,1)S(1)}, u32[]{:S(2)}, u32[]{:S(2)}) collective-permute-start(bf16[32,640]{1,0:T(8,128)(2,1)S(1)} %fusion.8), channel_id=1, source_target_pairs={{0,1},{1,0},{2,3},{3,2},{4,5},{5,4},{6,7},{7,6},{8,9},{9,8},{10,11... | collective-permute-start | bytes 122888 | tf_op jit(solution)/shard_map/ppermute | solution.py:103
  188.4 4.2 %collective-permute-start.24 = (bf16[32,640]{1,0:T(8,128)(2,1)S(1)}, bf16[32,640]{1,0:T(8,128)(2,1)S(1)}, u32[]{:S(2)}, u32[]{:S(2)}) collective-permute-start(bf16[32,640]{1,0:T(8,128)(2,1)S(1)} %fusion.16), channel_id=1, source_target_pairs={{0,3},{1,2},{2,1},{3,0},{4,7},{5,6},{6,5},{7,4},{8,11},{9,10},{10,... | collective-permute-start | bytes 122888 | tf_op jit(solution)/shard_map/ppermute | solution.py:103
  193.5 2.9 %collective-permute-start.25 = (bf16[32,640]{1,0:T(8,128)(2,1)S(1)}, bf16[32,640]{1,0:T(8,128)(2,1)S(1)}, u32[]{:S(2)}, u32[]{:S(2)}) collective-permute-start(bf16[32,640]{1,0:T(8,128)(2,1)S(1)} %fusion.9), channel_id=1, source_target_pairs={{0,4},{1,5},{2,6},{3,7},{4,0},{5,1},{6,2},{7,3},{8,12},{9,13},{10,... | collective-permute-start | bytes 122888 | tf_op jit(solution)/shard_map/ppermute | solution.py:103
  197.4 4.2 %collective-permute-start.26 = (bf16[32,640]{1,0:T(8,128)(2,1)S(1)}, bf16[32,640]{1,0:T(8,128)(2,1)S(1)}, u32[]{:S(2)}, u32[]{:S(2)}) collective-permute-start(bf16[32,640]{1,0:T(8,128)(2,1)S(1)} %get-tuple-element.29), channel_id=1, source_target_pairs={{0,28},{1,29},{2,30},{3,31},{4,8},{5,9},{6,10},{7,11},{8,4},{9,5},... | collective-permute-start | bytes 122888 | tf_op jit(solution)/shard_map/ppermute | solution.py:103
  201.5 2.9 %collective-permute-start.27 = (bf16[32,640]{1,0:T(8,128)(2,1)S(1)}, bf16[32,640]{1,0:T(8,128)(2,1)S(1)}, u32[]{:S(2)}, u32[]{:S(2)}) collective-permute-start(bf16[32,640]{1,0:T(8,128)(2,1)S(1)} %fusion.10), channel_id=1, source_target_pairs={{0,64},{1,65},{2,66},{3,67},{4,68},{5,69},{6,70},{7,71},{8,72},{9,... | collective-permute-start | bytes 122888 | tf_op jit(solution)/shard_map/ppermute | solution.py:103
  204.5 4.4 %collective-permute-start.28 = (bf16[32,640]{1,0:T(8,128)(2,1)S(1)}, bf16[32,640]{1,0:T(8,128)(2,1)S(1)}, u32[]{:S(2)}, u32[]{:S(2)}) collective-permute-start(bf16[32,640]{1,0:T(8,128)(2,1)S(1)} %fusion.17), channel_id=1, source_target_pairs={{0,192},{1,193},{2,194},{3,195},{4,196},{5,197},{6,198},{7,199},{8... | collective-permute-start | bytes 122888 | tf_op jit(solution)/shard_map/ppermute | solution.py:103
  209.0 5.0 %collective-permute-start.29 = (bf16[32,640]{1,0:T(8,128)(2,1)S(1)}, bf16[32,640]{1,0:T(8,128)(2,1)S(1)}, u32[]{:S(2)}, u32[]{:S(2)}) collective-permute-start(bf16[32,640]{1,0:T(8,128)(2,1)S(1)} %fusion.11), channel_id=1, source_target_pairs={{0,12},{1,13},{2,14},{3,15},{4,24},{5,25},{6,26},{7,27},{8,20},{9,... | collective-permute-start | bytes 122888 | tf_op jit(solution)/shard_map/ppermute | solution.py:103
  214.0 8.9 %copy-start.3 = (f32[32,640]{1,0:T(8,128)}, f32[32,640]{1,0:T(8,128)S(1)}, u32[]{:S(2)}) copy-start(f32[32,640]{1,0:T(8,128)S(1)} %convert_add_fusion.smine_ref) | copy-start | bytes 245764
  214.0 8.9 %collective-permute-start.30 = (f32[32,640]{1,0:T(8,128)S(1)}, f32[32,640]{1,0:T(8,128)S(1)}, u32[]{:S(2)}, u32[]{:S(2)}) collective-permute-start(f32[32,640]{1,0:T(8,128)S(1)} %convert_add_fusion.smine_ref), channel_id=1, source_target_pairs={{0,32},{32,0},{1,33},{33,1},{2,34},{34,2},{3,35},{35,3},{4,36},{36... | collective-permute-start | bytes 245768 | tf_op jit(solution)/shard_map/ppermute | solution.py:105
  222.9 0.6 copy-start.6

commit v2 on v1

v2 whole, which is shorter than its diff:
```python
import jax
import jax.numpy as jnp
from jax import lax
from jax.experimental import pallas as pl
from jax.experimental.pallas import tpu as pltpu
from jax.sharding import Mesh
from jax.sharding import PartitionSpec as P

STEPS = 3
Y, CORE, Z, X = 4, 2, 8, 4
ROWS = ("y", "core")
COLS = ("z", "x")
ALL = ("y", "core", "z", "x")
EPS = 1e-06
BF = jnp.bfloat16
F32 = jnp.float32


def padded(x, sides, width, wrap):
    for axis, dim in sides:
        count, length = (lax.axis_size(axis), x.shape[dim])
        up = [(i, (i + 1) % count) for i in range(count if wrap else count - 1)]
        down = [(j, i) for i, j in up]
        last = lax.slice_in_dim(x, length - width, length, axis=dim)
        initial = lax.slice_in_dim(x, 0, width, axis=dim)
        before = lax.ppermute(last, axis, up)
        after = lax.ppermute(initial, axis, down)
        x = jnp.concatenate([before, x, after], axis=dim)
    return x


def filter_columns(widened, column_taps, extent):
    summed = jnp.zeros((widened.shape[0], extent, widened.shape[2]), jnp.float32)
    for offset in range(column_taps.shape[0]):
        summed = summed + column_taps[offset] * widened[:, offset : offset + extent, :].astype(
            jnp.float32
        )
    return summed


def filter_rows(extended, row_taps, extent):
    summed = jnp.zeros((extent, extended.shape[1], extended.shape[2]), jnp.float32)
    for offset in range(row_taps.shape[0]):
        summed = summed + row_taps[offset] * extended[offset : offset + extent].astype(jnp.float32)
    return summed


def pair_4a(i):
    return i ^ 1


def pair_4b(i):
    return 3 - i


def pair_8a(i):
    return i ^ 1


def pair_8b(i):
    return (i + 1) % 8 if i % 2 else (i - 1) % 8


def pair_8c(i):
    return (3, 6, 5, 0, 7, 2, 1, 4)[i]


ROUNDS = [
    ("x", pair_4a), ("x", pair_4b), ("y", pair_4a), ("y", pair_4b),
    ("z", pair_8a), ("z", pair_8b), ("z", pair_8c),
]


def round_pairs(axis, rule):
    pairs = []
    for y in range(Y):
        for z in range(Z):
            for x in range(X):
                at = {"y": y, "z": z, "x": x}
                to = dict(at)
                to[axis] = rule(at[axis])
                flat = [((p["y"] * CORE + 1) * Z + p["z"]) * X + p["x"] for p in (at, to)]
                pairs.append(tuple(flat))
    return pairs


def summed_over_all(part):
    total = part + lax.ppermute(part.astype(BF), "core", [(0, 1)]).astype(F32)
    for axis, rule in ROUNDS:
        total = lax.optimization_barrier(total)
        got = lax.ppermute(total.astype(BF), ALL, round_pairs(axis, rule))
        total = total + got.astype(F32)
    return total, lax.ppermute(total, "core", [(1, 0)])


def split3(a):
    hi = a.astype(BF)
    return hi, (a - hi.astype(F32)).astype(BF)


def dot(a, b, dims):
    return lax.dot_general(a, b, (dims, ((), ())), preferred_element_type=F32)


def dot3(a, b, dims):
    ah, al = split3(a)
    bh, bl = split3(b)
    return dot(ah, bh, dims) + (dot(ah, bl, dims) + dot(al, bh, dims))


NN = ((1,), (0,))
NT = ((1,), (1,))
TN = ((0,), (0,))


def coeffs_of(basis, coeffs, numerator):
    gram = dot3(basis, basis, NT)
    return coeffs * numerator / (dot3(gram, coeffs, NN) + EPS)


def emit_sums(coeffs, feature, sums_ref):
    c = feature.shape[1]
    sums_ref[:, :c] = dot(coeffs.astype(BF), feature, NN)
    gram = dot3(coeffs, coeffs, NT)
    sums_ref[:, c:] = jnp.concatenate([gram, jnp.zeros_like(gram)], axis=1)


def first_kernel(mixed_ref, w_ref, basis_ref, feature_ref, coeffs_ref, sums_ref):
    feature = jnp.maximum(dot(mixed_ref[...], w_ref[...], NN), 0.0).astype(BF)
    feature_ref[...] = feature
    basis = basis_ref[...]
    scores = dot(basis.astype(BF), feature, NT)
    e = jnp.exp(scores - jnp.max(scores, axis=0, keepdims=True))
    soft = e / jnp.sum(e, axis=0, keepdims=True)
    coeffs = coeffs_of(basis, soft, scores)
    coeffs_ref[...] = coeffs
    emit_sums(coeffs, feature, sums_ref)


def updated_basis(core_ref, own_ref, got_ref, basis):
    both = jnp.where(core_ref[0] == 1, own_ref[...], got_ref[...])
    r, c = basis.shape
    gram = both[:, c : c + r]
    return basis * both[:, :c] / (dot3(gram, basis, TN) + EPS)


def step_kernel(
    core_ref, own_ref, got_ref, basis_ref, feature_ref, coeffs_ref,
    newbasis_ref, newcoeffs_ref, sums_ref,
):
    basis = updated_basis(core_ref, own_ref, got_ref, basis_ref[...])
    newbasis_ref[...] = basis
    feature = feature_ref[...]
    coeffs = coeffs_of(basis, coeffs_ref[...], dot(basis.astype(BF), feature, NT))
    newcoeffs_ref[...] = coeffs
    emit_sums(coeffs, feature, sums_ref)


def last_kernel(
    core_ref, own_ref, got_ref, basis_ref, feature_ref, coeffs_ref, wham_ref, walign_ref, out_ref
):
    basis = updated_basis(core_ref, own_ref, got_ref, basis_ref[...])
    feature = feature_ref[...]
    low = basis.astype(BF)
    coeffs = coeffs_of(basis, coeffs_ref[...], dot(low, feature, NT))
    rebuilt = dot(coeffs.astype(BF), low, TN).astype(BF)
    hammed = jnp.maximum(feature.astype(F32) + dot(rebuilt, wham_ref[...], NN), 0.0).astype(BF)
    out_ref[...] = dot(hammed, walign_ref[...], NN).astype(BF)


def call(kernel, outs, *args):
    scalar, whole = pl.BlockSpec(memory_space=pltpu.SMEM), pl.BlockSpec(memory_space=pltpu.VMEM)
    specs = [scalar if a.dtype == jnp.int32 else whole for a in args]
    return pl.pallas_call(
        kernel,
        out_shape=outs,
        in_specs=specs,
        out_specs=jax.tree.map(lambda _: pl.BlockSpec(memory_space=pltpu.VMEM), outs),
        compiler_params=pltpu.CompilerParams(vmem_limit_bytes=24 * 2**20),
    )(*args)


def on_device(band_input, column_taps, row_taps, w_squeeze, bases_init, w_ham, w_align):
    tile_rows, tile_cols, channels = band_input.shape
    margin = column_taps.shape[0] // 2
    core = lax.axis_index("core").astype(jnp.int32).reshape(1)
    framed = padded(band_input, ((ROWS, 0), (COLS, 1)), margin, False)
    col_filtered = filter_columns(framed, column_taps, tile_cols).astype(jnp.bfloat16)
    strip_sum = filter_rows(col_filtered, row_taps, tile_rows)
    mixed_tile = (
        (band_input.astype(jnp.float32) + strip_sum)
        .astype(jnp.bfloat16)
        .reshape(tile_rows * tile_cols, channels)
    )
    n, r = tile_rows * tile_cols, bases_init.shape[1]
    sds = jax.ShapeDtypeStruct
    sums = [sds((r, channels + 128), F32)]
    basis = bases_init.T
    feature, coeffs, part = call(
        first_kernel,
        [sds((n, channels), BF), sds((r, n), F32)] + sums,
        mixed_tile, w_squeeze, basis,
    )
    for _ in range(STEPS - 1):
        own, got = summed_over_all(part)
        basis, coeffs, part = call(
            step_kernel,
            [sds((r, channels), F32), sds((r, n), F32)] + sums,
            core, own, got, basis, feature, coeffs,
        )
    own, got = summed_over_all(part)
    head_out = call(
        last_kernel,
        sds((n, channels), BF),
        core, own, got, basis, feature, coeffs, w_ham, w_align,
    )
    return head_out.reshape(tile_rows, tile_cols, channels)


def solution(mesh):
    split = Mesh(mesh.devices.reshape(Y, CORE, Z, X), ALL)
    in_specs = (P(ROWS, COLS, None), P(), P(), P(), P(), P(), P())
    out_specs = P(ROWS, COLS, None)
    return jax.shard_map(
        on_device, mesh=split, in_specs=in_specs, out_specs=out_specs, check_vma=False
    )
```

time: 232 us -> 241 us (1.039)
  starting transfers between devices: 82 us -> 104 us
  waiting for transfers between devices: 74.7 us -> 85.8 us
  other arithmetic: 43.4 us -> 32.9 us
  Pallas kernels: 22.5 us -> 13.1 us
  local copies, waits for them, and re-layouts: 8.47 us -> 4.33 us
    ppermute x27, starting transfers between devices: 70.8 us -> 92.2 us  [the longest x21 84.3 us: summed_over_all(): got = lax.ppermute(total.astype(BF), ALL, round_pairs(axis, rule))]
    ppermute x27, waiting for transfers between devices: 50 us -> 61.3 us  [the longest x21 52.8 us: summed_over_all(): got = lax.ppermute(total.astype(BF), ALL, round_pairs(axis, rule))]
    convert_element_type x21 -> x24, other arithmetic: 11.1 us -> 0.29 us  [the longest x21 0.25 us: summed_over_all(): got = lax.ppermute(total.astype(BF), ALL, round_pairs(axis, rule))]
    pallas_call x4, Pallas kernels: 22.5 us -> 13.1 us  [call(): pl.pallas_call(kernel, out_shape=outs, in_specs=specs, out_specs=jax.tree...]
where the time goes in v2:
time: 241 us; the launch traced here: 240 us
  starting transfers between devices  104 us (43%)
  waiting for transfers between devices  85.8 us (36%)
  other arithmetic  32.9 us (14%)
  Pallas kernels  13.1 us (5%)
  local copies, waits for them, and re-layouts  4.33 us (2%)
    ppermute x21, starting transfers between devices, summed_over_all(): got = lax.ppermute(total.astype(BF), ALL, round_pairs(axis, rule))  84.3 us
    ppermute x21, waiting for transfers between devices, summed_over_all(): got = lax.ppermute(total.astype(BF), ALL, round_pairs(axis, rule))  52.8 us
    ppermute x2, waiting for transfers between devices, padded(): before = lax.ppermute(last, axis, up)  15.8 us
    convert_element_type x1, other arithmetic, on_device(): mixed_tile = (band_input.astype(jnp.float32) + strip_sum).astype(jnp.bflo...  14.4 us
    convert_element_type x1, other arithmetic, on_device(): filter_columns(framed, column_taps, tile_cols).astype(jnp.bfloat16)  13.4 us
    pallas_call x4, Pallas kernels, call(): pl.pallas_call(kernel, out_shape=outs, in_specs=specs, out_specs=jax.tree...  13.1 us
    ppermute x2, waiting for transfers between devices, padded(): after = lax.ppermute(initial, axis, down)  8.71 us
    ppermute x2, starting transfers between devices, padded(): before = lax.ppermute(last, axis, up)  8.05 us
  transfers between devices with their start and end apart: 31, of which 31 were waited for; matrix products, arithmetic and copies ran while one was open for 0% of the time, Pallas kernels for 0%

profile of v2, /device:TPU:1, one launch (start us, length us, event | category | flops | bytes accessed | tf_op | source)
XLA Modules:
  0.0 240.5 jit_solution(16192952039908753235)
XLA Ops:
  0.0 2.8 %copy.8 = bf16[64,32,512]{2,0,1:T(8,128)(2,1)S(1)} copy(bf16[64,32,512]{2,1,0:T(8,128)(2,1)} %param.7) | data formatting | bytes 4194304 | tf_op args[0]
  2.9 4.6 %collective-permute-start = (bf16[10,32,512]{2,0,1:T(8,128)(2,1)S(1)}, bf16[10,32,512]{2,0,1:T(8,128)(2,1)S(1)}, u32[]{:S(2)}, u32[]{:S(2)}) collective-permute-start(bf16[10,32,512]{2,0,1:T(8,128)(2,1)S(1)} %get-tuple-element.27), channel_id=1, source_target_pairs={{0,32},{32,64},{64,96},{96,128},{128,160},{160,192},{192,224},{1,3... | collective-permute-start | bytes 983048 | tf_op jit(solution)/shard_map/ppermute | solution.py:26
  7.6 2.1 collective-permute-start.1
  9.6 4.0 %collective-permute-done = bf16[10,32,512]{2,0,1:T(8,128)(2,1)S(1)} collective-permute-done((bf16[10,32,512]{2,0,1:T(8,128)(2,1)S(1)}, bf16[10,32,512]{2,0,1:T(8,128)(2,1)S(1)}, u32[]{:S(2)}, u32[]{:S(2)}) %collective-permute-start) | collective-permute-done | bytes 327712 | tf_op jit(solution)/shard_map/ppermute | solution.py:26
  13.6 4.6 %collective-permute-done.1 = bf16[10,32,512]{2,0,1:T(8,128)(2,1)S(1)} collective-permute-done((bf16[10,32,512]{2,0,1:T(8,128)(2,1)S(1)}, bf16[10,32,512]{2,0,1:T(8,128)(2,1)S(1)}, u32[]{:S(2)}, u32[]{:S(2)}) %collective-permute-start.1) | collective-permute-done | bytes 327712 | tf_op jit(solution)/shard_map/ppermute | solution.py:27
  19.9 3.5 %collective-permute-start.2 = (bf16[84,10,512]{2,0,1:T(8,128)(2,1)S(1)}, bf16[84,10,512]{2,0,1:T(8,128)(2,1)S(1)}, u32[]{:S(2)}, u32[]{:S(2)}) collective-permute-start(bf16[84,10,512]{2,0,1:T(8,128)(2,1)S(1)} %get-tuple-element.25), channel_id=1, source_target_pairs={{0,1},{1,2},{2,3},{3,4},{4,5},{5,6},{6,7},{7,8},{8,9},{9,10},{10,1... | collective-permute-start | bytes 2580488 | tf_op jit(solution)/shard_map/ppermute | solution.py:26
  24.8 11.8 %collective-permute-done.2 = bf16[84,10,512]{2,0,1:T(8,128)(2,1)S(1)} collective-permute-done((bf16[84,10,512]{2,0,1:T(8,128)(2,1)S(1)}, bf16[84,10,512]{2,0,1:T(8,128)(2,1)S(1)}, u32[]{:S(2)}, u32[]{:S(2)}) %collective-permute-start.2) | collective-permute-done | bytes 860192 | tf_op jit(solution)/shard_map/ppermute | solution.py:26
  36.6 4.2 %collective-permute-done.3 = bf16[84,10,512]{2,0,1:T(8,128)(2,1)S(1)} collective-permute-done((bf16[84,10,512]{2,0,1:T(8,128)(2,1)S(1)}, bf16[84,10,512]{2,0,1:T(8,128)(2,1)S(1)}, u32[]{:S(2)}, u32[]{:S(2)}) %collective-permute-start.3) | collective-permute-done | bytes 860192 | tf_op jit(solution)/shard_map/ppermute | solution.py:27
  40.7 2.8 %maximum_maximum_fusion = (bf16[84,42,512]{2,0,1:T(8,128)(2,1)S(1)}, bf16[84,42,512]{2,0,1:T(8,128)(2,1)S(1)}) fusion(bf16[10,32,512]{2,0,1:T(8,128)(2,1)S(1)} %collective-permute-done.1, bf16[64,32,512]{2,0,1:T(8,128)(2,1)S(1)} %copy.8, bf16[10,32,512]{2,0,1:T(8,128)(2,1)S(1)} %collective-permute-done, bf16[84,10,512]{2,0,1:T(8,128)(2,1)S(1)} %collective-permute-done.2, ...), kind=kLoop, calls=%fused_computation.2 | loop fusion | flops 28901376 | bytes 11698176 | tf_op jit(solution)/shard_map/concatenate | solution.py:28
  43.6 13.4 %add_convert_fusion = bf16[84,32,512]{2,0,1:T(8,128)(2,1)S(1)} fusion(bf16[84,42,512]{2,0,1:T(8,128)(2,1)S(1)} %get-tuple-element.24, bf16[84,42,512]{2,0,1:T(8,128)(2,1)S(1)} %get-tuple-element.23, f32[512]{0:T(512)S(1)} %bitcast.69, f32[512]{0:T(512)S(1)} %bitcast.68, f32[512]{0:T(512)S(1)} %bitcast.50, f32[512]{0:T(512)S(1)} %bitcast.51, ...), kind=kLoop, calls=%fused_computation | loop fusion | flops 93585408 | bytes 60598272 | tf_op jit(solution)/shard_map/convert_element_type | solution.py:188
  57.0 14.4 %add_convert_fusion.1 = bf16[64,32,512]{2,0,1:T(8,128)(2,1)S(1)} fusion(bf16[84,32,512]{2,0,1:T(8,128)(2,1)S(1)} %add_convert_fusion, f32[512]{0:T(512)S(1)} %bitcast.90, f32[512]{0:T(512)S(1)} %bitcast.89, f32[512]{0:T(512)S(1)} %bitcast.71, f32[512]{0:T(512)S(1)} %bitcast.72, f32[512]{0:T(512)S(1)} %bitcast.73, f32[512]{0:T(512)S(1)} %bitcast.74, ...), kind=kLoop, calls=%fused_computation.1 | loop fusion | flops 68157440 | bytes 48277504 | tf_op jit(solution)/shard_map/convert_element_type | solution.py:192
  72.6 3.0 %shard_map.73 = (bf16[2048,512]{1,0:T(8,128)(2,1)S(1)}, f32[64,2048]{1,0:T(8,128)S(1)}, f32[64,640]{1,0:T(8,128)S(1)}) custom-call(bf16[2048,512]{1,0:T(8,128)(2,1)S(1)} %bitcast.46, bf16[512,512]{1,0:T(8,128)(2,1)S(1)} %copy-done.2, f32[64,512]{1,0:T(8,128)S(1)} %bitcast.47), custom_call_target="tpu_custom_call" | custom-call | tf_op jit(solution)/shard_map/pallas_call | solution.py:174
  78.9 3.1 %collective-permute-start.5 = (bf16[64,640]{1,0:T(8,128)(2,1)S(1)}, bf16[64,640]{1,0:T(8,128)(2,1)S(1)}, u32[]{:S(2)}, u32[]{:S(2)}) collective-permute-start(bf16[64,640]{1,0:T(8,128)(2,1)S(1)} %convert_element_type.326), channel_id=1, source_target_pairs={{32,33},{33,32},{34,35},{35,34},{36,37},{37,36},{38,39},{39,38},{4... | collective-permute-start | bytes 245768 | tf_op jit(solution)/shard_map/ppermute | solution.py:91
  81.9 2.1 collective-permute-done.5
  84.1 6.8 %collective-permute-start.6 = (bf16[64,640]{1,0:T(8,128)(2,1)S(1)}, bf16[64,640]{1,0:T(8,128)(2,1)S(1)}, u32[]{:S(2)}, u32[]{:S(2)}) collective-permute-start(bf16[64,640]{1,0:T(8,128)(2,1)S(1)} %convert_element_type.328), channel_id=1, source_target_pairs={{32,35},{33,34},{34,33},{35,32},{36,39},{37,38},{38,37},{39,36},{4... | collective-permute-start | bytes 245768 | tf_op jit(solution)/shard_map/ppermute | solution.py:91
  92.7 8.5 %collective-permute-start.7 = (bf16[64,640]{1,0:T(8,128)(2,1)S(1)}, bf16[64,640]{1,0:T(8,128)(2,1)S(1)}, u32[]{:S(2)}, u32[]{:S(2)}) collective-permute-start(bf16[64,640]{1,0:T(8,128)(2,1)S(1)} %convert_element_type.330), channel_id=1, source_target_pairs={{32,96},{33,97},{34,98},{35,99},{36,100},{37,101},{38,102},{39,103... | collective-permute-start | bytes 245768 | tf_op jit(solution)/shard_map/ppermute | solution.py:91
  103.2 3.8 %collective-permute-start.8 = (bf16[64,640]{1,0:T(8,128)(2,1)S(1)}, bf16[64,640]{1,0:T(8,128)(2,1)S(1)}, u32[]{:S(2)}, u32[]{:S(2)}) collective-permute-start(bf16[64,640]{1,0:T(8,128)(2,1)S(1)} %convert_element_type.332), channel_id=1, source_target_pairs={{32,224},{33,225},{34,226},{35,227},{36,228},{37,229},{38,230},{39... | collective-permute-start | bytes 245768 | tf_op jit(solution)/shard_map/ppermute | solution.py:91
  107.0 2.6 %collective-permute-done.8 = bf16[64,640]{1,0:T(8,128)(2,1)S(1)} collective-permute-done((bf16[64,640]{1,0:T(8,128)(2,1)S(1)}, bf16[64,640]{1,0:T(8,128)(2,1)S(1)}, u32[]{:S(2)}, u32[]{:S(2)}) %collective-permute-start.8) | collective-permute-done | bytes 81952 | tf_op jit(solution)/shard_map/ppermute | solution.py:91
  109.6 3.5 %collective-permute-start.9 = (bf16[64,640]{1,0:T(8,128)(2,1)S(1)}, bf16[64,640]{1,0:T(8,128)(2,1)S(1)}, u32[]{:S(2)}, u32[]{:S(2)}) collective-permute-start(bf16[64,640]{1,0:T(8,128)(2,1)S(1)} %convert_element_type.334), channel_id=1, source_target_pairs={{32,36},{33,37},{34,38},{35,39},{36,32},{37,33},{38,34},{39,35},{4... | collective-permute-start | bytes 245768 | tf_op jit(solution)/shard_map/ppermute | solution.py:91
  115.0 5.7 %collective-permute-start.10 = (bf16[64,640]{1,0:T(8,128)(2,1)S(1)}, bf16[64,640]{1,0:T(8,128)(2,1)S(1)}, u32[]{:S(2)}, u32[]{:S(2)}) collective-permute-start(bf16[64,640]{1,0:T(8,128)(2,1)S(1)} %convert_element_type.336), channel_id=1, source_target_pairs={{32,60},{33,61},{34,62},{35,63},{36,40},{37,41},{38,42},{39,43},{4... | collective-permute-start | bytes 245768 | tf_op jit(solution)/shard_map/ppermute | solution.py:91
  122.5 7.4 %collective-permute-start.11 = (bf16[64,640]{1,0:T(8,128)(2,1)S(1)}, bf16[64,640]{1,0:T(8,128)(2,1)S(1)}, u32[]{:S(2)}, u32[]{:S(2)}) collective-permute-start(bf16[64,640]{1,0:T(8,128)(2,1)S(1)} %convert_element_type.338), channel_id=1, source_target_pairs={{32,44},{33,45},{34,46},{35,47},{36,56},{37,57},{38,58},{39,59},{4... | collective-permute-start | bytes 245768 | tf_op jit(solution)/shard_map/ppermute | solution.py:91
  134.1 2.2 shard_map.74
  139.5 1.9 collective-permute-start.14
  141.4 3.3 %collective-permute-done.14 = bf16[64,640]{1,0:T(8,128)(2,1)S(1)} collective-permute-done((bf16[64,640]{1,0:T(8,128)(2,1)S(1)}, bf16[64,640]{1,0:T(8,128)(2,1)S(1)}, u32[]{:S(2)}, u32[]{:S(2)}) %collective-permute-start.14) | collective-permute-done | bytes 81952 | tf_op jit(solution)/shard_map/ppermute | solution.py:91
  144.7 4.6 %collective-permute-start.15 = (bf16[64,640]{1,0:T(8,128)(2,1)S(1)}, bf16[64,640]{1,0:T(8,128)(2,1)S(1)}, u32[]{:S(2)}, u32[]{:S(2)}) collective-permute-start(bf16[64,640]{1,0:T(8,128)(2,1)S(1)} %convert_element_type.344), channel_id=1, source_target_pairs={{32,35},{33,34},{34,33},{35,32},{36,39},{37,38},{38,37},{39,36},{4... | collective-permute-start | bytes 245768 | tf_op jit(solution)/shard_map/ppermute | solution.py:91
  151.1 2.2 collective-permute-start.16
  153.3 3.0 %collective-permute-done.16 = bf16[64,640]{1,0:T(8,128)(2,1)S(1)} collective-permute-done((bf16[64,640]{1,0:T(8,128)(2,1)S(1)}, bf16[64,640]{1,0:T(8,128)(2,1)S(1)}, u32[]{:S(2)}, u32[]{:S(2)}) %collective-permute-start.16) | collective-permute-done | bytes 81952 | tf_op jit(solution)/shard_map/ppermute | solution.py:91
  156.4 3.8 %collective-permute-start.17 = (bf16[64,640]{1,0:T(8,128)(2,1)S(1)}, bf16[64,640]{1,0:T(8,128)(2,1)S(1)}, u32[]{:S(2)}, u32[]{:S(2)}) collective-permute-start(bf16[64,640]{1,0:T(8,128)(2,1)S(1)} %convert_element_type.348), channel_id=1, source_target_pairs={{32,224},{33,225},{34,226},{35,227},{36,228},{37,229},{38,230},{39... | collective-permute-start | bytes 245768 | tf_op jit(solution)/shard_map/ppermute | solution.py:91
  160.2 2.6 %collective-permute-done.17 = bf16[64,640]{1,0:T(8,128)(2,1)S(1)} collective-permute-done((bf16[64,640]{1,0:T(8,128)(2,1)S(1)}, bf16[64,640]{1,0:T(8,128)(2,1)S(1)}, u32[]{:S(2)}, u32[]{:S(2)}) %collective-permute-start.17) | collective-permute-done | bytes 81952 | tf_op jit(solution)/shard_map/ppermute | solution.py:91
  162.8 3.7 %collective-permute-start.18 = (bf16[64,640]{1,0:T(8,128)(2,1)S(1)}, bf16[64,640]{1,0:T(8,128)(2,1)S(1)}, u32[]{:S(2)}, u32[]{:S(2)}) collective-permute-start(bf16[64,640]{1,0:T(8,128)(2,1)S(1)} %convert_element_type.350), channel_id=1, source_target_pairs={{32,36},{33,37},{34,38},{35,39},{36,32},{37,33},{38,34},{39,35},{4... | collective-permute-start | bytes 245768 | tf_op jit(solution)/shard_map/ppermute | solution.py:91
  168.4 2.1 collective-permute-start.19
  170.5 4.3 %collective-permute-done.19 = bf16[64,640]{1,0:T(8,128)(2,1)S(1)} collective-permute-done((bf16[64,640]{1,0:T(8,128)(2,1)S(1)}, bf16[64,640]{1,0:T(8,128)(2,1)S(1)}, u32[]{:S(2)}, u32[]{:S(2)}) %collective-permute-start.19) | collective-permute-done | bytes 81952 | tf_op jit(solution)/shard_map/ppermute | solution.py:91
  174.8 4.8 %collective-permute-start.20 = (bf16[64,640]{1,0:T(8,128)(2,1)S(1)}, bf16[64,640]{1,0:T(8,128)(2,1)S(1)}, u32[]{:S(2)}, u32[]{:S(2)}) collective-permute-start(bf16[64,640]{1,0:T(8,128)(2,1)S(1)} %convert_element_type.354), channel_id=1, source_target_pairs={{32,44},{33,45},{34,46},{35,47},{36,56},{37,57},{38,58},{39,59},{4... | collective-permute-start | bytes 245768 | tf_op jit(solution)/shard_map/ppermute | solution.py:91
  179.7 2.1 collective-permute-done.20
  184.1 2.2 shard_map.75
  189.6 1.9 collective-permute-start.23
  191.5 3.3 %collective-permute-done.23 = bf16[64,640]{1,0:T(8,128)(2,1)S(1)} collective-permute-done((bf16[64,640]{1,0:T(8,128)(2,1)S(1)}, bf16[64,640]{1,0:T(8,128)(2,1)S(1)}, u32[]{:S(2)}, u32[]{:S(2)}) %collective-permute-start.23) | collective-permute-done | bytes 81952 | tf_op jit(solution)/shard_map/ppermute | solution.py:91
  194.8 4.6 %collective-permute-start.24 = (bf16[64,640]{1,0:T(8,128)(2,1)S(1)}, bf16[64,640]{1,0:T(8,128)(2,1)S(1)}, u32[]{:S(2)}, u32[]{:S(2)}) collective-permute-start(bf16[64,640]{1,0:T(8,128)(2,1)S(1)} %convert_element_type.360), channel_id=1, source_target_pairs={{32,35},{33,34},{34,33},{35,32},{36,39},{37,38},{38,37},{39,36},{4... | collective-permute-start | bytes 245768 | tf_op jit(solution)/shard_map/ppermute | solution.py:91
  201.2 1.9 collective-permute-start.25
  203.1 3.3 %collective-permute-done.25 = bf16[64,640]{1,0:T(8,128)(2,1)S(1)} collective-permute-done((bf16[64,640]{1,0:T(8,128)(2,1)S(1)}, bf16[64,640]{1,0:T(8,128)(2,1)S(1)}, u32[]{:S(2)}, u32[]{:S(2)}) %collective-permute-start.25) | collective-permute-done | bytes 81952 | tf_op jit(solution)/shard_map/ppermute | solution.py:91
  206.4 3.8 %collective-permute-start.26 = (bf16[64,640]{1,0:T(8,128)(2,1)S(1)}, bf16[64,640]{1,0:T(8,128)(2,1)S(1)}, u32[]{:S(2)}, u32[]{:S(2)}) collective-permute-start(bf16[64,640]{1,0:T(8,128)(2,1)S(1)} %convert_element_type.364), channel_id=1, source_target_pairs={{32,224},{33,225},{34,226},{35,227},{36,228},{37,229},{38,230},{39... | collective-permute-start | bytes 245768 | tf_op jit(solution)/shard_map/ppermute | solution.py:91
  210.3 2.6 %collective-permute-done.26 = bf16[64,640]{1,0:T(8,128)(2,1)S(1)} collective-permute-done((bf16[64,640]{1,0:T(8,128)(2,1)S(1)}, bf16[64,640]{1,0:T(8,128)(2,1)S(1)}, u32[]{:S(2)}, u32[]{:S(2)}) %collective-permute-start.26) | collective-permute-done | bytes 81952 | tf_op jit(solution)/shard_map/ppermute | solution.py:91
  212.9 4.2 %collective-permute-start.27 = (bf16[64,640]{1,0:T(8,128)(2,1)S(1)}, bf16[64,640]{1,0:T(8,128)(2,1)S(1)}, u32[]{:S(2)}, u32[]{:S(2)}) collective-permute-start(bf16[64,640]{1,0:T(8,128)(2,1)S(1)} %convert_element_type.366), channel_id=1, source_target_pairs={{32,36},{33,37},{34,38},{35,39},{36,32},{37,33},{38,34},{39,35},{4... | collective-permute-start | bytes 245768 | tf_op jit(solution)/shard_map/ppermute | solution.py:91
  219.0 1.9 collective-permute-start.28
  220.9 4.5 %collective-permute-done.28 = bf16[64,640]{1,0:T(8,128)(2,1)S(1)} collective-permute-done((bf16[64,640]{1,0:T(8,128)(2,1)S(1)}, bf16[64,640]{1,0:T(8,128)(2,1)S(1)}, u32[]{:S(2)}, u32[]{:S(2)}) %collective-permute-start.28) | collective-permute-done | bytes 81952 | tf_op jit(solution)/shard_map/ppermute | solution.py:91
  225.4 4.0 %collective-permute-start.29 = (bf16[64,640]{1,0:T(8,128)(2,1)S(1)}, bf16[64,640]{1,0:T(8,128)(2,1)S(1)}, u32[]{:S(2)}, u32[]{:S(2)}) collective-permute-start(bf16[64,640]{1,0:T(8,128)(2,1)S(1)} %convert_element_type.370), channel_id=1, source_target_pairs={{32,44},{33,45},{34,46},{35,47},{36,56},{37,57},{38,58},{39,59},{4... | collective-permute-start | bytes 245768 | tf_op jit(solution)/shard_map/ppermute | solution.py:91
  229.4 3.0 %collective-permute-done.29 = bf16[64,640]{1,0:T(8,128)(2,1)S(1)} collective-permute-done((bf16[64,640]{1,0:T(8,128)(2,1)S(1)}, bf16[64,640]{1,0:T(8,128)(2,1)S(1)}, u32[]{:S(2)}, u32[]{:S(2)}) %collective-permute-start.29) | collective-permute-done | bytes 81952 | tf_op jit(solution)/shard_map/ppermute | solution.py:91
  234.7 5.8 %shard_map.76 = bf16[2048,512]{1,0:T(8,128)(2,1)} custom-call(s32[1]{0:T(128)} %bitcast.core_ref, f32[64,640]{1,0:T(8,128)S(1)} %convert_add_fusion.own_ref, f32[64,640]{1,0:T(8,128)S(1)} %collective-permute-done.30.got_ref, f32[64,512]{1,0:T(8,128)S(1)} %get-tuple-element.21.basis_ref, bf16[2048,512]{1,0:T(8,128)(2,1)S(1)} %get-tuple-element.15.feature_ref, ...), custom_call_target="tpu_custom_call" | custom-call | tf_op jit(solution)/shard_map/pallas_call | solution.py:174
  (92 shorter events, 37.9 us)
Async XLA Ops:
  2.9 10.7 %collective-permute-start = (bf16[10,32,512]{2,0,1:T(8,128)(2,1)S(1)}, bf16[10,32,512]{2,0,1:T(8,128)(2,1)S(1)}, u32[]{:S(2)}, u32[]{:S(2)}) collective-permute-start(bf16[10,32,512]{2,0,1:T(8,128)(2,1)S(1)} %get-tuple-element.27), channel_id=1, source_target_pairs={{0,32},{32,64},{64,96},{96,128},{128,160},{160,192},{192,224},{1,3... | collective-permute-start | bytes 983048 | tf_op jit(solution)/shard_map/ppermute | solution.py:26
  7.5 17.1 %copy-start.5 = (f32[21,512]{1,0:T(8,128)S(1)}, f32[21,512]{1,0:T(8,128)}, u32[]{:S(2)}) copy-start(f32[21,512]{1,0:T(8,128)} %param.8) | copy-start | bytes 129028
  7.5 17.1 %copy-start.6 = (f32[21,512]{1,0:T(8,128)S(1)}, f32[21,512]{1,0:T(8,128)}, u32[]{:S(2)}) copy-start(f32[21,512]{1,0:T(8,128)} %param.9) | copy-start | bytes 129028
  7.6 10.6 %collective-permute-start.1 = (bf16[10,32,512]{2,0,1:T(8,128)(2,1)S(1)}, bf16[10,32,512]{2,0,1:T(8,128)(2,1)S(1)}, u32[]{:S(2)}, u32[]{:S(2)}) collective-permute-start(bf16[10,32,512]{2,0,1:T(8,128)(2,1)S(1)} %get-tuple-element.28), channel_id=1, source_target_pairs={{32,0},{64,32},{96,64},{128,96},{160,128},{192,160},{224,192},{33,... | collective-permute-start | bytes 983048 | tf_op jit(solution)/shard_map/ppermute | solution.py:27
  19.9 16.7 %collective-permute-start.2 = (bf16[84,10,512]{2,0,1:T(8,128)(2,1)S(1)}, bf16[84,10,512]{2,0,1:T(8,128)(2,1)S(1)}, u32[]{:S(2)}, u32[]{:S(2)}) collective-permute-start(bf16[84,10,512]{2,0,1:T(8,128)(2,1)S(1)} %get-tuple-element.25), channel_id=1, source_target_pairs={{0,1},{1,2},{2,3},{3,4},{4,5},{5,6},{6,7},{7,8},{8,9},{9,10},{10,1... | collective-permute-start | bytes 2580488 | tf_op jit(solution)/shard_map/ppermute | solution.py:26
  23.3 17.4 %collective-permute-start.3 = (bf16[84,10,512]{2,0,1:T(8,128)(2,1)S(1)}, bf16[84,10,512]{2,0,1:T(8,128)(2,1)S(1)}, u32[]{:S(2)}, u32[]{:S(2)}) collective-permute-start(bf16[84,10,512]{2,0,1:T(8,128)(2,1)S(1)} %get-tuple-element.26), channel_id=1, source_target_pairs={{1,0},{2,1},{3,2},{4,3},{5,4},{6,5},{7,6},{8,7},{9,8},{10,9},{11,1... | collective-permute-start | bytes 2580488 | tf_op jit(solution)/shard_map/ppermute | solution.py:27
  43.6 13.4 %copy-start.4 = (bf16[64,32,512]{2,1,0:T(8,128)(2,1)S(1)}, bf16[64,32,512]{2,1,0:T(8,128)(2,1)}, u32[]{:S(2)}) copy-start(bf16[64,32,512]{2,1,0:T(8,128)(2,1)} %param.7) | copy-start | bytes 6291460
  71.4 1.2 copy-start.2
  71.4 1.2 copy-start.3
  75.7 3.2 %collective-permute-start.4 = (bf16[64,640]{1,0:T(8,128)(2,1)S(1)}, bf16[64,640]{1,0:T(8,128)(2,1)S(1)}, u32[]{:S(2)}, u32[]{:S(2)}) collective-permute-start(bf16[64,640]{1,0:T(8,128)(2,1)S(1)} %convert_element_type.324), channel_id=1, source_target_pairs={{0,32},{1,33},{2,34},{3,35},{4,36},{5,37},{6,38},{7,39},{8,40},{9,... | collective-permute-start | bytes 245768 | tf_op jit(solution)/shard_map/ppermute | solution.py:88
  78.9 5.2 %collective-permute-start.5 = (bf16[64,640]{1,0:T(8,128)(2,1)S(1)}, bf16[64,640]{1,0:T(8,128)(2,1)S(1)}, u32[]{:S(2)}, u32[]{:S(2)}) collective-permute-start(bf16[64,640]{1,0:T(8,128)(2,1)S(1)} %convert_element_type.326), channel_id=1, source_target_pairs={{32,33},{33,32},{34,35},{35,34},{36,37},{37,36},{38,39},{39,38},{4... | collective-permute-start | bytes 245768 | tf_op jit(solution)/shard_map/ppermute | solution.py:91
  84.1 8.6 %collective-permute-start.6 = (bf16[64,640]{1,0:T(8,128)(2,1)S(1)}, bf16[64,640]{1,0:T(8,128)(2,1)S(1)}, u32[]{:S(2)}, u32[]{:S(2)}) collective-permute-start(bf16[64,640]{1,0:T(8,128)(2,1)S(1)} %convert_element_type.328), channel_id=1, source_target_pairs={{32,35},{33,34},{34,33},{35,32},{36,39},{37,38},{38,37},{39,36},{4... | collective-permute-start | bytes 245768 | tf_op jit(solution)/shard_map/ppermute | solution.py:91
  92.7 10.4 %collective-permute-start.7 = (bf16[64,640]{1,0:T(8,128)(2,1)S(1)}, bf16[64,640]{1,0:T(8,128)(2,1)S(1)}, u32[]{:S(2)}, u32[]{:S(2)}) collective-permute-start(bf16[64,640]{1,0:T(8,128)(2,1)S(1)} %convert_element_type.330), channel_id=1, source_target_pairs={{32,96},{33,97},{34,98},{35,99},{36,100},{37,101},{38,102},{39,103... | collective-permute-start | bytes 245768 | tf_op jit(solution)/shard_map/ppermute | solution.py:91
  103.2 6.4 %collective-permute-start.8 = (bf16[64,640]{1,0:T(8,128)(2,1)S(1)}, bf16[64,640]{1,0:T(8,128)(2,1)S(1)}, u32[]{:S(2)}, u32[]{:S(2)}) collective-permute-start(bf16[64,640]{1,0:T(8,128)(2,1)S(1)} %convert_element_type.332), channel_id=1, source_target_pairs={{32,224},{33,225},{34,226},{35,227},{36,228},{37,229},{38,230},{39... | collective-permute-start | bytes 245768 | tf_op jit(solution)/shard_map/ppermute | solution.py:91
  109.6 5.4 %collective-permute-start.9 = (bf16[64,640]{1,0:T(8,128)(2,1)S(1)}, bf16[64,640]{1,0:T(8,128)(2,1)S(1)}, u32[]{:S(2)}, u32[]{:S(2)}) collective-permute-start(bf16[64,640]{1,0:T(8,128)(2,1)S(1)} %convert_element_type.334), channel_id=1, source_target_pairs={{32,36},{33,37},{34,38},{35,39},{36,32},{37,33},{38,34},{39,35},{4... | collective-permute-start | bytes 245768 | tf_op jit(solution)/shard_map/ppermute | solution.py:91
  115.0 7.5 %collective-permute-start.10 = (bf16[64,640]{1,0:T(8,128)(2,1)S(1)}, bf16[64,640]{1,0:T(8,128)(2,1)S(1)}, u32[]{:S(2)}, u32[]{:S(2)}) collective-permute-start(bf16[64,640]{1,0:T(8,128)(2,1)S(1)} %convert_element_type.336), channel_id=1, source_target_pairs={{32,60},{33,61},{34,62},{35,63},{36,40},{37,41},{38,42},{39,43},{4... | collective-permute-start | bytes 245768 | tf_op jit(solution)/shard_map/ppermute | solution.py:91
  122.5 9.2 %collective-permute-start.11 = (bf16[64,640]{1,0:T(8,128)(2,1)S(1)}, bf16[64,640]{1,0:T(8,128)(2,1)S(1)}, u32[]{:S(2)}, u32[]{:S(2)}) collective-permute-start(bf16[64,640]{1,0:T(8,128)(2,1)S(1)} %convert_element_type.338), channel_id=1, source_target_pairs={{32,44},{33,45},{34,46},{35,47},{36,56},{37,57},{38,58},{39,59},{4... | collective-permute-start | bytes 245768 | tf_op jit(solution)/shard_map/ppermute | solution.py:91
  131.8 2.3 collective-permute-start.12
  136.3 3.2 %collective-permute-start.13 = (bf16[64,640]{1,0:T(8,128)(2,1)S(1)}, bf16[64,640]{1,0:T(8,128)(2,1)S(1)}, u32[]{:S(2)}, u32[]{:S(2)}) collective-permute-start(bf16[64,640]{1,0:T(8,128)(2,1)S(1)} %convert_element_type.340), channel_id=1, source_target_pairs={{0,32},{1,33},{2,34},{3,35},{4,36},{5,37},{6,38},{7,39},{8,40},{9,... | collective-permute-start | bytes 245768 | tf_op jit(solution)/shard_map/ppermute | solution.py:88
  139.5 5.2 %collective-permute-start.14 = (bf16[64,640]{1,0:T(8,128)(2,1)S(1)}, bf16[64,640]{1,0:T(8,128)(2,1)S(1)}, u32[]{:S(2)}, u32[]{:S(2)}) collective-permute-start(bf16[64,640]{1,0:T(8,128)(2,1)S(1)} %convert_element_type.342), channel_id=1, source_target_pairs={{32,33},{33,32},{34,35},{35,34},{36,37},{37,36},{38,39},{39,38},{4... | collective-permute-start | bytes 245768 | tf_op jit(solution)/shard_map/ppermute | solution.py:91
  144.7 6.4 %collective-permute-start.15 = (bf16[64,640]{1,0:T(8,128)(2,1)S(1)}, bf16[64,640]{1,0:T(8,128)(2,1)S(1)}, u32[]{:S(2)}, u32[]{:S(2)}) collective-permute-start(bf16[64,640]{1,0:T(8,128)(2,1)S(1)} %convert_element_type.344), channel_id=1, source_target_pairs={{32,35},{33,34},{34,33},{35,32},{36,39},{37,38},{38,37},{39,36},{4... | collective-permute-start | bytes 245768 | tf_op jit(solution)/shard_map/ppermute | solution.py:91
  151.1 5.2 %collective-permute-start.16 = (bf16[64,640]{1,0:T(8,128)(2,1)S(1)}, bf16[64,640]{1,0:T(8,128)(2,1)S(1)}, u32[]{:S(2)}, u32[]{:S(2)}) collective-permute-start(bf16[64,640]{1,0:T(8,128)(2,1)S(1)} %convert_element_type.346), channel_id=1, source_target_pairs={{32,96},{33,97},{34,98},{35,99},{36,100},{37,101},{38,102},{39,103... | collective-permute-start | bytes 245768 | tf_op jit(solution)/shard_map/ppermute | solution.py:91
  156.4 6.4 %collective-permute-start.17 = (bf16[64,640]{1,0:T(8,128)(2,1)S(1)}, bf16[64,640]{1,0:T(8,128)(2,1)S(1)}, u32[]{:S(2)}, u32[]{:S(2)}) collective-permute-start(bf16[64,640]{1,0:T(8,128)(2,1)S(1)} %convert_element_type.348), channel_id=1, source_target_pairs={{32,224},{33,225},{34,226},{35,227},{36,228},{37,229},{38,230},{39... | collective-permute-start | bytes 245768 | tf_op jit(solution)/shard_map/ppermute | solution.py:91
  162.8 5.5 %collective-permute-start.18 = (bf16[64,640]{1,0:T(8,128)(2,1)S(1)}, bf16[64,640]{1,0:T(8,128)(2,1)S(1)}, u32[]{:S(2)}, u32[]{:S(2)}) collective-permute-start(bf16[64,640]{1,0:T(8,128)(2,1)S(1)} %convert_element_type.350), channel_id=1, source_target_pairs={{32,36},{33,37},{34,38},{35,39},{36,32},{37,33},{38,34},{39,35},{4... | collective-permute-start | bytes 245768 | tf_op jit(solution)/shard_map/ppermute | solution.py:91
  168.4 6.4 %collective-permute-start.19 = (bf16[64,640]{1,0:T(8,128)(2,1)S(1)}, bf16[64,640]{1,0:T(8,128)(2,1)S(1)}, u32[]{:S(2)}, u32[]{:S(2)}) collective-permute-start(bf16[64,640]{1,0:T(8,128)(2,1)S(1)} %convert_element_type.352), channel_id=1, source_target_pairs={{32,60},{33,61},{34,62},{35,63},{36,40},{37,41},{38,42},{39,43},{4... | collective-permute-start | bytes 245768 | tf_op jit(solution)/shard_map/ppermute | solution.py:91
  174.8 7.0 %collective-permute-start.20 = (bf16[64,640]{1,0:T(8,128)(2,1)S(1)}, bf16[64,640]{1,0:T(8,128)(2,1)S(1)}, u32[]{:S(2)}, u32[]{:S(2)}) collective-permute-start(bf16[64,640]{1,0:T(8,128)(2,1)S(1)} %convert_element_type.354), channel_id=1, source_target_pairs={{32,44},{33,45},{34,46},{35,47},{36,56},{37,57},{38,58},{39,59},{4... | collective-permute-start | bytes 245768 | tf_op jit(solution)/shard_map/ppermute | solution.py:91
  181.8 2.3 collective-permute-start.21
  184.1 50.6 %copy-start = (bf16[512,512]{1,0:T(8,128)(2,1)S(1)}, bf16[512,512]{1,0:T(8,128)(2,1)}, u32[]{:S(2)}) copy-start(bf16[512,512]{1,0:T(8,128)(2,1)} %wham_ref.1) | copy-start | bytes 1572868
  184.1 50.6 %copy-start.1 = (bf16[512,512]{1,0:T(8,128)(2,1)S(1)}, bf16[512,512]{1,0:T(8,128)(2,1)}, u32[]{:S(2)}) copy-start(bf16[512,512]{1,0:T(8,128)(2,1)} %walign_ref.1) | copy-start | bytes 1572868
  186.3 3.2 %collective-permute-start.22 = (bf16[64,640]{1,0:T(8,128)(2,1)S(1)}, bf16[64,640]{1,0:T(8,128)(2,1)S(1)}, u32[]{:S(2)}, u32[]{:S(2)}) collective-permute-start(bf16[64,640]{1,0:T(8,128)(2,1)S(1)} %convert_element_type.356), channel_id=1, source_target_pairs={{0,32},{1,33},{2,34},{3,35},{4,36},{5,37},{6,38},{7,39},{8,40},{9,... | collective-permute-start | bytes 245768 | tf_op jit(solution)/shard_map/ppermute | solution.py:88
  189.6 5.2 %collective-permute-start.23 = (bf16[64,640]{1,0:T(8,128)(2,1)S(1)}, bf16[64,640]{1,0:T(8,128)(2,1)S(1)}, u32[]{:S(2)}, u32[]{:S(2)}) collective-permute-start(bf16[64,640]{1,0:T(8,128)(2,1)S(1)} %convert_element_type.358), channel_id=1, source_target_pairs={{32,33},{33,32},{34,35},{35,34},{36,37},{37,36},{38,39},{39,38},{4... | collective-permute-start | bytes 245768 | tf_op jit(solution)/shard_map/ppermute | solution.py:91
  194.8 6.4 %collective-permute-start.24 = (bf16[64,640]{1,0:T(8,128)(2,1)S(1)}, bf16[64,640]{1,0:T(8,128)(2,1)S(1)}, u32[]{:S(2)}, u32[]{:S(2)}) collective-permute-start(bf16[64,640]{1,0:T(8,128)(2,1)S(1)} %convert_element_type.360), channel_id=1, source_target_pairs={{32,35},{33,34},{34,33},{35,32},{36,39},{37,38},{38,37},{39,36},{4... | collective-permute-start | bytes 245768 | tf_op jit(solution)/shard_map/ppermute | solution.py:91
  201.2 5.2 %collective-permute-start.25 = (bf16[64,640]{1,0:T(8,128)(2,1)S(1)}, bf16[64,640]{1,0:T(8,128)(2,1)S(1)}, u32[]{:S(2)}, u32[]{:S(2)}) collective-permute-start(bf16[64,640]{1,0:T(8,128)(2,1)S(1)} %convert_element_type.362), channel_id=1, source_target_pairs={{32,96},{33,97},{34,98},{35,99},{36,100},{37,101},{38,102},{39,103... | collective-permute-start | bytes 245768 | tf_op jit(solution)/shard_map/ppermute | solution.py:91
  206.4 6.4 %collective-permute-start.26 = (bf16[64,640]{1,0:T(8,128)(2,1)S(1)}, bf16[64,640]{1,0:T(8,128)(2,1)S(1)}, u32[]{:S(2)}, u32[]{:S(2)}) collective-permute-start(bf16[64,640]{1,0:T(8,128)(2,1)S(1)} %convert_element_type.364), channel_id=1, source_target_pairs={{32,224},{33,225},{34,226},{35,227},{36,228},{37,229},{38,230},{39... | collective-permute-start | bytes 245768 | tf_op jit(solution)/shard_map/ppermute | solution.py:91
  212.9 6.0 %collective-permute-start.27 = (bf16[64,640]{1,0:T(8,128)(2,1)S(1)}, bf16[64,640]{1,0:T(8,128)(2,1)S(1)}, u32[]{:S(2)}, u32[]{:S(2)}) collective-permute-start(bf16[64,640]{1,0:T(8,128)(2,1)S(1)} %convert_element_type.366), channel_id=1, source_target_pairs={{32,36},{33,37},{34,38},{35,39},{36,32},{37,33},{38,34},{39,35},{4... | collective-permute-start | bytes 245768 | tf_op jit(solution)/shard_map/ppermute | solution.py:91
  219.0 6.4 %collective-permute-start.28 = (bf16[64,640]{1,0:T(8,128)(2,1)S(1)}, bf16[64,640]{1,0:T(8,128)(2,1)S(1)}, u32[]{:S(2)}, u32[]{:S(2)}) collective-permute-start(bf16[64,640]{1,0:T(8,128)(2,1)S(1)} %convert_element_type.368), channel_id=1, source_target_pairs={{32,60},{33,61},{34,62},{35,63},{36,40},{37,41},{38,42},{39,43},{4... | collective-permute-start | bytes 245768 | tf_op jit(solution)/shard_map/ppermute | solution.py:91
  225.4 7.0 %collective-permute-start.29 = (bf16[64,640]{1,0:T(8,128)(2,1)S(1)}, bf16[64,640]{1,0:T(8,128)(2,1)S(1)}, u32[]{:S(2)}, u32[]{:S(2)}) collective-permute-start(bf16[64,640]{1,0:T(8,128)(2,1)S(1)} %convert_element_type.370), channel_id=1, source_target_pairs={{32,44},{33,45},{34,46},{35,47},{36,56},{37,57},{38,58},{39,59},{4... | collective-permute-start | bytes 245768 | tf_op jit(solution)/shard_map/ppermute | solution.py:91
  232.4 2.3 collective-permute-start.30

commit v3 on v2

--- a/solution.py
+++ b/solution.py
@@ -74,23 +74,26 @@
 def round_pairs(axis, rule):
     pairs = []
     for y in range(Y):
-        for z in range(Z):
-            for x in range(X):
-                at = {"y": y, "z": z, "x": x}
-                to = dict(at)
-                to[axis] = rule(at[axis])
-                flat = [((p["y"] * CORE + 1) * Z + p["z"]) * X + p["x"] for p in (at, to)]
-                pairs.append(tuple(flat))
+        for core in range(CORE):
+            for z in range(Z):
+                for x in range(X):
+                    at = {"y": y, "core": core, "z": z, "x": x}
+                    to = dict(at, core=1 - core)
+                    to[axis] = rule(at[axis])
+                    pairs.append(
+                        tuple(((p["y"] * CORE + p["core"]) * Z + p["z"]) * X + p["x"] for p in (at, to))
+                    )
     return pairs
 
 
-def summed_over_all(part):
-    total = part + lax.ppermute(part.astype(BF), "core", [(0, 1)]).astype(F32)
+def summed_over_all(mine, theirs):
+    swap = [(0, 1), (1, 0)]
+    total = mine + lax.ppermute(theirs, "core", swap).astype(F32)
     for axis, rule in ROUNDS:
         total = lax.optimization_barrier(total)
         got = lax.ppermute(total.astype(BF), ALL, round_pairs(axis, rule))
         total = total + got.astype(F32)
-    return total, lax.ppermute(total, "core", [(1, 0)])
+    return total, lax.ppermute(total, "core", swap)
 
 
 def split3(a):
@@ -118,14 +121,21 @@
     return coeffs * numerator / (dot3(gram, coeffs, NN) + EPS)
 
 
-def emit_sums(coeffs, feature, sums_ref):
-    c = feature.shape[1]
-    sums_ref[:, :c] = dot(coeffs.astype(BF), feature, NN)
+def emit_sums(half_ref, coeffs, feature, mine_ref, theirs_ref):
+    c, rows = feature.shape[1], mine_ref.shape[0]
+    first = half_ref[0] == 0
+    num = dot(coeffs.astype(BF), feature, NN)
+    mine_ref[:, :c] = jnp.where(first, num[:rows], num[rows:])
+    theirs_ref[:, :c] = jnp.where(first, num[rows:], num[:rows]).astype(BF)
     gram = dot3(coeffs, coeffs, NT)
-    sums_ref[:, c:] = jnp.concatenate([gram, jnp.zeros_like(gram)], axis=1)
-
-
-def first_kernel(mixed_ref, w_ref, basis_ref, feature_ref, coeffs_ref, sums_ref):
+    gram = jnp.concatenate([gram, jnp.zeros_like(gram)], axis=1)
+    mine_ref[:, c:] = jnp.where(first, gram[:rows], gram[rows:])
+    theirs_ref[:, c:] = jnp.where(first, gram[rows:], gram[:rows]).astype(BF)
+
+
+def first_kernel(
+    half_ref, mixed_ref, w_ref, basis_ref, feature_ref, coeffs_ref, mine_ref, theirs_ref
+):
     feature = jnp.maximum(dot(mixed_ref[...], w_ref[...], NN), 0.0).astype(BF)
     feature_ref[...] = feature
     basis = basis_ref[...]
@@ -134,32 +144,34 @@
     soft = e / jnp.sum(e, axis=0, keepdims=True)
     coeffs = coeffs_of(basis, soft, scores)
     coeffs_ref[...] = coeffs
-    emit_sums(coeffs, feature, sums_ref)
-
-
-def updated_basis(core_ref, own_ref, got_ref, basis):
-    both = jnp.where(core_ref[0] == 1, own_ref[...], got_ref[...])
+    emit_sums(half_ref, coeffs, feature, mine_ref, theirs_ref)
+
+
+def updated_basis(half_ref, own_ref, got_ref, basis):
+    own, got = own_ref[...], got_ref[...]
+    first = half_ref[0] == 0
+    both = jnp.concatenate([jnp.where(first, own, got), jnp.where(first, got, own)], axis=0)
     r, c = basis.shape
     gram = both[:, c : c + r]
     return basis * both[:, :c] / (dot3(gram, basis, TN) + EPS)
 
 
 def step_kernel(
-    core_ref, own_ref, got_ref, basis_ref, feature_ref, coeffs_ref,
-    newbasis_ref, newcoeffs_ref, sums_ref,
+    half_ref, own_ref, got_ref, basis_ref, feature_ref, coeffs_ref,
+    newbasis_ref, newcoeffs_ref, mine_ref, theirs_ref,
 ):
-    basis = updated_basis(core_ref, own_ref, got_ref, basis_ref[...])
+    basis = updated_basis(half_ref, own_ref, got_ref, basis_ref[...])
     newbasis_ref[...] = basis
     feature = feature_ref[...]
     coeffs = coeffs_of(basis, coeffs_ref[...], dot(basis.astype(BF), feature, NT))
     newcoeffs_ref[...] = coeffs
-    emit_sums(coeffs, feature, sums_ref)
+    emit_sums(half_ref, coeffs, feature, mine_ref, theirs_ref)
 
 
 def last_kernel(
-    core_ref, own_ref, got_ref, basis_ref, feature_ref, coeffs_ref, wham_ref, walign_ref, out_ref
+    half_ref, own_ref, got_ref, basis_ref, feature_ref, coeffs_ref, wham_ref, walign_ref, out_ref
 ):
-    basis = updated_basis(core_ref, own_ref, got_ref, basis_ref[...])
+    basis = updated_basis(half_ref, own_ref, got_ref, basis_ref[...])
     feature = feature_ref[...]
     low = basis.astype(BF)
     coeffs = coeffs_of(basis, coeffs_ref[...], dot(low, feature, NT))
@@ -183,7 +195,8 @@
 def on_device(band_input, column_taps, row_taps, w_squeeze, bases_init, w_ham, w_align):
     tile_rows, tile_cols, channels = band_input.shape
     margin = column_taps.shape[0] // 2
-    core = lax.axis_index("core").astype(jnp.int32).reshape(1)
+    half = sum(lax.axis_index(a) for a in ALL) % 2
+    half = half.astype(jnp.int32).reshape(1)
     framed = padded(band_input, ((ROWS, 0), (COLS, 1)), margin, False)
     col_filtered = filter_columns(framed, column_taps, tile_cols).astype(jnp.bfloat16)
     strip_sum = filter_rows(col_filtered, row_taps, tile_rows)
@@ -194,25 +207,26 @@
     )
     n, r = tile_rows * tile_cols, bases_init.shape[1]
     sds = jax.ShapeDtypeStruct
-    sums = [sds((r, channels + 128), F32)]
+    width = channels + 128
+    sums = [sds((r // 2, width), F32), sds((r // 2, width), BF)]
     basis = bases_init.T
-    feature, coeffs, part = call(
+    feature, coeffs, mine, theirs = call(
         first_kernel,
         [sds((n, channels), BF), sds((r, n), F32)] + sums,
-        mixed_tile, w_squeeze, basis,
+        half, mixed_tile, w_squeeze, basis,
     )
     for _ in range(STEPS - 1):
-        own, got = summed_over_all(part)
-        basis, coeffs, part = call(
+        own, got = summed_over_all(mine, theirs)
+        basis, coeffs, mine, theirs = call(
             step_kernel,
             [sds((r, channels), F32), sds((r, n), F32)] + sums,
-            core, own, got, basis, feature, coeffs,
+            half, own, got, basis, feature, coeffs,
         )
-    own, got = summed_over_all(part)
+    own, got = summed_over_all(mine, theirs)
     head_out = call(
         last_kernel,
         sds((n, channels), BF),
-        core, own, got, basis, feature, coeffs, w_ham, w_align,
+        half, own, got, basis, feature, coeffs, w_ham, w_align,
     )
     return head_out.reshape(tile_rows, tile_cols, channels)
 

time: 241 us -> 200 us (0.83)
  starting transfers between devices: 104 us -> 68.6 us
  waiting for transfers between devices: 85.8 us -> 78.9 us
    ppermute x21, starting transfers between devices: 84.3 us -> 54.5 us  [summed_over_all(): got = lax.ppermute(total.astype(BF), ALL, round_pairs(axis, rule))]
    ppermute x6, starting transfers between devices: 7.96 us -> 2.92 us  [the longest x3 1.79 us: summed_over_all(): return (total, lax.ppermute(total, 'core', swap))]
    ppermute x21, waiting for transfers between devices: 52.8 us -> 48.4 us  [summed_over_all(): got = lax.ppermute(total.astype(BF), ALL, round_pairs(axis, rule))]
    ppermute x6, waiting for transfers between devices: 8.43 us -> 5.77 us  [the longest x3 2.97 us: summed_over_all(): total = mine + lax.ppermute(theirs, 'core', swap).astype(F32)]
where the time goes in v3:
time: 200 us; the launch traced here: 199 us
  waiting for transfers between devices  78.9 us (39%)
  starting transfers between devices  68.6 us (34%)
  other arithmetic  32.6 us (16%)
  Pallas kernels  13.3 us (7%)
  local copies, waits for them, and re-layouts  5.3 us (3%)
    ppermute x21, starting transfers between devices, summed_over_all(): got = lax.ppermute(total.astype(BF), ALL, round_pairs(axis, rule))  54.5 us
    ppermute x21, waiting for transfers between devices, summed_over_all(): got = lax.ppermute(total.astype(BF), ALL, round_pairs(axis, rule))  48.4 us
    ppermute x2, waiting for transfers between devices, padded(): before = lax.ppermute(last, axis, up)  16.3 us
    convert_element_type x1, other arithmetic, on_device(): mixed_tile = (band_input.astype(jnp.float32) + strip_sum).astype(jnp.bflo...  14.4 us
    convert_element_type x1, other arithmetic, on_device(): filter_columns(framed, column_taps, tile_cols).astype(jnp.bfloat16)  13.4 us
    pallas_call x4, Pallas kernels, call(): pl.pallas_call(kernel, out_shape=outs, in_specs=specs, out_specs=jax.tree...  13.3 us
    ppermute x2, waiting for transfers between devices, padded(): after = lax.ppermute(initial, axis, down)  8.44 us
    ppermute x2, starting transfers between devices, padded(): before = lax.ppermute(last, axis, up)  8.04 us
  transfers between devices with their start and end apart: 31, of which 31 were waited for; matrix products, arithmetic and copies ran while one was open for 0% of the time, Pallas kernels for 0%

profile of v3, /device:TPU:1, one launch (start us, length us, event | category | flops | bytes accessed | tf_op | source)
XLA Modules:
  0.0 199.3 jit_solution(1930096605344704404)
XLA Ops:
  0.0 2.8 %copy.8 = bf16[64,32,512]{2,0,1:T(8,128)(2,1)S(1)} copy(bf16[64,32,512]{2,1,0:T(8,128)(2,1)} %param.7) | data formatting | bytes 4194304 | tf_op args[0]
  3.9 4.6 %collective-permute-start = (bf16[10,32,512]{2,0,1:T(8,128)(2,1)}, bf16[10,32,512]{2,0,1:T(8,128)(2,1)S(1)}, u32[]{:S(2)}, u32[]{:S(2)}) collective-permute-start(bf16[10,32,512]{2,0,1:T(8,128)(2,1)} %get-tuple-element.33), channel_id=1, source_target_pairs={{0,32},{32,64},{64,96},{96,128},{128,160},{160,192},{192,224},{1,3... | collective-permute-start | bytes 983048 | tf_op jit(solution)/shard_map/ppermute | solution.py:26
  8.4 1.9 collective-permute-start.1
  10.4 4.5 %collective-permute-done = bf16[10,32,512]{2,0,1:T(8,128)(2,1)S(1)} collective-permute-done((bf16[10,32,512]{2,0,1:T(8,128)(2,1)}, bf16[10,32,512]{2,0,1:T(8,128)(2,1)S(1)}, u32[]{:S(2)}, u32[]{:S(2)}) %collective-permute-start) | collective-permute-done | bytes 327712 | tf_op jit(solution)/shard_map/ppermute | solution.py:26
  14.9 4.3 %collective-permute-done.1 = bf16[10,32,512]{2,0,1:T(8,128)(2,1)S(1)} collective-permute-done((bf16[10,32,512]{2,0,1:T(8,128)(2,1)}, bf16[10,32,512]{2,0,1:T(8,128)(2,1)S(1)}, u32[]{:S(2)}, u32[]{:S(2)}) %collective-permute-start.1) | collective-permute-done | bytes 327712 | tf_op jit(solution)/shard_map/ppermute | solution.py:27
  20.9 3.5 %collective-permute-start.2 = (bf16[84,10,512]{2,0,1:T(8,128)(2,1)S(1)}, bf16[84,10,512]{2,0,1:T(8,128)(2,1)S(1)}, u32[]{:S(2)}, u32[]{:S(2)}) collective-permute-start(bf16[84,10,512]{2,0,1:T(8,128)(2,1)S(1)} %get-tuple-element.31), channel_id=1, source_target_pairs={{0,1},{1,2},{2,3},{3,4},{4,5},{5,6},{6,7},{7,8},{8,9},{9,10},{10,1... | collective-permute-start | bytes 2580488 | tf_op jit(solution)/shard_map/ppermute | solution.py:26
  25.8 11.8 %collective-permute-done.2 = bf16[84,10,512]{2,0,1:T(8,128)(2,1)S(1)} collective-permute-done((bf16[84,10,512]{2,0,1:T(8,128)(2,1)S(1)}, bf16[84,10,512]{2,0,1:T(8,128)(2,1)S(1)}, u32[]{:S(2)}, u32[]{:S(2)}) %collective-permute-start.2) | collective-permute-done | bytes 860192 | tf_op jit(solution)/shard_map/ppermute | solution.py:26
  37.6 4.2 %collective-permute-done.3 = bf16[84,10,512]{2,0,1:T(8,128)(2,1)S(1)} collective-permute-done((bf16[84,10,512]{2,0,1:T(8,128)(2,1)S(1)}, bf16[84,10,512]{2,0,1:T(8,128)(2,1)S(1)}, u32[]{:S(2)}, u32[]{:S(2)}) %collective-permute-start.3) | collective-permute-done | bytes 860192 | tf_op jit(solution)/shard_map/ppermute | solution.py:27
  41.7 2.9 %maximum_maximum_fusion = (bf16[84,42,512]{2,0,1:T(8,128)(2,1)S(1)}, bf16[84,42,512]{2,0,1:T(8,128)(2,1)S(1)}) fusion(bf16[10,32,512]{2,0,1:T(8,128)(2,1)S(1)} %collective-permute-done.1, bf16[64,32,512]{2,0,1:T(8,128)(2,1)S(1)} %copy.8, bf16[10,32,512]{2,0,1:T(8,128)(2,1)S(1)} %collective-permute-done, bf16[84,10,512]{2,0,1:T(8,128)(2,1)S(1)} %collective-permute-done.2, ...), kind=kLoop, calls=%fused_computation.2 | loop fusion | flops 28901376 | bytes 11698176 | tf_op jit(solution)/shard_map/concatenate | solution.py:28
  44.6 13.4 %add_convert_fusion = bf16[84,32,512]{2,0,1:T(8,128)(2,1)S(1)} fusion(bf16[84,42,512]{2,0,1:T(8,128)(2,1)S(1)} %get-tuple-element.30, bf16[84,42,512]{2,0,1:T(8,128)(2,1)S(1)} %get-tuple-element.29, f32[512]{0:T(512)S(1)} %bitcast.69, f32[512]{0:T(512)S(1)} %bitcast.68, f32[512]{0:T(512)S(1)} %bitcast.50, f32[512]{0:T(512)S(1)} %bitcast.51, ...), kind=kLoop, calls=%fused_computation | loop fusion | flops 93585408 | bytes 60598272 | tf_op jit(solution)/shard_map/convert_element_type | solution.py:201
  58.0 14.4 %add_convert_fusion.1 = bf16[64,32,512]{2,0,1:T(8,128)(2,1)S(1)} fusion(bf16[84,32,512]{2,0,1:T(8,128)(2,1)S(1)} %add_convert_fusion, f32[512]{0:T(512)S(1)} %bitcast.90, f32[512]{0:T(512)S(1)} %bitcast.89, f32[512]{0:T(512)S(1)} %bitcast.71, f32[512]{0:T(512)S(1)} %bitcast.72, f32[512]{0:T(512)S(1)} %bitcast.73, f32[512]{0:T(512)S(1)} %bitcast.74, ...), kind=kLoop, calls=%fused_computation.1 | loop fusion | flops 68157440 | bytes 48277504 | tf_op jit(solution)/shard_map/convert_element_type | solution.py:205
  73.7 3.1 %shard_map.73 = (bf16[2048,512]{1,0:T(8,128)(2,1)S(1)}, f32[64,2048]{1,0:T(8,128)S(1)}, f32[32,640]{1,0:T(8,128)S(1)}, bf16[32,640]{1,0:T(8,128)(2,1)S(1)}) custom-call(s32[1]{0:T(128)} %bitcast.half_ref, bf16[2048,512]{1,0:T(8,128)(2,1)S(1)} %bitcast.46, bf16[512,512]{1,0:T(8,128)(2,1)S(1)} %copy-done.3, f32[64,512]{1,0:T(8,128)S(1)} %bitcast.47), custom_call_target="tpu_custom_call" | custom-call | tf_op jit(solution)/shard_map/pallas_call | solution.py:186
  79.6 2.2 %collective-permute-done.5 = bf16[32,640]{1,0:T(8,128)(2,1)S(1)} collective-permute-done((bf16[32,640]{1,0:T(8,128)(2,1)S(1)}, bf16[32,640]{1,0:T(8,128)(2,1)S(1)}, u32[]{:S(2)}, u32[]{:S(2)}) %collective-permute-start.5) | collective-permute-done | bytes 40992 | tf_op jit(solution)/shard_map/ppermute | solution.py:94
  81.8 5.0 %collective-permute-start.6 = (bf16[32,640]{1,0:T(8,128)(2,1)S(1)}, bf16[32,640]{1,0:T(8,128)(2,1)S(1)}, u32[]{:S(2)}, u32[]{:S(2)}) collective-permute-start(bf16[32,640]{1,0:T(8,128)(2,1)S(1)} %convert_element_type.318), channel_id=1, source_target_pairs={{0,35},{1,34},{2,33},{3,32},{4,39},{5,38},{6,37},{7,36},{8,43},{9,... | collective-permute-start | bytes 122888 | tf_op jit(solution)/shard_map/ppermute | solution.py:94
  86.8 1.8 collective-permute-done.6
  88.6 7.0 %collective-permute-start.7 = (bf16[32,640]{1,0:T(8,128)(2,1)S(1)}, bf16[32,640]{1,0:T(8,128)(2,1)S(1)}, u32[]{:S(2)}, u32[]{:S(2)}) collective-permute-start(bf16[32,640]{1,0:T(8,128)(2,1)S(1)} %convert_element_type.320), channel_id=1, source_target_pairs={{0,96},{1,97},{2,98},{3,99},{4,100},{5,101},{6,102},{7,103},{8,104... | collective-permute-start | bytes 122888 | tf_op jit(solution)/shard_map/ppermute | solution.py:94
  95.7 1.7 collective-permute-done.7
  97.4 2.5 %collective-permute-start.8 = (bf16[32,640]{1,0:T(8,128)(2,1)S(1)}, bf16[32,640]{1,0:T(8,128)(2,1)S(1)}, u32[]{:S(2)}, u32[]{:S(2)}) collective-permute-start(bf16[32,640]{1,0:T(8,128)(2,1)S(1)} %convert_element_type.322), channel_id=1, source_target_pairs={{0,224},{1,225},{2,226},{3,227},{4,228},{5,229},{6,230},{7,231},{8... | collective-permute-start | bytes 122888 | tf_op jit(solution)/shard_map/ppermute | solution.py:94
  99.8 2.2 %collective-permute-done.8 = bf16[32,640]{1,0:T(8,128)(2,1)S(1)} collective-permute-done((bf16[32,640]{1,0:T(8,128)(2,1)S(1)}, bf16[32,640]{1,0:T(8,128)(2,1)S(1)}, u32[]{:S(2)}, u32[]{:S(2)}) %collective-permute-start.8) | collective-permute-done | bytes 40992 | tf_op jit(solution)/shard_map/ppermute | solution.py:94
  102.1 1.8 collective-permute-start.9
  103.9 1.8 collective-permute-done.9
  105.7 4.3 %collective-permute-start.10 = (bf16[32,640]{1,0:T(8,128)(2,1)S(1)}, bf16[32,640]{1,0:T(8,128)(2,1)S(1)}, u32[]{:S(2)}, u32[]{:S(2)}) collective-permute-start(bf16[32,640]{1,0:T(8,128)(2,1)S(1)} %convert_element_type.326), channel_id=1, source_target_pairs={{0,60},{1,61},{2,62},{3,63},{4,40},{5,41},{6,42},{7,43},{8,36},{9,... | collective-permute-start | bytes 122888 | tf_op jit(solution)/shard_map/ppermute | solution.py:94
  110.0 1.7 collective-permute-done.10
  111.7 5.6 %collective-permute-start.11 = (bf16[32,640]{1,0:T(8,128)(2,1)S(1)}, bf16[32,640]{1,0:T(8,128)(2,1)S(1)}, u32[]{:S(2)}, u32[]{:S(2)}) collective-permute-start(bf16[32,640]{1,0:T(8,128)(2,1)S(1)} %convert_element_type.328), channel_id=1, source_target_pairs={{0,44},{1,45},{2,46},{3,47},{4,56},{5,57},{6,58},{7,59},{8,52},{9,... | collective-permute-start | bytes 122888 | tf_op jit(solution)/shard_map/ppermute | solution.py:94
  117.3 1.8 collective-permute-done.11
  120.5 2.2 %shard_map.74 = (f32[64,512]{1,0:T(8,128)S(1)}, f32[64,2048]{1,0:T(8,128)S(1)}, f32[32,640]{1,0:T(8,128)S(1)}, bf16[32,640]{1,0:T(8,128)(2,1)S(1)}) custom-call(s32[1]{0:T(128)} %bitcast.half_ref, f32[32,640]{1,0:T(8,128)S(1)} %convert_add_fusion.16.own_ref, f32[32,640]{1,0:T(8,128)S(1)} %collective-permute-done.12.got_ref, f32[64,512]{1,0:T(8,128)S(1)} %bitcast.48, ...), custom_call_target="tpu_custom_call" | custom-call | tf_op jit(solution)/shard_map/pallas_call | solution.py:186
  124.1 3.5 %collective-permute-done.14 = bf16[32,640]{1,0:T(8,128)(2,1)S(1)} collective-permute-done((bf16[32,640]{1,0:T(8,128)(2,1)S(1)}, bf16[32,640]{1,0:T(8,128)(2,1)S(1)}, u32[]{:S(2)}, u32[]{:S(2)}) %collective-permute-start.14) | collective-permute-done | bytes 40992 | tf_op jit(solution)/shard_map/ppermute | solution.py:94
  127.7 3.5 %collective-permute-start.15 = (bf16[32,640]{1,0:T(8,128)(2,1)S(1)}, bf16[32,640]{1,0:T(8,128)(2,1)S(1)}, u32[]{:S(2)}, u32[]{:S(2)}) collective-permute-start(bf16[32,640]{1,0:T(8,128)(2,1)S(1)} %convert_element_type.333), channel_id=1, source_target_pairs={{0,35},{1,34},{2,33},{3,32},{4,39},{5,38},{6,37},{7,36},{8,43},{9,... | collective-permute-start | bytes 122888 | tf_op jit(solution)/shard_map/ppermute | solution.py:94
  131.2 1.7 collective-permute-done.15
  133.7 2.7 %collective-permute-done.16 = bf16[32,640]{1,0:T(8,128)(2,1)S(1)} collective-permute-done((bf16[32,640]{1,0:T(8,128)(2,1)S(1)}, bf16[32,640]{1,0:T(8,128)(2,1)S(1)}, u32[]{:S(2)}, u32[]{:S(2)}) %collective-permute-start.16) | collective-permute-done | bytes 40992 | tf_op jit(solution)/shard_map/ppermute | solution.py:94
  136.4 2.8 %collective-permute-start.17 = (bf16[32,640]{1,0:T(8,128)(2,1)S(1)}, bf16[32,640]{1,0:T(8,128)(2,1)S(1)}, u32[]{:S(2)}, u32[]{:S(2)}) collective-permute-start(bf16[32,640]{1,0:T(8,128)(2,1)S(1)} %convert_element_type.337), channel_id=1, source_target_pairs={{0,224},{1,225},{2,226},{3,227},{4,228},{5,229},{6,230},{7,231},{8... | collective-permute-start | bytes 122888 | tf_op jit(solution)/shard_map/ppermute | solution.py:94
  139.2 2.0 collective-permute-done.17
  141.2 1.9 collective-permute-start.18
  143.0 1.7 collective-permute-done.18
  145.9 3.6 %collective-permute-done.19 = bf16[32,640]{1,0:T(8,128)(2,1)S(1)} collective-permute-done((bf16[32,640]{1,0:T(8,128)(2,1)S(1)}, bf16[32,640]{1,0:T(8,128)(2,1)S(1)}, u32[]{:S(2)}, u32[]{:S(2)}) %collective-permute-start.19) | collective-permute-done | bytes 40992 | tf_op jit(solution)/shard_map/ppermute | solution.py:94
  149.5 4.1 %collective-permute-start.20 = (bf16[32,640]{1,0:T(8,128)(2,1)S(1)}, bf16[32,640]{1,0:T(8,128)(2,1)S(1)}, u32[]{:S(2)}, u32[]{:S(2)}) collective-permute-start(bf16[32,640]{1,0:T(8,128)(2,1)S(1)} %convert_element_type.343), channel_id=1, source_target_pairs={{0,44},{1,45},{2,46},{3,47},{4,56},{5,57},{6,58},{7,59},{8,52},{9,... | collective-permute-start | bytes 122888 | tf_op jit(solution)/shard_map/ppermute | solution.py:94
  156.9 2.2 %shard_map.75 = (f32[64,512]{1,0:T(8,128)S(1)}, f32[64,2048]{1,0:T(8,128)S(1)}, f32[32,640]{1,0:T(8,128)S(1)}, bf16[32,640]{1,0:T(8,128)(2,1)S(1)}) custom-call(s32[1]{0:T(128)} %bitcast.half_ref, f32[32,640]{1,0:T(8,128)S(1)} %convert_add_fusion.8.own_ref, f32[32,640]{1,0:T(8,128)S(1)} %collective-permute-done.21.got_ref, ...), custom_call_target="tpu_custom_call" | custom-call | tf_op jit(solution)/shard_map/pallas_call | solution.py:186
  160.5 3.5 %collective-permute-done.23 = bf16[32,640]{1,0:T(8,128)(2,1)S(1)} collective-permute-done((bf16[32,640]{1,0:T(8,128)(2,1)S(1)}, bf16[32,640]{1,0:T(8,128)(2,1)S(1)}, u32[]{:S(2)}, u32[]{:S(2)}) %collective-permute-start.23) | collective-permute-done | bytes 40992 | tf_op jit(solution)/shard_map/ppermute | solution.py:94
  164.1 3.1 %collective-permute-start.24 = (bf16[32,640]{1,0:T(8,128)(2,1)S(1)}, bf16[32,640]{1,0:T(8,128)(2,1)S(1)}, u32[]{:S(2)}, u32[]{:S(2)}) collective-permute-start(bf16[32,640]{1,0:T(8,128)(2,1)S(1)} %convert_element_type.348), channel_id=1, source_target_pairs={{0,35},{1,34},{2,33},{3,32},{4,39},{5,38},{6,37},{7,36},{8,43},{9,... | collective-permute-start | bytes 122888 | tf_op jit(solution)/shard_map/ppermute | solution.py:94
  167.2 1.7 collective-permute-done.24
  169.0 3.4 %collective-permute-done.25 = bf16[32,640]{1,0:T(8,128)(2,1)S(1)} collective-permute-done((bf16[32,640]{1,0:T(8,128)(2,1)S(1)}, bf16[32,640]{1,0:T(8,128)(2,1)S(1)}, u32[]{:S(2)}, u32[]{:S(2)}) %collective-permute-start.25) | collective-permute-done | bytes 40992 | tf_op jit(solution)/shard_map/ppermute | solution.py:94
  172.5 2.7 %collective-permute-start.26 = (bf16[32,640]{1,0:T(8,128)(2,1)S(1)}, bf16[32,640]{1,0:T(8,128)(2,1)S(1)}, u32[]{:S(2)}, u32[]{:S(2)}) collective-permute-start(bf16[32,640]{1,0:T(8,128)(2,1)S(1)} %convert_element_type.352), channel_id=1, source_target_pairs={{0,224},{1,225},{2,226},{3,227},{4,228},{5,229},{6,230},{7,231},{8... | collective-permute-start | bytes 122888 | tf_op jit(solution)/shard_map/ppermute | solution.py:94
  175.2 2.1 %collective-permute-done.26 = bf16[32,640]{1,0:T(8,128)(2,1)S(1)} collective-permute-done((bf16[32,640]{1,0:T(8,128)(2,1)S(1)}, bf16[32,640]{1,0:T(8,128)(2,1)S(1)}, u32[]{:S(2)}, u32[]{:S(2)}) %collective-permute-start.26) | collective-permute-done | bytes 40992 | tf_op jit(solution)/shard_map/ppermute | solution.py:94
  177.3 2.1 %collective-permute-start.27 = (bf16[32,640]{1,0:T(8,128)(2,1)S(1)}, bf16[32,640]{1,0:T(8,128)(2,1)S(1)}, u32[]{:S(2)}, u32[]{:S(2)}) collective-permute-start(bf16[32,640]{1,0:T(8,128)(2,1)S(1)} %convert_element_type.354), channel_id=1, source_target_pairs={{0,36},{1,37},{2,38},{3,39},{4,32},{5,33},{6,34},{7,35},{8,44},{9,... | collective-permute-start | bytes 122888 | tf_op jit(solution)/shard_map/ppermute | solution.py:94
  179.4 1.8 collective-permute-done.27
  181.7 4.2 %collective-permute-done.28 = bf16[32,640]{1,0:T(8,128)(2,1)S(1)} collective-permute-done((bf16[32,640]{1,0:T(8,128)(2,1)S(1)}, bf16[32,640]{1,0:T(8,128)(2,1)S(1)}, u32[]{:S(2)}, u32[]{:S(2)}) %collective-permute-start.28) | collective-permute-done | bytes 40992 | tf_op jit(solution)/shard_map/ppermute | solution.py:94
  186.0 4.1 %collective-permute-start.29 = (bf16[32,640]{1,0:T(8,128)(2,1)S(1)}, bf16[32,640]{1,0:T(8,128)(2,1)S(1)}, u32[]{:S(2)}, u32[]{:S(2)}) collective-permute-start(bf16[32,640]{1,0:T(8,128)(2,1)S(1)} %convert_element_type.358), channel_id=1, source_target_pairs={{0,44},{1,45},{2,46},{3,47},{4,56},{5,57},{6,58},{7,59},{8,52},{9,... | collective-permute-start | bytes 122888 | tf_op jit(solution)/shard_map/ppermute | solution.py:94
  193.5 5.9 %shard_map.76 = bf16[2048,512]{1,0:T(8,128)(2,1)} custom-call(s32[1]{0:T(128)} %bitcast.half_ref, f32[32,640]{1,0:T(8,128)S(1)} %convert_add_fusion.own_ref, f32[32,640]{1,0:T(8,128)S(1)} %collective-permute-done.30.got_ref, f32[64,512]{1,0:T(8,128)S(1)} %get-tuple-element.27.basis_ref, bf16[2048,512]{1,0:T(8,128)(2,1)S(1)} %get-tuple-element.19.feature_ref, ...), custom_call_target="tpu_custom_call" | custom-call | tf_op jit(solution)/shard_map/pallas_call | solution.py:186
  (89 shorter events, 21.9 us)
Async XLA Ops:
  3.9 11.0 %collective-permute-start = (bf16[10,32,512]{2,0,1:T(8,128)(2,1)}, bf16[10,32,512]{2,0,1:T(8,128)(2,1)S(1)}, u32[]{:S(2)}, u32[]{:S(2)}) collective-permute-start(bf16[10,32,512]{2,0,1:T(8,128)(2,1)} %get-tuple-element.33), channel_id=1, source_target_pairs={{0,32},{32,64},{64,96},{96,128},{128,160},{160,192},{192,224},{1,3... | collective-permute-start | bytes 983048 | tf_op jit(solution)/shard_map/ppermute | solution.py:26
  8.4 10.7 %collective-permute-start.1 = (bf16[10,32,512]{2,0,1:T(8,128)(2,1)}, bf16[10,32,512]{2,0,1:T(8,128)(2,1)S(1)}, u32[]{:S(2)}, u32[]{:S(2)}) collective-permute-start(bf16[10,32,512]{2,0,1:T(8,128)(2,1)} %get-tuple-element.34), channel_id=1, source_target_pairs={{32,0},{64,32},{96,64},{128,96},{160,128},{192,160},{224,192},{33,... | collective-permute-start | bytes 983048 | tf_op jit(solution)/shard_map/ppermute | solution.py:27
  10.4 15.2 %copy-start.5 = (f32[21,512]{1,0:T(8,128)S(1)}, f32[21,512]{1,0:T(8,128)}, u32[]{:S(2)}) copy-start(f32[21,512]{1,0:T(8,128)} %param.8) | copy-start | bytes 129028
  10.4 15.3 %copy-start.6 = (f32[21,512]{1,0:T(8,128)S(1)}, f32[21,512]{1,0:T(8,128)}, u32[]{:S(2)}) copy-start(f32[21,512]{1,0:T(8,128)} %param.9) | copy-start | bytes 129028
  20.9 16.7 %collective-permute-start.2 = (bf16[84,10,512]{2,0,1:T(8,128)(2,1)S(1)}, bf16[84,10,512]{2,0,1:T(8,128)(2,1)S(1)}, u32[]{:S(2)}, u32[]{:S(2)}) collective-permute-start(bf16[84,10,512]{2,0,1:T(8,128)(2,1)S(1)} %get-tuple-element.31), channel_id=1, source_target_pairs={{0,1},{1,2},{2,3},{3,4},{4,5},{5,6},{6,7},{7,8},{8,9},{9,10},{10,1... | collective-permute-start | bytes 2580488 | tf_op jit(solution)/shard_map/ppermute | solution.py:26
  24.3 17.4 %collective-permute-start.3 = (bf16[84,10,512]{2,0,1:T(8,128)(2,1)S(1)}, bf16[84,10,512]{2,0,1:T(8,128)(2,1)S(1)}, u32[]{:S(2)}, u32[]{:S(2)}) collective-permute-start(bf16[84,10,512]{2,0,1:T(8,128)(2,1)S(1)} %get-tuple-element.32), channel_id=1, source_target_pairs={{1,0},{2,1},{3,2},{4,3},{5,4},{6,5},{7,6},{8,7},{9,8},{10,9},{11,1... | collective-permute-start | bytes 2580488 | tf_op jit(solution)/shard_map/ppermute | solution.py:27
  44.6 13.4 %copy-start.4 = (bf16[64,32,512]{2,1,0:T(8,128)(2,1)S(1)}, bf16[64,32,512]{2,1,0:T(8,128)(2,1)}, u32[]{:S(2)}) copy-start(bf16[64,32,512]{2,1,0:T(8,128)(2,1)} %param.7) | copy-start | bytes 6291460
  72.5 1.2 copy-start.2
  72.5 1.2 copy-start.3
  76.7 1.5 collective-permute-start.4
  78.3 3.5 %collective-permute-start.5 = (bf16[32,640]{1,0:T(8,128)(2,1)S(1)}, bf16[32,640]{1,0:T(8,128)(2,1)S(1)}, u32[]{:S(2)}, u32[]{:S(2)}) collective-permute-start(bf16[32,640]{1,0:T(8,128)(2,1)S(1)} %convert_element_type.316), channel_id=1, source_target_pairs={{0,33},{1,32},{2,35},{3,34},{4,37},{5,36},{6,39},{7,38},{8,41},{9,... | collective-permute-start | bytes 122888 | tf_op jit(solution)/shard_map/ppermute | solution.py:94
  81.8 6.8 %collective-permute-start.6 = (bf16[32,640]{1,0:T(8,128)(2,1)S(1)}, bf16[32,640]{1,0:T(8,128)(2,1)S(1)}, u32[]{:S(2)}, u32[]{:S(2)}) collective-permute-start(bf16[32,640]{1,0:T(8,128)(2,1)S(1)} %convert_element_type.318), channel_id=1, source_target_pairs={{0,35},{1,34},{2,33},{3,32},{4,39},{5,38},{6,37},{7,36},{8,43},{9,... | collective-permute-start | bytes 122888 | tf_op jit(solution)/shard_map/ppermute | solution.py:94
  88.6 8.7 %collective-permute-start.7 = (bf16[32,640]{1,0:T(8,128)(2,1)S(1)}, bf16[32,640]{1,0:T(8,128)(2,1)S(1)}, u32[]{:S(2)}, u32[]{:S(2)}) collective-permute-start(bf16[32,640]{1,0:T(8,128)(2,1)S(1)} %convert_element_type.320), channel_id=1, source_target_pairs={{0,96},{1,97},{2,98},{3,99},{4,100},{5,101},{6,102},{7,103},{8,104... | collective-permute-start | bytes 122888 | tf_op jit(solution)/shard_map/ppermute | solution.py:94
  97.4 4.7 %collective-permute-start.8 = (bf16[32,640]{1,0:T(8,128)(2,1)S(1)}, bf16[32,640]{1,0:T(8,128)(2,1)S(1)}, u32[]{:S(2)}, u32[]{:S(2)}) collective-permute-start(bf16[32,640]{1,0:T(8,128)(2,1)S(1)} %convert_element_type.322), channel_id=1, source_target_pairs={{0,224},{1,225},{2,226},{3,227},{4,228},{5,229},{6,230},{7,231},{8... | collective-permute-start | bytes 122888 | tf_op jit(solution)/shard_map/ppermute | solution.py:94
  102.1 3.6 %collective-permute-start.9 = (bf16[32,640]{1,0:T(8,128)(2,1)S(1)}, bf16[32,640]{1,0:T(8,128)(2,1)S(1)}, u32[]{:S(2)}, u32[]{:S(2)}) collective-permute-start(bf16[32,640]{1,0:T(8,128)(2,1)S(1)} %convert_element_type.324), channel_id=1, source_target_pairs={{0,36},{1,37},{2,38},{3,39},{4,32},{5,33},{6,34},{7,35},{8,44},{9,... | collective-permute-start | bytes 122888 | tf_op jit(solution)/shard_map/ppermute | solution.py:94
  105.7 6.0 %collective-permute-start.10 = (bf16[32,640]{1,0:T(8,128)(2,1)S(1)}, bf16[32,640]{1,0:T(8,128)(2,1)S(1)}, u32[]{:S(2)}, u32[]{:S(2)}) collective-permute-start(bf16[32,640]{1,0:T(8,128)(2,1)S(1)} %convert_element_type.326), channel_id=1, source_target_pairs={{0,60},{1,61},{2,62},{3,63},{4,40},{5,41},{6,42},{7,43},{8,36},{9,... | collective-permute-start | bytes 122888 | tf_op jit(solution)/shard_map/ppermute | solution.py:94
  111.7 7.4 %collective-permute-start.11 = (bf16[32,640]{1,0:T(8,128)(2,1)S(1)}, bf16[32,640]{1,0:T(8,128)(2,1)S(1)}, u32[]{:S(2)}, u32[]{:S(2)}) collective-permute-start(bf16[32,640]{1,0:T(8,128)(2,1)S(1)} %convert_element_type.328), channel_id=1, source_target_pairs={{0,44},{1,45},{2,46},{3,47},{4,56},{5,57},{6,58},{7,59},{8,52},{9,... | collective-permute-start | bytes 122888 | tf_op jit(solution)/shard_map/ppermute | solution.py:94
  119.1 1.4 collective-permute-start.12
  122.7 1.3 collective-permute-start.13
  124.0 69.4 %copy-start = (bf16[512,512]{1,0:T(8,128)(2,1)S(1)}, bf16[512,512]{1,0:T(8,128)(2,1)}, u32[]{:S(2)}) copy-start(bf16[512,512]{1,0:T(8,128)(2,1)} %wham_ref.1) | copy-start | bytes 1572868
  124.0 69.4 %copy-start.1 = (bf16[512,512]{1,0:T(8,128)(2,1)S(1)}, bf16[512,512]{1,0:T(8,128)(2,1)}, u32[]{:S(2)}) copy-start(bf16[512,512]{1,0:T(8,128)(2,1)} %walign_ref.1) | copy-start | bytes 1572868
  124.0 3.6 %collective-permute-start.14 = (bf16[32,640]{1,0:T(8,128)(2,1)S(1)}, bf16[32,640]{1,0:T(8,128)(2,1)S(1)}, u32[]{:S(2)}, u32[]{:S(2)}) collective-permute-start(bf16[32,640]{1,0:T(8,128)(2,1)S(1)} %convert_element_type.331), channel_id=1, source_target_pairs={{0,33},{1,32},{2,35},{3,34},{4,37},{5,36},{6,39},{7,38},{8,41},{9,... | collective-permute-start | bytes 122888 | tf_op jit(solution)/shard_map/ppermute | solution.py:94
  127.7 5.2 %collective-permute-start.15 = (bf16[32,640]{1,0:T(8,128)(2,1)S(1)}, bf16[32,640]{1,0:T(8,128)(2,1)S(1)}, u32[]{:S(2)}, u32[]{:S(2)}) collective-permute-start(bf16[32,640]{1,0:T(8,128)(2,1)S(1)} %convert_element_type.333), channel_id=1, source_target_pairs={{0,35},{1,34},{2,33},{3,32},{4,39},{5,38},{6,37},{7,36},{8,43},{9,... | collective-permute-start | bytes 122888 | tf_op jit(solution)/shard_map/ppermute | solution.py:94
  132.9 3.5 %collective-permute-start.16 = (bf16[32,640]{1,0:T(8,128)(2,1)S(1)}, bf16[32,640]{1,0:T(8,128)(2,1)S(1)}, u32[]{:S(2)}, u32[]{:S(2)}) collective-permute-start(bf16[32,640]{1,0:T(8,128)(2,1)S(1)} %convert_element_type.335), channel_id=1, source_target_pairs={{0,96},{1,97},{2,98},{3,99},{4,100},{5,101},{6,102},{7,103},{8,104... | collective-permute-start | bytes 122888 | tf_op jit(solution)/shard_map/ppermute | solution.py:94
  136.4 4.7 %collective-permute-start.17 = (bf16[32,640]{1,0:T(8,128)(2,1)S(1)}, bf16[32,640]{1,0:T(8,128)(2,1)S(1)}, u32[]{:S(2)}, u32[]{:S(2)}) collective-permute-start(bf16[32,640]{1,0:T(8,128)(2,1)S(1)} %convert_element_type.337), channel_id=1, source_target_pairs={{0,224},{1,225},{2,226},{3,227},{4,228},{5,229},{6,230},{7,231},{8... | collective-permute-start | bytes 122888 | tf_op jit(solution)/shard_map/ppermute | solution.py:94
  141.2 3.6 %collective-permute-start.18 = (bf16[32,640]{1,0:T(8,128)(2,1)S(1)}, bf16[32,640]{1,0:T(8,128)(2,1)S(1)}, u32[]{:S(2)}, u32[]{:S(2)}) collective-permute-start(bf16[32,640]{1,0:T(8,128)(2,1)S(1)} %convert_element_type.339), channel_id=1, source_target_pairs={{0,36},{1,37},{2,38},{3,39},{4,32},{5,33},{6,34},{7,35},{8,44},{9,... | collective-permute-start | bytes 122888 | tf_op jit(solution)/shard_map/ppermute | solution.py:94
  144.8 4.7 %collective-permute-start.19 = (bf16[32,640]{1,0:T(8,128)(2,1)S(1)}, bf16[32,640]{1,0:T(8,128)(2,1)S(1)}, u32[]{:S(2)}, u32[]{:S(2)}) collective-permute-start(bf16[32,640]{1,0:T(8,128)(2,1)S(1)} %convert_element_type.341), channel_id=1, source_target_pairs={{0,60},{1,61},{2,62},{3,63},{4,40},{5,41},{6,42},{7,43},{8,36},{9,... | collective-permute-start | bytes 122888 | tf_op jit(solution)/shard_map/ppermute | solution.py:94
  149.5 5.8 %collective-permute-start.20 = (bf16[32,640]{1,0:T(8,128)(2,1)S(1)}, bf16[32,640]{1,0:T(8,128)(2,1)S(1)}, u32[]{:S(2)}, u32[]{:S(2)}) collective-permute-start(bf16[32,640]{1,0:T(8,128)(2,1)S(1)} %convert_element_type.343), channel_id=1, source_target_pairs={{0,44},{1,45},{2,46},{3,47},{4,56},{5,57},{6,58},{7,59},{8,52},{9,... | collective-permute-start | bytes 122888 | tf_op jit(solution)/shard_map/ppermute | solution.py:94
  155.3 1.6 collective-permute-start.21
  159.1 1.3 collective-permute-start.22
  160.4 3.6 %collective-permute-start.23 = (bf16[32,640]{1,0:T(8,128)(2,1)S(1)}, bf16[32,640]{1,0:T(8,128)(2,1)S(1)}, u32[]{:S(2)}, u32[]{:S(2)}) collective-permute-start(bf16[32,640]{1,0:T(8,128)(2,1)S(1)} %convert_element_type.346), channel_id=1, source_target_pairs={{0,33},{1,32},{2,35},{3,34},{4,37},{5,36},{6,39},{7,38},{8,41},{9,... | collective-permute-start | bytes 122888 | tf_op jit(solution)/shard_map/ppermute | solution.py:94
  164.1 4.8 %collective-permute-start.24 = (bf16[32,640]{1,0:T(8,128)(2,1)S(1)}, bf16[32,640]{1,0:T(8,128)(2,1)S(1)}, u32[]{:S(2)}, u32[]{:S(2)}) collective-permute-start(bf16[32,640]{1,0:T(8,128)(2,1)S(1)} %convert_element_type.348), channel_id=1, source_target_pairs={{0,35},{1,34},{2,33},{3,32},{4,39},{5,38},{6,37},{7,36},{8,43},{9,... | collective-permute-start | bytes 122888 | tf_op jit(solution)/shard_map/ppermute | solution.py:94
  168.9 3.5 %collective-permute-start.25 = (bf16[32,640]{1,0:T(8,128)(2,1)S(1)}, bf16[32,640]{1,0:T(8,128)(2,1)S(1)}, u32[]{:S(2)}, u32[]{:S(2)}) collective-permute-start(bf16[32,640]{1,0:T(8,128)(2,1)S(1)} %convert_element_type.350), channel_id=1, source_target_pairs={{0,96},{1,97},{2,98},{3,99},{4,100},{5,101},{6,102},{7,103},{8,104... | collective-permute-start | bytes 122888 | tf_op jit(solution)/shard_map/ppermute | solution.py:94
  172.5 4.8 %collective-permute-start.26 = (bf16[32,640]{1,0:T(8,128)(2,1)S(1)}, bf16[32,640]{1,0:T(8,128)(2,1)S(1)}, u32[]{:S(2)}, u32[]{:S(2)}) collective-permute-start(bf16[32,640]{1,0:T(8,128)(2,1)S(1)} %convert_element_type.352), channel_id=1, source_target_pairs={{0,224},{1,225},{2,226},{3,227},{4,228},{5,229},{6,230},{7,231},{8... | collective-permute-start | bytes 122888 | tf_op jit(solution)/shard_map/ppermute | solution.py:94
  177.3 3.9 %collective-permute-start.27 = (bf16[32,640]{1,0:T(8,128)(2,1)S(1)}, bf16[32,640]{1,0:T(8,128)(2,1)S(1)}, u32[]{:S(2)}, u32[]{:S(2)}) collective-permute-start(bf16[32,640]{1,0:T(8,128)(2,1)S(1)} %convert_element_type.354), channel_id=1, source_target_pairs={{0,36},{1,37},{2,38},{3,39},{4,32},{5,33},{6,34},{7,35},{8,44},{9,... | collective-permute-start | bytes 122888 | tf_op jit(solution)/shard_map/ppermute | solution.py:94
  181.2 4.8 %collective-permute-start.28 = (bf16[32,640]{1,0:T(8,128)(2,1)S(1)}, bf16[32,640]{1,0:T(8,128)(2,1)S(1)}, u32[]{:S(2)}, u32[]{:S(2)}) collective-permute-start(bf16[32,640]{1,0:T(8,128)(2,1)S(1)} %convert_element_type.356), channel_id=1, source_target_pairs={{0,60},{1,61},{2,62},{3,63},{4,40},{5,41},{6,42},{7,43},{8,36},{9,... | collective-permute-start | bytes 122888 | tf_op jit(solution)/shard_map/ppermute | solution.py:94
  186.0 5.8 %collective-permute-start.29 = (bf16[32,640]{1,0:T(8,128)(2,1)S(1)}, bf16[32,640]{1,0:T(8,128)(2,1)S(1)}, u32[]{:S(2)}, u32[]{:S(2)}) collective-permute-start(bf16[32,640]{1,0:T(8,128)(2,1)S(1)} %convert_element_type.358), channel_id=1, source_target_pairs={{0,44},{1,45},{2,46},{3,47},{4,56},{5,57},{6,58},{7,59},{8,52},{9,... | collective-permute-start | bytes 122888 | tf_op jit(solution)/shard_map/ppermute | solution.py:94
  191.8 1.6 collective-permute-start.30

commit v4 on v3

--- a/solution.py
+++ b/solution.py
@@ -16,33 +16,120 @@
 F32 = jnp.float32
 
 
-def padded(x, sides, width, wrap):
-    for axis, dim in sides:
-        count, length = (lax.axis_size(axis), x.shape[dim])
-        up = [(i, (i + 1) % count) for i in range(count if wrap else count - 1)]
-        down = [(j, i) for i, j in up]
-        last = lax.slice_in_dim(x, length - width, length, axis=dim)
-        initial = lax.slice_in_dim(x, 0, width, axis=dim)
-        before = lax.ppermute(last, axis, up)
-        after = lax.ppermute(initial, axis, down)
-        x = jnp.concatenate([before, x, after], axis=dim)
-    return x
-
-
-def filter_columns(widened, column_taps, extent):
-    summed = jnp.zeros((widened.shape[0], extent, widened.shape[2]), jnp.float32)
-    for offset in range(column_taps.shape[0]):
-        summed = summed + column_taps[offset] * widened[:, offset : offset + extent, :].astype(
-            jnp.float32
-        )
-    return summed
-
-
-def filter_rows(extended, row_taps, extent):
-    summed = jnp.zeros((extent, extended.shape[1], extended.shape[2]), jnp.float32)
-    for offset in range(row_taps.shape[0]):
-        summed = summed + row_taps[offset] * extended[offset : offset + extent].astype(jnp.float32)
-    return summed
+TAPS = 21
+MARGIN = TAPS // 2
+LANES = 128
+
+
+def weighted(taps_ref, items, rows):
+    outs = [None] * len(items)
+    for k in range(TAPS):
+        if not any(k in pairs for pairs in items):
+            continue
+        tap = jnp.broadcast_to(taps_ref[k : k + 1, :], (rows, LANES))
+        for i, pairs in enumerate(items):
+            if k in pairs:
+                term = tap * pairs[k]
+                outs[i] = term if outs[i] is None else outs[i] + term
+    return outs
+
+
+def own_sums(taps_ref, load, length, group, emit):
+    for start in range(0, length, group):
+        lo, hi = max(0, start - MARGIN), min(length, start + group + MARGIN)
+        window = {i: load(i) for i in range(lo, hi)}
+        items = [
+            {k: window[o + k - MARGIN] for k in range(TAPS) if o + k - MARGIN in window}
+            for o in range(start, start + group)
+        ]
+        for i, value in enumerate(weighted(taps_ref, items, 8)):
+            emit(start + i, value)
+
+
+def columns_own_kernel(band_ref, taps_ref, out_ref, flat, turned):
+    h, w, lanes = band_ref.shape
+    flat[...] = band_ref[...].astype(F32).reshape(h * w, lanes)
+    for j in range(w):
+        turned[j] = flat[pl.ds(j, h, stride=w), :]
+
+    def body(i, carry):
+        rows = pl.ds(pl.multiple_of(i * 8, 8), 8)
+
+        def emit(o, value):
+            out_ref[o, rows, :] = value
+
+        own_sums(taps_ref, lambda j: turned[j, rows, :], w, 8, emit)
+        return carry
+
+    lax.fori_loop(0, h // 8, body, 0)
+
+
+def columns_rest_kernel(flags_ref, own_ref, left_ref, right_ref, taps_ref, out_ref, lefts, rights, flat):
+    w, h, lanes = own_ref.shape
+    lefts[...] = jnp.where(flags_ref[1] == 1, left_ref[...].astype(F32), 0.0)
+    rights[...] = jnp.where(flags_ref[2] == 1, right_ref[...].astype(F32), 0.0)
+
+    def body(i, carry):
+        rows = pl.ds(pl.multiple_of(i * 8, 8), 8)
+
+        def put(o, value):
+            flat[pl.ds(i * (8 * w) + o, 8, stride=w), :] = value
+
+        before = [lefts[j, rows, :] for j in range(MARGIN)]
+        items = [{j - o: before[j] for j in range(o, MARGIN)} for o in range(MARGIN)]
+        for o, value in enumerate(weighted(taps_ref, items, 8)):
+            put(o, own_ref[o, rows, :] + value)
+        for o in range(MARGIN, w - MARGIN):
+            put(o, own_ref[o, rows, :])
+        after = [rights[j, rows, :] for j in range(MARGIN)]
+        items = [{2 * MARGIN + j - o: after[j] for j in range(o + 1)} for o in range(MARGIN)]
+        for o, value in enumerate(weighted(taps_ref, items, 8)):
+            put(w - MARGIN + o, own_ref[w - MARGIN + o, rows, :] + value)
+        return carry
+
+    lax.fori_loop(0, h // 8, body, 0)
+    out_ref[...] = flat[...].reshape(h, w, lanes).astype(BF)
+
+
+def rows_own_kernel(filtered_ref, band_ref, taps_ref, mid_ref, top_ref, low_ref, source, residual, mixed):
+    h, w, _ = filtered_ref.shape
+    source[...] = filtered_ref[...].astype(F32)
+    residual[...] = band_ref[...].astype(F32)
+
+    def body(i, carry):
+        cols = pl.ds(pl.multiple_of(i * 8, 8), 8)
+
+        def emit(o, value):
+            value = residual[o, cols, :] + value
+            if o < MARGIN:
+                top_ref[o, cols, :] = value
+            elif o >= h - MARGIN:
+                low_ref[o - (h - MARGIN), cols, :] = value
+            else:
+                mixed[o - MARGIN, cols, :] = value
+
+        own_sums(taps_ref, lambda j: source[j, cols, :], h, 8, emit)
+        return carry
+
+    lax.fori_loop(0, w // 8, body, 0)
+    mid_ref[...] = mixed[...].astype(BF)
+
+
+def finished_edge(part_ref, halo_ref, taps_ref, present, pairs_of):
+    blocks = []
+    for start in range(0, part_ref.shape[2], LANES):
+        lanes = slice(start, start + LANES)
+        halo = [
+            jnp.where(present, halo_ref[j, :, lanes].astype(F32), 0.0) for j in range(MARGIN)
+        ]
+        rows = []
+        for o in range(MARGIN):
+            value = part_ref[o, :, lanes]
+            for k, j in pairs_of(o):
+                value = value + taps_ref[k : k + 1, lanes] * halo[j]
+            rows.append(value.astype(BF))
+        blocks.append(jnp.concatenate(rows, axis=0))
+    return jnp.concatenate(blocks, axis=1)
 
 
 def pair_4a(i):
@@ -134,17 +221,33 @@
 
 
 def first_kernel(
-    half_ref, mixed_ref, w_ref, basis_ref, feature_ref, coeffs_ref, mine_ref, theirs_ref
+    flags_ref, mid_ref, top_ref, low_ref, above_ref, below_ref, taps_ref, w_ref, basis_ref,
+    feature_ref, coeffs_ref, mine_ref, theirs_ref,
 ):
-    feature = jnp.maximum(dot(mixed_ref[...], w_ref[...], NN), 0.0).astype(BF)
-    feature_ref[...] = feature
+    rows, cols, channels = mid_ref.shape
+    edge, mid = MARGIN * cols, rows * cols
+    w = w_ref[...]
+    top = finished_edge(
+        top_ref, above_ref, taps_ref, flags_ref[3] == 1, lambda o: [(j - o, j) for j in range(o, MARGIN)]
+    )
+    low = finished_edge(
+        low_ref, below_ref, taps_ref, flags_ref[4] == 1, lambda o: [(2 * MARGIN + j - o, j) for j in range(o + 1)]
+    )
+
+    def squeezed(mixed):
+        return jnp.maximum(dot(mixed, w, NN), 0.0).astype(BF)
+
+    feature_ref[:edge] = squeezed(top)
+    feature_ref[edge : edge + mid] = squeezed(mid_ref[...].reshape(mid, channels))
+    feature_ref[edge + mid :] = squeezed(low)
+    feature = feature_ref[...]
     basis = basis_ref[...]
     scores = dot(basis.astype(BF), feature, NT)
     e = jnp.exp(scores - jnp.max(scores, axis=0, keepdims=True))
     soft = e / jnp.sum(e, axis=0, keepdims=True)
     coeffs = coeffs_of(basis, soft, scores)
     coeffs_ref[...] = coeffs
-    emit_sums(half_ref, coeffs, feature, mine_ref, theirs_ref)
+    emit_sums(flags_ref, coeffs, feature, mine_ref, theirs_ref)
 
 
 def updated_basis(half_ref, own_ref, got_ref, basis):
@@ -195,38 +298,94 @@
 def on_device(band_input, column_taps, row_taps, w_squeeze, bases_init, w_ham, w_align):
     tile_rows, tile_cols, channels = band_input.shape
     margin = column_taps.shape[0] // 2
-    half = sum(lax.axis_index(a) for a in ALL) % 2
-    half = half.astype(jnp.int32).reshape(1)
-    framed = padded(band_input, ((ROWS, 0), (COLS, 1)), margin, False)
-    col_filtered = filter_columns(framed, column_taps, tile_cols).astype(jnp.bfloat16)
-    strip_sum = filter_rows(col_filtered, row_taps, tile_rows)
-    mixed_tile = (
-        (band_input.astype(jnp.float32) + strip_sum)
-        .astype(jnp.bfloat16)
-        .reshape(tile_rows * tile_cols, channels)
-    )
+    index = {name: lax.axis_index(name) for name in ALL}
+    half = sum(index.values()) % 2
+    row, col = lax.axis_index(ROWS), lax.axis_index(COLS)
+    flags = [half, col > 0, col < Z * X - 1, row > 0, row < Y * CORE - 1]
+    flags = jnp.stack([f.astype(jnp.int32) for f in flags])
+    sds = jax.ShapeDtypeStruct
+
+    def ring(count, by):
+        return [(i, (i + by) % count) for i in range(count)]
+
+    left = band_input[:, tile_cols - margin :].transpose(1, 0, 2)
+    right = band_input[:, :margin].transpose(1, 0, 2)
+    left = lax.ppermute(left, COLS, ring(Z * X, 1))
+    right = lax.ppermute(right, COLS, ring(Z * X, -1))
+
+    def blocks(*dims):
+        return pl.BlockSpec((*dims, LANES), lambda i: (*(0 for _ in dims), i))
+
+    scalar = pl.BlockSpec(memory_space=pltpu.SMEM)
+    tile, turned = blocks(tile_rows, tile_cols), blocks(tile_cols, tile_rows)
+    side, edge = blocks(margin, tile_rows), blocks(margin, tile_cols)
+    taps = blocks(TAPS)
+    grid = (channels // LANES,)
+    flat = pltpu.VMEM((tile_rows * tile_cols, LANES), F32)
+    params = pltpu.CompilerParams(vmem_limit_bytes=20 * 2**20)
+    pixels = tile_rows * tile_cols * channels
+    cost = pl.CostEstimate(flops=2 * TAPS * pixels, bytes_accessed=6 * pixels, transcendentals=0)
+    own = pl.pallas_call(
+        columns_own_kernel,
+        grid=grid,
+        in_specs=[tile, taps],
+        out_specs=turned,
+        out_shape=sds((tile_cols, tile_rows, channels), F32),
+        scratch_shapes=[flat, pltpu.VMEM((tile_cols, tile_rows, LANES), F32)],
+        compiler_params=params,
+        cost_estimate=cost,
+    )(band_input, column_taps)
+    filtered = pl.pallas_call(
+        columns_rest_kernel,
+        grid=grid,
+        in_specs=[scalar, turned, side, side, taps],
+        out_specs=tile,
+        out_shape=sds(band_input.shape, BF),
+        scratch_shapes=[pltpu.VMEM((margin, tile_rows, LANES), F32)] * 2 + [flat],
+        compiler_params=params,
+    )(flags, own, left, right, column_taps)
+    above = lax.ppermute(filtered[tile_rows - margin :], ROWS, ring(Y * CORE, 1))
+    below = lax.ppermute(filtered[:margin], ROWS, ring(Y * CORE, -1))
+    rest = tile_rows - 2 * margin
+    mid, top, low = pl.pallas_call(
+        rows_own_kernel,
+        grid=grid,
+        in_specs=[tile, tile, taps],
+        out_specs=[blocks(rest, tile_cols), edge, edge],
+        out_shape=[
+            sds((rest, tile_cols, channels), BF),
+            sds((margin, tile_cols, channels), F32),
+            sds((margin, tile_cols, channels), F32),
+        ],
+        scratch_shapes=[
+            pltpu.VMEM((tile_rows, tile_cols, LANES), F32),
+            pltpu.VMEM((tile_rows, tile_cols, LANES), F32),
+            pltpu.VMEM((rest, tile_cols, LANES), F32),
+        ],
+        compiler_params=params,
+        cost_estimate=cost,
+    )(filtered, band_input, row_taps)
     n, r = tile_rows * tile_cols, bases_init.shape[1]
-    sds = jax.ShapeDtypeStruct
     width = channels + 128
     sums = [sds((r // 2, width), F32), sds((r // 2, width), BF)]
     basis = bases_init.T
     feature, coeffs, mine, theirs = call(
         first_kernel,
         [sds((n, channels), BF), sds((r, n), F32)] + sums,
-        half, mixed_tile, w_squeeze, basis,
+        flags, mid, top, low, above, below, row_taps, w_squeeze, basis,
     )
     for _ in range(STEPS - 1):
         own, got = summed_over_all(mine, theirs)
         basis, coeffs, mine, theirs = call(
             step_kernel,
             [sds((r, channels), F32), sds((r, n), F32)] + sums,
-            half, own, got, basis, feature, coeffs,
+            flags, own, got, basis, feature, coeffs,
         )
     own, got = summed_over_all(mine, theirs)
     head_out = call(
         last_kernel,
         sds((n, channels), BF),
-        half, own, got, basis, feature, coeffs, w_ham, w_align,
+        flags, own, got, basis, feature, coeffs, w_ham, w_align,
     )
     return head_out.reshape(tile_rows, tile_cols, channels)
 

time: 200 us -> 161 us (0.81)
  other arithmetic: 32.6 us -> 0.39 us
  Pallas kernels: 13.3 us -> 37.4 us
  starting transfers between devices: 68.6 us -> 53.1 us
  waiting for transfers between devices: 78.9 us -> 64.8 us
    convert_element_type x2 -> x0, other arithmetic: 27.8 us -> none  [the longest x1 14.4 us: on_device(): mixed_tile = (band_input.astype(jnp.float32) + strip_sum).astype(jnp.bflo...]
    pallas_call x0 -> x3, Pallas kernels: none -> 21.6 us  [the longest x1 8.92 us: on_device(): pl.pallas_call(columns_own_kernel, grid=grid, in_specs=[tile, taps], out_...]
    ppermute x4, waiting for transfers between devices: 24.7 us -> 4.71 us  [the longest x1 4.42 us: on_device(): left = lax.ppermute(left, COLS, ring(Z * X, 1))]
    ppermute x21, starting transfers between devices: 54.5 us -> 39.6 us  [summed_over_all(): got = lax.ppermute(total.astype(BF), ALL, round_pairs(axis, rule))]
    ppermute x21, waiting for transfers between devices: 48.4 us -> 54.1 us  [summed_over_all(): got = lax.ppermute(total.astype(BF), ALL, round_pairs(axis, rule))]
    concatenate x2 -> x0, other arithmetic: 4.41 us -> none  [padded(): x = jnp.concatenate([before, x, after], axis=dim)]
    pallas_call x4, Pallas kernels: 13.3 us -> 15.8 us  [call(): pl.pallas_call(kernel, out_shape=outs, in_specs=specs, out_specs=jax.tree...]
  transfers between devices with their start and end apart: 31 -> 31, of which waited for: 31 -> 29; matrix products, arithmetic and copies ran while one was open for 0% -> 1% of each run, Pallas kernels for 0% -> 10%
where the time goes in v4:
time: 161 us
  waiting for transfers between devices  64.8 us (40%)
  starting transfers between devices  53.1 us (33%)
  Pallas kernels  37.4 us (23%)
  local copies, waits for them, and re-layouts  4.55 us (3%)
    ppermute x21, waiting for transfers between devices, summed_over_all(): got = lax.ppermute(total.astype(BF), ALL, round_pairs(axis, rule))  54.1 us
    ppermute x21, starting transfers between devices, summed_over_all(): got = lax.ppermute(total.astype(BF), ALL, round_pairs(axis, rule))  39.6 us
    pallas_call x4, Pallas kernels, call(): pl.pallas_call(kernel, out_shape=outs, in_specs=specs, out_specs=jax.tree...  15.8 us
    pallas_call x1, Pallas kernels, on_device(): pl.pallas_call(columns_own_kernel, grid=grid, in_specs=[tile, taps], out_...  8.92 us
    pallas_call x1, Pallas kernels, on_device(): pl.pallas_call(rows_own_kernel, grid=grid, in_specs=[tile, tile, taps], o...  7.66 us
    ppermute x1, starting transfers between devices, on_device(): right = lax.ppermute(right, COLS, ring(Z * X, -1))  6.56 us
    pallas_call x1, Pallas kernels, on_device(): pl.pallas_call(columns_rest_kernel, grid=grid, in_specs=[scalar, turned,...  5.01 us
    ppermute x1, waiting for transfers between devices, on_device(): left = lax.ppermute(left, COLS, ring(Z * X, 1))  4.42 us
  transfers between devices with their start and end apart: 31, of which 29 were waited for; matrix products, arithmetic and copies ran while one was open for 1% of the time, Pallas kernels for 10%

profile of v4, /device:TPU:1, one launch (start us, length us, event | category | flops | bytes accessed | tf_op | source)
XLA Modules:
  0.0 160.6 jit_solution(8688831391556914987)
XLA Ops:
  0.0 2.0 %fusion.1 = (bf16[64,10,512]{2,1,0:T(8,128)(2,1)S(1)}, bf16[64,10,512]{2,1,0:T(8,128)(2,1)S(1)}) fusion(bf16[64,32,512]{2,1,0:T(8,128)(2,1)} %band_ref.3), kind=kLoop, calls=%fused_computation.27 | loop fusion | bytes 2621440 | tf_op jit(solution)/shard_map/slice | solution.py:312
  2.0 1.2 copy.15
  3.2 2.0 %collective-permute-start = (bf16[10,64,512]{2,1,0:T(8,128)(2,1)}, bf16[10,64,512]{2,1,0:T(8,128)(2,1)S(1)}, u32[]{:S(2)}, u32[]{:S(2)}) collective-permute-start(bf16[10,64,512]{2,1,0:T(8,128)(2,1)} %bitcast.12), channel_id=1, source_target_pairs={{0,1},{1,2},{2,3},{3,4},{4,5},{5,6},{6,7},{7,8},{8,9},{9,10},{10,1... | collective-permute-start | bytes 1966088 | tf_op jit(solution)/shard_map/ppermute | solution.py:313
  5.3 1.2 copy.14
  6.5 6.6 %collective-permute-start.1 = (bf16[10,64,512]{2,1,0:T(8,128)(2,1)}, bf16[10,64,512]{2,1,0:T(8,128)(2,1)S(1)}, u32[]{:S(2)}, u32[]{:S(2)}) collective-permute-start(bf16[10,64,512]{2,1,0:T(8,128)(2,1)} %bitcast.11), channel_id=1, source_target_pairs={{0,31},{1,0},{2,1},{3,2},{4,3},{5,4},{6,5},{7,6},{8,7},{9,8},{10,9... | collective-permute-start | bytes 1966088 | tf_op jit(solution)/shard_map/ppermute | solution.py:314
  13.1 8.9 %shard_map.73.own_ref = f32[32,64,512]{2,1,0:T(8,128)S(1)} custom-call(bf16[64,32,512]{2,1,0:T(8,128)(2,1)S(1)} %copy-done, f32[21,512]{1,0:T(8,128)S(1)} %copy-done.5), custom_call_target="tpu_custom_call" | custom-call | flops 44040192 | bytes 6291456 | tf_op jit(solution)/shard_map/pallas_call | solution.py:328
  22.0 4.4 %collective-permute-done.left_ref = bf16[10,64,512]{2,1,0:T(8,128)(2,1)S(1)} collective-permute-done((bf16[10,64,512]{2,1,0:T(8,128)(2,1)}, bf16[10,64,512]{2,1,0:T(8,128)(2,1)S(1)}, u32[]{:S(2)}, u32[]{:S(2)}) %collective-permute-start) | collective-permute-done | bytes 655392 | tf_op jit(solution)/shard_map/ppermute | solution.py:313
  26.7 5.0 %shard_map.74.filtered_ref = bf16[64,32,512]{2,1,0:T(8,128)(2,1)S(1)} custom-call(s32[5]{0:T(128)S(1)} %stack.39.flags_ref.half_ref, f32[32,64,512]{2,1,0:T(8,128)S(1)} %shard_map.73.own_ref, bf16[10,64,512]{2,1,0:T(8,128)(2,1)S(1)} %collective-permute-done.left_ref, bf16[10,64,512]{2,1,0:T(8,128)(2,1)S(1)} %collective-permute-done.1.right_ref, ...), custom_call_target="tpu_custom_call" | custom-call | tf_op jit(solution)/shard_map/pallas_call | solution.py:338
  31.8 1.5 collective-permute-start.3
  33.4 1.2 collective-permute-start.2
  34.6 7.7 %shard_map.75 = (bf16[44,32,512]{2,1,0:T(8,128)(2,1)S(1)}, f32[10,32,512]{2,1,0:T(8,128)S(1)}, f32[10,32,512]{2,1,0:T(8,128)S(1)}) custom-call(bf16[64,32,512]{2,1,0:T(8,128)(2,1)S(1)} %shard_map.74.filtered_ref, bf16[64,32,512]{2,1,0:T(8,128)(2,1)S(1)} %copy-done, f32[21,512]{1,0:T(8,128)S(1)} %copy-done.6), custom_call_target="tpu_custom_call" | custom-call | flops 44040192 | bytes 6291456 | tf_op jit(solution)/shard_map/pallas_call | solution.py:350
  42.3 4.0 %shard_map.76 = (bf16[2048,512]{1,0:T(8,128)(2,1)S(1)}, f32[64,2048]{1,0:T(8,128)S(1)}, f32[32,640]{1,0:T(8,128)S(1)}, bf16[32,640]{1,0:T(8,128)(2,1)S(1)}) custom-call(s32[5]{0:T(128)S(1)} %stack.39.flags_ref.half_ref, bf16[44,32,512]{2,1,0:T(8,128)(2,1)S(1)} %get-tuple-element.20.mid_ref, f32[10,32,512]{2,1,0:T(8,128)S(1)} %get-tuple-element.21.top_ref, ...), custom_call_target="tpu_custom_call" | custom-call | tf_op jit(solution)/shard_map/pallas_call | solution.py:289
  47.8 3.5 %collective-permute-done.5 = bf16[32,640]{1,0:T(8,128)(2,1)S(1)} collective-permute-done((bf16[32,640]{1,0:T(8,128)(2,1)S(1)}, bf16[32,640]{1,0:T(8,128)(2,1)S(1)}, u32[]{:S(2)}, u32[]{:S(2)}) %collective-permute-start.5) | collective-permute-done | bytes 40992 | tf_op jit(solution)/shard_map/ppermute | solution.py:181
  51.8 4.4 %collective-permute-done.6 = bf16[32,640]{1,0:T(8,128)(2,1)S(1)} collective-permute-done((bf16[32,640]{1,0:T(8,128)(2,1)S(1)}, bf16[32,640]{1,0:T(8,128)(2,1)S(1)}, u32[]{:S(2)}, u32[]{:S(2)}) %collective-permute-start.6) | collective-permute-done | bytes 40992 | tf_op jit(solution)/shard_map/ppermute | solution.py:181
  57.3 2.4 %collective-permute-done.7 = bf16[32,640]{1,0:T(8,128)(2,1)S(1)} collective-permute-done((bf16[32,640]{1,0:T(8,128)(2,1)S(1)}, bf16[32,640]{1,0:T(8,128)(2,1)S(1)}, u32[]{:S(2)}, u32[]{:S(2)}) %collective-permute-start.7) | collective-permute-done | bytes 40992 | tf_op jit(solution)/shard_map/ppermute | solution.py:181
  59.8 2.7 %collective-permute-start.8 = (bf16[32,640]{1,0:T(8,128)(2,1)S(1)}, bf16[32,640]{1,0:T(8,128)(2,1)S(1)}, u32[]{:S(2)}, u32[]{:S(2)}) collective-permute-start(bf16[32,640]{1,0:T(8,128)(2,1)S(1)} %convert_element_type.146), channel_id=1, source_target_pairs={{0,224},{1,225},{2,226},{3,227},{4,228},{5,229},{6,230},{7,231},{8... | collective-permute-start | bytes 122888 | tf_op jit(solution)/shard_map/ppermute | solution.py:181
  62.5 2.1 %collective-permute-done.8 = bf16[32,640]{1,0:T(8,128)(2,1)S(1)} collective-permute-done((bf16[32,640]{1,0:T(8,128)(2,1)S(1)}, bf16[32,640]{1,0:T(8,128)(2,1)S(1)}, u32[]{:S(2)}, u32[]{:S(2)}) %collective-permute-start.8) | collective-permute-done | bytes 40992 | tf_op jit(solution)/shard_map/ppermute | solution.py:181
  64.7 3.5 %collective-permute-done.9 = bf16[32,640]{1,0:T(8,128)(2,1)S(1)} collective-permute-done((bf16[32,640]{1,0:T(8,128)(2,1)S(1)}, bf16[32,640]{1,0:T(8,128)(2,1)S(1)}, u32[]{:S(2)}, u32[]{:S(2)}) %collective-permute-start.9) | collective-permute-done | bytes 40992 | tf_op jit(solution)/shard_map/ppermute | solution.py:181
  68.3 2.8 %collective-permute-start.10 = (bf16[32,640]{1,0:T(8,128)(2,1)S(1)}, bf16[32,640]{1,0:T(8,128)(2,1)S(1)}, u32[]{:S(2)}, u32[]{:S(2)}) collective-permute-start(bf16[32,640]{1,0:T(8,128)(2,1)S(1)} %convert_element_type.150), channel_id=1, source_target_pairs={{0,60},{1,61},{2,62},{3,63},{4,40},{5,41},{6,42},{7,43},{8,36},{9,... | collective-permute-start | bytes 122888 | tf_op jit(solution)/shard_map/ppermute | solution.py:181
  71.1 2.0 %collective-permute-done.10 = bf16[32,640]{1,0:T(8,128)(2,1)S(1)} collective-permute-done((bf16[32,640]{1,0:T(8,128)(2,1)S(1)}, bf16[32,640]{1,0:T(8,128)(2,1)S(1)}, u32[]{:S(2)}, u32[]{:S(2)}) %collective-permute-start.10) | collective-permute-done | bytes 40992 | tf_op jit(solution)/shard_map/ppermute | solution.py:181
  73.1 4.7 %collective-permute-start.11 = (bf16[32,640]{1,0:T(8,128)(2,1)S(1)}, bf16[32,640]{1,0:T(8,128)(2,1)S(1)}, u32[]{:S(2)}, u32[]{:S(2)}) collective-permute-start(bf16[32,640]{1,0:T(8,128)(2,1)S(1)} %convert_element_type.152), channel_id=1, source_target_pairs={{0,44},{1,45},{2,46},{3,47},{4,56},{5,57},{6,58},{7,59},{8,52},{9,... | collective-permute-start | bytes 122888 | tf_op jit(solution)/shard_map/ppermute | solution.py:181
  77.8 1.7 %collective-permute-done.11 = bf16[32,640]{1,0:T(8,128)(2,1)S(1)} collective-permute-done((bf16[32,640]{1,0:T(8,128)(2,1)S(1)}, bf16[32,640]{1,0:T(8,128)(2,1)S(1)}, u32[]{:S(2)}, u32[]{:S(2)}) %collective-permute-start.11) | collective-permute-done | bytes 40992 | tf_op jit(solution)/shard_map/ppermute | solution.py:181
  80.8 2.7 %shard_map.77 = (f32[64,512]{1,0:T(8,128)S(1)}, f32[64,2048]{1,0:T(8,128)S(1)}, f32[32,640]{1,0:T(8,128)S(1)}, bf16[32,640]{1,0:T(8,128)(2,1)S(1)}) custom-call(s32[5]{0:T(128)S(1)} %stack.39.flags_ref.half_ref, f32[32,640]{1,0:T(8,128)S(1)} %convert_add_fusion.16.own_ref, f32[32,640]{1,0:T(8,128)S(1)} %collective-permute-done.12.got_ref, ...), custom_call_target="tpu_custom_call" | custom-call | tf_op jit(solution)/shard_map/pallas_call | solution.py:289
  85.0 3.4 %collective-permute-done.14 = bf16[32,640]{1,0:T(8,128)(2,1)S(1)} collective-permute-done((bf16[32,640]{1,0:T(8,128)(2,1)S(1)}, bf16[32,640]{1,0:T(8,128)(2,1)S(1)}, u32[]{:S(2)}, u32[]{:S(2)}) %collective-permute-start.14) | collective-permute-done | bytes 40992 | tf_op jit(solution)/shard_map/ppermute | solution.py:181
  88.5 2.8 %collective-permute-start.15 = (bf16[32,640]{1,0:T(8,128)(2,1)S(1)}, bf16[32,640]{1,0:T(8,128)(2,1)S(1)}, u32[]{:S(2)}, u32[]{:S(2)}) collective-permute-start(bf16[32,640]{1,0:T(8,128)(2,1)S(1)} %convert_element_type.157), channel_id=1, source_target_pairs={{0,35},{1,34},{2,33},{3,32},{4,39},{5,38},{6,37},{7,36},{8,43},{9,... | collective-permute-start | bytes 122888 | tf_op jit(solution)/shard_map/ppermute | solution.py:181
  91.2 2.0 %collective-permute-done.15 = bf16[32,640]{1,0:T(8,128)(2,1)S(1)} collective-permute-done((bf16[32,640]{1,0:T(8,128)(2,1)S(1)}, bf16[32,640]{1,0:T(8,128)(2,1)S(1)}, u32[]{:S(2)}, u32[]{:S(2)}) %collective-permute-start.15) | collective-permute-done | bytes 40992 | tf_op jit(solution)/shard_map/ppermute | solution.py:181
  93.5 3.3 %collective-permute-done.16 = bf16[32,640]{1,0:T(8,128)(2,1)S(1)} collective-permute-done((bf16[32,640]{1,0:T(8,128)(2,1)S(1)}, bf16[32,640]{1,0:T(8,128)(2,1)S(1)}, u32[]{:S(2)}, u32[]{:S(2)}) %collective-permute-start.16) | collective-permute-done | bytes 40992 | tf_op jit(solution)/shard_map/ppermute | solution.py:181
  96.8 2.8 %collective-permute-start.17 = (bf16[32,640]{1,0:T(8,128)(2,1)S(1)}, bf16[32,640]{1,0:T(8,128)(2,1)S(1)}, u32[]{:S(2)}, u32[]{:S(2)}) collective-permute-start(bf16[32,640]{1,0:T(8,128)(2,1)S(1)} %convert_element_type.161), channel_id=1, source_target_pairs={{0,224},{1,225},{2,226},{3,227},{4,228},{5,229},{6,230},{7,231},{8... | collective-permute-start | bytes 122888 | tf_op jit(solution)/shard_map/ppermute | solution.py:181
  99.6 1.9 %collective-permute-done.17 = bf16[32,640]{1,0:T(8,128)(2,1)S(1)} collective-permute-done((bf16[32,640]{1,0:T(8,128)(2,1)S(1)}, bf16[32,640]{1,0:T(8,128)(2,1)S(1)}, u32[]{:S(2)}, u32[]{:S(2)}) %collective-permute-start.17) | collective-permute-done | bytes 40992 | tf_op jit(solution)/shard_map/ppermute | solution.py:181
  101.5 1.3 collective-permute-start.18
  102.9 2.2 %collective-permute-done.18 = bf16[32,640]{1,0:T(8,128)(2,1)S(1)} collective-permute-done((bf16[32,640]{1,0:T(8,128)(2,1)S(1)}, bf16[32,640]{1,0:T(8,128)(2,1)S(1)}, u32[]{:S(2)}, u32[]{:S(2)}) %collective-permute-start.18) | collective-permute-done | bytes 40992 | tf_op jit(solution)/shard_map/ppermute | solution.py:181
  105.1 3.6 %collective-permute-start.19 = (bf16[32,640]{1,0:T(8,128)(2,1)S(1)}, bf16[32,640]{1,0:T(8,128)(2,1)S(1)}, u32[]{:S(2)}, u32[]{:S(2)}) collective-permute-start(bf16[32,640]{1,0:T(8,128)(2,1)S(1)} %convert_element_type.165), channel_id=1, source_target_pairs={{0,60},{1,61},{2,62},{3,63},{4,40},{5,41},{6,42},{7,43},{8,36},{9,... | collective-permute-start | bytes 122888 | tf_op jit(solution)/shard_map/ppermute | solution.py:181
  108.6 1.8 %collective-permute-done.19 = bf16[32,640]{1,0:T(8,128)(2,1)S(1)} collective-permute-done((bf16[32,640]{1,0:T(8,128)(2,1)S(1)}, bf16[32,640]{1,0:T(8,128)(2,1)S(1)}, u32[]{:S(2)}, u32[]{:S(2)}) %collective-permute-start.19) | collective-permute-done | bytes 40992 | tf_op jit(solution)/shard_map/ppermute | solution.py:181
  110.4 3.6 %collective-permute-start.20 = (bf16[32,640]{1,0:T(8,128)(2,1)S(1)}, bf16[32,640]{1,0:T(8,128)(2,1)S(1)}, u32[]{:S(2)}, u32[]{:S(2)}) collective-permute-start(bf16[32,640]{1,0:T(8,128)(2,1)S(1)} %convert_element_type.167), channel_id=1, source_target_pairs={{0,44},{1,45},{2,46},{3,47},{4,56},{5,57},{6,58},{7,59},{8,52},{9,... | collective-permute-start | bytes 122888 | tf_op jit(solution)/shard_map/ppermute | solution.py:181
  114.1 1.9 %collective-permute-done.20 = bf16[32,640]{1,0:T(8,128)(2,1)S(1)} collective-permute-done((bf16[32,640]{1,0:T(8,128)(2,1)S(1)}, bf16[32,640]{1,0:T(8,128)(2,1)S(1)}, u32[]{:S(2)}, u32[]{:S(2)}) %collective-permute-start.20) | collective-permute-done | bytes 40992 | tf_op jit(solution)/shard_map/ppermute | solution.py:181
  117.3 2.7 %shard_map.78 = (f32[64,512]{1,0:T(8,128)S(1)}, f32[64,2048]{1,0:T(8,128)S(1)}, f32[32,640]{1,0:T(8,128)S(1)}, bf16[32,640]{1,0:T(8,128)(2,1)S(1)}) custom-call(s32[5]{0:T(128)S(1)} %stack.39.flags_ref.half_ref, f32[32,640]{1,0:T(8,128)S(1)} %convert_add_fusion.8.own_ref, f32[32,640]{1,0:T(8,128)S(1)} %collective-permute-done.21.got_ref, ...), custom_call_target="tpu_custom_call" | custom-call | tf_op jit(solution)/shard_map/pallas_call | solution.py:289
  121.5 3.5 %collective-permute-done.23 = bf16[32,640]{1,0:T(8,128)(2,1)S(1)} collective-permute-done((bf16[32,640]{1,0:T(8,128)(2,1)S(1)}, bf16[32,640]{1,0:T(8,128)(2,1)S(1)}, u32[]{:S(2)}, u32[]{:S(2)}) %collective-permute-start.23) | collective-permute-done | bytes 40992 | tf_op jit(solution)/shard_map/ppermute | solution.py:181
  125.0 2.5 %collective-permute-start.24 = (bf16[32,640]{1,0:T(8,128)(2,1)S(1)}, bf16[32,640]{1,0:T(8,128)(2,1)S(1)}, u32[]{:S(2)}, u32[]{:S(2)}) collective-permute-start(bf16[32,640]{1,0:T(8,128)(2,1)S(1)} %convert_element_type.172), channel_id=1, source_target_pairs={{0,35},{1,34},{2,33},{3,32},{4,39},{5,38},{6,37},{7,36},{8,43},{9,... | collective-permute-start | bytes 122888 | tf_op jit(solution)/shard_map/ppermute | solution.py:181
  127.6 2.3 %collective-permute-done.24 = bf16[32,640]{1,0:T(8,128)(2,1)S(1)} collective-permute-done((bf16[32,640]{1,0:T(8,128)(2,1)S(1)}, bf16[32,640]{1,0:T(8,128)(2,1)S(1)}, u32[]{:S(2)}, u32[]{:S(2)}) %collective-permute-start.24) | collective-permute-done | bytes 40992 | tf_op jit(solution)/shard_map/ppermute | solution.py:181
  130.0 3.5 %collective-permute-done.25 = bf16[32,640]{1,0:T(8,128)(2,1)S(1)} collective-permute-done((bf16[32,640]{1,0:T(8,128)(2,1)S(1)}, bf16[32,640]{1,0:T(8,128)(2,1)S(1)}, u32[]{:S(2)}, u32[]{:S(2)}) %collective-permute-start.25) | collective-permute-done | bytes 40992 | tf_op jit(solution)/shard_map/ppermute | solution.py:181
  133.5 2.7 %collective-permute-start.26 = (bf16[32,640]{1,0:T(8,128)(2,1)S(1)}, bf16[32,640]{1,0:T(8,128)(2,1)S(1)}, u32[]{:S(2)}, u32[]{:S(2)}) collective-permute-start(bf16[32,640]{1,0:T(8,128)(2,1)S(1)} %convert_element_type.176), channel_id=1, source_target_pairs={{0,224},{1,225},{2,226},{3,227},{4,228},{5,229},{6,230},{7,231},{8... | collective-permute-start | bytes 122888 | tf_op jit(solution)/shard_map/ppermute | solution.py:181
  136.2 2.1 %collective-permute-done.26 = bf16[32,640]{1,0:T(8,128)(2,1)S(1)} collective-permute-done((bf16[32,640]{1,0:T(8,128)(2,1)S(1)}, bf16[32,640]{1,0:T(8,128)(2,1)S(1)}, u32[]{:S(2)}, u32[]{:S(2)}) %collective-permute-start.26) | collective-permute-done | bytes 40992 | tf_op jit(solution)/shard_map/ppermute | solution.py:181
  139.1 2.8 %collective-permute-done.27 = bf16[32,640]{1,0:T(8,128)(2,1)S(1)} collective-permute-done((bf16[32,640]{1,0:T(8,128)(2,1)S(1)}, bf16[32,640]{1,0:T(8,128)(2,1)S(1)}, u32[]{:S(2)}, u32[]{:S(2)}) %collective-permute-start.27) | collective-permute-done | bytes 40992 | tf_op jit(solution)/shard_map/ppermute | solution.py:181
  141.9 3.9 %collective-permute-start.28 = (bf16[32,640]{1,0:T(8,128)(2,1)S(1)}, bf16[32,640]{1,0:T(8,128)(2,1)S(1)}, u32[]{:S(2)}, u32[]{:S(2)}) collective-permute-start(bf16[32,640]{1,0:T(8,128)(2,1)S(1)} %convert_element_type.180), channel_id=1, source_target_pairs={{0,60},{1,61},{2,62},{3,63},{4,40},{5,41},{6,42},{7,43},{8,36},{9,... | collective-permute-start | bytes 122888 | tf_op jit(solution)/shard_map/ppermute | solution.py:181
  145.8 1.7 %collective-permute-done.28 = bf16[32,640]{1,0:T(8,128)(2,1)S(1)} collective-permute-done((bf16[32,640]{1,0:T(8,128)(2,1)S(1)}, bf16[32,640]{1,0:T(8,128)(2,1)S(1)}, u32[]{:S(2)}, u32[]{:S(2)}) %collective-permute-start.28) | collective-permute-done | bytes 40992 | tf_op jit(solution)/shard_map/ppermute | solution.py:181
  147.5 3.0 %collective-permute-start.29 = (bf16[32,640]{1,0:T(8,128)(2,1)S(1)}, bf16[32,640]{1,0:T(8,128)(2,1)S(1)}, u32[]{:S(2)}, u32[]{:S(2)}) collective-permute-start(bf16[32,640]{1,0:T(8,128)(2,1)S(1)} %convert_element_type.182), channel_id=1, source_target_pairs={{0,44},{1,45},{2,46},{3,47},{4,56},{5,57},{6,58},{7,59},{8,52},{9,... | collective-permute-start | bytes 122888 | tf_op jit(solution)/shard_map/ppermute | solution.py:181
  150.6 2.3 %collective-permute-done.29 = bf16[32,640]{1,0:T(8,128)(2,1)S(1)} collective-permute-done((bf16[32,640]{1,0:T(8,128)(2,1)S(1)}, bf16[32,640]{1,0:T(8,128)(2,1)S(1)}, u32[]{:S(2)}, u32[]{:S(2)}) %collective-permute-start.29) | collective-permute-done | bytes 40992 | tf_op jit(solution)/shard_map/ppermute | solution.py:181
  154.2 6.4 %shard_map.79 = bf16[2048,512]{1,0:T(8,128)(2,1)} custom-call(s32[5]{0:T(128)S(1)} %stack.39.flags_ref.half_ref, f32[32,640]{1,0:T(8,128)S(1)} %convert_add_fusion.own_ref, f32[32,640]{1,0:T(8,128)S(1)} %collective-permute-done.30.got_ref, f32[64,512]{1,0:T(8,128)S(1)} %get-tuple-element.33.basis_ref, bf16[2048,512]{1,0:T(8,128)(2,1)S(1)} %get-tuple-element.25.feature_ref, ...), custom_call_target="tpu_custom_call" | custom-call | tf_op jit(solution)/shard_map/pallas_call | solution.py:289
  (85 shorter events, 12.1 us)
Async XLA Ops:
  2.0 11.1 %copy-start = (bf16[64,32,512]{2,1,0:T(8,128)(2,1)S(1)}, bf16[64,32,512]{2,1,0:T(8,128)(2,1)}, u32[]{:S(2)}) copy-start(bf16[64,32,512]{2,1,0:T(8,128)(2,1)} %band_ref.3) | copy-start | bytes 6291460
  2.0 11.1 %copy-start.5 = (f32[21,512]{1,0:T(8,128)S(1)}, f32[21,512]{1,0:T(8,128)}, u32[]{:S(2)}) copy-start(f32[21,512]{1,0:T(8,128)} %taps_ref.5) | copy-start | bytes 129028
  3.2 23.2 %collective-permute-start = (bf16[10,64,512]{2,1,0:T(8,128)(2,1)}, bf16[10,64,512]{2,1,0:T(8,128)(2,1)S(1)}, u32[]{:S(2)}, u32[]{:S(2)}) collective-permute-start(bf16[10,64,512]{2,1,0:T(8,128)(2,1)} %bitcast.12), channel_id=1, source_target_pairs={{0,1},{1,2},{2,3},{3,4},{4,5},{5,6},{6,7},{7,8},{8,9},{9,10},{10,1... | collective-permute-start | bytes 1966088 | tf_op jit(solution)/shard_map/ppermute | solution.py:313
  6.5 20.3 %collective-permute-start.1 = (bf16[10,64,512]{2,1,0:T(8,128)(2,1)}, bf16[10,64,512]{2,1,0:T(8,128)(2,1)S(1)}, u32[]{:S(2)}, u32[]{:S(2)}) collective-permute-start(bf16[10,64,512]{2,1,0:T(8,128)(2,1)} %bitcast.11), channel_id=1, source_target_pairs={{0,31},{1,0},{2,1},{3,2},{4,3},{5,4},{6,5},{7,6},{8,7},{9,8},{10,9... | collective-permute-start | bytes 1966088 | tf_op jit(solution)/shard_map/ppermute | solution.py:314
  22.0 12.6 %copy-start.6 = (f32[21,512]{1,0:T(8,128)S(1)}, f32[21,512]{1,0:T(8,128)}, u32[]{:S(2)}) copy-start(f32[21,512]{1,0:T(8,128)} %taps_ref.7) | copy-start | bytes 129028
  31.8 10.4 %collective-permute-start.3 = (bf16[10,32,512]{2,1,0:T(8,128)(2,1)S(1)}, bf16[10,32,512]{2,1,0:T(8,128)(2,1)S(1)}, u32[]{:S(2)}, u32[]{:S(2)}) collective-permute-start(bf16[10,32,512]{2,1,0:T(8,128)(2,1)S(1)} %get-tuple-element.35), channel_id=1, source_target_pairs={{0,224},{32,0},{64,32},{96,64},{128,96},{160,128},{192,160},{224,1... | collective-permute-start | bytes 983048 | tf_op jit(solution)/shard_map/ppermute | solution.py:348
  33.4 8.9 %copy-start.1 = (bf16[512,512]{1,0:T(8,128)(2,1)S(1)}, bf16[512,512]{1,0:T(8,128)(2,1)}, u32[]{:S(2)}) copy-start(bf16[512,512]{1,0:T(8,128)(2,1)} %w_ref.1) | copy-start | bytes 1572868
  33.4 8.9 %copy-start.4 = (f32[512,64]{0,1:T(8,128)S(1)}, f32[512,64]{0,1:T(8,128)}, u32[]{:S(2)}) copy-start(f32[512,64]{0,1:T(8,128)} %param.11) | copy-start | bytes 393220
  33.4 8.9 %collective-permute-start.2 = (bf16[10,32,512]{2,1,0:T(8,128)(2,1)S(1)}, bf16[10,32,512]{2,1,0:T(8,128)(2,1)S(1)}, u32[]{:S(2)}, u32[]{:S(2)}) collective-permute-start(bf16[10,32,512]{2,1,0:T(8,128)(2,1)S(1)} %get-tuple-element.36), channel_id=1, source_target_pairs={{0,32},{32,64},{64,96},{96,128},{128,160},{160,192},{192,224},{224... | collective-permute-start | bytes 983048 | tf_op jit(solution)/shard_map/ppermute | solution.py:347
  46.3 1.4 collective-permute-start.4
  47.7 3.6 %collective-permute-start.5 = (bf16[32,640]{1,0:T(8,128)(2,1)S(1)}, bf16[32,640]{1,0:T(8,128)(2,1)S(1)}, u32[]{:S(2)}, u32[]{:S(2)}) collective-permute-start(bf16[32,640]{1,0:T(8,128)(2,1)S(1)} %convert_element_type.140), channel_id=1, source_target_pairs={{0,33},{1,32},{2,35},{3,34},{4,37},{5,36},{6,39},{7,38},{8,41},{9,... | collective-permute-start | bytes 122888 | tf_op jit(solution)/shard_map/ppermute | solution.py:181
  51.3 4.8 %collective-permute-start.6 = (bf16[32,640]{1,0:T(8,128)(2,1)S(1)}, bf16[32,640]{1,0:T(8,128)(2,1)S(1)}, u32[]{:S(2)}, u32[]{:S(2)}) collective-permute-start(bf16[32,640]{1,0:T(8,128)(2,1)S(1)} %convert_element_type.142), channel_id=1, source_target_pairs={{0,35},{1,34},{2,33},{3,32},{4,39},{5,38},{6,37},{7,36},{8,43},{9,... | collective-permute-start | bytes 122888 | tf_op jit(solution)/shard_map/ppermute | solution.py:181
  56.1 3.6 %collective-permute-start.7 = (bf16[32,640]{1,0:T(8,128)(2,1)S(1)}, bf16[32,640]{1,0:T(8,128)(2,1)S(1)}, u32[]{:S(2)}, u32[]{:S(2)}) collective-permute-start(bf16[32,640]{1,0:T(8,128)(2,1)S(1)} %convert_element_type.144), channel_id=1, source_target_pairs={{0,96},{1,97},{2,98},{3,99},{4,100},{5,101},{6,102},{7,103},{8,104... | collective-permute-start | bytes 122888 | tf_op jit(solution)/shard_map/ppermute | solution.py:181
  59.8 4.8 %collective-permute-start.8 = (bf16[32,640]{1,0:T(8,128)(2,1)S(1)}, bf16[32,640]{1,0:T(8,128)(2,1)S(1)}, u32[]{:S(2)}, u32[]{:S(2)}) collective-permute-start(bf16[32,640]{1,0:T(8,128)(2,1)S(1)} %convert_element_type.146), channel_id=1, source_target_pairs={{0,224},{1,225},{2,226},{3,227},{4,228},{5,229},{6,230},{7,231},{8... | collective-permute-start | bytes 122888 | tf_op jit(solution)/shard_map/ppermute | solution.py:181
  64.6 3.6 %collective-permute-start.9 = (bf16[32,640]{1,0:T(8,128)(2,1)S(1)}, bf16[32,640]{1,0:T(8,128)(2,1)S(1)}, u32[]{:S(2)}, u32[]{:S(2)}) collective-permute-start(bf16[32,640]{1,0:T(8,128)(2,1)S(1)} %convert_element_type.148), channel_id=1, source_target_pairs={{0,36},{1,37},{2,38},{3,39},{4,32},{5,33},{6,34},{7,35},{8,44},{9,... | collective-permute-start | bytes 122888 | tf_op jit(solution)/shard_map/ppermute | solution.py:181
  68.3 4.8 %collective-permute-start.10 = (bf16[32,640]{1,0:T(8,128)(2,1)S(1)}, bf16[32,640]{1,0:T(8,128)(2,1)S(1)}, u32[]{:S(2)}, u32[]{:S(2)}) collective-permute-start(bf16[32,640]{1,0:T(8,128)(2,1)S(1)} %convert_element_type.150), channel_id=1, source_target_pairs={{0,60},{1,61},{2,62},{3,63},{4,40},{5,41},{6,42},{7,43},{8,36},{9,... | collective-permute-start | bytes 122888 | tf_op jit(solution)/shard_map/ppermute | solution.py:181
  73.1 6.4 %collective-permute-start.11 = (bf16[32,640]{1,0:T(8,128)(2,1)S(1)}, bf16[32,640]{1,0:T(8,128)(2,1)S(1)}, u32[]{:S(2)}, u32[]{:S(2)}) collective-permute-start(bf16[32,640]{1,0:T(8,128)(2,1)S(1)} %convert_element_type.152), channel_id=1, source_target_pairs={{0,44},{1,45},{2,46},{3,47},{4,56},{5,57},{6,58},{7,59},{8,52},{9,... | collective-permute-start | bytes 122888 | tf_op jit(solution)/shard_map/ppermute | solution.py:181
  79.5 1.4 collective-permute-start.12
  83.6 1.3 collective-permute-start.13
  84.9 3.5 %collective-permute-start.14 = (bf16[32,640]{1,0:T(8,128)(2,1)S(1)}, bf16[32,640]{1,0:T(8,128)(2,1)S(1)}, u32[]{:S(2)}, u32[]{:S(2)}) collective-permute-start(bf16[32,640]{1,0:T(8,128)(2,1)S(1)} %convert_element_type.155), channel_id=1, source_target_pairs={{0,33},{1,32},{2,35},{3,34},{4,37},{5,36},{6,39},{7,38},{8,41},{9,... | collective-permute-start | bytes 122888 | tf_op jit(solution)/shard_map/ppermute | solution.py:181
  88.5 4.7 %collective-permute-start.15 = (bf16[32,640]{1,0:T(8,128)(2,1)S(1)}, bf16[32,640]{1,0:T(8,128)(2,1)S(1)}, u32[]{:S(2)}, u32[]{:S(2)}) collective-permute-start(bf16[32,640]{1,0:T(8,128)(2,1)S(1)} %convert_element_type.157), channel_id=1, source_target_pairs={{0,35},{1,34},{2,33},{3,32},{4,39},{5,38},{6,37},{7,36},{8,43},{9,... | collective-permute-start | bytes 122888 | tf_op jit(solution)/shard_map/ppermute | solution.py:181
  93.2 3.5 %collective-permute-start.16 = (bf16[32,640]{1,0:T(8,128)(2,1)S(1)}, bf16[32,640]{1,0:T(8,128)(2,1)S(1)}, u32[]{:S(2)}, u32[]{:S(2)}) collective-permute-start(bf16[32,640]{1,0:T(8,128)(2,1)S(1)} %convert_element_type.159), channel_id=1, source_target_pairs={{0,96},{1,97},{2,98},{3,99},{4,100},{5,101},{6,102},{7,103},{8,104... | collective-permute-start | bytes 122888 | tf_op jit(solution)/shard_map/ppermute | solution.py:181
  96.8 4.7 %collective-permute-start.17 = (bf16[32,640]{1,0:T(8,128)(2,1)S(1)}, bf16[32,640]{1,0:T(8,128)(2,1)S(1)}, u32[]{:S(2)}, u32[]{:S(2)}) collective-permute-start(bf16[32,640]{1,0:T(8,128)(2,1)S(1)} %convert_element_type.161), channel_id=1, source_target_pairs={{0,224},{1,225},{2,226},{3,227},{4,228},{5,229},{6,230},{7,231},{8... | collective-permute-start | bytes 122888 | tf_op jit(solution)/shard_map/ppermute | solution.py:181
  101.5 3.5 %collective-permute-start.18 = (bf16[32,640]{1,0:T(8,128)(2,1)S(1)}, bf16[32,640]{1,0:T(8,128)(2,1)S(1)}, u32[]{:S(2)}, u32[]{:S(2)}) collective-permute-start(bf16[32,640]{1,0:T(8,128)(2,1)S(1)} %convert_element_type.163), channel_id=1, source_target_pairs={{0,36},{1,37},{2,38},{3,39},{4,32},{5,33},{6,34},{7,35},{8,44},{9,... | collective-permute-start | bytes 122888 | tf_op jit(solution)/shard_map/ppermute | solution.py:181
  105.1 5.4 %collective-permute-start.19 = (bf16[32,640]{1,0:T(8,128)(2,1)S(1)}, bf16[32,640]{1,0:T(8,128)(2,1)S(1)}, u32[]{:S(2)}, u32[]{:S(2)}) collective-permute-start(bf16[32,640]{1,0:T(8,128)(2,1)S(1)} %convert_element_type.165), channel_id=1, source_target_pairs={{0,60},{1,61},{2,62},{3,63},{4,40},{5,41},{6,42},{7,43},{8,36},{9,... | collective-permute-start | bytes 122888 | tf_op jit(solution)/shard_map/ppermute | solution.py:181
  110.4 5.5 %collective-permute-start.20 = (bf16[32,640]{1,0:T(8,128)(2,1)S(1)}, bf16[32,640]{1,0:T(8,128)(2,1)S(1)}, u32[]{:S(2)}, u32[]{:S(2)}) collective-permute-start(bf16[32,640]{1,0:T(8,128)(2,1)S(1)} %convert_element_type.167), channel_id=1, source_target_pairs={{0,44},{1,45},{2,46},{3,47},{4,56},{5,57},{6,58},{7,59},{8,52},{9,... | collective-permute-start | bytes 122888 | tf_op jit(solution)/shard_map/ppermute | solution.py:181
  115.9 1.4 collective-permute-start.21
  117.3 36.9 %copy-start.2 = (bf16[512,512]{1,0:T(8,128)(2,1)S(1)}, bf16[512,512]{1,0:T(8,128)(2,1)}, u32[]{:S(2)}) copy-start(bf16[512,512]{1,0:T(8,128)(2,1)} %wham_ref.1) | copy-start | bytes 1572868
  117.3 36.9 %copy-start.3 = (bf16[512,512]{1,0:T(8,128)(2,1)S(1)}, bf16[512,512]{1,0:T(8,128)(2,1)}, u32[]{:S(2)}) copy-start(bf16[512,512]{1,0:T(8,128)(2,1)} %walign_ref.1) | copy-start | bytes 1572868
  120.1 1.3 collective-permute-start.22
  121.4 3.6 %collective-permute-start.23 = (bf16[32,640]{1,0:T(8,128)(2,1)S(1)}, bf16[32,640]{1,0:T(8,128)(2,1)S(1)}, u32[]{:S(2)}, u32[]{:S(2)}) collective-permute-start(bf16[32,640]{1,0:T(8,128)(2,1)S(1)} %convert_element_type.170), channel_id=1, source_target_pairs={{0,33},{1,32},{2,35},{3,34},{4,37},{5,36},{6,39},{7,38},{8,41},{9,... | collective-permute-start | bytes 122888 | tf_op jit(solution)/shard_map/ppermute | solution.py:181
  125.0 4.8 %collective-permute-start.24 = (bf16[32,640]{1,0:T(8,128)(2,1)S(1)}, bf16[32,640]{1,0:T(8,128)(2,1)S(1)}, u32[]{:S(2)}, u32[]{:S(2)}) collective-permute-start(bf16[32,640]{1,0:T(8,128)(2,1)S(1)} %convert_element_type.172), channel_id=1, source_target_pairs={{0,35},{1,34},{2,33},{3,32},{4,39},{5,38},{6,37},{7,36},{8,43},{9,... | collective-permute-start | bytes 122888 | tf_op jit(solution)/shard_map/ppermute | solution.py:181
  129.9 3.6 %collective-permute-start.25 = (bf16[32,640]{1,0:T(8,128)(2,1)S(1)}, bf16[32,640]{1,0:T(8,128)(2,1)S(1)}, u32[]{:S(2)}, u32[]{:S(2)}) collective-permute-start(bf16[32,640]{1,0:T(8,128)(2,1)S(1)} %convert_element_type.174), channel_id=1, source_target_pairs={{0,96},{1,97},{2,98},{3,99},{4,100},{5,101},{6,102},{7,103},{8,104... | collective-permute-start | bytes 122888 | tf_op jit(solution)/shard_map/ppermute | solution.py:181
  133.5 4.8 %collective-permute-start.26 = (bf16[32,640]{1,0:T(8,128)(2,1)S(1)}, bf16[32,640]{1,0:T(8,128)(2,1)S(1)}, u32[]{:S(2)}, u32[]{:S(2)}) collective-permute-start(bf16[32,640]{1,0:T(8,128)(2,1)S(1)} %convert_element_type.176), channel_id=1, source_target_pairs={{0,224},{1,225},{2,226},{3,227},{4,228},{5,229},{6,230},{7,231},{8... | collective-permute-start | bytes 122888 | tf_op jit(solution)/shard_map/ppermute | solution.py:181
  138.3 3.6 %collective-permute-start.27 = (bf16[32,640]{1,0:T(8,128)(2,1)S(1)}, bf16[32,640]{1,0:T(8,128)(2,1)S(1)}, u32[]{:S(2)}, u32[]{:S(2)}) collective-permute-start(bf16[32,640]{1,0:T(8,128)(2,1)S(1)} %convert_element_type.178), channel_id=1, source_target_pairs={{0,36},{1,37},{2,38},{3,39},{4,32},{5,33},{6,34},{7,35},{8,44},{9,... | collective-permute-start | bytes 122888 | tf_op jit(solution)/shard_map/ppermute | solution.py:181
  141.9 5.5 %collective-permute-start.28 = (bf16[32,640]{1,0:T(8,128)(2,1)S(1)}, bf16[32,640]{1,0:T(8,128)(2,1)S(1)}, u32[]{:S(2)}, u32[]{:S(2)}) collective-permute-start(bf16[32,640]{1,0:T(8,128)(2,1)S(1)} %convert_element_type.180), channel_id=1, source_target_pairs={{0,60},{1,61},{2,62},{3,63},{4,40},{5,41},{6,42},{7,43},{8,36},{9,... | collective-permute-start | bytes 122888 | tf_op jit(solution)/shard_map/ppermute | solution.py:181
  147.5 5.3 %collective-permute-start.29 = (bf16[32,640]{1,0:T(8,128)(2,1)S(1)}, bf16[32,640]{1,0:T(8,128)(2,1)S(1)}, u32[]{:S(2)}, u32[]{:S(2)}) collective-permute-start(bf16[32,640]{1,0:T(8,128)(2,1)S(1)} %convert_element_type.182), channel_id=1, source_target_pairs={{0,44},{1,45},{2,46},{3,47},{4,56},{5,57},{6,58},{7,59},{8,52},{9,... | collective-permute-start | bytes 122888 | tf_op jit(solution)/shard_map/ppermute | solution.py:181
  152.8 1.4 collective-permute-start.30

commit v5 on v4

--- a/solution.py
+++ b/solution.py
@@ -19,6 +19,7 @@
 TAPS = 21
 MARGIN = TAPS // 2
 LANES = 128
+PARTS = 2
 
 
 def weighted(taps_ref, items, rows):
@@ -46,6 +47,14 @@
             emit(start + i, value)
 
 
+def pack_kernel(band_ref, first_ref, last_ref, flat):
+    h, w, lanes = band_ref.shape
+    flat[...] = band_ref[...].astype(F32).reshape(h * w, lanes)
+    for j in range(MARGIN):
+        first_ref[j] = flat[pl.ds(j, h, stride=w), :].astype(BF)
+        last_ref[j] = flat[pl.ds(w - MARGIN + j, h, stride=w), :].astype(BF)
+
+
 def columns_own_kernel(band_ref, taps_ref, out_ref, flat, turned):
     h, w, lanes = band_ref.shape
     flat[...] = band_ref[...].astype(F32).reshape(h * w, lanes)
@@ -115,10 +124,10 @@
     mid_ref[...] = mixed[...].astype(BF)
 
 
-def finished_edge(part_ref, halo_ref, taps_ref, present, pairs_of):
+def finished_edge(part_ref, halo_ref, taps_ref, start, present, pairs_of):
     blocks = []
-    for start in range(0, part_ref.shape[2], LANES):
-        lanes = slice(start, start + LANES)
+    for at in range(0, part_ref.shape[2], LANES):
+        lanes, tap_lanes = slice(at, at + LANES), slice(start + at, start + at + LANES)
         halo = [
             jnp.where(present, halo_ref[j, :, lanes].astype(F32), 0.0) for j in range(MARGIN)
         ]
@@ -126,7 +135,7 @@
         for o in range(MARGIN):
             value = part_ref[o, :, lanes]
             for k, j in pairs_of(o):
-                value = value + taps_ref[k : k + 1, lanes] * halo[j]
+                value = value + taps_ref[k : k + 1, tap_lanes] * halo[j]
             rows.append(value.astype(BF))
         blocks.append(jnp.concatenate(rows, axis=0))
     return jnp.concatenate(blocks, axis=1)
@@ -220,26 +229,30 @@
     theirs_ref[:, c:] = jnp.where(first, gram[rows:], gram[:rows]).astype(BF)
 
 
-def first_kernel(
-    flags_ref, mid_ref, top_ref, low_ref, above_ref, below_ref, taps_ref, w_ref, basis_ref,
-    feature_ref, coeffs_ref, mine_ref, theirs_ref,
-):
-    rows, cols, channels = mid_ref.shape
+def above_pairs(o):
+    return [(j - o, j) for j in range(o, MARGIN)]
+
+
+def below_pairs(o):
+    return [(2 * MARGIN + j - o, j) for j in range(o + 1)]
+
+
+def first_kernel(flags_ref, *refs):
+    parts = [refs[i * 5 : i * 5 + 5] for i in range(PARTS)]
+    taps_ref, w_ref, basis_ref, feature_ref, coeffs_ref, mine_ref, theirs_ref = refs[PARTS * 5 :]
+    rows, cols, width = parts[0][0].shape
     edge, mid = MARGIN * cols, rows * cols
-    w = w_ref[...]
-    top = finished_edge(
-        top_ref, above_ref, taps_ref, flags_ref[3] == 1, lambda o: [(j - o, j) for j in range(o, MARGIN)]
-    )
-    low = finished_edge(
-        low_ref, below_ref, taps_ref, flags_ref[4] == 1, lambda o: [(2 * MARGIN + j - o, j) for j in range(o + 1)]
-    )
-
-    def squeezed(mixed):
-        return jnp.maximum(dot(mixed, w, NN), 0.0).astype(BF)
-
-    feature_ref[:edge] = squeezed(top)
-    feature_ref[edge : edge + mid] = squeezed(mid_ref[...].reshape(mid, channels))
-    feature_ref[edge + mid :] = squeezed(low)
+    tops, mids, lows = 0.0, 0.0, 0.0
+    for i, (mid_ref, top_ref, low_ref, above_ref, below_ref) in enumerate(parts):
+        w = w_ref[i * width : (i + 1) * width, :]
+        top = finished_edge(top_ref, above_ref, taps_ref, i * width, flags_ref[3] == 1, above_pairs)
+        low = finished_edge(low_ref, below_ref, taps_ref, i * width, flags_ref[4] == 1, below_pairs)
+        tops += dot(top, w, NN)
+        lows += dot(low, w, NN)
+        mids += dot(mid_ref[...].reshape(mid, width), w, NN)
+    feature_ref[:edge] = jnp.maximum(tops, 0.0).astype(BF)
+    feature_ref[edge : edge + mid] = jnp.maximum(mids, 0.0).astype(BF)
+    feature_ref[edge + mid :] = jnp.maximum(lows, 0.0).astype(BF)
     feature = feature_ref[...]
     basis = basis_ref[...]
     scores = dot(basis.astype(BF), feature, NT)
@@ -308,71 +321,98 @@
     def ring(count, by):
         return [(i, (i + by) % count) for i in range(count)]
 
-    left = band_input[:, tile_cols - margin :].transpose(1, 0, 2)
-    right = band_input[:, :margin].transpose(1, 0, 2)
-    left = lax.ppermute(left, COLS, ring(Z * X, 1))
-    right = lax.ppermute(right, COLS, ring(Z * X, -1))
-
-    def blocks(*dims):
-        return pl.BlockSpec((*dims, LANES), lambda i: (*(0 for _ in dims), i))
+    width = channels // PARTS
+    blocks_in_part = width // LANES
+
+    def blocks(*dims, start=0):
+        return pl.BlockSpec((*dims, LANES), lambda i: (*(0 for _ in dims), i + start))
 
     scalar = pl.BlockSpec(memory_space=pltpu.SMEM)
-    tile, turned = blocks(tile_rows, tile_cols), blocks(tile_cols, tile_rows)
+    turned, tile = blocks(tile_cols, tile_rows), blocks(tile_rows, tile_cols)
     side, edge = blocks(margin, tile_rows), blocks(margin, tile_cols)
-    taps = blocks(TAPS)
-    grid = (channels // LANES,)
+    grid = (blocks_in_part,)
     flat = pltpu.VMEM((tile_rows * tile_cols, LANES), F32)
     params = pltpu.CompilerParams(vmem_limit_bytes=20 * 2**20)
-    pixels = tile_rows * tile_cols * channels
-    cost = pl.CostEstimate(flops=2 * TAPS * pixels, bytes_accessed=6 * pixels, transcendentals=0)
-    own = pl.pallas_call(
-        columns_own_kernel,
-        grid=grid,
-        in_specs=[tile, taps],
-        out_specs=turned,
-        out_shape=sds((tile_cols, tile_rows, channels), F32),
-        scratch_shapes=[flat, pltpu.VMEM((tile_cols, tile_rows, LANES), F32)],
-        compiler_params=params,
-        cost_estimate=cost,
-    )(band_input, column_taps)
-    filtered = pl.pallas_call(
-        columns_rest_kernel,
-        grid=grid,
-        in_specs=[scalar, turned, side, side, taps],
-        out_specs=tile,
-        out_shape=sds(band_input.shape, BF),
-        scratch_shapes=[pltpu.VMEM((margin, tile_rows, LANES), F32)] * 2 + [flat],
-        compiler_params=params,
-    )(flags, own, left, right, column_taps)
-    above = lax.ppermute(filtered[tile_rows - margin :], ROWS, ring(Y * CORE, 1))
-    below = lax.ppermute(filtered[:margin], ROWS, ring(Y * CORE, -1))
+    pixels = tile_rows * tile_cols * width
     rest = tile_rows - 2 * margin
-    mid, top, low = pl.pallas_call(
-        rows_own_kernel,
-        grid=grid,
-        in_specs=[tile, tile, taps],
-        out_specs=[blocks(rest, tile_cols), edge, edge],
-        out_shape=[
-            sds((rest, tile_cols, channels), BF),
-            sds((margin, tile_cols, channels), F32),
-            sds((margin, tile_cols, channels), F32),
-        ],
-        scratch_shapes=[
-            pltpu.VMEM((tile_rows, tile_cols, LANES), F32),
-            pltpu.VMEM((tile_rows, tile_cols, LANES), F32),
-            pltpu.VMEM((rest, tile_cols, LANES), F32),
-        ],
-        compiler_params=params,
-        cost_estimate=cost,
-    )(filtered, band_input, row_taps)
+
+    def cost(taps, moved):
+        return pl.CostEstimate(flops=2 * taps * pixels, bytes_accessed=moved * pixels, transcendentals=0)
+
+    sides = []
+    for i in range(PARTS):
+        first, last = pl.pallas_call(
+            pack_kernel,
+            grid=grid,
+            in_specs=[blocks(tile_rows, tile_cols, start=i * blocks_in_part)],
+            out_specs=[side, side],
+            out_shape=[sds((margin, tile_rows, width), BF)] * 2,
+            scratch_shapes=[flat],
+            compiler_params=params,
+            cost_estimate=cost(1, 3),
+        )(band_input)
+        sides.append(
+            (lax.ppermute(last, COLS, ring(Z * X, 1)), lax.ppermute(first, COLS, ring(Z * X, -1)))
+        )
+    owns = []
+    for i in range(PARTS):
+        start = i * blocks_in_part
+        owns.append(
+            pl.pallas_call(
+                columns_own_kernel,
+                grid=grid,
+                in_specs=[blocks(tile_rows, tile_cols, start=start), blocks(TAPS, start=start)],
+                out_specs=turned,
+                out_shape=sds((tile_cols, tile_rows, width), F32),
+                scratch_shapes=[flat, pltpu.VMEM((tile_cols, tile_rows, LANES), F32)],
+                compiler_params=params,
+                cost_estimate=cost(TAPS, 6),
+            )(band_input, column_taps)
+        )
+    parts = []
+    for i in range(PARTS):
+        start = i * blocks_in_part
+        filtered = pl.pallas_call(
+            columns_rest_kernel,
+            grid=grid,
+            in_specs=[scalar, turned, side, side, blocks(TAPS, start=start)],
+            out_specs=tile,
+            out_shape=sds((tile_rows, tile_cols, width), BF),
+            scratch_shapes=[pltpu.VMEM((margin, tile_rows, LANES), F32)] * 2 + [flat],
+            compiler_params=params,
+            cost_estimate=cost(TAPS // 2, 6),
+        )(flags, owns[i], *sides[i], column_taps)
+        above = lax.ppermute(filtered[tile_rows - margin :], ROWS, ring(Y * CORE, 1))
+        below = lax.ppermute(filtered[:margin], ROWS, ring(Y * CORE, -1))
+        mid, top, low = pl.pallas_call(
+            rows_own_kernel,
+            grid=grid,
+            in_specs=[tile, blocks(tile_rows, tile_cols, start=start), blocks(TAPS, start=start)],
+            out_specs=[blocks(rest, tile_cols), edge, edge],
+            out_shape=[
+                sds((rest, tile_cols, width), BF),
+                sds((margin, tile_cols, width), F32),
+                sds((margin, tile_cols, width), F32),
+            ],
+            scratch_shapes=[
+                pltpu.VMEM((tile_rows, tile_cols, LANES), F32),
+                pltpu.VMEM((tile_rows, tile_cols, LANES), F32),
+                pltpu.VMEM((rest, tile_cols, LANES), F32),
+            ],
+            compiler_params=params,
+            cost_estimate=cost(TAPS, 6),
+        )(filtered, band_input, row_taps)
+        parts += [mid, top, low, above, below]
+        if i + 1 < PARTS:
+            owns[i + 1], parts[-4] = lax.optimization_barrier((owns[i + 1], parts[-4]))
     n, r = tile_rows * tile_cols, bases_init.shape[1]
-    width = channels + 128
-    sums = [sds((r // 2, width), F32), sds((r // 2, width), BF)]
+    packed = (r // 2, channels + LANES)
+    sums = [sds(packed, F32), sds(packed, BF)]
     basis = bases_init.T
     feature, coeffs, mine, theirs = call(
         first_kernel,
         [sds((n, channels), BF), sds((r, n), F32)] + sums,
-        flags, mid, top, low, above, below, row_taps, w_squeeze, basis,
+        flags, *parts, row_taps, w_squeeze, basis,
     )
     for _ in range(STEPS - 1):
         own, got = summed_over_all(mine, theirs)

time: 161 us -> 167 us (1.037)
  waiting for transfers between devices: 64.8 us -> 88.8 us
  starting transfers between devices: 53.1 us -> 34.6 us
  Pallas kernels: 37.4 us -> 41.2 us
  local copies, waits for them, and re-layouts: 4.55 us -> 1.76 us
    ppermute x21, waiting for transfers between devices: 54.1 us -> 83.4 us  [summed_over_all(): got = lax.ppermute(total.astype(BF), ALL, round_pairs(axis, rule))]
    ppermute x21, starting transfers between devices: 39.6 us -> 10.4 us  [summed_over_all(): got = lax.ppermute(total.astype(BF), ALL, round_pairs(axis, rule))]
    ppermute x2 -> x4, starting transfers between devices: 8.59 us -> 13.4 us  [the longest x2 11.3 us: on_device(): lax.ppermute(first, COLS, ring(Z * X, -1))]
    ppermute x2 -> x4, waiting for transfers between devices: 4.71 us -> 0.01 us  [the longest x2 0.01 us: on_device(): lax.ppermute(first, COLS, ring(Z * X, -1))]
    ppermute x3, starting transfers between devices: 1.16 us -> 4.81 us  [summed_over_all(): total = mine + lax.ppermute(theirs, 'core', swap).astype(F32)]
    pallas_call x2 -> x6, Pallas kernels: 16.6 us -> 20 us  [the longest x2 8.73 us: on_device(): pl.pallas_call(columns_own_kernel, grid=grid, in_specs=[blocks(tile_rows,...]
    slice x1 -> x0, local copies, waits for them, and re-layouts: 1.99 us -> none  [on_device(): right = band_input[:, :margin].transpose(1, 0, 2)]
    pallas_call x1 -> x2, Pallas kernels: 5.01 us -> 5.27 us  [on_device(): pl.pallas_call(columns_rest_kernel, grid=grid, in_specs=[scalar, turned,...]
  transfers between devices with their start and end apart: 31 -> 35, of which waited for: 29 -> 27; matrix products, arithmetic and copies ran while one was open for 1% -> 0% of each run, Pallas kernels for 10% -> 14%
where the time goes in v5:
time: 167 us
  waiting for transfers between devices  88.8 us (53%)
  Pallas kernels  41.2 us (25%)
  starting transfers between devices  34.6 us (21%)
  local copies, waits for them, and re-layouts  1.76 us (1%)
    ppermute x21, waiting for transfers between devices, summed_over_all(): got = lax.ppermute(total.astype(BF), ALL, round_pairs(axis, rule))  83.4 us
    pallas_call x4, Pallas kernels, call(): pl.pallas_call(kernel, out_shape=outs, in_specs=specs, out_specs=jax.tree...  15.9 us
    ppermute x2, starting transfers between devices, on_device(): lax.ppermute(first, COLS, ring(Z * X, -1))  11.3 us
    ppermute x21, starting transfers between devices, summed_over_all(): got = lax.ppermute(total.astype(BF), ALL, round_pairs(axis, rule))  10.4 us
    pallas_call x2, Pallas kernels, on_device(): pl.pallas_call(columns_own_kernel, grid=grid, in_specs=[blocks(tile_rows,...  8.73 us
    pallas_call x2, Pallas kernels, on_device(): pl.pallas_call(rows_own_kernel, grid=grid, in_specs=[tile, blocks(tile_ro...  7.65 us
    pallas_call x2, Pallas kernels, on_device(): pl.pallas_call(columns_rest_kernel, grid=grid, in_specs=[scalar, turned,...  5.27 us
    ppermute x3, starting transfers between devices, summed_over_all(): total = mine + lax.ppermute(theirs, 'core', swap).astype(F32)  4.81 us
  transfers between devices with their start and end apart: 35, of which 27 were waited for; matrix products, arithmetic and copies ran while one was open for 0% of the time, Pallas kernels for 14%

profile of v5, /device:TPU:1, one launch (start us, length us, event | category | flops | bytes accessed | tf_op | source)
XLA Modules:
  0.0 167.3 jit_solution(15401453976319250159)
XLA Ops:
  0.0 1.6 copy-done
  1.6 1.8 %shard_map.74 = (bf16[10,64,256]{2,1,0:T(8,128)(2,1)}, bf16[10,64,256]{2,1,0:T(8,128)(2,1)}) custom-call(bf16[64,32,512]{2,1,0:T(8,128)(2,1)S(1)} %copy-done), custom_call_target="tpu_custom_call" | custom-call | flops 1048576 | bytes 1572864 | tf_op jit(solution)/shard_map/pallas_call | solution.py:344
  3.4 2.0 %collective-permute-start = (bf16[10,64,256]{2,1,0:T(8,128)(2,1)}, bf16[10,64,256]{2,1,0:T(8,128)(2,1)S(1)}, u32[]{:S(2)}, u32[]{:S(2)}) collective-permute-start(bf16[10,64,256]{2,1,0:T(8,128)(2,1)} %get-tuple-element.29), channel_id=1, source_target_pairs={{0,1},{1,2},{2,3},{3,4},{4,5},{5,6},{6,7},{7,8},{8,9},{9,10},{10,1... | collective-permute-start | bytes 983048 | tf_op jit(solution)/shard_map/ppermute | solution.py:355
  5.4 6.6 %collective-permute-start.1 = (bf16[10,64,256]{2,1,0:T(8,128)(2,1)}, bf16[10,64,256]{2,1,0:T(8,128)(2,1)S(1)}, u32[]{:S(2)}, u32[]{:S(2)}) collective-permute-start(bf16[10,64,256]{2,1,0:T(8,128)(2,1)} %get-tuple-element.30), channel_id=1, source_target_pairs={{0,31},{1,0},{2,1},{3,2},{4,3},{5,4},{6,5},{7,6},{8,7},{9,8},{10,9... | collective-permute-start | bytes 983048 | tf_op jit(solution)/shard_map/ppermute | solution.py:355
  12.0 1.8 %shard_map.78 = (bf16[10,64,256]{2,1,0:T(8,128)(2,1)}, bf16[10,64,256]{2,1,0:T(8,128)(2,1)}) custom-call(bf16[64,32,512]{2,1,0:T(8,128)(2,1)S(1)} %copy-done), custom_call_target="tpu_custom_call" | custom-call | flops 1048576 | bytes 1572864 | tf_op jit(solution)/shard_map/pallas_call | solution.py:344
  13.8 4.8 %collective-permute-start.5 = (bf16[10,64,256]{2,1,0:T(8,128)(2,1)}, bf16[10,64,256]{2,1,0:T(8,128)(2,1)S(1)}, u32[]{:S(2)}, u32[]{:S(2)}) collective-permute-start(bf16[10,64,256]{2,1,0:T(8,128)(2,1)} %get-tuple-element.37), channel_id=1, source_target_pairs={{0,31},{1,0},{2,1},{3,2},{4,3},{5,4},{6,5},{7,6},{8,7},{9,8},{10,9... | collective-permute-start | bytes 983048 | tf_op jit(solution)/shard_map/ppermute | solution.py:355
  18.7 4.4 %shard_map.73.own_ref = f32[32,64,256]{2,1,0:T(8,128)S(1)} custom-call(bf16[64,32,512]{2,1,0:T(8,128)(2,1)S(1)} %copy-done.1, f32[21,512]{1,0:T(8,128)S(1)} %copy-done.2), custom_call_target="tpu_custom_call" | custom-call | flops 22020096 | bytes 3145728 | tf_op jit(solution)/shard_map/pallas_call | solution.py:361
  23.1 4.4 %shard_map.77.own_ref = f32[32,64,256]{2,1,0:T(8,128)S(1)} custom-call(bf16[64,32,512]{2,1,0:T(8,128)(2,1)S(1)} %copy-done.1, f32[21,512]{1,0:T(8,128)S(1)} %copy-done.2), custom_call_target="tpu_custom_call" | custom-call | flops 22020096 | bytes 3145728 | tf_op jit(solution)/shard_map/pallas_call | solution.py:361
  27.5 2.6 %shard_map.75.filtered_ref = bf16[64,32,256]{2,1,0:T(8,128)(2,1)S(1)} custom-call(s32[5]{0:T(128)S(1)} %stack.39.flags_ref.half_ref, f32[32,64,256]{2,1,0:T(8,128)S(1)} %shard_map.73.own_ref, bf16[10,64,256]{2,1,0:T(8,128)(2,1)S(1)} %collective-permute-done.left_ref, bf16[10,64,256]{2,1,0:T(8,128)(2,1)S(1)} %collective-permute-done.1.right_ref, ...), custom_call_target="tpu_custom_call" | custom-call | flops 10485760 | bytes 3145728 | tf_op jit(solution)/shard_map/pallas_call | solution.py:375
  30.1 1.5 collective-permute-start.3
  31.7 1.2 collective-permute-start.2
  32.9 3.8 %shard_map.76 = (bf16[44,32,256]{2,1,0:T(8,128)(2,1)S(1)}, f32[10,32,256]{2,1,0:T(8,128)S(1)}, f32[10,32,256]{2,1,0:T(8,128)S(1)}) custom-call(bf16[64,32,256]{2,1,0:T(8,128)(2,1)S(1)} %shard_map.75.filtered_ref, bf16[64,32,512]{2,1,0:T(8,128)(2,1)S(1)} %copy-done.1, f32[21,512]{1,0:T(8,128)S(1)} %copy-done.7), custom_call_target="tpu_custom_call" | custom-call | flops 22020096 | bytes 3145728 | tf_op jit(solution)/shard_map/pallas_call | solution.py:387
  36.7 2.6 %shard_map.79.filtered_ref = bf16[64,32,256]{2,1,0:T(8,128)(2,1)S(1)} custom-call(s32[5]{0:T(128)S(1)} %stack.39.flags_ref.half_ref, f32[32,64,256]{2,1,0:T(8,128)S(1)} %shard_map.77.own_ref, bf16[10,64,256]{2,1,0:T(8,128)(2,1)S(1)} %collective-permute-done.4.left_ref, bf16[10,64,256]{2,1,0:T(8,128)(2,1)S(1)} %collective-permute-done.5.right_ref, ...), custom_call_target="tpu_custom_call" | custom-call | flops 10485760 | bytes 3145728 | tf_op jit(solution)/shard_map/pallas_call | solution.py:375
  39.9 1.3 collective-permute-start.6
  41.2 3.8 %shard_map.80 = (bf16[44,32,256]{2,1,0:T(8,128)(2,1)S(1)}, f32[10,32,256]{2,1,0:T(8,128)S(1)}, f32[10,32,256]{2,1,0:T(8,128)S(1)}) custom-call(bf16[64,32,256]{2,1,0:T(8,128)(2,1)S(1)} %shard_map.79.filtered_ref, bf16[64,32,512]{2,1,0:T(8,128)(2,1)S(1)} %copy-done.1, f32[21,512]{1,0:T(8,128)S(1)} %copy-done.7), custom_call_target="tpu_custom_call" | custom-call | flops 22020096 | bytes 3145728 | tf_op jit(solution)/shard_map/pallas_call | solution.py:387
  45.1 4.0 %shard_map.81 = (bf16[2048,512]{1,0:T(8,128)(2,1)S(1)}, f32[64,2048]{1,0:T(8,128)S(1)}, f32[32,640]{1,0:T(8,128)S(1)}, bf16[32,640]{1,0:T(8,128)(2,1)S(1)}) custom-call(s32[5]{0:T(128)S(1)} %stack.39.flags_ref.half_ref, bf16[44,32,256]{2,1,0:T(8,128)(2,1)S(1)} %get-tuple-element.31.refs_0_, f32[10,32,256]{2,1,0:T(8,128)S(1)} %get-tuple-element.33.refs_1_, ...), custom_call_target="tpu_custom_call" | custom-call | tf_op jit(solution)/shard_map/pallas_call | solution.py:302
  49.1 3.9 %collective-permute-start.8 = (bf16[32,640]{1,0:T(8,128)(2,1)S(1)}, bf16[32,640]{1,0:T(8,128)(2,1)S(1)}, u32[]{:S(2)}, u32[]{:S(2)}) collective-permute-start(bf16[32,640]{1,0:T(8,128)(2,1)S(1)} %get-tuple-element.42), channel_id=1, source_target_pairs={{0,32},{32,0},{1,33},{33,1},{2,34},{34,2},{3,35},{35,3},{4,36},{36... | collective-permute-start | bytes 122888 | tf_op jit(solution)/shard_map/ppermute | solution.py:187
  54.1 3.5 %collective-permute-done.9 = bf16[32,640]{1,0:T(8,128)(2,1)S(1)} collective-permute-done((bf16[32,640]{1,0:T(8,128)(2,1)S(1)}, bf16[32,640]{1,0:T(8,128)(2,1)S(1)}, u32[]{:S(2)}, u32[]{:S(2)}) %collective-permute-start.9) | collective-permute-done | bytes 40992 | tf_op jit(solution)/shard_map/ppermute | solution.py:190
  57.7 4.7 %collective-permute-done.10 = bf16[32,640]{1,0:T(8,128)(2,1)S(1)} collective-permute-done((bf16[32,640]{1,0:T(8,128)(2,1)S(1)}, bf16[32,640]{1,0:T(8,128)(2,1)S(1)}, u32[]{:S(2)}, u32[]{:S(2)}) %collective-permute-start.10) | collective-permute-done | bytes 40992 | tf_op jit(solution)/shard_map/ppermute | solution.py:190
  62.5 3.5 %collective-permute-done.11 = bf16[32,640]{1,0:T(8,128)(2,1)S(1)} collective-permute-done((bf16[32,640]{1,0:T(8,128)(2,1)S(1)}, bf16[32,640]{1,0:T(8,128)(2,1)S(1)}, u32[]{:S(2)}, u32[]{:S(2)}) %collective-permute-start.11) | collective-permute-done | bytes 40992 | tf_op jit(solution)/shard_map/ppermute | solution.py:190
  66.8 4.1 %collective-permute-done.12 = bf16[32,640]{1,0:T(8,128)(2,1)S(1)} collective-permute-done((bf16[32,640]{1,0:T(8,128)(2,1)S(1)}, bf16[32,640]{1,0:T(8,128)(2,1)S(1)}, u32[]{:S(2)}, u32[]{:S(2)}) %collective-permute-start.12) | collective-permute-done | bytes 40992 | tf_op jit(solution)/shard_map/ppermute | solution.py:190
  71.0 3.5 %collective-permute-done.13 = bf16[32,640]{1,0:T(8,128)(2,1)S(1)} collective-permute-done((bf16[32,640]{1,0:T(8,128)(2,1)S(1)}, bf16[32,640]{1,0:T(8,128)(2,1)S(1)}, u32[]{:S(2)}, u32[]{:S(2)}) %collective-permute-start.13) | collective-permute-done | bytes 40992 | tf_op jit(solution)/shard_map/ppermute | solution.py:190
  75.0 4.3 %collective-permute-done.14 = bf16[32,640]{1,0:T(8,128)(2,1)S(1)} collective-permute-done((bf16[32,640]{1,0:T(8,128)(2,1)S(1)}, bf16[32,640]{1,0:T(8,128)(2,1)S(1)}, u32[]{:S(2)}, u32[]{:S(2)}) %collective-permute-start.14) | collective-permute-done | bytes 40992 | tf_op jit(solution)/shard_map/ppermute | solution.py:190
  79.4 1.5 collective-permute-start.15
  80.9 3.9 %collective-permute-done.15 = bf16[32,640]{1,0:T(8,128)(2,1)S(1)} collective-permute-done((bf16[32,640]{1,0:T(8,128)(2,1)S(1)}, bf16[32,640]{1,0:T(8,128)(2,1)S(1)}, u32[]{:S(2)}, u32[]{:S(2)}) %collective-permute-start.15) | collective-permute-done | bytes 40992 | tf_op jit(solution)/shard_map/ppermute | solution.py:190
  85.3 0.9 collective-permute-done.16.got_ref
  86.2 2.7 %shard_map.82 = (f32[64,512]{1,0:T(8,128)S(1)}, f32[64,2048]{1,0:T(8,128)S(1)}, f32[32,640]{1,0:T(8,128)S(1)}, bf16[32,640]{1,0:T(8,128)(2,1)S(1)}) custom-call(s32[5]{0:T(128)S(1)} %stack.39.flags_ref.half_ref, f32[32,640]{1,0:T(8,128)S(1)} %convert_add_fusion.16.own_ref, f32[32,640]{1,0:T(8,128)S(1)} %collective-permute-done.16.got_ref, ...), custom_call_target="tpu_custom_call" | custom-call | tf_op jit(solution)/shard_map/pallas_call | solution.py:302
  89.4 0.9 collective-permute-done.17
  90.4 3.5 %collective-permute-done.18 = bf16[32,640]{1,0:T(8,128)(2,1)S(1)} collective-permute-done((bf16[32,640]{1,0:T(8,128)(2,1)S(1)}, bf16[32,640]{1,0:T(8,128)(2,1)S(1)}, u32[]{:S(2)}, u32[]{:S(2)}) %collective-permute-start.18) | collective-permute-done | bytes 40992 | tf_op jit(solution)/shard_map/ppermute | solution.py:190
  94.2 4.5 %collective-permute-done.19 = bf16[32,640]{1,0:T(8,128)(2,1)S(1)} collective-permute-done((bf16[32,640]{1,0:T(8,128)(2,1)S(1)}, bf16[32,640]{1,0:T(8,128)(2,1)S(1)}, u32[]{:S(2)}, u32[]{:S(2)}) %collective-permute-start.19) | collective-permute-done | bytes 40992 | tf_op jit(solution)/shard_map/ppermute | solution.py:190
  98.9 3.5 %collective-permute-done.20 = bf16[32,640]{1,0:T(8,128)(2,1)S(1)} collective-permute-done((bf16[32,640]{1,0:T(8,128)(2,1)S(1)}, bf16[32,640]{1,0:T(8,128)(2,1)S(1)}, u32[]{:S(2)}, u32[]{:S(2)}) %collective-permute-start.20) | collective-permute-done | bytes 40992 | tf_op jit(solution)/shard_map/ppermute | solution.py:190
  103.1 4.1 %collective-permute-done.21 = bf16[32,640]{1,0:T(8,128)(2,1)S(1)} collective-permute-done((bf16[32,640]{1,0:T(8,128)(2,1)S(1)}, bf16[32,640]{1,0:T(8,128)(2,1)S(1)}, u32[]{:S(2)}, u32[]{:S(2)}) %collective-permute-start.21) | collective-permute-done | bytes 40992 | tf_op jit(solution)/shard_map/ppermute | solution.py:190
  107.3 3.5 %collective-permute-done.22 = bf16[32,640]{1,0:T(8,128)(2,1)S(1)} collective-permute-done((bf16[32,640]{1,0:T(8,128)(2,1)S(1)}, bf16[32,640]{1,0:T(8,128)(2,1)S(1)}, u32[]{:S(2)}, u32[]{:S(2)}) %collective-permute-start.22) | collective-permute-done | bytes 40992 | tf_op jit(solution)/shard_map/ppermute | solution.py:190
  111.3 4.4 %collective-permute-done.23 = bf16[32,640]{1,0:T(8,128)(2,1)S(1)} collective-permute-done((bf16[32,640]{1,0:T(8,128)(2,1)S(1)}, bf16[32,640]{1,0:T(8,128)(2,1)S(1)}, u32[]{:S(2)}, u32[]{:S(2)}) %collective-permute-start.23) | collective-permute-done | bytes 40992 | tf_op jit(solution)/shard_map/ppermute | solution.py:190
  115.7 2.4 %collective-permute-start.24 = (bf16[32,640]{1,0:T(8,128)(2,1)S(1)}, bf16[32,640]{1,0:T(8,128)(2,1)S(1)}, u32[]{:S(2)}, u32[]{:S(2)}) collective-permute-start(bf16[32,640]{1,0:T(8,128)(2,1)S(1)} %convert_element_type.167), channel_id=1, source_target_pairs={{0,44},{1,45},{2,46},{3,47},{4,56},{5,57},{6,58},{7,59},{8,52},{9,... | collective-permute-start | bytes 122888 | tf_op jit(solution)/shard_map/ppermute | solution.py:190
  118.2 3.8 %collective-permute-done.24 = bf16[32,640]{1,0:T(8,128)(2,1)S(1)} collective-permute-done((bf16[32,640]{1,0:T(8,128)(2,1)S(1)}, bf16[32,640]{1,0:T(8,128)(2,1)S(1)}, u32[]{:S(2)}, u32[]{:S(2)}) %collective-permute-start.24) | collective-permute-done | bytes 40992 | tf_op jit(solution)/shard_map/ppermute | solution.py:190
  122.7 0.9 collective-permute-done.25.got_ref
  123.6 2.7 %shard_map.83 = (f32[64,512]{1,0:T(8,128)S(1)}, f32[64,2048]{1,0:T(8,128)S(1)}, f32[32,640]{1,0:T(8,128)S(1)}, bf16[32,640]{1,0:T(8,128)(2,1)S(1)}) custom-call(s32[5]{0:T(128)S(1)} %stack.39.flags_ref.half_ref, f32[32,640]{1,0:T(8,128)S(1)} %convert_add_fusion.8.own_ref, f32[32,640]{1,0:T(8,128)S(1)} %collective-permute-done.25.got_ref, ...), custom_call_target="tpu_custom_call" | custom-call | tf_op jit(solution)/shard_map/pallas_call | solution.py:302
  127.8 3.5 %collective-permute-done.27 = bf16[32,640]{1,0:T(8,128)(2,1)S(1)} collective-permute-done((bf16[32,640]{1,0:T(8,128)(2,1)S(1)}, bf16[32,640]{1,0:T(8,128)(2,1)S(1)}, u32[]{:S(2)}, u32[]{:S(2)}) %collective-permute-start.27) | collective-permute-done | bytes 40992 | tf_op jit(solution)/shard_map/ppermute | solution.py:190
  131.4 4.7 %collective-permute-done.28 = bf16[32,640]{1,0:T(8,128)(2,1)S(1)} collective-permute-done((bf16[32,640]{1,0:T(8,128)(2,1)S(1)}, bf16[32,640]{1,0:T(8,128)(2,1)S(1)}, u32[]{:S(2)}, u32[]{:S(2)}) %collective-permute-start.28) | collective-permute-done | bytes 40992 | tf_op jit(solution)/shard_map/ppermute | solution.py:190
  136.3 3.5 %collective-permute-done.29 = bf16[32,640]{1,0:T(8,128)(2,1)S(1)} collective-permute-done((bf16[32,640]{1,0:T(8,128)(2,1)S(1)}, bf16[32,640]{1,0:T(8,128)(2,1)S(1)}, u32[]{:S(2)}, u32[]{:S(2)}) %collective-permute-start.29) | collective-permute-done | bytes 40992 | tf_op jit(solution)/shard_map/ppermute | solution.py:190
  140.5 4.1 %collective-permute-done.30 = bf16[32,640]{1,0:T(8,128)(2,1)S(1)} collective-permute-done((bf16[32,640]{1,0:T(8,128)(2,1)S(1)}, bf16[32,640]{1,0:T(8,128)(2,1)S(1)}, u32[]{:S(2)}, u32[]{:S(2)}) %collective-permute-start.30) | collective-permute-done | bytes 40992 | tf_op jit(solution)/shard_map/ppermute | solution.py:190
  144.8 3.5 %collective-permute-done.31 = bf16[32,640]{1,0:T(8,128)(2,1)S(1)} collective-permute-done((bf16[32,640]{1,0:T(8,128)(2,1)S(1)}, bf16[32,640]{1,0:T(8,128)(2,1)S(1)}, u32[]{:S(2)}, u32[]{:S(2)}) %collective-permute-start.31) | collective-permute-done | bytes 40992 | tf_op jit(solution)/shard_map/ppermute | solution.py:190
  148.4 4.7 %collective-permute-done.32 = bf16[32,640]{1,0:T(8,128)(2,1)S(1)} collective-permute-done((bf16[32,640]{1,0:T(8,128)(2,1)S(1)}, bf16[32,640]{1,0:T(8,128)(2,1)S(1)}, u32[]{:S(2)}, u32[]{:S(2)}) %collective-permute-start.32) | collective-permute-done | bytes 40992 | tf_op jit(solution)/shard_map/ppermute | solution.py:190
  153.2 2.0 %collective-permute-start.33 = (bf16[32,640]{1,0:T(8,128)(2,1)S(1)}, bf16[32,640]{1,0:T(8,128)(2,1)S(1)}, u32[]{:S(2)}, u32[]{:S(2)}) collective-permute-start(bf16[32,640]{1,0:T(8,128)(2,1)S(1)} %convert_element_type.182), channel_id=1, source_target_pairs={{0,44},{1,45},{2,46},{3,47},{4,56},{5,57},{6,58},{7,59},{8,52},{9,... | collective-permute-start | bytes 122888 | tf_op jit(solution)/shard_map/ppermute | solution.py:190
  155.1 4.3 %collective-permute-done.33 = bf16[32,640]{1,0:T(8,128)(2,1)S(1)} collective-permute-done((bf16[32,640]{1,0:T(8,128)(2,1)S(1)}, bf16[32,640]{1,0:T(8,128)(2,1)S(1)}, u32[]{:S(2)}, u32[]{:S(2)}) %collective-permute-start.33) | collective-permute-done | bytes 40992 | tf_op jit(solution)/shard_map/ppermute | solution.py:190
  159.9 0.9 collective-permute-done.34.got_ref
  160.9 6.4 %shard_map.84 = bf16[2048,512]{1,0:T(8,128)(2,1)} custom-call(s32[5]{0:T(128)S(1)} %stack.39.flags_ref.half_ref, f32[32,640]{1,0:T(8,128)S(1)} %convert_add_fusion.own_ref, f32[32,640]{1,0:T(8,128)S(1)} %collective-permute-done.34.got_ref, f32[64,512]{1,0:T(8,128)S(1)} %get-tuple-element.51.basis_ref, bf16[2048,512]{1,0:T(8,128)(2,1)S(1)} %get-tuple-element.43.feature_ref, ...), custom_call_target="tpu_custom_call" | custom-call | tf_op jit(solution)/shard_map/pallas_call | solution.py:302
  (98 shorter events, 9.6 us)
Async XLA Ops:
  0.0 1.6 copy-start
  1.6 17.1 %copy-start.1 = (bf16[64,32,512]{2,1,0:T(8,128)(2,1)S(1)}, bf16[64,32,512]{2,1,0:T(8,128)(2,1)}, u32[]{:S(2)}) copy-start(bf16[64,32,512]{2,1,0:T(8,128)(2,1)} %band_ref.11) | copy-start | bytes 6291460
  1.6 17.1 %copy-start.2 = (f32[21,512]{1,0:T(8,128)S(1)}, f32[21,512]{1,0:T(8,128)}, u32[]{:S(2)}) copy-start(f32[21,512]{1,0:T(8,128)} %taps_ref.10) | copy-start | bytes 129028
  3.4 24.1 %collective-permute-start = (bf16[10,64,256]{2,1,0:T(8,128)(2,1)}, bf16[10,64,256]{2,1,0:T(8,128)(2,1)S(1)}, u32[]{:S(2)}, u32[]{:S(2)}) collective-permute-start(bf16[10,64,256]{2,1,0:T(8,128)(2,1)} %get-tuple-element.29), channel_id=1, source_target_pairs={{0,1},{1,2},{2,3},{3,4},{4,5},{5,6},{6,7},{7,8},{8,9},{9,10},{10,1... | collective-permute-start | bytes 983048 | tf_op jit(solution)/shard_map/ppermute | solution.py:355
  5.4 22.0 %collective-permute-start.1 = (bf16[10,64,256]{2,1,0:T(8,128)(2,1)}, bf16[10,64,256]{2,1,0:T(8,128)(2,1)S(1)}, u32[]{:S(2)}, u32[]{:S(2)}) collective-permute-start(bf16[10,64,256]{2,1,0:T(8,128)(2,1)} %get-tuple-element.30), channel_id=1, source_target_pairs={{0,31},{1,0},{2,1},{3,2},{4,3},{5,4},{6,5},{7,6},{8,7},{9,8},{10,9... | collective-permute-start | bytes 983048 | tf_op jit(solution)/shard_map/ppermute | solution.py:355
  13.8 22.9 %collective-permute-start.4 = (bf16[10,64,256]{2,1,0:T(8,128)(2,1)}, bf16[10,64,256]{2,1,0:T(8,128)(2,1)S(1)}, u32[]{:S(2)}, u32[]{:S(2)}) collective-permute-start(bf16[10,64,256]{2,1,0:T(8,128)(2,1)} %get-tuple-element.36), channel_id=1, source_target_pairs={{0,1},{1,2},{2,3},{3,4},{4,5},{5,6},{6,7},{7,8},{8,9},{9,10},{10,1... | collective-permute-start | bytes 983048 | tf_op jit(solution)/shard_map/ppermute | solution.py:355
  13.8 22.9 %collective-permute-start.5 = (bf16[10,64,256]{2,1,0:T(8,128)(2,1)}, bf16[10,64,256]{2,1,0:T(8,128)(2,1)S(1)}, u32[]{:S(2)}, u32[]{:S(2)}) collective-permute-start(bf16[10,64,256]{2,1,0:T(8,128)(2,1)} %get-tuple-element.37), channel_id=1, source_target_pairs={{0,31},{1,0},{2,1},{3,2},{4,3},{5,4},{6,5},{7,6},{8,7},{9,8},{10,9... | collective-permute-start | bytes 983048 | tf_op jit(solution)/shard_map/ppermute | solution.py:355
  27.4 5.4 %copy-start.7 = (f32[21,512]{1,0:T(8,128)S(1)}, f32[21,512]{1,0:T(8,128)}, u32[]{:S(2)}) copy-start(f32[21,512]{1,0:T(8,128)} %refs_10_.1) | copy-start | bytes 129028
  30.1 14.9 %collective-permute-start.3 = (bf16[10,32,256]{2,1,0:T(8,128)(2,1)S(1)}, bf16[10,32,256]{2,1,0:T(8,128)(2,1)S(1)}, u32[]{:S(2)}, u32[]{:S(2)}) collective-permute-start(bf16[10,32,256]{2,1,0:T(8,128)(2,1)S(1)} %get-tuple-element.55), channel_id=1, source_target_pairs={{0,224},{32,0},{64,32},{96,64},{128,96},{160,128},{192,160},{224,1... | collective-permute-start | bytes 491528 | tf_op jit(solution)/shard_map/ppermute | solution.py:386
  31.7 13.4 %collective-permute-start.2 = (bf16[10,32,256]{2,1,0:T(8,128)(2,1)S(1)}, bf16[10,32,256]{2,1,0:T(8,128)(2,1)S(1)}, u32[]{:S(2)}, u32[]{:S(2)}) collective-permute-start(bf16[10,32,256]{2,1,0:T(8,128)(2,1)S(1)} %get-tuple-element.56), channel_id=1, source_target_pairs={{0,32},{32,64},{64,96},{96,128},{128,160},{160,192},{192,224},{224... | collective-permute-start | bytes 491528 | tf_op jit(solution)/shard_map/ppermute | solution.py:385
  39.4 5.7 %copy-start.3 = (bf16[512,512]{1,0:T(8,128)(2,1)S(1)}, bf16[512,512]{1,0:T(8,128)(2,1)}, u32[]{:S(2)}) copy-start(bf16[512,512]{1,0:T(8,128)(2,1)} %refs_11_.1) | copy-start | bytes 1572868
  39.4 5.7 %copy-start.6 = (f32[512,64]{0,1:T(8,128)S(1)}, f32[512,64]{0,1:T(8,128)}, u32[]{:S(2)}) copy-start(f32[512,64]{0,1:T(8,128)} %param.11) | copy-start | bytes 393220
  39.4 5.6 %collective-permute-start.7 = (bf16[10,32,256]{2,1,0:T(8,128)(2,1)S(1)}, bf16[10,32,256]{2,1,0:T(8,128)(2,1)S(1)}, u32[]{:S(2)}, u32[]{:S(2)}) collective-permute-start(bf16[10,32,256]{2,1,0:T(8,128)(2,1)S(1)} %get-tuple-element.53), channel_id=1, source_target_pairs={{0,224},{32,0},{64,32},{96,64},{128,96},{160,128},{192,160},{224,1... | collective-permute-start | bytes 491528 | tf_op jit(solution)/shard_map/ppermute | solution.py:386
  39.9 5.2 %collective-permute-start.6 = (bf16[10,32,256]{2,1,0:T(8,128)(2,1)S(1)}, bf16[10,32,256]{2,1,0:T(8,128)(2,1)S(1)}, u32[]{:S(2)}, u32[]{:S(2)}) collective-permute-start(bf16[10,32,256]{2,1,0:T(8,128)(2,1)S(1)} %get-tuple-element.54), channel_id=1, source_target_pairs={{0,32},{32,64},{64,96},{96,128},{128,160},{160,192},{192,224},{224... | collective-permute-start | bytes 491528 | tf_op jit(solution)/shard_map/ppermute | solution.py:385
  49.1 4.8 %collective-permute-start.8 = (bf16[32,640]{1,0:T(8,128)(2,1)S(1)}, bf16[32,640]{1,0:T(8,128)(2,1)S(1)}, u32[]{:S(2)}, u32[]{:S(2)}) collective-permute-start(bf16[32,640]{1,0:T(8,128)(2,1)S(1)} %get-tuple-element.42), channel_id=1, source_target_pairs={{0,32},{32,0},{1,33},{33,1},{2,34},{34,2},{3,35},{35,3},{4,36},{36... | collective-permute-start | bytes 122888 | tf_op jit(solution)/shard_map/ppermute | solution.py:187
  54.0 3.6 %collective-permute-start.9 = (bf16[32,640]{1,0:T(8,128)(2,1)S(1)}, bf16[32,640]{1,0:T(8,128)(2,1)S(1)}, u32[]{:S(2)}, u32[]{:S(2)}) collective-permute-start(bf16[32,640]{1,0:T(8,128)(2,1)S(1)} %convert_element_type.140), channel_id=1, source_target_pairs={{0,33},{1,32},{2,35},{3,34},{4,37},{5,36},{6,39},{7,38},{8,41},{9,... | collective-permute-start | bytes 122888 | tf_op jit(solution)/shard_map/ppermute | solution.py:190
  57.6 4.8 %collective-permute-start.10 = (bf16[32,640]{1,0:T(8,128)(2,1)S(1)}, bf16[32,640]{1,0:T(8,128)(2,1)S(1)}, u32[]{:S(2)}, u32[]{:S(2)}) collective-permute-start(bf16[32,640]{1,0:T(8,128)(2,1)S(1)} %convert_element_type.142), channel_id=1, source_target_pairs={{0,35},{1,34},{2,33},{3,32},{4,39},{5,38},{6,37},{7,36},{8,43},{9,... | collective-permute-start | bytes 122888 | tf_op jit(solution)/shard_map/ppermute | solution.py:190
  62.4 3.6 %collective-permute-start.11 = (bf16[32,640]{1,0:T(8,128)(2,1)S(1)}, bf16[32,640]{1,0:T(8,128)(2,1)S(1)}, u32[]{:S(2)}, u32[]{:S(2)}) collective-permute-start(bf16[32,640]{1,0:T(8,128)(2,1)S(1)} %convert_element_type.144), channel_id=1, source_target_pairs={{0,96},{1,97},{2,98},{3,99},{4,100},{5,101},{6,102},{7,103},{8,104... | collective-permute-start | bytes 122888 | tf_op jit(solution)/shard_map/ppermute | solution.py:190
  66.1 4.8 %collective-permute-start.12 = (bf16[32,640]{1,0:T(8,128)(2,1)S(1)}, bf16[32,640]{1,0:T(8,128)(2,1)S(1)}, u32[]{:S(2)}, u32[]{:S(2)}) collective-permute-start(bf16[32,640]{1,0:T(8,128)(2,1)S(1)} %convert_element_type.146), channel_id=1, source_target_pairs={{0,224},{1,225},{2,226},{3,227},{4,228},{5,229},{6,230},{7,231},{8... | collective-permute-start | bytes 122888 | tf_op jit(solution)/shard_map/ppermute | solution.py:190
  70.9 3.6 %collective-permute-start.13 = (bf16[32,640]{1,0:T(8,128)(2,1)S(1)}, bf16[32,640]{1,0:T(8,128)(2,1)S(1)}, u32[]{:S(2)}, u32[]{:S(2)}) collective-permute-start(bf16[32,640]{1,0:T(8,128)(2,1)S(1)} %convert_element_type.148), channel_id=1, source_target_pairs={{0,36},{1,37},{2,38},{3,39},{4,32},{5,33},{6,34},{7,35},{8,44},{9,... | collective-permute-start | bytes 122888 | tf_op jit(solution)/shard_map/ppermute | solution.py:190
  74.6 4.8 %collective-permute-start.14 = (bf16[32,640]{1,0:T(8,128)(2,1)S(1)}, bf16[32,640]{1,0:T(8,128)(2,1)S(1)}, u32[]{:S(2)}, u32[]{:S(2)}) collective-permute-start(bf16[32,640]{1,0:T(8,128)(2,1)S(1)} %convert_element_type.150), channel_id=1, source_target_pairs={{0,60},{1,61},{2,62},{3,63},{4,40},{5,41},{6,42},{7,43},{8,36},{9,... | collective-permute-start | bytes 122888 | tf_op jit(solution)/shard_map/ppermute | solution.py:190
  79.4 5.4 %collective-permute-start.15 = (bf16[32,640]{1,0:T(8,128)(2,1)S(1)}, bf16[32,640]{1,0:T(8,128)(2,1)S(1)}, u32[]{:S(2)}, u32[]{:S(2)}) collective-permute-start(bf16[32,640]{1,0:T(8,128)(2,1)S(1)} %convert_element_type.152), channel_id=1, source_target_pairs={{0,44},{1,45},{2,46},{3,47},{4,56},{5,57},{6,58},{7,59},{8,52},{9,... | collective-permute-start | bytes 122888 | tf_op jit(solution)/shard_map/ppermute | solution.py:190
  84.8 1.4 collective-permute-start.16
  88.9 1.3 collective-permute-start.17
  90.3 3.6 %collective-permute-start.18 = (bf16[32,640]{1,0:T(8,128)(2,1)S(1)}, bf16[32,640]{1,0:T(8,128)(2,1)S(1)}, u32[]{:S(2)}, u32[]{:S(2)}) collective-permute-start(bf16[32,640]{1,0:T(8,128)(2,1)S(1)} %convert_element_type.155), channel_id=1, source_target_pairs={{0,33},{1,32},{2,35},{3,34},{4,37},{5,36},{6,39},{7,38},{8,41},{9,... | collective-permute-start | bytes 122888 | tf_op jit(solution)/shard_map/ppermute | solution.py:190
  93.9 4.8 %collective-permute-start.19 = (bf16[32,640]{1,0:T(8,128)(2,1)S(1)}, bf16[32,640]{1,0:T(8,128)(2,1)S(1)}, u32[]{:S(2)}, u32[]{:S(2)}) collective-permute-start(bf16[32,640]{1,0:T(8,128)(2,1)S(1)} %convert_element_type.157), channel_id=1, source_target_pairs={{0,35},{1,34},{2,33},{3,32},{4,39},{5,38},{6,37},{7,36},{8,43},{9,... | collective-permute-start | bytes 122888 | tf_op jit(solution)/shard_map/ppermute | solution.py:190
  98.8 3.6 %collective-permute-start.20 = (bf16[32,640]{1,0:T(8,128)(2,1)S(1)}, bf16[32,640]{1,0:T(8,128)(2,1)S(1)}, u32[]{:S(2)}, u32[]{:S(2)}) collective-permute-start(bf16[32,640]{1,0:T(8,128)(2,1)S(1)} %convert_element_type.159), channel_id=1, source_target_pairs={{0,96},{1,97},{2,98},{3,99},{4,100},{5,101},{6,102},{7,103},{8,104... | collective-permute-start | bytes 122888 | tf_op jit(solution)/shard_map/ppermute | solution.py:190
  102.4 4.8 %collective-permute-start.21 = (bf16[32,640]{1,0:T(8,128)(2,1)S(1)}, bf16[32,640]{1,0:T(8,128)(2,1)S(1)}, u32[]{:S(2)}, u32[]{:S(2)}) collective-permute-start(bf16[32,640]{1,0:T(8,128)(2,1)S(1)} %convert_element_type.161), channel_id=1, source_target_pairs={{0,224},{1,225},{2,226},{3,227},{4,228},{5,229},{6,230},{7,231},{8... | collective-permute-start | bytes 122888 | tf_op jit(solution)/shard_map/ppermute | solution.py:190
  107.2 3.6 %collective-permute-start.22 = (bf16[32,640]{1,0:T(8,128)(2,1)S(1)}, bf16[32,640]{1,0:T(8,128)(2,1)S(1)}, u32[]{:S(2)}, u32[]{:S(2)}) collective-permute-start(bf16[32,640]{1,0:T(8,128)(2,1)S(1)} %convert_element_type.163), channel_id=1, source_target_pairs={{0,36},{1,37},{2,38},{3,39},{4,32},{5,33},{6,34},{7,35},{8,44},{9,... | collective-permute-start | bytes 122888 | tf_op jit(solution)/shard_map/ppermute | solution.py:190
  110.9 4.8 %collective-permute-start.23 = (bf16[32,640]{1,0:T(8,128)(2,1)S(1)}, bf16[32,640]{1,0:T(8,128)(2,1)S(1)}, u32[]{:S(2)}, u32[]{:S(2)}) collective-permute-start(bf16[32,640]{1,0:T(8,128)(2,1)S(1)} %convert_element_type.165), channel_id=1, source_target_pairs={{0,60},{1,61},{2,62},{3,63},{4,40},{5,41},{6,42},{7,43},{8,36},{9,... | collective-permute-start | bytes 122888 | tf_op jit(solution)/shard_map/ppermute | solution.py:190
  115.7 6.3 %collective-permute-start.24 = (bf16[32,640]{1,0:T(8,128)(2,1)S(1)}, bf16[32,640]{1,0:T(8,128)(2,1)S(1)}, u32[]{:S(2)}, u32[]{:S(2)}) collective-permute-start(bf16[32,640]{1,0:T(8,128)(2,1)S(1)} %convert_element_type.167), channel_id=1, source_target_pairs={{0,44},{1,45},{2,46},{3,47},{4,56},{5,57},{6,58},{7,59},{8,52},{9,... | collective-permute-start | bytes 122888 | tf_op jit(solution)/shard_map/ppermute | solution.py:190
  122.0 1.6 collective-permute-start.25
  123.6 37.3 %copy-start.4 = (bf16[512,512]{1,0:T(8,128)(2,1)S(1)}, bf16[512,512]{1,0:T(8,128)(2,1)}, u32[]{:S(2)}) copy-start(bf16[512,512]{1,0:T(8,128)(2,1)} %wham_ref.1) | copy-start | bytes 1572868
  123.6 37.3 %copy-start.5 = (bf16[512,512]{1,0:T(8,128)(2,1)S(1)}, bf16[512,512]{1,0:T(8,128)(2,1)}, u32[]{:S(2)}) copy-start(bf16[512,512]{1,0:T(8,128)(2,1)} %walign_ref.1) | copy-start | bytes 1572868
  126.4 1.3 collective-permute-start.26
  127.7 3.6 %collective-permute-start.27 = (bf16[32,640]{1,0:T(8,128)(2,1)S(1)}, bf16[32,640]{1,0:T(8,128)(2,1)S(1)}, u32[]{:S(2)}, u32[]{:S(2)}) collective-permute-start(bf16[32,640]{1,0:T(8,128)(2,1)S(1)} %convert_element_type.170), channel_id=1, source_target_pairs={{0,33},{1,32},{2,35},{3,34},{4,37},{5,36},{6,39},{7,38},{8,41},{9,... | collective-permute-start | bytes 122888 | tf_op jit(solution)/shard_map/ppermute | solution.py:190
  131.3 4.8 %collective-permute-start.28 = (bf16[32,640]{1,0:T(8,128)(2,1)S(1)}, bf16[32,640]{1,0:T(8,128)(2,1)S(1)}, u32[]{:S(2)}, u32[]{:S(2)}) collective-permute-start(bf16[32,640]{1,0:T(8,128)(2,1)S(1)} %convert_element_type.172), channel_id=1, source_target_pairs={{0,35},{1,34},{2,33},{3,32},{4,39},{5,38},{6,37},{7,36},{8,43},{9,... | collective-permute-start | bytes 122888 | tf_op jit(solution)/shard_map/ppermute | solution.py:190
  136.2 3.6 %collective-permute-start.29 = (bf16[32,640]{1,0:T(8,128)(2,1)S(1)}, bf16[32,640]{1,0:T(8,128)(2,1)S(1)}, u32[]{:S(2)}, u32[]{:S(2)}) collective-permute-start(bf16[32,640]{1,0:T(8,128)(2,1)S(1)} %convert_element_type.174), channel_id=1, source_target_pairs={{0,96},{1,97},{2,98},{3,99},{4,100},{5,101},{6,102},{7,103},{8,104... | collective-permute-start | bytes 122888 | tf_op jit(solution)/shard_map/ppermute | solution.py:190
  139.8 4.8 %collective-permute-start.30 = (bf16[32,640]{1,0:T(8,128)(2,1)S(1)}, bf16[32,640]{1,0:T(8,128)(2,1)S(1)}, u32[]{:S(2)}, u32[]{:S(2)}) collective-permute-start(bf16[32,640]{1,0:T(8,128)(2,1)S(1)} %convert_element_type.176), channel_id=1, source_target_pairs={{0,224},{1,225},{2,226},{3,227},{4,228},{5,229},{6,230},{7,231},{8... | collective-permute-start | bytes 122888 | tf_op jit(solution)/shard_map/ppermute | solution.py:190
  144.7 3.6 %collective-permute-start.31 = (bf16[32,640]{1,0:T(8,128)(2,1)S(1)}, bf16[32,640]{1,0:T(8,128)(2,1)S(1)}, u32[]{:S(2)}, u32[]{:S(2)}) collective-permute-start(bf16[32,640]{1,0:T(8,128)(2,1)S(1)} %convert_element_type.178), channel_id=1, source_target_pairs={{0,36},{1,37},{2,38},{3,39},{4,32},{5,33},{6,34},{7,35},{8,44},{9,... | collective-permute-start | bytes 122888 | tf_op jit(solution)/shard_map/ppermute | solution.py:190
  148.3 4.8 %collective-permute-start.32 = (bf16[32,640]{1,0:T(8,128)(2,1)S(1)}, bf16[32,640]{1,0:T(8,128)(2,1)S(1)}, u32[]{:S(2)}, u32[]{:S(2)}) collective-permute-start(bf16[32,640]{1,0:T(8,128)(2,1)S(1)} %convert_element_type.180), channel_id=1, source_target_pairs={{0,60},{1,61},{2,62},{3,63},{4,40},{5,41},{6,42},{7,43},{8,36},{9,... | collective-permute-start | bytes 122888 | tf_op jit(solution)/shard_map/ppermute | solution.py:190
  153.2 6.3 %collective-permute-start.33 = (bf16[32,640]{1,0:T(8,128)(2,1)S(1)}, bf16[32,640]{1,0:T(8,128)(2,1)S(1)}, u32[]{:S(2)}, u32[]{:S(2)}) collective-permute-start(bf16[32,640]{1,0:T(8,128)(2,1)S(1)} %convert_element_type.182), channel_id=1, source_target_pairs={{0,44},{1,45},{2,46},{3,47},{4,56},{5,57},{6,58},{7,59},{8,52},{9,... | collective-permute-start | bytes 122888 | tf_op jit(solution)/shard_map/ppermute | solution.py:190
  159.5 1.4 collective-permute-start.34

commit v6 on v4

--- a/solution.py
+++ b/solution.py
@@ -19,6 +19,7 @@
 TAPS = 21
 MARGIN = TAPS // 2
 LANES = 128
+PARTS = 2
 
 
 def weighted(taps_ref, items, rows):
@@ -46,8 +47,18 @@
             emit(start + i, value)
 
 
-def columns_own_kernel(band_ref, taps_ref, out_ref, flat, turned):
+def pack_kernel(band_ref, *refs):
+    first_ref, last_ref, flat = refs[-3:]
     h, w, lanes = band_ref.shape
+    flat[...] = band_ref[...].astype(F32).reshape(h * w, lanes)
+    for j in range(MARGIN):
+        first_ref[j] = flat[pl.ds(j, h, stride=w), :].astype(BF)
+        last_ref[j] = flat[pl.ds(w - MARGIN + j, h, stride=w), :].astype(BF)
+
+
+def columns_own_kernel(band_ref, taps_ref, out_ref, token_ref, flat, turned):
+    h, w, lanes = band_ref.shape
+    token_ref[...] = jnp.zeros_like(token_ref)
     flat[...] = band_ref[...].astype(F32).reshape(h * w, lanes)
     for j in range(w):
         turned[j] = flat[pl.ds(j, h, stride=w), :]
@@ -64,7 +75,8 @@
     lax.fori_loop(0, h // 8, body, 0)
 
 
-def columns_rest_kernel(flags_ref, own_ref, left_ref, right_ref, taps_ref, out_ref, lefts, rights, flat):
+def columns_rest_kernel(flags_ref, own_ref, left_ref, right_ref, taps_ref, *refs):
+    out_ref, lefts, rights, flat = refs[-4:]
     w, h, lanes = own_ref.shape
     lefts[...] = jnp.where(flags_ref[1] == 1, left_ref[...].astype(F32), 0.0)
     rights[...] = jnp.where(flags_ref[2] == 1, right_ref[...].astype(F32), 0.0)
@@ -220,6 +232,14 @@
     theirs_ref[:, c:] = jnp.where(first, gram[rows:], gram[:rows]).astype(BF)
 
 
+def above_pairs(o):
+    return [(j - o, j) for j in range(o, MARGIN)]
+
+
+def below_pairs(o):
+    return [(2 * MARGIN + j - o, j) for j in range(o + 1)]
+
+
 def first_kernel(
     flags_ref, mid_ref, top_ref, low_ref, above_ref, below_ref, taps_ref, w_ref, basis_ref,
     feature_ref, coeffs_ref, mine_ref, theirs_ref,
@@ -308,49 +328,77 @@
     def ring(count, by):
         return [(i, (i + by) % count) for i in range(count)]
 
-    left = band_input[:, tile_cols - margin :].transpose(1, 0, 2)
-    right = band_input[:, :margin].transpose(1, 0, 2)
-    left = lax.ppermute(left, COLS, ring(Z * X, 1))
-    right = lax.ppermute(right, COLS, ring(Z * X, -1))
-
-    def blocks(*dims):
-        return pl.BlockSpec((*dims, LANES), lambda i: (*(0 for _ in dims), i))
+    width = channels // PARTS
+    blocks_in_part = width // LANES
+
+    def blocks(*dims, start=0):
+        return pl.BlockSpec((*dims, LANES), lambda i: (*(0 for _ in dims), i + start))
 
     scalar = pl.BlockSpec(memory_space=pltpu.SMEM)
-    tile, turned = blocks(tile_rows, tile_cols), blocks(tile_cols, tile_rows)
+    turned, tile = blocks(tile_cols, tile_rows), blocks(tile_rows, tile_cols)
     side, edge = blocks(margin, tile_rows), blocks(margin, tile_cols)
-    taps = blocks(TAPS)
-    grid = (channels // LANES,)
+    grid = (blocks_in_part,)
     flat = pltpu.VMEM((tile_rows * tile_cols, LANES), F32)
     params = pltpu.CompilerParams(vmem_limit_bytes=20 * 2**20)
-    pixels = tile_rows * tile_cols * channels
-    cost = pl.CostEstimate(flops=2 * TAPS * pixels, bytes_accessed=6 * pixels, transcendentals=0)
-    own = pl.pallas_call(
-        columns_own_kernel,
-        grid=grid,
-        in_specs=[tile, taps],
-        out_specs=turned,
-        out_shape=sds((tile_cols, tile_rows, channels), F32),
-        scratch_shapes=[flat, pltpu.VMEM((tile_cols, tile_rows, LANES), F32)],
-        compiler_params=params,
-        cost_estimate=cost,
-    )(band_input, column_taps)
-    filtered = pl.pallas_call(
-        columns_rest_kernel,
-        grid=grid,
-        in_specs=[scalar, turned, side, side, taps],
-        out_specs=tile,
-        out_shape=sds(band_input.shape, BF),
-        scratch_shapes=[pltpu.VMEM((margin, tile_rows, LANES), F32)] * 2 + [flat],
-        compiler_params=params,
-    )(flags, own, left, right, column_taps)
+    wide = pltpu.CompilerParams(vmem_limit_bytes=58 * 2**20)
+    pixels = tile_rows * tile_cols * width
+    rest = tile_rows - 2 * margin
+
+    def cost(taps, moved):
+        return pl.CostEstimate(flops=2 * taps * pixels, bytes_accessed=moved * pixels, transcendentals=0)
+
+    whole = pl.BlockSpec(memory_space=pl.ANY)
+    sides, owns, tokens = [], [], []
+    for i in range(PARTS):
+        start = i * blocks_in_part
+        first, last = pl.pallas_call(
+            pack_kernel,
+            grid=grid,
+            in_specs=[blocks(tile_rows, tile_cols, start=start)] + [whole] * i,
+            out_specs=[side, side],
+            out_shape=[sds((margin, tile_rows, width), BF)] * 2,
+            scratch_shapes=[flat],
+            compiler_params=wide,
+            cost_estimate=cost(1, 3),
+        )(band_input, *tokens)
+        sides.append(
+            (lax.ppermute(last, COLS, ring(Z * X, 1)), lax.ppermute(first, COLS, ring(Z * X, -1)))
+        )
+        own, token = pl.pallas_call(
+            columns_own_kernel,
+            grid=grid,
+            in_specs=[blocks(tile_rows, tile_cols, start=start), blocks(TAPS, start=start)],
+            out_specs=[turned, pl.BlockSpec((8, LANES), lambda i: (0, 0))],
+            out_shape=[sds((tile_cols, tile_rows, width), F32), sds((8, LANES), F32)],
+            scratch_shapes=[flat, pltpu.VMEM((tile_cols, tile_rows, LANES), F32)],
+            compiler_params=params if i else wide,
+            cost_estimate=cost(TAPS, 6),
+        )(band_input, column_taps)
+        owns.append(own)
+        tokens.append(token)
+    filtered = []
+    for i in range(PARTS):
+        start = i * blocks_in_part
+        filtered = [
+            pl.pallas_call(
+                columns_rest_kernel,
+                grid=grid,
+                in_specs=[scalar, turned, side, side, blocks(TAPS, start=start)] + [whole] * len(filtered),
+                out_specs=blocks(tile_rows, tile_cols, start=start),
+                out_shape=sds((tile_rows, tile_cols, channels), BF),
+                scratch_shapes=[pltpu.VMEM((margin, tile_rows, LANES), F32)] * 2 + [flat],
+                input_output_aliases={5: 0} if filtered else {},
+                compiler_params=params,
+                cost_estimate=cost(TAPS // 2, 6),
+            )(flags, owns[i], *sides[i], column_taps, *filtered)
+        ]
+    filtered = filtered[0]
     above = lax.ppermute(filtered[tile_rows - margin :], ROWS, ring(Y * CORE, 1))
     below = lax.ppermute(filtered[:margin], ROWS, ring(Y * CORE, -1))
-    rest = tile_rows - 2 * margin
     mid, top, low = pl.pallas_call(
         rows_own_kernel,
-        grid=grid,
-        in_specs=[tile, tile, taps],
+        grid=(channels // LANES,),
+        in_specs=[tile, tile, blocks(TAPS)],
         out_specs=[blocks(rest, tile_cols), edge, edge],
         out_shape=[
             sds((rest, tile_cols, channels), BF),
@@ -363,11 +411,11 @@
             pltpu.VMEM((rest, tile_cols, LANES), F32),
         ],
         compiler_params=params,
-        cost_estimate=cost,
+        cost_estimate=cost(2 * TAPS, 12),
     )(filtered, band_input, row_taps)
     n, r = tile_rows * tile_cols, bases_init.shape[1]
-    width = channels + 128
-    sums = [sds((r // 2, width), F32), sds((r // 2, width), BF)]
+    packed = (r // 2, channels + LANES)
+    sums = [sds(packed, F32), sds(packed, BF)]
     basis = bases_init.T
     feature, coeffs, mine, theirs = call(
         first_kernel,

time: 161 us -> 163 us (1.012)
  Pallas kernels: 37.4 us -> 45 us
  local copies, waits for them, and re-layouts: 4.55 us -> 0.17 us
  starting transfers between devices: 53.1 us -> 50.1 us
  waiting for transfers between devices: 64.8 us -> 66.6 us
    ppermute x21, starting transfers between devices: 39.6 us -> 31.2 us  [summed_over_all(): got = lax.ppermute(total.astype(BF), ALL, round_pairs(axis, rule))]
    pallas_call x2 -> x5, Pallas kernels: 16.6 us -> 23.9 us  [the longest x2 10.9 us: on_device(): pl.pallas_call(columns_own_kernel, grid=grid, in_specs=[blocks(tile_rows,...]
    ppermute x21, waiting for transfers between devices: 54.1 us -> 61.1 us  [summed_over_all(): got = lax.ppermute(total.astype(BF), ALL, round_pairs(axis, rule))]
    ppermute x2 -> x4, starting transfers between devices: 8.59 us -> 13.5 us  [the longest x2 11.4 us: on_device(): lax.ppermute(first, COLS, ring(Z * X, -1))]
    ppermute x2 -> x4, waiting for transfers between devices: 4.71 us -> 0.01 us  [the longest x2 0.01 us: on_device(): lax.ppermute(last, COLS, ring(Z * X, 1))]
    unnamed x16, local copies, waits for them, and re-layouts: 2.43 us -> 0.03 us
    slice x1 -> x0, local copies, waits for them, and re-layouts: 1.99 us -> none  [on_device(): right = band_input[:, :margin].transpose(1, 0, 2)]
    pallas_call x1 -> x2, Pallas kernels: 5.01 us -> 5.27 us  [on_device(): pl.pallas_call(columns_rest_kernel, grid=grid, in_specs=[scalar, turned,...]
  transfers between devices with their start and end apart: 31 -> 33, of which waited for: 29 -> 27; matrix products, arithmetic and copies ran while one was open for 1% -> 0% of each run, Pallas kernels for 10% -> 15%
where the time goes in v6:
time: 163 us
  waiting for transfers between devices  66.6 us (41%)
  starting transfers between devices  50.1 us (31%)
  Pallas kernels  45 us (28%)
    ppermute x21, waiting for transfers between devices, summed_over_all(): got = lax.ppermute(total.astype(BF), ALL, round_pairs(axis, rule))  61.1 us
    ppermute x21, starting transfers between devices, summed_over_all(): got = lax.ppermute(total.astype(BF), ALL, round_pairs(axis, rule))  31.2 us
    pallas_call x4, Pallas kernels, call(): pl.pallas_call(kernel, out_shape=outs, in_specs=specs, out_specs=jax.tree...  15.8 us
    ppermute x2, starting transfers between devices, on_device(): lax.ppermute(first, COLS, ring(Z * X, -1))  11.4 us
    pallas_call x2, Pallas kernels, on_device(): pl.pallas_call(columns_own_kernel, grid=grid, in_specs=[blocks(tile_rows,...  10.9 us
    pallas_call x1, Pallas kernels, on_device(): pl.pallas_call(rows_own_kernel, grid=(channels // LANES,), in_specs=[tile...  7.67 us
    pallas_call x2, Pallas kernels, on_device(): pl.pallas_call(pack_kernel, grid=grid, in_specs=[blocks(tile_rows, tile_c...  5.32 us
    pallas_call x2, Pallas kernels, on_device(): pl.pallas_call(columns_rest_kernel, grid=grid, in_specs=[scalar, turned,...  5.27 us
  transfers between devices with their start and end apart: 33, of which 27 were waited for; matrix products, arithmetic and copies ran while one was open for 0% of the time, Pallas kernels for 15%

profile of v6, /device:TPU:1, one launch (start us, length us, event | category | flops | bytes accessed | tf_op | source)
XLA Modules:
  0.0 162.7 jit_solution(1230664484279737399)
XLA Ops:
  0.0 2.7 %shard_map.76 = (bf16[10,64,256]{2,1,0:T(8,128)(2,1)}, bf16[10,64,256]{2,1,0:T(8,128)(2,1)}) custom-call(bf16[64,32,512]{2,1,0:T(8,128)(2,1)} %band_ref.9), custom_call_target="tpu_custom_call" | custom-call | flops 1048576 | bytes 1572864 | tf_op jit(solution)/shard_map/pallas_call | solution.py:354
  2.7 2.0 %collective-permute-start.2 = (bf16[10,64,256]{2,1,0:T(8,128)(2,1)}, bf16[10,64,256]{2,1,0:T(8,128)(2,1)S(1)}, u32[]{:S(2)}, u32[]{:S(2)}) collective-permute-start(bf16[10,64,256]{2,1,0:T(8,128)(2,1)} %get-tuple-element.32), channel_id=1, source_target_pairs={{0,1},{1,2},{2,3},{3,4},{4,5},{5,6},{6,7},{7,8},{8,9},{9,10},{10,1... | collective-permute-start | bytes 983048 | tf_op jit(solution)/shard_map/ppermute | solution.py:365
  4.7 6.6 %collective-permute-start.3 = (bf16[10,64,256]{2,1,0:T(8,128)(2,1)}, bf16[10,64,256]{2,1,0:T(8,128)(2,1)S(1)}, u32[]{:S(2)}, u32[]{:S(2)}) collective-permute-start(bf16[10,64,256]{2,1,0:T(8,128)(2,1)} %get-tuple-element.33), channel_id=1, source_target_pairs={{0,31},{1,0},{2,1},{3,2},{4,3},{5,4},{6,5},{7,6},{8,7},{9,8},{10,9... | collective-permute-start | bytes 983048 | tf_op jit(solution)/shard_map/ppermute | solution.py:365
  11.4 6.0 %shard_map.74 = (f32[32,64,256]{2,1,0:T(8,128)}, f32[8,128]{1,0:T(8,128)}) custom-call(bf16[64,32,512]{2,1,0:T(8,128)(2,1)} %band_ref.9, f32[21,512]{1,0:T(8,128)} %taps_ref.9), custom_call_target="tpu_custom_call" | custom-call | flops 22020096 | bytes 3145728 | tf_op jit(solution)/shard_map/pallas_call | solution.py:367
  17.3 2.7 %shard_map.75 = (bf16[10,64,256]{2,1,0:T(8,128)(2,1)}, bf16[10,64,256]{2,1,0:T(8,128)(2,1)}) custom-call(bf16[64,32,512]{2,1,0:T(8,128)(2,1)} %band_ref.9, f32[8,128]{1,0:T(8,128)} %get-tuple-element.28.refs_0_), custom_call_target="tpu_custom_call" | custom-call | flops 1048576 | bytes 1572864 | tf_op jit(solution)/shard_map/pallas_call | solution.py:354
  20.0 4.8 %collective-permute-start.1 = (bf16[10,64,256]{2,1,0:T(8,128)(2,1)}, bf16[10,64,256]{2,1,0:T(8,128)(2,1)S(1)}, u32[]{:S(2)}, u32[]{:S(2)}) collective-permute-start(bf16[10,64,256]{2,1,0:T(8,128)(2,1)} %get-tuple-element.30), channel_id=1, source_target_pairs={{0,31},{1,0},{2,1},{3,2},{4,3},{5,4},{6,5},{7,6},{8,7},{9,8},{10,9... | collective-permute-start | bytes 983048 | tf_op jit(solution)/shard_map/ppermute | solution.py:365
  24.9 4.9 %shard_map.73 = (f32[32,64,256]{2,1,0:T(8,128)S(1)}, f32[8,128]{1,0:T(8,128)}) custom-call(bf16[64,32,512]{2,1,0:T(8,128)(2,1)S(1)} %copy-done, f32[21,512]{1,0:T(8,128)S(1)} %copy-done.2), custom_call_target="tpu_custom_call" | custom-call | flops 22020096 | bytes 3145728 | tf_op jit(solution)/shard_map/pallas_call | solution.py:367
  29.8 2.6 %shard_map.77.refs_0_ = bf16[64,32,512]{2,1,0:T(8,128)(2,1)S(1)} custom-call(s32[5]{0:T(128)S(1)} %stack.39.flags_ref.half_ref, f32[32,64,256]{2,1,0:T(8,128)S(1)} %copy-done.1, bf16[10,64,256]{2,1,0:T(8,128)(2,1)S(1)} %collective-permute-done.2.left_ref, bf16[10,64,256]{2,1,0:T(8,128)(2,1)S(1)} %collective-permute-done.3.right_ref, f32[21,512]{1,0:T(8,128)S(1)} %copy-done.2), custom_call_target="tpu_custom_call" | custom-call | flops 10485760 | bytes 3145728 | tf_op jit(solution)/shard_map/pallas_call | solution.py:383
  32.5 2.6 %shard_map.78.filtered_ref = bf16[64,32,512]{2,1,0:T(8,128)(2,1)S(1)} custom-call(s32[5]{0:T(128)S(1)} %stack.39.flags_ref.half_ref, f32[32,64,256]{2,1,0:T(8,128)S(1)} %get-tuple-element.27.own_ref, bf16[10,64,256]{2,1,0:T(8,128)(2,1)S(1)} %collective-permute-done.left_ref, ...), custom_call_target="tpu_custom_call", output_to_operand_aliasing={{}: (5, {})} | custom-call | flops 10485760 | bytes 3145728 | tf_op jit(solution)/shard_map/pallas_call | solution.py:383
  35.2 1.5 collective-permute-start.5
  36.7 1.2 collective-permute-start.4
  38.0 7.7 %shard_map.79 = (bf16[44,32,512]{2,1,0:T(8,128)(2,1)S(1)}, f32[10,32,512]{2,1,0:T(8,128)S(1)}, f32[10,32,512]{2,1,0:T(8,128)S(1)}) custom-call(bf16[64,32,512]{2,1,0:T(8,128)(2,1)S(1)} %shard_map.78.filtered_ref, bf16[64,32,512]{2,1,0:T(8,128)(2,1)S(1)} %copy-done, f32[21,512]{1,0:T(8,128)S(1)} %copy-done.7), custom_call_target="tpu_custom_call" | custom-call | flops 44040192 | bytes 6291456 | tf_op jit(solution)/shard_map/pallas_call | solution.py:398
  45.7 4.0 %shard_map.80 = (bf16[2048,512]{1,0:T(8,128)(2,1)S(1)}, f32[64,2048]{1,0:T(8,128)S(1)}, f32[32,640]{1,0:T(8,128)S(1)}, bf16[32,640]{1,0:T(8,128)(2,1)S(1)}) custom-call(s32[5]{0:T(128)S(1)} %stack.39.flags_ref.half_ref, bf16[44,32,512]{2,1,0:T(8,128)(2,1)S(1)} %get-tuple-element.34.mid_ref, f32[10,32,512]{2,1,0:T(8,128)S(1)} %get-tuple-element.35.top_ref, ...), custom_call_target="tpu_custom_call" | custom-call | tf_op jit(solution)/shard_map/pallas_call | solution.py:309
  51.1 3.5 %collective-permute-done.7 = bf16[32,640]{1,0:T(8,128)(2,1)S(1)} collective-permute-done((bf16[32,640]{1,0:T(8,128)(2,1)S(1)}, bf16[32,640]{1,0:T(8,128)(2,1)S(1)}, u32[]{:S(2)}, u32[]{:S(2)}) %collective-permute-start.7) | collective-permute-done | bytes 40992 | tf_op jit(solution)/shard_map/ppermute | solution.py:193
  55.0 4.7 %collective-permute-done.8 = bf16[32,640]{1,0:T(8,128)(2,1)S(1)} collective-permute-done((bf16[32,640]{1,0:T(8,128)(2,1)S(1)}, bf16[32,640]{1,0:T(8,128)(2,1)S(1)}, u32[]{:S(2)}, u32[]{:S(2)}) %collective-permute-start.8) | collective-permute-done | bytes 40992 | tf_op jit(solution)/shard_map/ppermute | solution.py:193
  60.9 2.4 %collective-permute-done.9 = bf16[32,640]{1,0:T(8,128)(2,1)S(1)} collective-permute-done((bf16[32,640]{1,0:T(8,128)(2,1)S(1)}, bf16[32,640]{1,0:T(8,128)(2,1)S(1)}, u32[]{:S(2)}, u32[]{:S(2)}) %collective-permute-start.9) | collective-permute-done | bytes 40992 | tf_op jit(solution)/shard_map/ppermute | solution.py:193
  63.3 2.7 %collective-permute-start.10 = (bf16[32,640]{1,0:T(8,128)(2,1)S(1)}, bf16[32,640]{1,0:T(8,128)(2,1)S(1)}, u32[]{:S(2)}, u32[]{:S(2)}) collective-permute-start(bf16[32,640]{1,0:T(8,128)(2,1)S(1)} %convert_element_type.146), channel_id=1, source_target_pairs={{0,224},{1,225},{2,226},{3,227},{4,228},{5,229},{6,230},{7,231},{8... | collective-permute-start | bytes 122888 | tf_op jit(solution)/shard_map/ppermute | solution.py:193
  66.1 2.1 %collective-permute-done.10 = bf16[32,640]{1,0:T(8,128)(2,1)S(1)} collective-permute-done((bf16[32,640]{1,0:T(8,128)(2,1)S(1)}, bf16[32,640]{1,0:T(8,128)(2,1)S(1)}, u32[]{:S(2)}, u32[]{:S(2)}) %collective-permute-start.10) | collective-permute-done | bytes 40992 | tf_op jit(solution)/shard_map/ppermute | solution.py:193
  68.3 3.5 %collective-permute-done.11 = bf16[32,640]{1,0:T(8,128)(2,1)S(1)} collective-permute-done((bf16[32,640]{1,0:T(8,128)(2,1)S(1)}, bf16[32,640]{1,0:T(8,128)(2,1)S(1)}, u32[]{:S(2)}, u32[]{:S(2)}) %collective-permute-start.11) | collective-permute-done | bytes 40992 | tf_op jit(solution)/shard_map/ppermute | solution.py:193
  71.8 1.9 %collective-permute-start.12 = (bf16[32,640]{1,0:T(8,128)(2,1)S(1)}, bf16[32,640]{1,0:T(8,128)(2,1)S(1)}, u32[]{:S(2)}, u32[]{:S(2)}) collective-permute-start(bf16[32,640]{1,0:T(8,128)(2,1)S(1)} %convert_element_type.150), channel_id=1, source_target_pairs={{0,60},{1,61},{2,62},{3,63},{4,40},{5,41},{6,42},{7,43},{8,36},{9,... | collective-permute-start | bytes 122888 | tf_op jit(solution)/shard_map/ppermute | solution.py:193
  73.8 2.9 %collective-permute-done.12 = bf16[32,640]{1,0:T(8,128)(2,1)S(1)} collective-permute-done((bf16[32,640]{1,0:T(8,128)(2,1)S(1)}, bf16[32,640]{1,0:T(8,128)(2,1)S(1)}, u32[]{:S(2)}, u32[]{:S(2)}) %collective-permute-start.12) | collective-permute-done | bytes 40992 | tf_op jit(solution)/shard_map/ppermute | solution.py:193
  76.7 3.4 %collective-permute-start.13 = (bf16[32,640]{1,0:T(8,128)(2,1)S(1)}, bf16[32,640]{1,0:T(8,128)(2,1)S(1)}, u32[]{:S(2)}, u32[]{:S(2)}) collective-permute-start(bf16[32,640]{1,0:T(8,128)(2,1)S(1)} %convert_element_type.152), channel_id=1, source_target_pairs={{0,44},{1,45},{2,46},{3,47},{4,56},{5,57},{6,58},{7,59},{8,52},{9,... | collective-permute-start | bytes 122888 | tf_op jit(solution)/shard_map/ppermute | solution.py:193
  80.1 2.0 %collective-permute-done.13 = bf16[32,640]{1,0:T(8,128)(2,1)S(1)} collective-permute-done((bf16[32,640]{1,0:T(8,128)(2,1)S(1)}, bf16[32,640]{1,0:T(8,128)(2,1)S(1)}, u32[]{:S(2)}, u32[]{:S(2)}) %collective-permute-start.13) | collective-permute-done | bytes 40992 | tf_op jit(solution)/shard_map/ppermute | solution.py:193
  83.5 2.7 %shard_map.81 = (f32[64,512]{1,0:T(8,128)S(1)}, f32[64,2048]{1,0:T(8,128)S(1)}, f32[32,640]{1,0:T(8,128)S(1)}, bf16[32,640]{1,0:T(8,128)(2,1)S(1)}) custom-call(s32[5]{0:T(128)S(1)} %stack.39.flags_ref.half_ref, f32[32,640]{1,0:T(8,128)S(1)} %convert_add_fusion.16.own_ref, f32[32,640]{1,0:T(8,128)S(1)} %collective-permute-done.14.got_ref, ...), custom_call_target="tpu_custom_call" | custom-call | tf_op jit(solution)/shard_map/pallas_call | solution.py:309
  87.6 3.5 %collective-permute-done.16 = bf16[32,640]{1,0:T(8,128)(2,1)S(1)} collective-permute-done((bf16[32,640]{1,0:T(8,128)(2,1)S(1)}, bf16[32,640]{1,0:T(8,128)(2,1)S(1)}, u32[]{:S(2)}, u32[]{:S(2)}) %collective-permute-start.16) | collective-permute-done | bytes 40992 | tf_op jit(solution)/shard_map/ppermute | solution.py:193
  91.2 2.3 %collective-permute-start.17 = (bf16[32,640]{1,0:T(8,128)(2,1)S(1)}, bf16[32,640]{1,0:T(8,128)(2,1)S(1)}, u32[]{:S(2)}, u32[]{:S(2)}) collective-permute-start(bf16[32,640]{1,0:T(8,128)(2,1)S(1)} %convert_element_type.157), channel_id=1, source_target_pairs={{0,35},{1,34},{2,33},{3,32},{4,39},{5,38},{6,37},{7,36},{8,43},{9,... | collective-permute-start | bytes 122888 | tf_op jit(solution)/shard_map/ppermute | solution.py:193
  93.5 2.5 %collective-permute-done.17 = bf16[32,640]{1,0:T(8,128)(2,1)S(1)} collective-permute-done((bf16[32,640]{1,0:T(8,128)(2,1)S(1)}, bf16[32,640]{1,0:T(8,128)(2,1)S(1)}, u32[]{:S(2)}, u32[]{:S(2)}) %collective-permute-start.17) | collective-permute-done | bytes 40992 | tf_op jit(solution)/shard_map/ppermute | solution.py:193
  96.1 3.5 %collective-permute-done.18 = bf16[32,640]{1,0:T(8,128)(2,1)S(1)} collective-permute-done((bf16[32,640]{1,0:T(8,128)(2,1)S(1)}, bf16[32,640]{1,0:T(8,128)(2,1)S(1)}, u32[]{:S(2)}, u32[]{:S(2)}) %collective-permute-start.18) | collective-permute-done | bytes 40992 | tf_op jit(solution)/shard_map/ppermute | solution.py:193
  99.7 2.1 %collective-permute-start.19 = (bf16[32,640]{1,0:T(8,128)(2,1)S(1)}, bf16[32,640]{1,0:T(8,128)(2,1)S(1)}, u32[]{:S(2)}, u32[]{:S(2)}) collective-permute-start(bf16[32,640]{1,0:T(8,128)(2,1)S(1)} %convert_element_type.161), channel_id=1, source_target_pairs={{0,224},{1,225},{2,226},{3,227},{4,228},{5,229},{6,230},{7,231},{8... | collective-permute-start | bytes 122888 | tf_op jit(solution)/shard_map/ppermute | solution.py:193
  101.7 2.7 %collective-permute-done.19 = bf16[32,640]{1,0:T(8,128)(2,1)S(1)} collective-permute-done((bf16[32,640]{1,0:T(8,128)(2,1)S(1)}, bf16[32,640]{1,0:T(8,128)(2,1)S(1)}, u32[]{:S(2)}, u32[]{:S(2)}) %collective-permute-start.19) | collective-permute-done | bytes 40992 | tf_op jit(solution)/shard_map/ppermute | solution.py:193
  105.2 2.9 %collective-permute-done.20 = bf16[32,640]{1,0:T(8,128)(2,1)S(1)} collective-permute-done((bf16[32,640]{1,0:T(8,128)(2,1)S(1)}, bf16[32,640]{1,0:T(8,128)(2,1)S(1)}, u32[]{:S(2)}, u32[]{:S(2)}) %collective-permute-start.20) | collective-permute-done | bytes 40992 | tf_op jit(solution)/shard_map/ppermute | solution.py:193
  108.1 2.2 %collective-permute-start.21 = (bf16[32,640]{1,0:T(8,128)(2,1)S(1)}, bf16[32,640]{1,0:T(8,128)(2,1)S(1)}, u32[]{:S(2)}, u32[]{:S(2)}) collective-permute-start(bf16[32,640]{1,0:T(8,128)(2,1)S(1)} %convert_element_type.165), channel_id=1, source_target_pairs={{0,60},{1,61},{2,62},{3,63},{4,40},{5,41},{6,42},{7,43},{8,36},{9,... | collective-permute-start | bytes 122888 | tf_op jit(solution)/shard_map/ppermute | solution.py:193
  110.3 2.7 %collective-permute-done.21 = bf16[32,640]{1,0:T(8,128)(2,1)S(1)} collective-permute-done((bf16[32,640]{1,0:T(8,128)(2,1)S(1)}, bf16[32,640]{1,0:T(8,128)(2,1)S(1)}, u32[]{:S(2)}, u32[]{:S(2)}) %collective-permute-start.21) | collective-permute-done | bytes 40992 | tf_op jit(solution)/shard_map/ppermute | solution.py:193
  113.0 3.4 %collective-permute-start.22 = (bf16[32,640]{1,0:T(8,128)(2,1)S(1)}, bf16[32,640]{1,0:T(8,128)(2,1)S(1)}, u32[]{:S(2)}, u32[]{:S(2)}) collective-permute-start(bf16[32,640]{1,0:T(8,128)(2,1)S(1)} %convert_element_type.167), channel_id=1, source_target_pairs={{0,44},{1,45},{2,46},{3,47},{4,56},{5,57},{6,58},{7,59},{8,52},{9,... | collective-permute-start | bytes 122888 | tf_op jit(solution)/shard_map/ppermute | solution.py:193
  116.4 2.0 %collective-permute-done.22 = bf16[32,640]{1,0:T(8,128)(2,1)S(1)} collective-permute-done((bf16[32,640]{1,0:T(8,128)(2,1)S(1)}, bf16[32,640]{1,0:T(8,128)(2,1)S(1)}, u32[]{:S(2)}, u32[]{:S(2)}) %collective-permute-start.22) | collective-permute-done | bytes 40992 | tf_op jit(solution)/shard_map/ppermute | solution.py:193
  119.8 2.7 %shard_map.82 = (f32[64,512]{1,0:T(8,128)S(1)}, f32[64,2048]{1,0:T(8,128)S(1)}, f32[32,640]{1,0:T(8,128)S(1)}, bf16[32,640]{1,0:T(8,128)(2,1)S(1)}) custom-call(s32[5]{0:T(128)S(1)} %stack.39.flags_ref.half_ref, f32[32,640]{1,0:T(8,128)S(1)} %convert_add_fusion.8.own_ref, f32[32,640]{1,0:T(8,128)S(1)} %collective-permute-done.23.got_ref, ...), custom_call_target="tpu_custom_call" | custom-call | tf_op jit(solution)/shard_map/pallas_call | solution.py:309
  124.0 3.5 %collective-permute-done.25 = bf16[32,640]{1,0:T(8,128)(2,1)S(1)} collective-permute-done((bf16[32,640]{1,0:T(8,128)(2,1)S(1)}, bf16[32,640]{1,0:T(8,128)(2,1)S(1)}, u32[]{:S(2)}, u32[]{:S(2)}) %collective-permute-start.25) | collective-permute-done | bytes 40992 | tf_op jit(solution)/shard_map/ppermute | solution.py:193
  127.5 2.4 %collective-permute-start.26 = (bf16[32,640]{1,0:T(8,128)(2,1)S(1)}, bf16[32,640]{1,0:T(8,128)(2,1)S(1)}, u32[]{:S(2)}, u32[]{:S(2)}) collective-permute-start(bf16[32,640]{1,0:T(8,128)(2,1)S(1)} %convert_element_type.172), channel_id=1, source_target_pairs={{0,35},{1,34},{2,33},{3,32},{4,39},{5,38},{6,37},{7,36},{8,43},{9,... | collective-permute-start | bytes 122888 | tf_op jit(solution)/shard_map/ppermute | solution.py:193
  129.9 2.6 %collective-permute-done.26 = bf16[32,640]{1,0:T(8,128)(2,1)S(1)} collective-permute-done((bf16[32,640]{1,0:T(8,128)(2,1)S(1)}, bf16[32,640]{1,0:T(8,128)(2,1)S(1)}, u32[]{:S(2)}, u32[]{:S(2)}) %collective-permute-start.26) | collective-permute-done | bytes 40992 | tf_op jit(solution)/shard_map/ppermute | solution.py:193
  132.7 3.5 %collective-permute-done.27 = bf16[32,640]{1,0:T(8,128)(2,1)S(1)} collective-permute-done((bf16[32,640]{1,0:T(8,128)(2,1)S(1)}, bf16[32,640]{1,0:T(8,128)(2,1)S(1)}, u32[]{:S(2)}, u32[]{:S(2)}) %collective-permute-start.27) | collective-permute-done | bytes 40992 | tf_op jit(solution)/shard_map/ppermute | solution.py:193
  136.2 1.6 collective-permute-start.28
  137.8 3.2 %collective-permute-done.28 = bf16[32,640]{1,0:T(8,128)(2,1)S(1)} collective-permute-done((bf16[32,640]{1,0:T(8,128)(2,1)S(1)}, bf16[32,640]{1,0:T(8,128)(2,1)S(1)}, u32[]{:S(2)}, u32[]{:S(2)}) %collective-permute-start.28) | collective-permute-done | bytes 40992 | tf_op jit(solution)/shard_map/ppermute | solution.py:193
  141.7 3.0 %collective-permute-done.29 = bf16[32,640]{1,0:T(8,128)(2,1)S(1)} collective-permute-done((bf16[32,640]{1,0:T(8,128)(2,1)S(1)}, bf16[32,640]{1,0:T(8,128)(2,1)S(1)}, u32[]{:S(2)}, u32[]{:S(2)}) %collective-permute-start.29) | collective-permute-done | bytes 40992 | tf_op jit(solution)/shard_map/ppermute | solution.py:193
  144.7 2.4 %collective-permute-start.30 = (bf16[32,640]{1,0:T(8,128)(2,1)S(1)}, bf16[32,640]{1,0:T(8,128)(2,1)S(1)}, u32[]{:S(2)}, u32[]{:S(2)}) collective-permute-start(bf16[32,640]{1,0:T(8,128)(2,1)S(1)} %convert_element_type.180), channel_id=1, source_target_pairs={{0,60},{1,61},{2,62},{3,63},{4,40},{5,41},{6,42},{7,43},{8,36},{9,... | collective-permute-start | bytes 122888 | tf_op jit(solution)/shard_map/ppermute | solution.py:193
  147.1 2.4 %collective-permute-done.30 = bf16[32,640]{1,0:T(8,128)(2,1)S(1)} collective-permute-done((bf16[32,640]{1,0:T(8,128)(2,1)S(1)}, bf16[32,640]{1,0:T(8,128)(2,1)S(1)}, u32[]{:S(2)}, u32[]{:S(2)}) %collective-permute-start.30) | collective-permute-done | bytes 40992 | tf_op jit(solution)/shard_map/ppermute | solution.py:193
  149.5 3.4 %collective-permute-start.31 = (bf16[32,640]{1,0:T(8,128)(2,1)S(1)}, bf16[32,640]{1,0:T(8,128)(2,1)S(1)}, u32[]{:S(2)}, u32[]{:S(2)}) collective-permute-start(bf16[32,640]{1,0:T(8,128)(2,1)S(1)} %convert_element_type.182), channel_id=1, source_target_pairs={{0,44},{1,45},{2,46},{3,47},{4,56},{5,57},{6,58},{7,59},{8,52},{9,... | collective-permute-start | bytes 122888 | tf_op jit(solution)/shard_map/ppermute | solution.py:193
  152.9 2.0 %collective-permute-done.31 = bf16[32,640]{1,0:T(8,128)(2,1)S(1)} collective-permute-done((bf16[32,640]{1,0:T(8,128)(2,1)S(1)}, bf16[32,640]{1,0:T(8,128)(2,1)S(1)}, u32[]{:S(2)}, u32[]{:S(2)}) %collective-permute-start.31) | collective-permute-done | bytes 40992 | tf_op jit(solution)/shard_map/ppermute | solution.py:193
  156.3 6.4 %shard_map.83 = bf16[2048,512]{1,0:T(8,128)(2,1)} custom-call(s32[5]{0:T(128)S(1)} %stack.39.flags_ref.half_ref, f32[32,640]{1,0:T(8,128)S(1)} %convert_add_fusion.own_ref, f32[32,640]{1,0:T(8,128)S(1)} %collective-permute-done.32.got_ref, f32[64,512]{1,0:T(8,128)S(1)} %get-tuple-element.47.basis_ref, bf16[2048,512]{1,0:T(8,128)(2,1)S(1)} %get-tuple-element.39.feature_ref, ...), custom_call_target="tpu_custom_call" | custom-call | tf_op jit(solution)/shard_map/pallas_call | solution.py:309
  (92 shorter events, 12.0 us)
Async XLA Ops:
  2.7 27.1 %collective-permute-start.2 = (bf16[10,64,256]{2,1,0:T(8,128)(2,1)}, bf16[10,64,256]{2,1,0:T(8,128)(2,1)S(1)}, u32[]{:S(2)}, u32[]{:S(2)}) collective-permute-start(bf16[10,64,256]{2,1,0:T(8,128)(2,1)} %get-tuple-element.32), channel_id=1, source_target_pairs={{0,1},{1,2},{2,3},{3,4},{4,5},{5,6},{6,7},{7,8},{8,9},{9,10},{10,1... | collective-permute-start | bytes 983048 | tf_op jit(solution)/shard_map/ppermute | solution.py:365
  4.7 20.2 %copy-start = (bf16[64,32,512]{2,1,0:T(8,128)(2,1)S(1)}, bf16[64,32,512]{2,1,0:T(8,128)(2,1)}, u32[]{:S(2)}) copy-start(bf16[64,32,512]{2,1,0:T(8,128)(2,1)} %band_ref.9) | copy-start | bytes 6291460
  4.7 20.2 %copy-start.2 = (f32[21,512]{1,0:T(8,128)S(1)}, f32[21,512]{1,0:T(8,128)}, u32[]{:S(2)}) copy-start(f32[21,512]{1,0:T(8,128)} %taps_ref.9) | copy-start | bytes 129028
  4.7 25.1 %collective-permute-start.3 = (bf16[10,64,256]{2,1,0:T(8,128)(2,1)}, bf16[10,64,256]{2,1,0:T(8,128)(2,1)S(1)}, u32[]{:S(2)}, u32[]{:S(2)}) collective-permute-start(bf16[10,64,256]{2,1,0:T(8,128)(2,1)} %get-tuple-element.33), channel_id=1, source_target_pairs={{0,31},{1,0},{2,1},{3,2},{4,3},{5,4},{6,5},{7,6},{8,7},{9,8},{10,9... | collective-permute-start | bytes 983048 | tf_op jit(solution)/shard_map/ppermute | solution.py:365
  20.0 12.5 %collective-permute-start = (bf16[10,64,256]{2,1,0:T(8,128)(2,1)}, bf16[10,64,256]{2,1,0:T(8,128)(2,1)S(1)}, u32[]{:S(2)}, u32[]{:S(2)}) collective-permute-start(bf16[10,64,256]{2,1,0:T(8,128)(2,1)} %get-tuple-element.29), channel_id=1, source_target_pairs={{0,1},{1,2},{2,3},{3,4},{4,5},{5,6},{6,7},{7,8},{8,9},{9,10},{10,1... | collective-permute-start | bytes 983048 | tf_op jit(solution)/shard_map/ppermute | solution.py:365
  20.0 12.5 %collective-permute-start.1 = (bf16[10,64,256]{2,1,0:T(8,128)(2,1)}, bf16[10,64,256]{2,1,0:T(8,128)(2,1)S(1)}, u32[]{:S(2)}, u32[]{:S(2)}) collective-permute-start(bf16[10,64,256]{2,1,0:T(8,128)(2,1)} %get-tuple-element.30), channel_id=1, source_target_pairs={{0,31},{1,0},{2,1},{3,2},{4,3},{5,4},{6,5},{7,6},{8,7},{9,8},{10,9... | collective-permute-start | bytes 983048 | tf_op jit(solution)/shard_map/ppermute | solution.py:365
  24.9 5.0 %copy-start.1 = (f32[32,64,256]{2,1,0:T(8,128)S(1)}, f32[32,64,256]{2,1,0:T(8,128)}, u32[]{:S(2)}) copy-start(f32[32,64,256]{2,1,0:T(8,128)} %get-tuple-element.31.own_ref) | copy-start | bytes 6291460
  32.5 5.5 %copy-start.7 = (f32[21,512]{1,0:T(8,128)S(1)}, f32[21,512]{1,0:T(8,128)}, u32[]{:S(2)}) copy-start(f32[21,512]{1,0:T(8,128)} %taps_ref.11) | copy-start | bytes 129028
  35.2 10.4 %collective-permute-start.5 = (bf16[10,32,512]{2,1,0:T(8,128)(2,1)S(1)}, bf16[10,32,512]{2,1,0:T(8,128)(2,1)S(1)}, u32[]{:S(2)}, u32[]{:S(2)}) collective-permute-start(bf16[10,32,512]{2,1,0:T(8,128)(2,1)S(1)} %get-tuple-element.49), channel_id=1, source_target_pairs={{0,224},{32,0},{64,32},{96,64},{128,96},{160,128},{192,160},{224,1... | collective-permute-start | bytes 983048 | tf_op jit(solution)/shard_map/ppermute | solution.py:397
  36.7 8.9 %copy-start.3 = (bf16[512,512]{1,0:T(8,128)(2,1)S(1)}, bf16[512,512]{1,0:T(8,128)(2,1)}, u32[]{:S(2)}) copy-start(bf16[512,512]{1,0:T(8,128)(2,1)} %w_ref.1) | copy-start | bytes 1572868
  36.7 8.9 %copy-start.6 = (f32[512,64]{0,1:T(8,128)S(1)}, f32[512,64]{0,1:T(8,128)}, u32[]{:S(2)}) copy-start(f32[512,64]{0,1:T(8,128)} %param.11) | copy-start | bytes 393220
  36.7 8.9 %collective-permute-start.4 = (bf16[10,32,512]{2,1,0:T(8,128)(2,1)S(1)}, bf16[10,32,512]{2,1,0:T(8,128)(2,1)S(1)}, u32[]{:S(2)}, u32[]{:S(2)}) collective-permute-start(bf16[10,32,512]{2,1,0:T(8,128)(2,1)S(1)} %get-tuple-element.50), channel_id=1, source_target_pairs={{0,32},{32,64},{64,96},{96,128},{128,160},{160,192},{192,224},{224... | collective-permute-start | bytes 983048 | tf_op jit(solution)/shard_map/ppermute | solution.py:396
  49.6 1.4 collective-permute-start.6
  51.0 3.6 %collective-permute-start.7 = (bf16[32,640]{1,0:T(8,128)(2,1)S(1)}, bf16[32,640]{1,0:T(8,128)(2,1)S(1)}, u32[]{:S(2)}, u32[]{:S(2)}) collective-permute-start(bf16[32,640]{1,0:T(8,128)(2,1)S(1)} %convert_element_type.140), channel_id=1, source_target_pairs={{0,33},{1,32},{2,35},{3,34},{4,37},{5,36},{6,39},{7,38},{8,41},{9,... | collective-permute-start | bytes 122888 | tf_op jit(solution)/shard_map/ppermute | solution.py:193
  54.7 5.0 %collective-permute-start.8 = (bf16[32,640]{1,0:T(8,128)(2,1)S(1)}, bf16[32,640]{1,0:T(8,128)(2,1)S(1)}, u32[]{:S(2)}, u32[]{:S(2)}) collective-permute-start(bf16[32,640]{1,0:T(8,128)(2,1)S(1)} %convert_element_type.142), channel_id=1, source_target_pairs={{0,35},{1,34},{2,33},{3,32},{4,39},{5,38},{6,37},{7,36},{8,43},{9,... | collective-permute-start | bytes 122888 | tf_op jit(solution)/shard_map/ppermute | solution.py:193
  59.7 3.6 %collective-permute-start.9 = (bf16[32,640]{1,0:T(8,128)(2,1)S(1)}, bf16[32,640]{1,0:T(8,128)(2,1)S(1)}, u32[]{:S(2)}, u32[]{:S(2)}) collective-permute-start(bf16[32,640]{1,0:T(8,128)(2,1)S(1)} %convert_element_type.144), channel_id=1, source_target_pairs={{0,96},{1,97},{2,98},{3,99},{4,100},{5,101},{6,102},{7,103},{8,104... | collective-permute-start | bytes 122888 | tf_op jit(solution)/shard_map/ppermute | solution.py:193
  63.3 4.8 %collective-permute-start.10 = (bf16[32,640]{1,0:T(8,128)(2,1)S(1)}, bf16[32,640]{1,0:T(8,128)(2,1)S(1)}, u32[]{:S(2)}, u32[]{:S(2)}) collective-permute-start(bf16[32,640]{1,0:T(8,128)(2,1)S(1)} %convert_element_type.146), channel_id=1, source_target_pairs={{0,224},{1,225},{2,226},{3,227},{4,228},{5,229},{6,230},{7,231},{8... | collective-permute-start | bytes 122888 | tf_op jit(solution)/shard_map/ppermute | solution.py:193
  68.2 3.6 %collective-permute-start.11 = (bf16[32,640]{1,0:T(8,128)(2,1)S(1)}, bf16[32,640]{1,0:T(8,128)(2,1)S(1)}, u32[]{:S(2)}, u32[]{:S(2)}) collective-permute-start(bf16[32,640]{1,0:T(8,128)(2,1)S(1)} %convert_element_type.148), channel_id=1, source_target_pairs={{0,36},{1,37},{2,38},{3,39},{4,32},{5,33},{6,34},{7,35},{8,44},{9,... | collective-permute-start | bytes 122888 | tf_op jit(solution)/shard_map/ppermute | solution.py:193
  71.8 4.8 %collective-permute-start.12 = (bf16[32,640]{1,0:T(8,128)(2,1)S(1)}, bf16[32,640]{1,0:T(8,128)(2,1)S(1)}, u32[]{:S(2)}, u32[]{:S(2)}) collective-permute-start(bf16[32,640]{1,0:T(8,128)(2,1)S(1)} %convert_element_type.150), channel_id=1, source_target_pairs={{0,60},{1,61},{2,62},{3,63},{4,40},{5,41},{6,42},{7,43},{8,36},{9,... | collective-permute-start | bytes 122888 | tf_op jit(solution)/shard_map/ppermute | solution.py:193
  76.7 5.4 %collective-permute-start.13 = (bf16[32,640]{1,0:T(8,128)(2,1)S(1)}, bf16[32,640]{1,0:T(8,128)(2,1)S(1)}, u32[]{:S(2)}, u32[]{:S(2)}) collective-permute-start(bf16[32,640]{1,0:T(8,128)(2,1)S(1)} %convert_element_type.152), channel_id=1, source_target_pairs={{0,44},{1,45},{2,46},{3,47},{4,56},{5,57},{6,58},{7,59},{8,52},{9,... | collective-permute-start | bytes 122888 | tf_op jit(solution)/shard_map/ppermute | solution.py:193
  82.1 1.4 collective-permute-start.14
  86.2 1.3 collective-permute-start.15
  87.5 3.6 %collective-permute-start.16 = (bf16[32,640]{1,0:T(8,128)(2,1)S(1)}, bf16[32,640]{1,0:T(8,128)(2,1)S(1)}, u32[]{:S(2)}, u32[]{:S(2)}) collective-permute-start(bf16[32,640]{1,0:T(8,128)(2,1)S(1)} %convert_element_type.155), channel_id=1, source_target_pairs={{0,33},{1,32},{2,35},{3,34},{4,37},{5,36},{6,39},{7,38},{8,41},{9,... | collective-permute-start | bytes 122888 | tf_op jit(solution)/shard_map/ppermute | solution.py:193
  91.2 4.8 %collective-permute-start.17 = (bf16[32,640]{1,0:T(8,128)(2,1)S(1)}, bf16[32,640]{1,0:T(8,128)(2,1)S(1)}, u32[]{:S(2)}, u32[]{:S(2)}) collective-permute-start(bf16[32,640]{1,0:T(8,128)(2,1)S(1)} %convert_element_type.157), channel_id=1, source_target_pairs={{0,35},{1,34},{2,33},{3,32},{4,39},{5,38},{6,37},{7,36},{8,43},{9,... | collective-permute-start | bytes 122888 | tf_op jit(solution)/shard_map/ppermute | solution.py:193
  96.0 3.6 %collective-permute-start.18 = (bf16[32,640]{1,0:T(8,128)(2,1)S(1)}, bf16[32,640]{1,0:T(8,128)(2,1)S(1)}, u32[]{:S(2)}, u32[]{:S(2)}) collective-permute-start(bf16[32,640]{1,0:T(8,128)(2,1)S(1)} %convert_element_type.159), channel_id=1, source_target_pairs={{0,96},{1,97},{2,98},{3,99},{4,100},{5,101},{6,102},{7,103},{8,104... | collective-permute-start | bytes 122888 | tf_op jit(solution)/shard_map/ppermute | solution.py:193
  99.7 4.8 %collective-permute-start.19 = (bf16[32,640]{1,0:T(8,128)(2,1)S(1)}, bf16[32,640]{1,0:T(8,128)(2,1)S(1)}, u32[]{:S(2)}, u32[]{:S(2)}) collective-permute-start(bf16[32,640]{1,0:T(8,128)(2,1)S(1)} %convert_element_type.161), channel_id=1, source_target_pairs={{0,224},{1,225},{2,226},{3,227},{4,228},{5,229},{6,230},{7,231},{8... | collective-permute-start | bytes 122888 | tf_op jit(solution)/shard_map/ppermute | solution.py:193
  104.5 3.6 %collective-permute-start.20 = (bf16[32,640]{1,0:T(8,128)(2,1)S(1)}, bf16[32,640]{1,0:T(8,128)(2,1)S(1)}, u32[]{:S(2)}, u32[]{:S(2)}) collective-permute-start(bf16[32,640]{1,0:T(8,128)(2,1)S(1)} %convert_element_type.163), channel_id=1, source_target_pairs={{0,36},{1,37},{2,38},{3,39},{4,32},{5,33},{6,34},{7,35},{8,44},{9,... | collective-permute-start | bytes 122888 | tf_op jit(solution)/shard_map/ppermute | solution.py:193
  108.1 4.8 %collective-permute-start.21 = (bf16[32,640]{1,0:T(8,128)(2,1)S(1)}, bf16[32,640]{1,0:T(8,128)(2,1)S(1)}, u32[]{:S(2)}, u32[]{:S(2)}) collective-permute-start(bf16[32,640]{1,0:T(8,128)(2,1)S(1)} %convert_element_type.165), channel_id=1, source_target_pairs={{0,60},{1,61},{2,62},{3,63},{4,40},{5,41},{6,42},{7,43},{8,36},{9,... | collective-permute-start | bytes 122888 | tf_op jit(solution)/shard_map/ppermute | solution.py:193
  113.0 5.4 %collective-permute-start.22 = (bf16[32,640]{1,0:T(8,128)(2,1)S(1)}, bf16[32,640]{1,0:T(8,128)(2,1)S(1)}, u32[]{:S(2)}, u32[]{:S(2)}) collective-permute-start(bf16[32,640]{1,0:T(8,128)(2,1)S(1)} %convert_element_type.167), channel_id=1, source_target_pairs={{0,44},{1,45},{2,46},{3,47},{4,56},{5,57},{6,58},{7,59},{8,52},{9,... | collective-permute-start | bytes 122888 | tf_op jit(solution)/shard_map/ppermute | solution.py:193
  118.4 1.4 collective-permute-start.23
  119.8 36.5 %copy-start.4 = (bf16[512,512]{1,0:T(8,128)(2,1)S(1)}, bf16[512,512]{1,0:T(8,128)(2,1)}, u32[]{:S(2)}) copy-start(bf16[512,512]{1,0:T(8,128)(2,1)} %wham_ref.1) | copy-start | bytes 1572868
  119.8 36.5 %copy-start.5 = (bf16[512,512]{1,0:T(8,128)(2,1)S(1)}, bf16[512,512]{1,0:T(8,128)(2,1)}, u32[]{:S(2)}) copy-start(bf16[512,512]{1,0:T(8,128)(2,1)} %walign_ref.1) | copy-start | bytes 1572868
  122.5 1.3 collective-permute-start.24
  123.9 3.6 %collective-permute-start.25 = (bf16[32,640]{1,0:T(8,128)(2,1)S(1)}, bf16[32,640]{1,0:T(8,128)(2,1)S(1)}, u32[]{:S(2)}, u32[]{:S(2)}) collective-permute-start(bf16[32,640]{1,0:T(8,128)(2,1)S(1)} %convert_element_type.170), channel_id=1, source_target_pairs={{0,33},{1,32},{2,35},{3,34},{4,37},{5,36},{6,39},{7,38},{8,41},{9,... | collective-permute-start | bytes 122888 | tf_op jit(solution)/shard_map/ppermute | solution.py:193
  127.5 5.0 %collective-permute-start.26 = (bf16[32,640]{1,0:T(8,128)(2,1)S(1)}, bf16[32,640]{1,0:T(8,128)(2,1)S(1)}, u32[]{:S(2)}, u32[]{:S(2)}) collective-permute-start(bf16[32,640]{1,0:T(8,128)(2,1)S(1)} %convert_element_type.172), channel_id=1, source_target_pairs={{0,35},{1,34},{2,33},{3,32},{4,39},{5,38},{6,37},{7,36},{8,43},{9,... | collective-permute-start | bytes 122888 | tf_op jit(solution)/shard_map/ppermute | solution.py:193
  132.6 3.6 %collective-permute-start.27 = (bf16[32,640]{1,0:T(8,128)(2,1)S(1)}, bf16[32,640]{1,0:T(8,128)(2,1)S(1)}, u32[]{:S(2)}, u32[]{:S(2)}) collective-permute-start(bf16[32,640]{1,0:T(8,128)(2,1)S(1)} %convert_element_type.174), channel_id=1, source_target_pairs={{0,96},{1,97},{2,98},{3,99},{4,100},{5,101},{6,102},{7,103},{8,104... | collective-permute-start | bytes 122888 | tf_op jit(solution)/shard_map/ppermute | solution.py:193
  136.2 4.8 %collective-permute-start.28 = (bf16[32,640]{1,0:T(8,128)(2,1)S(1)}, bf16[32,640]{1,0:T(8,128)(2,1)S(1)}, u32[]{:S(2)}, u32[]{:S(2)}) collective-permute-start(bf16[32,640]{1,0:T(8,128)(2,1)S(1)} %convert_element_type.176), channel_id=1, source_target_pairs={{0,224},{1,225},{2,226},{3,227},{4,228},{5,229},{6,230},{7,231},{8... | collective-permute-start | bytes 122888 | tf_op jit(solution)/shard_map/ppermute | solution.py:193
  141.0 3.6 %collective-permute-start.29 = (bf16[32,640]{1,0:T(8,128)(2,1)S(1)}, bf16[32,640]{1,0:T(8,128)(2,1)S(1)}, u32[]{:S(2)}, u32[]{:S(2)}) collective-permute-start(bf16[32,640]{1,0:T(8,128)(2,1)S(1)} %convert_element_type.178), channel_id=1, source_target_pairs={{0,36},{1,37},{2,38},{3,39},{4,32},{5,33},{6,34},{7,35},{8,44},{9,... | collective-permute-start | bytes 122888 | tf_op jit(solution)/shard_map/ppermute | solution.py:193
  144.7 4.8 %collective-permute-start.30 = (bf16[32,640]{1,0:T(8,128)(2,1)S(1)}, bf16[32,640]{1,0:T(8,128)(2,1)S(1)}, u32[]{:S(2)}, u32[]{:S(2)}) collective-permute-start(bf16[32,640]{1,0:T(8,128)(2,1)S(1)} %convert_element_type.180), channel_id=1, source_target_pairs={{0,60},{1,61},{2,62},{3,63},{4,40},{5,41},{6,42},{7,43},{8,36},{9,... | collective-permute-start | bytes 122888 | tf_op jit(solution)/shard_map/ppermute | solution.py:193
  149.5 5.4 %collective-permute-start.31 = (bf16[32,640]{1,0:T(8,128)(2,1)S(1)}, bf16[32,640]{1,0:T(8,128)(2,1)S(1)}, u32[]{:S(2)}, u32[]{:S(2)}) collective-permute-start(bf16[32,640]{1,0:T(8,128)(2,1)S(1)} %convert_element_type.182), channel_id=1, source_target_pairs={{0,44},{1,45},{2,46},{3,47},{4,56},{5,57},{6,58},{7,59},{8,52},{9,... | collective-permute-start | bytes 122888 | tf_op jit(solution)/shard_map/ppermute | solution.py:193
  154.9 1.4 collective-permute-start.32

commit v7 on v6

--- a/solution.py
+++ b/solution.py
@@ -20,6 +20,7 @@
 MARGIN = TAPS // 2
 LANES = 128
 PARTS = 2
+HEAD_BLOCKS = 4
 
 
 def weighted(taps_ref, items, rows):
@@ -47,8 +48,7 @@
             emit(start + i, value)
 
 
-def pack_kernel(band_ref, *refs):
-    first_ref, last_ref, flat = refs[-3:]
+def pack_kernel(band_ref, first_ref, last_ref, flat):
     h, w, lanes = band_ref.shape
     flat[...] = band_ref[...].astype(F32).reshape(h * w, lanes)
     for j in range(MARGIN):
@@ -56,9 +56,8 @@
         last_ref[j] = flat[pl.ds(w - MARGIN + j, h, stride=w), :].astype(BF)
 
 
-def columns_own_kernel(band_ref, taps_ref, out_ref, token_ref, flat, turned):
+def columns_own_kernel(band_ref, taps_ref, out_ref, flat, turned):
     h, w, lanes = band_ref.shape
-    token_ref[...] = jnp.zeros_like(token_ref)
     flat[...] = band_ref[...].astype(F32).reshape(h * w, lanes)
     for j in range(w):
         turned[j] = flat[pl.ds(j, h, stride=w), :]
@@ -292,9 +291,13 @@
 
 
 def last_kernel(
-    half_ref, own_ref, got_ref, basis_ref, feature_ref, coeffs_ref, wham_ref, walign_ref, out_ref
+    half_ref, own_ref, got_ref, basis_ref, feature_ref, coeffs_ref, wham_ref, walign_ref, out_ref, now
 ):
-    basis = updated_basis(half_ref, own_ref, got_ref, basis_ref[...])
+    @pl.when(pl.program_id(0) == 0)
+    def _():
+        now[...] = updated_basis(half_ref, own_ref, got_ref, basis_ref[...])
+
+    basis = now[...]
     feature = feature_ref[...]
     low = basis.astype(BF)
     coeffs = coeffs_of(basis, coeffs_ref[...], dot(low, feature, NT))
@@ -348,34 +351,32 @@
         return pl.CostEstimate(flops=2 * taps * pixels, bytes_accessed=moved * pixels, transcendentals=0)
 
     whole = pl.BlockSpec(memory_space=pl.ANY)
-    sides, owns, tokens = [], [], []
+    sides = []
     for i in range(PARTS):
         start = i * blocks_in_part
         first, last = pl.pallas_call(
             pack_kernel,
             grid=grid,
-            in_specs=[blocks(tile_rows, tile_cols, start=start)] + [whole] * i,
+            in_specs=[blocks(tile_rows, tile_cols, start=start)],
             out_specs=[side, side],
             out_shape=[sds((margin, tile_rows, width), BF)] * 2,
             scratch_shapes=[flat],
-            compiler_params=wide,
+            compiler_params=wide if i == 0 else params,
             cost_estimate=cost(1, 3),
-        )(band_input, *tokens)
+        )(band_input)
         sides.append(
             (lax.ppermute(last, COLS, ring(Z * X, 1)), lax.ppermute(first, COLS, ring(Z * X, -1)))
         )
-        own, token = pl.pallas_call(
-            columns_own_kernel,
-            grid=grid,
-            in_specs=[blocks(tile_rows, tile_cols, start=start), blocks(TAPS, start=start)],
-            out_specs=[turned, pl.BlockSpec((8, LANES), lambda i: (0, 0))],
-            out_shape=[sds((tile_cols, tile_rows, width), F32), sds((8, LANES), F32)],
-            scratch_shapes=[flat, pltpu.VMEM((tile_cols, tile_rows, LANES), F32)],
-            compiler_params=params if i else wide,
-            cost_estimate=cost(TAPS, 6),
-        )(band_input, column_taps)
-        owns.append(own)
-        tokens.append(token)
+    own = pl.pallas_call(
+        columns_own_kernel,
+        grid=(channels // LANES,),
+        in_specs=[tile, blocks(TAPS)],
+        out_specs=turned,
+        out_shape=sds((tile_cols, tile_rows, channels), F32),
+        scratch_shapes=[flat, pltpu.VMEM((tile_cols, tile_rows, LANES), F32)],
+        compiler_params=params,
+        cost_estimate=cost(2 * TAPS, 12),
+    )(band_input, column_taps)
     filtered = []
     for i in range(PARTS):
         start = i * blocks_in_part
@@ -383,14 +384,14 @@
             pl.pallas_call(
                 columns_rest_kernel,
                 grid=grid,
-                in_specs=[scalar, turned, side, side, blocks(TAPS, start=start)] + [whole] * len(filtered),
+                in_specs=[scalar, blocks(tile_cols, tile_rows, start=start), side, side, blocks(TAPS, start=start)] + [whole] * len(filtered),
                 out_specs=blocks(tile_rows, tile_cols, start=start),
                 out_shape=sds((tile_rows, tile_cols, channels), BF),
                 scratch_shapes=[pltpu.VMEM((margin, tile_rows, LANES), F32)] * 2 + [flat],
                 input_output_aliases={5: 0} if filtered else {},
                 compiler_params=params,
                 cost_estimate=cost(TAPS // 2, 6),
-            )(flags, owns[i], *sides[i], column_taps, *filtered)
+            )(flags, own, *sides[i], column_taps, *filtered)
         ]
     filtered = filtered[0]
     above = lax.ppermute(filtered[tile_rows - margin :], ROWS, ring(Y * CORE, 1))
@@ -430,11 +431,19 @@
             flags, own, got, basis, feature, coeffs,
         )
     own, got = summed_over_all(mine, theirs)
-    head_out = call(
+    vmem = pl.BlockSpec(memory_space=pltpu.VMEM)
+    pixel_block = n // HEAD_BLOCKS
+    pixels_by_channel = pl.BlockSpec((pixel_block, channels), lambda i: (i, 0))
+    head_out = pl.pallas_call(
         last_kernel,
-        sds((n, channels), BF),
-        flags, own, got, basis, feature, coeffs, w_ham, w_align,
-    )
+        grid=(HEAD_BLOCKS,),
+        in_specs=[scalar, vmem, vmem, vmem, pixels_by_channel]
+        + [pl.BlockSpec((r, pixel_block), lambda i: (0, i)), vmem, vmem],
+        out_specs=pixels_by_channel,
+        out_shape=sds((n, channels), BF),
+        scratch_shapes=[pltpu.VMEM((r, channels), F32)],
+        compiler_params=pltpu.CompilerParams(vmem_limit_bytes=24 * 2**20),
+    )(flags, own, got, basis, feature, coeffs, w_ham, w_align)
     return head_out.reshape(tile_rows, tile_cols, channels)
 
 

time: 163 us -> 163 us (level)
  waiting for transfers between devices: 66.6 us -> 82 us
  starting transfers between devices: 50.1 us -> 36.5 us
    ppermute x21, waiting for transfers between devices: 61.1 us -> 76.6 us  [summed_over_all(): got = lax.ppermute(total.astype(BF), ALL, round_pairs(axis, rule))]
    ppermute x21, starting transfers between devices: 31.2 us -> 17.6 us  [summed_over_all(): got = lax.ppermute(total.astype(BF), ALL, round_pairs(axis, rule))]
    pallas_call x4 -> x3, Pallas kernels: 15.8 us -> 9.43 us  [call(): pl.pallas_call(kernel, out_shape=outs, in_specs=specs, out_specs=jax.tree...]
    pallas_call x4, Pallas kernels: 16.2 us -> 21.8 us  [the longest x1 8.91 us: on_device(): pl.pallas_call(columns_own_kernel, grid=(channels // LANES,), in_specs=[t...]
  transfers between devices with their start and end apart: 33 -> 33, of which waited for: 27 -> 27; matrix products, arithmetic and copies ran while one was open for 0% -> 0% of each run, Pallas kernels for 15% -> 13%
where the time goes in v7:
time: 163 us
  waiting for transfers between devices  82 us (50%)
  Pallas kernels  43.5 us (27%)
  starting transfers between devices  36.5 us (22%)
    ppermute x21, waiting for transfers between devices, summed_over_all(): got = lax.ppermute(total.astype(BF), ALL, round_pairs(axis, rule))  76.6 us
    ppermute x21, starting transfers between devices, summed_over_all(): got = lax.ppermute(total.astype(BF), ALL, round_pairs(axis, rule))  17.6 us
    ppermute x2, starting transfers between devices, on_device(): lax.ppermute(first, COLS, ring(Z * X, -1))  11.3 us
    pallas_call x3, Pallas kernels, call(): pl.pallas_call(kernel, out_shape=outs, in_specs=specs, out_specs=jax.tree...  9.43 us
    pallas_call x1, Pallas kernels, on_device(): pl.pallas_call(columns_own_kernel, grid=(channels // LANES,), in_specs=[t...  8.91 us
    pallas_call x1, Pallas kernels, on_device(): pl.pallas_call(rows_own_kernel, grid=(channels // LANES,), in_specs=[tile...  7.67 us
    pallas_call x1, Pallas kernels, on_device(): pl.pallas_call(last_kernel, grid=(HEAD_BLOCKS,), in_specs=[scalar, vmem,...  7.46 us
    pallas_call x2, Pallas kernels, on_device(): pl.pallas_call(columns_rest_kernel, grid=grid, in_specs=[scalar, blocks(t...  5.41 us
  transfers between devices with their start and end apart: 33, of which 27 were waited for; matrix products, arithmetic and copies ran while one was open for 0% of the time, Pallas kernels for 13%

profile of v7, /device:TPU:1, one launch (start us, length us, event | category | flops | bytes accessed | tf_op | source)
XLA Modules:
  0.0 163.0 jit_solution(1212421980731913845)
XLA Ops:
  0.0 2.8 %shard_map.75 = (bf16[10,64,256]{2,1,0:T(8,128)(2,1)}, bf16[10,64,256]{2,1,0:T(8,128)(2,1)}) custom-call(bf16[64,32,512]{2,1,0:T(8,128)(2,1)} %band_ref.7), custom_call_target="tpu_custom_call" | custom-call | flops 1048576 | bytes 1572864 | tf_op jit(solution)/shard_map/pallas_call | solution.py:357
  2.8 2.0 %collective-permute-start.2 = (bf16[10,64,256]{2,1,0:T(8,128)(2,1)}, bf16[10,64,256]{2,1,0:T(8,128)(2,1)S(1)}, u32[]{:S(2)}, u32[]{:S(2)}) collective-permute-start(bf16[10,64,256]{2,1,0:T(8,128)(2,1)} %get-tuple-element.26), channel_id=1, source_target_pairs={{0,1},{1,2},{2,3},{3,4},{4,5},{5,6},{6,7},{7,8},{8,9},{9,10},{10,1... | collective-permute-start | bytes 983048 | tf_op jit(solution)/shard_map/ppermute | solution.py:368
  4.8 6.6 %collective-permute-start.3 = (bf16[10,64,256]{2,1,0:T(8,128)(2,1)}, bf16[10,64,256]{2,1,0:T(8,128)(2,1)S(1)}, u32[]{:S(2)}, u32[]{:S(2)}) collective-permute-start(bf16[10,64,256]{2,1,0:T(8,128)(2,1)} %get-tuple-element.27), channel_id=1, source_target_pairs={{0,31},{1,0},{2,1},{3,2},{4,3},{5,4},{6,5},{7,6},{8,7},{9,8},{10,9... | collective-permute-start | bytes 983048 | tf_op jit(solution)/shard_map/ppermute | solution.py:368
  11.4 1.8 %shard_map.74 = (bf16[10,64,256]{2,1,0:T(8,128)(2,1)}, bf16[10,64,256]{2,1,0:T(8,128)(2,1)}) custom-call(bf16[64,32,512]{2,1,0:T(8,128)(2,1)S(1)} %copy-done), custom_call_target="tpu_custom_call" | custom-call | flops 1048576 | bytes 1572864 | tf_op jit(solution)/shard_map/pallas_call | solution.py:357
  13.2 4.8 %collective-permute-start.1 = (bf16[10,64,256]{2,1,0:T(8,128)(2,1)}, bf16[10,64,256]{2,1,0:T(8,128)(2,1)S(1)}, u32[]{:S(2)}, u32[]{:S(2)}) collective-permute-start(bf16[10,64,256]{2,1,0:T(8,128)(2,1)} %get-tuple-element.25), channel_id=1, source_target_pairs={{0,31},{1,0},{2,1},{3,2},{4,3},{5,4},{6,5},{7,6},{8,7},{9,8},{10,9... | collective-permute-start | bytes 983048 | tf_op jit(solution)/shard_map/ppermute | solution.py:368
  18.1 8.9 %shard_map.73.own_ref = f32[32,64,512]{2,1,0:T(8,128)S(1)} custom-call(bf16[64,32,512]{2,1,0:T(8,128)(2,1)S(1)} %copy-done, f32[21,512]{1,0:T(8,128)S(1)} %copy-done.5), custom_call_target="tpu_custom_call" | custom-call | flops 44040192 | bytes 6291456 | tf_op jit(solution)/shard_map/pallas_call | solution.py:370
  27.0 2.7 %shard_map.76.refs_0_ = bf16[64,32,512]{2,1,0:T(8,128)(2,1)S(1)} custom-call(s32[5]{0:T(128)S(1)} %stack.39.flags_ref.half_ref, f32[32,64,512]{2,1,0:T(8,128)S(1)} %shard_map.73.own_ref, bf16[10,64,256]{2,1,0:T(8,128)(2,1)S(1)} %collective-permute-done.2.left_ref, bf16[10,64,256]{2,1,0:T(8,128)(2,1)S(1)} %collective-permute-done.3.right_ref, ...), custom_call_target="tpu_custom_call" | custom-call | flops 10485760 | bytes 3145728 | tf_op jit(solution)/shard_map/pallas_call | solution.py:384
  29.8 2.7 %shard_map.77.filtered_ref = bf16[64,32,512]{2,1,0:T(8,128)(2,1)S(1)} custom-call(s32[5]{0:T(128)S(1)} %stack.39.flags_ref.half_ref, f32[32,64,512]{2,1,0:T(8,128)S(1)} %shard_map.73.own_ref, bf16[10,64,256]{2,1,0:T(8,128)(2,1)S(1)} %collective-permute-done.left_ref, ...), custom_call_target="tpu_custom_call", output_to_operand_aliasing={{}: (5, {})} | custom-call | flops 10485760 | bytes 3145728 | tf_op jit(solution)/shard_map/pallas_call | solution.py:384
  32.5 1.5 collective-permute-start.5
  34.1 1.2 collective-permute-start.4
  35.3 7.7 %shard_map.78 = (bf16[44,32,512]{2,1,0:T(8,128)(2,1)S(1)}, f32[10,32,512]{2,1,0:T(8,128)S(1)}, f32[10,32,512]{2,1,0:T(8,128)S(1)}) custom-call(bf16[64,32,512]{2,1,0:T(8,128)(2,1)S(1)} %shard_map.77.filtered_ref, bf16[64,32,512]{2,1,0:T(8,128)(2,1)S(1)} %copy-done, f32[21,512]{1,0:T(8,128)S(1)} %copy-done.6), custom_call_target="tpu_custom_call" | custom-call | flops 44040192 | bytes 6291456 | tf_op jit(solution)/shard_map/pallas_call | solution.py:399
  43.0 3.9 %shard_map.79 = (bf16[2048,512]{1,0:T(8,128)(2,1)S(1)}, f32[64,2048]{1,0:T(8,128)S(1)}, f32[32,640]{1,0:T(8,128)S(1)}, bf16[32,640]{1,0:T(8,128)(2,1)S(1)}) custom-call(s32[5]{0:T(128)S(1)} %stack.39.flags_ref.half_ref, bf16[44,32,512]{2,1,0:T(8,128)(2,1)S(1)} %get-tuple-element.28.mid_ref, f32[10,32,512]{2,1,0:T(8,128)S(1)} %get-tuple-element.29.top_ref, ...), custom_call_target="tpu_custom_call" | custom-call | tf_op jit(solution)/shard_map/pallas_call | solution.py:312
  47.4 0.9 collective-permute-done.6
  48.4 3.5 %collective-permute-done.7 = bf16[32,640]{1,0:T(8,128)(2,1)S(1)} collective-permute-done((bf16[32,640]{1,0:T(8,128)(2,1)S(1)}, bf16[32,640]{1,0:T(8,128)(2,1)S(1)}, u32[]{:S(2)}, u32[]{:S(2)}) %collective-permute-start.7) | collective-permute-done | bytes 40992 | tf_op jit(solution)/shard_map/ppermute | solution.py:192
  52.1 4.7 %collective-permute-done.8 = bf16[32,640]{1,0:T(8,128)(2,1)S(1)} collective-permute-done((bf16[32,640]{1,0:T(8,128)(2,1)S(1)}, bf16[32,640]{1,0:T(8,128)(2,1)S(1)}, u32[]{:S(2)}, u32[]{:S(2)}) %collective-permute-start.8) | collective-permute-done | bytes 40992 | tf_op jit(solution)/shard_map/ppermute | solution.py:192
  56.8 1.4 collective-permute-start.9
  58.2 2.4 %collective-permute-done.9 = bf16[32,640]{1,0:T(8,128)(2,1)S(1)} collective-permute-done((bf16[32,640]{1,0:T(8,128)(2,1)S(1)}, bf16[32,640]{1,0:T(8,128)(2,1)S(1)}, u32[]{:S(2)}, u32[]{:S(2)}) %collective-permute-start.9) | collective-permute-done | bytes 40992 | tf_op jit(solution)/shard_map/ppermute | solution.py:192
  60.7 2.7 %collective-permute-start.10 = (bf16[32,640]{1,0:T(8,128)(2,1)S(1)}, bf16[32,640]{1,0:T(8,128)(2,1)S(1)}, u32[]{:S(2)}, u32[]{:S(2)}) collective-permute-start(bf16[32,640]{1,0:T(8,128)(2,1)S(1)} %convert_element_type.146), channel_id=1, source_target_pairs={{0,224},{1,225},{2,226},{3,227},{4,228},{5,229},{6,230},{7,231},{8... | collective-permute-start | bytes 122888 | tf_op jit(solution)/shard_map/ppermute | solution.py:192
  63.4 2.1 %collective-permute-done.10 = bf16[32,640]{1,0:T(8,128)(2,1)S(1)} collective-permute-done((bf16[32,640]{1,0:T(8,128)(2,1)S(1)}, bf16[32,640]{1,0:T(8,128)(2,1)S(1)}, u32[]{:S(2)}, u32[]{:S(2)}) %collective-permute-start.10) | collective-permute-done | bytes 40992 | tf_op jit(solution)/shard_map/ppermute | solution.py:192
  65.6 3.5 %collective-permute-done.11 = bf16[32,640]{1,0:T(8,128)(2,1)S(1)} collective-permute-done((bf16[32,640]{1,0:T(8,128)(2,1)S(1)}, bf16[32,640]{1,0:T(8,128)(2,1)S(1)}, u32[]{:S(2)}, u32[]{:S(2)}) %collective-permute-start.11) | collective-permute-done | bytes 40992 | tf_op jit(solution)/shard_map/ppermute | solution.py:192
  69.2 4.7 %collective-permute-done.12 = bf16[32,640]{1,0:T(8,128)(2,1)S(1)} collective-permute-done((bf16[32,640]{1,0:T(8,128)(2,1)S(1)}, bf16[32,640]{1,0:T(8,128)(2,1)S(1)}, u32[]{:S(2)}, u32[]{:S(2)}) %collective-permute-start.12) | collective-permute-done | bytes 40992 | tf_op jit(solution)/shard_map/ppermute | solution.py:192
  74.0 1.4 collective-permute-start.13
  75.4 4.0 %collective-permute-done.13 = bf16[32,640]{1,0:T(8,128)(2,1)S(1)} collective-permute-done((bf16[32,640]{1,0:T(8,128)(2,1)S(1)}, bf16[32,640]{1,0:T(8,128)(2,1)S(1)}, u32[]{:S(2)}, u32[]{:S(2)}) %collective-permute-start.13) | collective-permute-done | bytes 40992 | tf_op jit(solution)/shard_map/ppermute | solution.py:192
  79.8 0.9 collective-permute-done.14.got_ref
  80.8 2.7 %shard_map.80 = (f32[64,512]{1,0:T(8,128)S(1)}, f32[64,2048]{1,0:T(8,128)S(1)}, f32[32,640]{1,0:T(8,128)S(1)}, bf16[32,640]{1,0:T(8,128)(2,1)S(1)}) custom-call(s32[5]{0:T(128)S(1)} %stack.39.flags_ref.half_ref, f32[32,640]{1,0:T(8,128)S(1)} %convert_add_fusion.16.own_ref, f32[32,640]{1,0:T(8,128)S(1)} %collective-permute-done.14.got_ref, ...), custom_call_target="tpu_custom_call" | custom-call | tf_op jit(solution)/shard_map/pallas_call | solution.py:312
  83.9 0.9 collective-permute-done.15
  85.0 3.5 %collective-permute-done.16 = bf16[32,640]{1,0:T(8,128)(2,1)S(1)} collective-permute-done((bf16[32,640]{1,0:T(8,128)(2,1)S(1)}, bf16[32,640]{1,0:T(8,128)(2,1)S(1)}, u32[]{:S(2)}, u32[]{:S(2)}) %collective-permute-start.16) | collective-permute-done | bytes 40992 | tf_op jit(solution)/shard_map/ppermute | solution.py:192
  88.6 4.7 %collective-permute-done.17 = bf16[32,640]{1,0:T(8,128)(2,1)S(1)} collective-permute-done((bf16[32,640]{1,0:T(8,128)(2,1)S(1)}, bf16[32,640]{1,0:T(8,128)(2,1)S(1)}, u32[]{:S(2)}, u32[]{:S(2)}) %collective-permute-start.17) | collective-permute-done | bytes 40992 | tf_op jit(solution)/shard_map/ppermute | solution.py:192
  93.4 3.5 %collective-permute-done.18 = bf16[32,640]{1,0:T(8,128)(2,1)S(1)} collective-permute-done((bf16[32,640]{1,0:T(8,128)(2,1)S(1)}, bf16[32,640]{1,0:T(8,128)(2,1)S(1)}, u32[]{:S(2)}, u32[]{:S(2)}) %collective-permute-start.18) | collective-permute-done | bytes 40992 | tf_op jit(solution)/shard_map/ppermute | solution.py:192
  97.0 2.7 %collective-permute-start.19 = (bf16[32,640]{1,0:T(8,128)(2,1)S(1)}, bf16[32,640]{1,0:T(8,128)(2,1)S(1)}, u32[]{:S(2)}, u32[]{:S(2)}) collective-permute-start(bf16[32,640]{1,0:T(8,128)(2,1)S(1)} %convert_element_type.161), channel_id=1, source_target_pairs={{0,224},{1,225},{2,226},{3,227},{4,228},{5,229},{6,230},{7,231},{8... | collective-permute-start | bytes 122888 | tf_op jit(solution)/shard_map/ppermute | solution.py:192
  99.7 2.1 %collective-permute-done.19 = bf16[32,640]{1,0:T(8,128)(2,1)S(1)} collective-permute-done((bf16[32,640]{1,0:T(8,128)(2,1)S(1)}, bf16[32,640]{1,0:T(8,128)(2,1)S(1)}, u32[]{:S(2)}, u32[]{:S(2)}) %collective-permute-start.19) | collective-permute-done | bytes 40992 | tf_op jit(solution)/shard_map/ppermute | solution.py:192
  101.9 3.5 %collective-permute-done.20 = bf16[32,640]{1,0:T(8,128)(2,1)S(1)} collective-permute-done((bf16[32,640]{1,0:T(8,128)(2,1)S(1)}, bf16[32,640]{1,0:T(8,128)(2,1)S(1)}, u32[]{:S(2)}, u32[]{:S(2)}) %collective-permute-start.20) | collective-permute-done | bytes 40992 | tf_op jit(solution)/shard_map/ppermute | solution.py:192
  106.1 4.1 %collective-permute-done.21 = bf16[32,640]{1,0:T(8,128)(2,1)S(1)} collective-permute-done((bf16[32,640]{1,0:T(8,128)(2,1)S(1)}, bf16[32,640]{1,0:T(8,128)(2,1)S(1)}, u32[]{:S(2)}, u32[]{:S(2)}) %collective-permute-start.21) | collective-permute-done | bytes 40992 | tf_op jit(solution)/shard_map/ppermute | solution.py:192
  110.3 2.3 %collective-permute-start.22 = (bf16[32,640]{1,0:T(8,128)(2,1)S(1)}, bf16[32,640]{1,0:T(8,128)(2,1)S(1)}, u32[]{:S(2)}, u32[]{:S(2)}) collective-permute-start(bf16[32,640]{1,0:T(8,128)(2,1)S(1)} %convert_element_type.167), channel_id=1, source_target_pairs={{0,44},{1,45},{2,46},{3,47},{4,56},{5,57},{6,58},{7,59},{8,52},{9,... | collective-permute-start | bytes 122888 | tf_op jit(solution)/shard_map/ppermute | solution.py:192
  112.6 4.1 %collective-permute-done.22 = bf16[32,640]{1,0:T(8,128)(2,1)S(1)} collective-permute-done((bf16[32,640]{1,0:T(8,128)(2,1)S(1)}, bf16[32,640]{1,0:T(8,128)(2,1)S(1)}, u32[]{:S(2)}, u32[]{:S(2)}) %collective-permute-start.22) | collective-permute-done | bytes 40992 | tf_op jit(solution)/shard_map/ppermute | solution.py:192
  117.1 0.9 collective-permute-done.23.got_ref
  118.1 2.7 %shard_map.81 = (f32[64,512]{1,0:T(8,128)S(1)}, f32[64,2048]{1,0:T(8,128)S(1)}, f32[32,640]{1,0:T(8,128)S(1)}, bf16[32,640]{1,0:T(8,128)(2,1)S(1)}) custom-call(s32[5]{0:T(128)S(1)} %stack.39.flags_ref.half_ref, f32[32,640]{1,0:T(8,128)S(1)} %convert_add_fusion.8.own_ref, f32[32,640]{1,0:T(8,128)S(1)} %collective-permute-done.23.got_ref, ...), custom_call_target="tpu_custom_call" | custom-call | tf_op jit(solution)/shard_map/pallas_call | solution.py:312
  122.3 3.5 %collective-permute-done.25 = bf16[32,640]{1,0:T(8,128)(2,1)S(1)} collective-permute-done((bf16[32,640]{1,0:T(8,128)(2,1)S(1)}, bf16[32,640]{1,0:T(8,128)(2,1)S(1)}, u32[]{:S(2)}, u32[]{:S(2)}) %collective-permute-start.25) | collective-permute-done | bytes 40992 | tf_op jit(solution)/shard_map/ppermute | solution.py:192
  126.3 4.3 %collective-permute-done.26 = bf16[32,640]{1,0:T(8,128)(2,1)S(1)} collective-permute-done((bf16[32,640]{1,0:T(8,128)(2,1)S(1)}, bf16[32,640]{1,0:T(8,128)(2,1)S(1)}, u32[]{:S(2)}, u32[]{:S(2)}) %collective-permute-start.26) | collective-permute-done | bytes 40992 | tf_op jit(solution)/shard_map/ppermute | solution.py:192
  131.0 3.5 %collective-permute-done.27 = bf16[32,640]{1,0:T(8,128)(2,1)S(1)} collective-permute-done((bf16[32,640]{1,0:T(8,128)(2,1)S(1)}, bf16[32,640]{1,0:T(8,128)(2,1)S(1)}, u32[]{:S(2)}, u32[]{:S(2)}) %collective-permute-start.27) | collective-permute-done | bytes 40992 | tf_op jit(solution)/shard_map/ppermute | solution.py:192
  134.5 2.6 %collective-permute-start.28 = (bf16[32,640]{1,0:T(8,128)(2,1)S(1)}, bf16[32,640]{1,0:T(8,128)(2,1)S(1)}, u32[]{:S(2)}, u32[]{:S(2)}) collective-permute-start(bf16[32,640]{1,0:T(8,128)(2,1)S(1)} %convert_element_type.176), channel_id=1, source_target_pairs={{0,224},{1,225},{2,226},{3,227},{4,228},{5,229},{6,230},{7,231},{8... | collective-permute-start | bytes 122888 | tf_op jit(solution)/shard_map/ppermute | solution.py:192
  137.1 2.2 %collective-permute-done.28 = bf16[32,640]{1,0:T(8,128)(2,1)S(1)} collective-permute-done((bf16[32,640]{1,0:T(8,128)(2,1)S(1)}, bf16[32,640]{1,0:T(8,128)(2,1)S(1)}, u32[]{:S(2)}, u32[]{:S(2)}) %collective-permute-start.28) | collective-permute-done | bytes 40992 | tf_op jit(solution)/shard_map/ppermute | solution.py:192
  139.4 3.5 %collective-permute-done.29 = bf16[32,640]{1,0:T(8,128)(2,1)S(1)} collective-permute-done((bf16[32,640]{1,0:T(8,128)(2,1)S(1)}, bf16[32,640]{1,0:T(8,128)(2,1)S(1)}, u32[]{:S(2)}, u32[]{:S(2)}) %collective-permute-start.29) | collective-permute-done | bytes 40992 | tf_op jit(solution)/shard_map/ppermute | solution.py:192
  143.1 4.7 %collective-permute-done.30 = bf16[32,640]{1,0:T(8,128)(2,1)S(1)} collective-permute-done((bf16[32,640]{1,0:T(8,128)(2,1)S(1)}, bf16[32,640]{1,0:T(8,128)(2,1)S(1)}, u32[]{:S(2)}, u32[]{:S(2)}) %collective-permute-start.30) | collective-permute-done | bytes 40992 | tf_op jit(solution)/shard_map/ppermute | solution.py:192
  147.8 2.0 %collective-permute-start.31 = (bf16[32,640]{1,0:T(8,128)(2,1)S(1)}, bf16[32,640]{1,0:T(8,128)(2,1)S(1)}, u32[]{:S(2)}, u32[]{:S(2)}) collective-permute-start(bf16[32,640]{1,0:T(8,128)(2,1)S(1)} %convert_element_type.182), channel_id=1, source_target_pairs={{0,44},{1,45},{2,46},{3,47},{4,56},{5,57},{6,58},{7,59},{8,52},{9,... | collective-permute-start | bytes 122888 | tf_op jit(solution)/shard_map/ppermute | solution.py:192
  149.8 4.3 %collective-permute-done.31 = bf16[32,640]{1,0:T(8,128)(2,1)S(1)} collective-permute-done((bf16[32,640]{1,0:T(8,128)(2,1)S(1)}, bf16[32,640]{1,0:T(8,128)(2,1)S(1)}, u32[]{:S(2)}, u32[]{:S(2)}) %collective-permute-start.31) | collective-permute-done | bytes 40992 | tf_op jit(solution)/shard_map/ppermute | solution.py:192
  154.6 0.9 collective-permute-done.32.got_ref
  155.5 7.5 %shard_map.82 = bf16[2048,512]{1,0:T(8,128)(2,1)} custom-call(s32[5]{0:T(128)S(1)} %stack.39.flags_ref.half_ref, f32[32,640]{1,0:T(8,128)S(1)} %convert_add_fusion.own_ref, f32[32,640]{1,0:T(8,128)S(1)} %collective-permute-done.32.got_ref, f32[64,512]{1,0:T(8,128)S(1)} %get-tuple-element.41.basis_ref, bf16[2048,512]{1,0:T(8,128)(2,1)S(1)} %get-tuple-element.33.feature_ref, ...), custom_call_target="tpu_custom_call" | custom-call | tf_op jit(solution)/shard_map/pallas_call | solution.py:437
  (89 shorter events, 6.7 us)
Async XLA Ops:
  0.0 11.4 %copy-start = (bf16[64,32,512]{2,1,0:T(8,128)(2,1)S(1)}, bf16[64,32,512]{2,1,0:T(8,128)(2,1)}, u32[]{:S(2)}) copy-start(bf16[64,32,512]{2,1,0:T(8,128)(2,1)} %band_ref.7) | copy-start | bytes 6291460
  0.0 18.1 %copy-start.5 = (f32[21,512]{1,0:T(8,128)S(1)}, f32[21,512]{1,0:T(8,128)}, u32[]{:S(2)}) copy-start(f32[21,512]{1,0:T(8,128)} %taps_ref.7) | copy-start | bytes 129028
  2.8 24.2 %collective-permute-start.2 = (bf16[10,64,256]{2,1,0:T(8,128)(2,1)}, bf16[10,64,256]{2,1,0:T(8,128)(2,1)S(1)}, u32[]{:S(2)}, u32[]{:S(2)}) collective-permute-start(bf16[10,64,256]{2,1,0:T(8,128)(2,1)} %get-tuple-element.26), channel_id=1, source_target_pairs={{0,1},{1,2},{2,3},{3,4},{4,5},{5,6},{6,7},{7,8},{8,9},{9,10},{10,1... | collective-permute-start | bytes 983048 | tf_op jit(solution)/shard_map/ppermute | solution.py:368
  4.8 22.2 %collective-permute-start.3 = (bf16[10,64,256]{2,1,0:T(8,128)(2,1)}, bf16[10,64,256]{2,1,0:T(8,128)(2,1)S(1)}, u32[]{:S(2)}, u32[]{:S(2)}) collective-permute-start(bf16[10,64,256]{2,1,0:T(8,128)(2,1)} %get-tuple-element.27), channel_id=1, source_target_pairs={{0,31},{1,0},{2,1},{3,2},{4,3},{5,4},{6,5},{7,6},{8,7},{9,8},{10,9... | collective-permute-start | bytes 983048 | tf_op jit(solution)/shard_map/ppermute | solution.py:368
  13.2 16.5 %collective-permute-start = (bf16[10,64,256]{2,1,0:T(8,128)(2,1)}, bf16[10,64,256]{2,1,0:T(8,128)(2,1)S(1)}, u32[]{:S(2)}, u32[]{:S(2)}) collective-permute-start(bf16[10,64,256]{2,1,0:T(8,128)(2,1)} %get-tuple-element.24), channel_id=1, source_target_pairs={{0,1},{1,2},{2,3},{3,4},{4,5},{5,6},{6,7},{7,8},{8,9},{9,10},{10,1... | collective-permute-start | bytes 983048 | tf_op jit(solution)/shard_map/ppermute | solution.py:368
  13.2 16.5 %collective-permute-start.1 = (bf16[10,64,256]{2,1,0:T(8,128)(2,1)}, bf16[10,64,256]{2,1,0:T(8,128)(2,1)S(1)}, u32[]{:S(2)}, u32[]{:S(2)}) collective-permute-start(bf16[10,64,256]{2,1,0:T(8,128)(2,1)} %get-tuple-element.25), channel_id=1, source_target_pairs={{0,31},{1,0},{2,1},{3,2},{4,3},{5,4},{6,5},{7,6},{8,7},{9,8},{10,9... | collective-permute-start | bytes 983048 | tf_op jit(solution)/shard_map/ppermute | solution.py:368
  29.7 5.6 %copy-start.6 = (f32[21,512]{1,0:T(8,128)S(1)}, f32[21,512]{1,0:T(8,128)}, u32[]{:S(2)}) copy-start(f32[21,512]{1,0:T(8,128)} %taps_ref.9) | copy-start | bytes 129028
  32.5 10.4 %collective-permute-start.5 = (bf16[10,32,512]{2,1,0:T(8,128)(2,1)S(1)}, bf16[10,32,512]{2,1,0:T(8,128)(2,1)S(1)}, u32[]{:S(2)}, u32[]{:S(2)}) collective-permute-start(bf16[10,32,512]{2,1,0:T(8,128)(2,1)S(1)} %get-tuple-element.43), channel_id=1, source_target_pairs={{0,224},{32,0},{64,32},{96,64},{128,96},{160,128},{192,160},{224,1... | collective-permute-start | bytes 983048 | tf_op jit(solution)/shard_map/ppermute | solution.py:398
  34.1 8.9 %copy-start.1 = (bf16[512,512]{1,0:T(8,128)(2,1)S(1)}, bf16[512,512]{1,0:T(8,128)(2,1)}, u32[]{:S(2)}) copy-start(bf16[512,512]{1,0:T(8,128)(2,1)} %w_ref.1) | copy-start | bytes 1572868
  34.1 8.9 %copy-start.4 = (f32[512,64]{0,1:T(8,128)S(1)}, f32[512,64]{0,1:T(8,128)}, u32[]{:S(2)}) copy-start(f32[512,64]{0,1:T(8,128)} %param.11) | copy-start | bytes 393220
  34.1 8.9 %collective-permute-start.4 = (bf16[10,32,512]{2,1,0:T(8,128)(2,1)S(1)}, bf16[10,32,512]{2,1,0:T(8,128)(2,1)S(1)}, u32[]{:S(2)}, u32[]{:S(2)}) collective-permute-start(bf16[10,32,512]{2,1,0:T(8,128)(2,1)S(1)} %get-tuple-element.44), channel_id=1, source_target_pairs={{0,32},{32,64},{64,96},{96,128},{128,160},{160,192},{192,224},{224... | collective-permute-start | bytes 983048 | tf_op jit(solution)/shard_map/ppermute | solution.py:397
  47.0 1.4 collective-permute-start.6
  48.3 3.6 %collective-permute-start.7 = (bf16[32,640]{1,0:T(8,128)(2,1)S(1)}, bf16[32,640]{1,0:T(8,128)(2,1)S(1)}, u32[]{:S(2)}, u32[]{:S(2)}) collective-permute-start(bf16[32,640]{1,0:T(8,128)(2,1)S(1)} %convert_element_type.140), channel_id=1, source_target_pairs={{0,33},{1,32},{2,35},{3,34},{4,37},{5,36},{6,39},{7,38},{8,41},{9,... | collective-permute-start | bytes 122888 | tf_op jit(solution)/shard_map/ppermute | solution.py:192
  52.0 4.8 %collective-permute-start.8 = (bf16[32,640]{1,0:T(8,128)(2,1)S(1)}, bf16[32,640]{1,0:T(8,128)(2,1)S(1)}, u32[]{:S(2)}, u32[]{:S(2)}) collective-permute-start(bf16[32,640]{1,0:T(8,128)(2,1)S(1)} %convert_element_type.142), channel_id=1, source_target_pairs={{0,35},{1,34},{2,33},{3,32},{4,39},{5,38},{6,37},{7,36},{8,43},{9,... | collective-permute-start | bytes 122888 | tf_op jit(solution)/shard_map/ppermute | solution.py:192
  56.8 3.8 %collective-permute-start.9 = (bf16[32,640]{1,0:T(8,128)(2,1)S(1)}, bf16[32,640]{1,0:T(8,128)(2,1)S(1)}, u32[]{:S(2)}, u32[]{:S(2)}) collective-permute-start(bf16[32,640]{1,0:T(8,128)(2,1)S(1)} %convert_element_type.144), channel_id=1, source_target_pairs={{0,96},{1,97},{2,98},{3,99},{4,100},{5,101},{6,102},{7,103},{8,104... | collective-permute-start | bytes 122888 | tf_op jit(solution)/shard_map/ppermute | solution.py:192
  60.7 4.8 %collective-permute-start.10 = (bf16[32,640]{1,0:T(8,128)(2,1)S(1)}, bf16[32,640]{1,0:T(8,128)(2,1)S(1)}, u32[]{:S(2)}, u32[]{:S(2)}) collective-permute-start(bf16[32,640]{1,0:T(8,128)(2,1)S(1)} %convert_element_type.146), channel_id=1, source_target_pairs={{0,224},{1,225},{2,226},{3,227},{4,228},{5,229},{6,230},{7,231},{8... | collective-permute-start | bytes 122888 | tf_op jit(solution)/shard_map/ppermute | solution.py:192
  65.5 3.6 %collective-permute-start.11 = (bf16[32,640]{1,0:T(8,128)(2,1)S(1)}, bf16[32,640]{1,0:T(8,128)(2,1)S(1)}, u32[]{:S(2)}, u32[]{:S(2)}) collective-permute-start(bf16[32,640]{1,0:T(8,128)(2,1)S(1)} %convert_element_type.148), channel_id=1, source_target_pairs={{0,36},{1,37},{2,38},{3,39},{4,32},{5,33},{6,34},{7,35},{8,44},{9,... | collective-permute-start | bytes 122888 | tf_op jit(solution)/shard_map/ppermute | solution.py:192
  69.1 4.8 %collective-permute-start.12 = (bf16[32,640]{1,0:T(8,128)(2,1)S(1)}, bf16[32,640]{1,0:T(8,128)(2,1)S(1)}, u32[]{:S(2)}, u32[]{:S(2)}) collective-permute-start(bf16[32,640]{1,0:T(8,128)(2,1)S(1)} %convert_element_type.150), channel_id=1, source_target_pairs={{0,60},{1,61},{2,62},{3,63},{4,40},{5,41},{6,42},{7,43},{8,36},{9,... | collective-permute-start | bytes 122888 | tf_op jit(solution)/shard_map/ppermute | solution.py:192
  74.0 5.4 %collective-permute-start.13 = (bf16[32,640]{1,0:T(8,128)(2,1)S(1)}, bf16[32,640]{1,0:T(8,128)(2,1)S(1)}, u32[]{:S(2)}, u32[]{:S(2)}) collective-permute-start(bf16[32,640]{1,0:T(8,128)(2,1)S(1)} %convert_element_type.152), channel_id=1, source_target_pairs={{0,44},{1,45},{2,46},{3,47},{4,56},{5,57},{6,58},{7,59},{8,52},{9,... | collective-permute-start | bytes 122888 | tf_op jit(solution)/shard_map/ppermute | solution.py:192
  79.4 1.4 collective-permute-start.14
  83.5 1.3 collective-permute-start.15
  84.9 3.6 %collective-permute-start.16 = (bf16[32,640]{1,0:T(8,128)(2,1)S(1)}, bf16[32,640]{1,0:T(8,128)(2,1)S(1)}, u32[]{:S(2)}, u32[]{:S(2)}) collective-permute-start(bf16[32,640]{1,0:T(8,128)(2,1)S(1)} %convert_element_type.155), channel_id=1, source_target_pairs={{0,33},{1,32},{2,35},{3,34},{4,37},{5,36},{6,39},{7,38},{8,41},{9,... | collective-permute-start | bytes 122888 | tf_op jit(solution)/shard_map/ppermute | solution.py:192
  88.5 4.8 %collective-permute-start.17 = (bf16[32,640]{1,0:T(8,128)(2,1)S(1)}, bf16[32,640]{1,0:T(8,128)(2,1)S(1)}, u32[]{:S(2)}, u32[]{:S(2)}) collective-permute-start(bf16[32,640]{1,0:T(8,128)(2,1)S(1)} %convert_element_type.157), channel_id=1, source_target_pairs={{0,35},{1,34},{2,33},{3,32},{4,39},{5,38},{6,37},{7,36},{8,43},{9,... | collective-permute-start | bytes 122888 | tf_op jit(solution)/shard_map/ppermute | solution.py:192
  93.3 3.6 %collective-permute-start.18 = (bf16[32,640]{1,0:T(8,128)(2,1)S(1)}, bf16[32,640]{1,0:T(8,128)(2,1)S(1)}, u32[]{:S(2)}, u32[]{:S(2)}) collective-permute-start(bf16[32,640]{1,0:T(8,128)(2,1)S(1)} %convert_element_type.159), channel_id=1, source_target_pairs={{0,96},{1,97},{2,98},{3,99},{4,100},{5,101},{6,102},{7,103},{8,104... | collective-permute-start | bytes 122888 | tf_op jit(solution)/shard_map/ppermute | solution.py:192
  97.0 4.8 %collective-permute-start.19 = (bf16[32,640]{1,0:T(8,128)(2,1)S(1)}, bf16[32,640]{1,0:T(8,128)(2,1)S(1)}, u32[]{:S(2)}, u32[]{:S(2)}) collective-permute-start(bf16[32,640]{1,0:T(8,128)(2,1)S(1)} %convert_element_type.161), channel_id=1, source_target_pairs={{0,224},{1,225},{2,226},{3,227},{4,228},{5,229},{6,230},{7,231},{8... | collective-permute-start | bytes 122888 | tf_op jit(solution)/shard_map/ppermute | solution.py:192
  101.8 3.6 %collective-permute-start.20 = (bf16[32,640]{1,0:T(8,128)(2,1)S(1)}, bf16[32,640]{1,0:T(8,128)(2,1)S(1)}, u32[]{:S(2)}, u32[]{:S(2)}) collective-permute-start(bf16[32,640]{1,0:T(8,128)(2,1)S(1)} %convert_element_type.163), channel_id=1, source_target_pairs={{0,36},{1,37},{2,38},{3,39},{4,32},{5,33},{6,34},{7,35},{8,44},{9,... | collective-permute-start | bytes 122888 | tf_op jit(solution)/shard_map/ppermute | solution.py:192
  105.4 4.8 %collective-permute-start.21 = (bf16[32,640]{1,0:T(8,128)(2,1)S(1)}, bf16[32,640]{1,0:T(8,128)(2,1)S(1)}, u32[]{:S(2)}, u32[]{:S(2)}) collective-permute-start(bf16[32,640]{1,0:T(8,128)(2,1)S(1)} %convert_element_type.165), channel_id=1, source_target_pairs={{0,60},{1,61},{2,62},{3,63},{4,40},{5,41},{6,42},{7,43},{8,36},{9,... | collective-permute-start | bytes 122888 | tf_op jit(solution)/shard_map/ppermute | solution.py:192
  110.3 6.4 %collective-permute-start.22 = (bf16[32,640]{1,0:T(8,128)(2,1)S(1)}, bf16[32,640]{1,0:T(8,128)(2,1)S(1)}, u32[]{:S(2)}, u32[]{:S(2)}) collective-permute-start(bf16[32,640]{1,0:T(8,128)(2,1)S(1)} %convert_element_type.167), channel_id=1, source_target_pairs={{0,44},{1,45},{2,46},{3,47},{4,56},{5,57},{6,58},{7,59},{8,52},{9,... | collective-permute-start | bytes 122888 | tf_op jit(solution)/shard_map/ppermute | solution.py:192
  116.7 1.4 collective-permute-start.23
  118.1 37.4 %copy-start.2 = (bf16[512,512]{1,0:T(8,128)(2,1)S(1)}, bf16[512,512]{1,0:T(8,128)(2,1)}, u32[]{:S(2)}) copy-start(bf16[512,512]{1,0:T(8,128)(2,1)} %wham_ref.1) | copy-start | bytes 1572868
  118.1 37.4 %copy-start.3 = (bf16[512,512]{1,0:T(8,128)(2,1)S(1)}, bf16[512,512]{1,0:T(8,128)(2,1)}, u32[]{:S(2)}) copy-start(bf16[512,512]{1,0:T(8,128)(2,1)} %walign_ref.1) | copy-start | bytes 1572868
  120.8 1.3 collective-permute-start.24
  122.2 3.6 %collective-permute-start.25 = (bf16[32,640]{1,0:T(8,128)(2,1)S(1)}, bf16[32,640]{1,0:T(8,128)(2,1)S(1)}, u32[]{:S(2)}, u32[]{:S(2)}) collective-permute-start(bf16[32,640]{1,0:T(8,128)(2,1)S(1)} %convert_element_type.170), channel_id=1, source_target_pairs={{0,33},{1,32},{2,35},{3,34},{4,37},{5,36},{6,39},{7,38},{8,41},{9,... | collective-permute-start | bytes 122888 | tf_op jit(solution)/shard_map/ppermute | solution.py:192
  125.8 4.8 %collective-permute-start.26 = (bf16[32,640]{1,0:T(8,128)(2,1)S(1)}, bf16[32,640]{1,0:T(8,128)(2,1)S(1)}, u32[]{:S(2)}, u32[]{:S(2)}) collective-permute-start(bf16[32,640]{1,0:T(8,128)(2,1)S(1)} %convert_element_type.172), channel_id=1, source_target_pairs={{0,35},{1,34},{2,33},{3,32},{4,39},{5,38},{6,37},{7,36},{8,43},{9,... | collective-permute-start | bytes 122888 | tf_op jit(solution)/shard_map/ppermute | solution.py:192
  130.6 3.8 %collective-permute-start.27 = (bf16[32,640]{1,0:T(8,128)(2,1)S(1)}, bf16[32,640]{1,0:T(8,128)(2,1)S(1)}, u32[]{:S(2)}, u32[]{:S(2)}) collective-permute-start(bf16[32,640]{1,0:T(8,128)(2,1)S(1)} %convert_element_type.174), channel_id=1, source_target_pairs={{0,96},{1,97},{2,98},{3,99},{4,100},{5,101},{6,102},{7,103},{8,104... | collective-permute-start | bytes 122888 | tf_op jit(solution)/shard_map/ppermute | solution.py:192
  134.5 4.8 %collective-permute-start.28 = (bf16[32,640]{1,0:T(8,128)(2,1)S(1)}, bf16[32,640]{1,0:T(8,128)(2,1)S(1)}, u32[]{:S(2)}, u32[]{:S(2)}) collective-permute-start(bf16[32,640]{1,0:T(8,128)(2,1)S(1)} %convert_element_type.176), channel_id=1, source_target_pairs={{0,224},{1,225},{2,226},{3,227},{4,228},{5,229},{6,230},{7,231},{8... | collective-permute-start | bytes 122888 | tf_op jit(solution)/shard_map/ppermute | solution.py:192
  139.3 3.6 %collective-permute-start.29 = (bf16[32,640]{1,0:T(8,128)(2,1)S(1)}, bf16[32,640]{1,0:T(8,128)(2,1)S(1)}, u32[]{:S(2)}, u32[]{:S(2)}) collective-permute-start(bf16[32,640]{1,0:T(8,128)(2,1)S(1)} %convert_element_type.178), channel_id=1, source_target_pairs={{0,36},{1,37},{2,38},{3,39},{4,32},{5,33},{6,34},{7,35},{8,44},{9,... | collective-permute-start | bytes 122888 | tf_op jit(solution)/shard_map/ppermute | solution.py:192
  143.0 4.8 %collective-permute-start.30 = (bf16[32,640]{1,0:T(8,128)(2,1)S(1)}, bf16[32,640]{1,0:T(8,128)(2,1)S(1)}, u32[]{:S(2)}, u32[]{:S(2)}) collective-permute-start(bf16[32,640]{1,0:T(8,128)(2,1)S(1)} %convert_element_type.180), channel_id=1, source_target_pairs={{0,60},{1,61},{2,62},{3,63},{4,40},{5,41},{6,42},{7,43},{8,36},{9,... | collective-permute-start | bytes 122888 | tf_op jit(solution)/shard_map/ppermute | solution.py:192
  147.8 6.2 %collective-permute-start.31 = (bf16[32,640]{1,0:T(8,128)(2,1)S(1)}, bf16[32,640]{1,0:T(8,128)(2,1)S(1)}, u32[]{:S(2)}, u32[]{:S(2)}) collective-permute-start(bf16[32,640]{1,0:T(8,128)(2,1)S(1)} %convert_element_type.182), channel_id=1, source_target_pairs={{0,44},{1,45},{2,46},{3,47},{4,56},{5,57},{6,58},{7,59},{8,52},{9,... | collective-permute-start | bytes 122888 | tf_op jit(solution)/shard_map/ppermute | solution.py:192
  154.1 1.4 collective-permute-start.32

commit v8 on v7

--- a/solution.py
+++ b/solution.py
@@ -20,7 +20,6 @@
 MARGIN = TAPS // 2
 LANES = 128
 PARTS = 2
-HEAD_BLOCKS = 4
 
 
 def weighted(taps_ref, items, rows):
@@ -216,16 +215,16 @@
 
 def coeffs_of(basis, coeffs, numerator):
     gram = dot3(basis, basis, NT)
-    return coeffs * numerator / (dot3(gram, coeffs, NN) + EPS)
+    return coeffs * numerator / (dot3(coeffs, gram, NN) + EPS)
 
 
 def emit_sums(half_ref, coeffs, feature, mine_ref, theirs_ref):
     c, rows = feature.shape[1], mine_ref.shape[0]
     first = half_ref[0] == 0
-    num = dot(coeffs.astype(BF), feature, NN)
+    num = dot(coeffs.astype(BF), feature, TN)
     mine_ref[:, :c] = jnp.where(first, num[:rows], num[rows:])
     theirs_ref[:, :c] = jnp.where(first, num[rows:], num[:rows]).astype(BF)
-    gram = dot3(coeffs, coeffs, NT)
+    gram = dot3(coeffs, coeffs, TN)
     gram = jnp.concatenate([gram, jnp.zeros_like(gram)], axis=1)
     mine_ref[:, c:] = jnp.where(first, gram[:rows], gram[rows:])
     theirs_ref[:, c:] = jnp.where(first, gram[rows:], gram[:rows]).astype(BF)
@@ -261,9 +260,9 @@
     feature_ref[edge + mid :] = squeezed(low)
     feature = feature_ref[...]
     basis = basis_ref[...]
-    scores = dot(basis.astype(BF), feature, NT)
-    e = jnp.exp(scores - jnp.max(scores, axis=0, keepdims=True))
-    soft = e / jnp.sum(e, axis=0, keepdims=True)
+    scores = dot(feature, basis.astype(BF), NT)
+    e = jnp.exp(scores - jnp.max(scores, axis=1, keepdims=True))
+    soft = e / jnp.sum(e, axis=1, keepdims=True)
     coeffs = coeffs_of(basis, soft, scores)
     coeffs_ref[...] = coeffs
     emit_sums(flags_ref, coeffs, feature, mine_ref, theirs_ref)
@@ -285,23 +284,19 @@
     basis = updated_basis(half_ref, own_ref, got_ref, basis_ref[...])
     newbasis_ref[...] = basis
     feature = feature_ref[...]
-    coeffs = coeffs_of(basis, coeffs_ref[...], dot(basis.astype(BF), feature, NT))
+    coeffs = coeffs_of(basis, coeffs_ref[...], dot(feature, basis.astype(BF), NT))
     newcoeffs_ref[...] = coeffs
     emit_sums(half_ref, coeffs, feature, mine_ref, theirs_ref)
 
 
 def last_kernel(
-    half_ref, own_ref, got_ref, basis_ref, feature_ref, coeffs_ref, wham_ref, walign_ref, out_ref, now
+    half_ref, own_ref, got_ref, basis_ref, feature_ref, coeffs_ref, wham_ref, walign_ref, out_ref
 ):
-    @pl.when(pl.program_id(0) == 0)
-    def _():
-        now[...] = updated_basis(half_ref, own_ref, got_ref, basis_ref[...])
-
-    basis = now[...]
+    basis = updated_basis(half_ref, own_ref, got_ref, basis_ref[...])
     feature = feature_ref[...]
     low = basis.astype(BF)
-    coeffs = coeffs_of(basis, coeffs_ref[...], dot(low, feature, NT))
-    rebuilt = dot(coeffs.astype(BF), low, TN).astype(BF)
+    coeffs = coeffs_of(basis, coeffs_ref[...], dot(feature, low, NT))
+    rebuilt = dot(coeffs.astype(BF), low, NN).astype(BF)
     hammed = jnp.maximum(feature.astype(F32) + dot(rebuilt, wham_ref[...], NN), 0.0).astype(BF)
     out_ref[...] = dot(hammed, walign_ref[...], NN).astype(BF)
 
@@ -420,30 +415,22 @@
     basis = bases_init.T
     feature, coeffs, mine, theirs = call(
         first_kernel,
-        [sds((n, channels), BF), sds((r, n), F32)] + sums,
+        [sds((n, channels), BF), sds((n, r), F32)] + sums,
         flags, mid, top, low, above, below, row_taps, w_squeeze, basis,
     )
     for _ in range(STEPS - 1):
         own, got = summed_over_all(mine, theirs)
         basis, coeffs, mine, theirs = call(
             step_kernel,
-            [sds((r, channels), F32), sds((r, n), F32)] + sums,
+            [sds((r, channels), F32), sds((n, r), F32)] + sums,
             flags, own, got, basis, feature, coeffs,
         )
     own, got = summed_over_all(mine, theirs)
-    vmem = pl.BlockSpec(memory_space=pltpu.VMEM)
-    pixel_block = n // HEAD_BLOCKS
-    pixels_by_channel = pl.BlockSpec((pixel_block, channels), lambda i: (i, 0))
-    head_out = pl.pallas_call(
+    head_out = call(
         last_kernel,
-        grid=(HEAD_BLOCKS,),
-        in_specs=[scalar, vmem, vmem, vmem, pixels_by_channel]
-        + [pl.BlockSpec((r, pixel_block), lambda i: (0, i)), vmem, vmem],
-        out_specs=pixels_by_channel,
-        out_shape=sds((n, channels), BF),
-        scratch_shapes=[pltpu.VMEM((r, channels), F32)],
-        compiler_params=pltpu.CompilerParams(vmem_limit_bytes=24 * 2**20),
-    )(flags, own, got, basis, feature, coeffs, w_ham, w_align)
+        sds((n, channels), BF),
+        flags, own, got, basis, feature, coeffs, w_ham, w_align,
+    )
     return head_out.reshape(tile_rows, tile_cols, channels)
 
 

time: 163 us -> 162 us (level)
    pallas_call x1 -> x0, Pallas kernels: 7.46 us -> none  [on_device(): pl.pallas_call(last_kernel, grid=(HEAD_BLOCKS,), in_specs=[scalar, vmem,...]
    pallas_call x3 -> x4, Pallas kernels: 9.43 us -> 16.1 us  [call(): pl.pallas_call(kernel, out_shape=outs, in_specs=specs, out_specs=jax.tree...]
where the time goes in v8:
time: 162 us
  waiting for transfers between devices  82.1 us (51%)
  Pallas kernels  42.7 us (26%)
  starting transfers between devices  36.4 us (22%)
    ppermute x21, waiting for transfers between devices, summed_over_all(): got = lax.ppermute(total.astype(BF), ALL, round_pairs(axis, rule))  76.7 us
    ppermute x21, starting transfers between devices, summed_over_all(): got = lax.ppermute(total.astype(BF), ALL, round_pairs(axis, rule))  17.3 us
    pallas_call x4, Pallas kernels, call(): pl.pallas_call(kernel, out_shape=outs, in_specs=specs, out_specs=jax.tree...  16.1 us
    ppermute x2, starting transfers between devices, on_device(): lax.ppermute(first, COLS, ring(Z * X, -1))  11.3 us
    pallas_call x1, Pallas kernels, on_device(): pl.pallas_call(columns_own_kernel, grid=(channels // LANES,), in_specs=[t...  8.91 us
    pallas_call x1, Pallas kernels, on_device(): pl.pallas_call(rows_own_kernel, grid=(channels // LANES,), in_specs=[tile...  7.67 us
    pallas_call x2, Pallas kernels, on_device(): pl.pallas_call(columns_rest_kernel, grid=grid, in_specs=[scalar, blocks(t...  5.41 us
    pallas_call x2, Pallas kernels, on_device(): pl.pallas_call(pack_kernel, grid=grid, in_specs=[blocks(tile_rows, tile_c...  4.61 us
  transfers between devices with their start and end apart: 33, of which 27 were waited for; matrix products, arithmetic and copies ran while one was open for 0% of the time, Pallas kernels for 13%

profile of v8, /device:TPU:1, one launch (start us, length us, event | category | flops | bytes accessed | tf_op | source)
XLA Modules:
  0.0 162.3 jit_solution(17623017402235921773)
XLA Ops:
  0.0 2.8 %shard_map.75 = (bf16[10,64,256]{2,1,0:T(8,128)(2,1)}, bf16[10,64,256]{2,1,0:T(8,128)(2,1)}) custom-call(bf16[64,32,512]{2,1,0:T(8,128)(2,1)} %band_ref.7), custom_call_target="tpu_custom_call" | custom-call | flops 1048576 | bytes 1572864 | tf_op jit(solution)/shard_map/pallas_call | solution.py:352
  2.8 2.0 %collective-permute-start.2 = (bf16[10,64,256]{2,1,0:T(8,128)(2,1)}, bf16[10,64,256]{2,1,0:T(8,128)(2,1)S(1)}, u32[]{:S(2)}, u32[]{:S(2)}) collective-permute-start(bf16[10,64,256]{2,1,0:T(8,128)(2,1)} %get-tuple-element.26), channel_id=1, source_target_pairs={{0,1},{1,2},{2,3},{3,4},{4,5},{5,6},{6,7},{7,8},{8,9},{9,10},{10,1... | collective-permute-start | bytes 983048 | tf_op jit(solution)/shard_map/ppermute | solution.py:363
  4.8 6.6 %collective-permute-start.3 = (bf16[10,64,256]{2,1,0:T(8,128)(2,1)}, bf16[10,64,256]{2,1,0:T(8,128)(2,1)S(1)}, u32[]{:S(2)}, u32[]{:S(2)}) collective-permute-start(bf16[10,64,256]{2,1,0:T(8,128)(2,1)} %get-tuple-element.27), channel_id=1, source_target_pairs={{0,31},{1,0},{2,1},{3,2},{4,3},{5,4},{6,5},{7,6},{8,7},{9,8},{10,9... | collective-permute-start | bytes 983048 | tf_op jit(solution)/shard_map/ppermute | solution.py:363
  11.4 1.8 %shard_map.74 = (bf16[10,64,256]{2,1,0:T(8,128)(2,1)}, bf16[10,64,256]{2,1,0:T(8,128)(2,1)}) custom-call(bf16[64,32,512]{2,1,0:T(8,128)(2,1)S(1)} %copy-done), custom_call_target="tpu_custom_call" | custom-call | flops 1048576 | bytes 1572864 | tf_op jit(solution)/shard_map/pallas_call | solution.py:352
  13.2 4.8 %collective-permute-start.1 = (bf16[10,64,256]{2,1,0:T(8,128)(2,1)}, bf16[10,64,256]{2,1,0:T(8,128)(2,1)S(1)}, u32[]{:S(2)}, u32[]{:S(2)}) collective-permute-start(bf16[10,64,256]{2,1,0:T(8,128)(2,1)} %get-tuple-element.25), channel_id=1, source_target_pairs={{0,31},{1,0},{2,1},{3,2},{4,3},{5,4},{6,5},{7,6},{8,7},{9,8},{10,9... | collective-permute-start | bytes 983048 | tf_op jit(solution)/shard_map/ppermute | solution.py:363
  18.1 8.9 %shard_map.73.own_ref = f32[32,64,512]{2,1,0:T(8,128)S(1)} custom-call(bf16[64,32,512]{2,1,0:T(8,128)(2,1)S(1)} %copy-done, f32[21,512]{1,0:T(8,128)S(1)} %copy-done.5), custom_call_target="tpu_custom_call" | custom-call | flops 44040192 | bytes 6291456 | tf_op jit(solution)/shard_map/pallas_call | solution.py:365
  27.0 2.7 %shard_map.76.refs_0_ = bf16[64,32,512]{2,1,0:T(8,128)(2,1)S(1)} custom-call(s32[5]{0:T(128)S(1)} %stack.39.flags_ref.half_ref, f32[32,64,512]{2,1,0:T(8,128)S(1)} %shard_map.73.own_ref, bf16[10,64,256]{2,1,0:T(8,128)(2,1)S(1)} %collective-permute-done.2.left_ref, bf16[10,64,256]{2,1,0:T(8,128)(2,1)S(1)} %collective-permute-done.3.right_ref, ...), custom_call_target="tpu_custom_call" | custom-call | flops 10485760 | bytes 3145728 | tf_op jit(solution)/shard_map/pallas_call | solution.py:379
  29.8 2.7 %shard_map.77.filtered_ref = bf16[64,32,512]{2,1,0:T(8,128)(2,1)S(1)} custom-call(s32[5]{0:T(128)S(1)} %stack.39.flags_ref.half_ref, f32[32,64,512]{2,1,0:T(8,128)S(1)} %shard_map.73.own_ref, bf16[10,64,256]{2,1,0:T(8,128)(2,1)S(1)} %collective-permute-done.left_ref, ...), custom_call_target="tpu_custom_call", output_to_operand_aliasing={{}: (5, {})} | custom-call | flops 10485760 | bytes 3145728 | tf_op jit(solution)/shard_map/pallas_call | solution.py:379
  32.5 1.5 collective-permute-start.5
  34.1 1.2 collective-permute-start.4
  35.3 7.7 %shard_map.78 = (bf16[44,32,512]{2,1,0:T(8,128)(2,1)S(1)}, f32[10,32,512]{2,1,0:T(8,128)S(1)}, f32[10,32,512]{2,1,0:T(8,128)S(1)}) custom-call(bf16[64,32,512]{2,1,0:T(8,128)(2,1)S(1)} %shard_map.77.filtered_ref, bf16[64,32,512]{2,1,0:T(8,128)(2,1)S(1)} %copy-done, f32[21,512]{1,0:T(8,128)S(1)} %copy-done.6), custom_call_target="tpu_custom_call" | custom-call | flops 44040192 | bytes 6291456 | tf_op jit(solution)/shard_map/pallas_call | solution.py:394
  43.0 4.7 %shard_map.79 = (bf16[2048,512]{1,0:T(8,128)(2,1)S(1)}, f32[2048,64]{1,0:T(8,128)S(1)}, f32[32,640]{1,0:T(8,128)S(1)}, bf16[32,640]{1,0:T(8,128)(2,1)S(1)}) custom-call(s32[5]{0:T(128)S(1)} %stack.39.flags_ref.half_ref, bf16[44,32,512]{2,1,0:T(8,128)(2,1)S(1)} %get-tuple-element.28.mid_ref, f32[10,32,512]{2,1,0:T(8,128)S(1)} %get-tuple-element.29.top_ref, ...), custom_call_target="tpu_custom_call" | custom-call | tf_op jit(solution)/shard_map/pallas_call | solution.py:307
  49.2 3.5 %collective-permute-done.7 = bf16[32,640]{1,0:T(8,128)(2,1)S(1)} collective-permute-done((bf16[32,640]{1,0:T(8,128)(2,1)S(1)}, bf16[32,640]{1,0:T(8,128)(2,1)S(1)}, u32[]{:S(2)}, u32[]{:S(2)}) %collective-permute-start.7) | collective-permute-done | bytes 40992 | tf_op jit(solution)/shard_map/ppermute | solution.py:191
  53.1 4.7 %collective-permute-done.8 = bf16[32,640]{1,0:T(8,128)(2,1)S(1)} collective-permute-done((bf16[32,640]{1,0:T(8,128)(2,1)S(1)}, bf16[32,640]{1,0:T(8,128)(2,1)S(1)}, u32[]{:S(2)}, u32[]{:S(2)}) %collective-permute-start.8) | collective-permute-done | bytes 40992 | tf_op jit(solution)/shard_map/ppermute | solution.py:191
  57.8 1.2 collective-permute-start.9
  59.0 2.4 %collective-permute-done.9 = bf16[32,640]{1,0:T(8,128)(2,1)S(1)} collective-permute-done((bf16[32,640]{1,0:T(8,128)(2,1)S(1)}, bf16[32,640]{1,0:T(8,128)(2,1)S(1)}, u32[]{:S(2)}, u32[]{:S(2)}) %collective-permute-start.9) | collective-permute-done | bytes 40992 | tf_op jit(solution)/shard_map/ppermute | solution.py:191
  61.4 2.7 %collective-permute-start.10 = (bf16[32,640]{1,0:T(8,128)(2,1)S(1)}, bf16[32,640]{1,0:T(8,128)(2,1)S(1)}, u32[]{:S(2)}, u32[]{:S(2)}) collective-permute-start(bf16[32,640]{1,0:T(8,128)(2,1)S(1)} %convert_element_type.146), channel_id=1, source_target_pairs={{0,224},{1,225},{2,226},{3,227},{4,228},{5,229},{6,230},{7,231},{8... | collective-permute-start | bytes 122888 | tf_op jit(solution)/shard_map/ppermute | solution.py:191
  64.2 2.1 %collective-permute-done.10 = bf16[32,640]{1,0:T(8,128)(2,1)S(1)} collective-permute-done((bf16[32,640]{1,0:T(8,128)(2,1)S(1)}, bf16[32,640]{1,0:T(8,128)(2,1)S(1)}, u32[]{:S(2)}, u32[]{:S(2)}) %collective-permute-start.10) | collective-permute-done | bytes 40992 | tf_op jit(solution)/shard_map/ppermute | solution.py:191
  66.4 3.5 %collective-permute-done.11 = bf16[32,640]{1,0:T(8,128)(2,1)S(1)} collective-permute-done((bf16[32,640]{1,0:T(8,128)(2,1)S(1)}, bf16[32,640]{1,0:T(8,128)(2,1)S(1)}, u32[]{:S(2)}, u32[]{:S(2)}) %collective-permute-start.11) | collective-permute-done | bytes 40992 | tf_op jit(solution)/shard_map/ppermute | solution.py:191
  70.0 4.7 %collective-permute-done.12 = bf16[32,640]{1,0:T(8,128)(2,1)S(1)} collective-permute-done((bf16[32,640]{1,0:T(8,128)(2,1)S(1)}, bf16[32,640]{1,0:T(8,128)(2,1)S(1)}, u32[]{:S(2)}, u32[]{:S(2)}) %collective-permute-start.12) | collective-permute-done | bytes 40992 | tf_op jit(solution)/shard_map/ppermute | solution.py:191
  74.8 1.4 collective-permute-start.13
  76.1 4.0 %collective-permute-done.13 = bf16[32,640]{1,0:T(8,128)(2,1)S(1)} collective-permute-done((bf16[32,640]{1,0:T(8,128)(2,1)S(1)}, bf16[32,640]{1,0:T(8,128)(2,1)S(1)}, u32[]{:S(2)}, u32[]{:S(2)}) %collective-permute-start.13) | collective-permute-done | bytes 40992 | tf_op jit(solution)/shard_map/ppermute | solution.py:191
  80.6 0.9 collective-permute-done.14.got_ref
  81.6 2.6 %shard_map.80 = (f32[64,512]{1,0:T(8,128)S(1)}, f32[2048,64]{1,0:T(8,128)S(1)}, f32[32,640]{1,0:T(8,128)S(1)}, bf16[32,640]{1,0:T(8,128)(2,1)S(1)}) custom-call(s32[5]{0:T(128)S(1)} %stack.39.flags_ref.half_ref, f32[32,640]{1,0:T(8,128)S(1)} %convert_add_fusion.16.own_ref, f32[32,640]{1,0:T(8,128)S(1)} %collective-permute-done.14.got_ref, ...), custom_call_target="tpu_custom_call" | custom-call | tf_op jit(solution)/shard_map/pallas_call | solution.py:307
  84.6 0.9 collective-permute-done.15
  85.6 3.5 %collective-permute-done.16 = bf16[32,640]{1,0:T(8,128)(2,1)S(1)} collective-permute-done((bf16[32,640]{1,0:T(8,128)(2,1)S(1)}, bf16[32,640]{1,0:T(8,128)(2,1)S(1)}, u32[]{:S(2)}, u32[]{:S(2)}) %collective-permute-start.16) | collective-permute-done | bytes 40992 | tf_op jit(solution)/shard_map/ppermute | solution.py:191
  89.2 4.7 %collective-permute-done.17 = bf16[32,640]{1,0:T(8,128)(2,1)S(1)} collective-permute-done((bf16[32,640]{1,0:T(8,128)(2,1)S(1)}, bf16[32,640]{1,0:T(8,128)(2,1)S(1)}, u32[]{:S(2)}, u32[]{:S(2)}) %collective-permute-start.17) | collective-permute-done | bytes 40992 | tf_op jit(solution)/shard_map/ppermute | solution.py:191
  94.1 3.5 %collective-permute-done.18 = bf16[32,640]{1,0:T(8,128)(2,1)S(1)} collective-permute-done((bf16[32,640]{1,0:T(8,128)(2,1)S(1)}, bf16[32,640]{1,0:T(8,128)(2,1)S(1)}, u32[]{:S(2)}, u32[]{:S(2)}) %collective-permute-start.18) | collective-permute-done | bytes 40992 | tf_op jit(solution)/shard_map/ppermute | solution.py:191
  97.6 2.7 %collective-permute-start.19 = (bf16[32,640]{1,0:T(8,128)(2,1)S(1)}, bf16[32,640]{1,0:T(8,128)(2,1)S(1)}, u32[]{:S(2)}, u32[]{:S(2)}) collective-permute-start(bf16[32,640]{1,0:T(8,128)(2,1)S(1)} %convert_element_type.161), channel_id=1, source_target_pairs={{0,224},{1,225},{2,226},{3,227},{4,228},{5,229},{6,230},{7,231},{8... | collective-permute-start | bytes 122888 | tf_op jit(solution)/shard_map/ppermute | solution.py:191
  100.3 2.1 %collective-permute-done.19 = bf16[32,640]{1,0:T(8,128)(2,1)S(1)} collective-permute-done((bf16[32,640]{1,0:T(8,128)(2,1)S(1)}, bf16[32,640]{1,0:T(8,128)(2,1)S(1)}, u32[]{:S(2)}, u32[]{:S(2)}) %collective-permute-start.19) | collective-permute-done | bytes 40992 | tf_op jit(solution)/shard_map/ppermute | solution.py:191
  102.5 3.5 %collective-permute-done.20 = bf16[32,640]{1,0:T(8,128)(2,1)S(1)} collective-permute-done((bf16[32,640]{1,0:T(8,128)(2,1)S(1)}, bf16[32,640]{1,0:T(8,128)(2,1)S(1)}, u32[]{:S(2)}, u32[]{:S(2)}) %collective-permute-start.20) | collective-permute-done | bytes 40992 | tf_op jit(solution)/shard_map/ppermute | solution.py:191
  106.8 4.1 %collective-permute-done.21 = bf16[32,640]{1,0:T(8,128)(2,1)S(1)} collective-permute-done((bf16[32,640]{1,0:T(8,128)(2,1)S(1)}, bf16[32,640]{1,0:T(8,128)(2,1)S(1)}, u32[]{:S(2)}, u32[]{:S(2)}) %collective-permute-start.21) | collective-permute-done | bytes 40992 | tf_op jit(solution)/shard_map/ppermute | solution.py:191
  110.9 2.3 %collective-permute-start.22 = (bf16[32,640]{1,0:T(8,128)(2,1)S(1)}, bf16[32,640]{1,0:T(8,128)(2,1)S(1)}, u32[]{:S(2)}, u32[]{:S(2)}) collective-permute-start(bf16[32,640]{1,0:T(8,128)(2,1)S(1)} %convert_element_type.167), channel_id=1, source_target_pairs={{0,44},{1,45},{2,46},{3,47},{4,56},{5,57},{6,58},{7,59},{8,52},{9,... | collective-permute-start | bytes 122888 | tf_op jit(solution)/shard_map/ppermute | solution.py:191
  113.2 4.1 %collective-permute-done.22 = bf16[32,640]{1,0:T(8,128)(2,1)S(1)} collective-permute-done((bf16[32,640]{1,0:T(8,128)(2,1)S(1)}, bf16[32,640]{1,0:T(8,128)(2,1)S(1)}, u32[]{:S(2)}, u32[]{:S(2)}) %collective-permute-start.22) | collective-permute-done | bytes 40992 | tf_op jit(solution)/shard_map/ppermute | solution.py:191
  117.8 0.9 collective-permute-done.23.got_ref
  118.7 2.6 %shard_map.81 = (f32[64,512]{1,0:T(8,128)S(1)}, f32[2048,64]{1,0:T(8,128)S(1)}, f32[32,640]{1,0:T(8,128)S(1)}, bf16[32,640]{1,0:T(8,128)(2,1)S(1)}) custom-call(s32[5]{0:T(128)S(1)} %stack.39.flags_ref.half_ref, f32[32,640]{1,0:T(8,128)S(1)} %convert_add_fusion.8.own_ref, f32[32,640]{1,0:T(8,128)S(1)} %collective-permute-done.23.got_ref, ...), custom_call_target="tpu_custom_call" | custom-call | tf_op jit(solution)/shard_map/pallas_call | solution.py:307
  122.0 0.9 collective-permute-done.24
  123.0 3.5 %collective-permute-done.25 = bf16[32,640]{1,0:T(8,128)(2,1)S(1)} collective-permute-done((bf16[32,640]{1,0:T(8,128)(2,1)S(1)}, bf16[32,640]{1,0:T(8,128)(2,1)S(1)}, u32[]{:S(2)}, u32[]{:S(2)}) %collective-permute-start.25) | collective-permute-done | bytes 40992 | tf_op jit(solution)/shard_map/ppermute | solution.py:191
  127.0 4.3 %collective-permute-done.26 = bf16[32,640]{1,0:T(8,128)(2,1)S(1)} collective-permute-done((bf16[32,640]{1,0:T(8,128)(2,1)S(1)}, bf16[32,640]{1,0:T(8,128)(2,1)S(1)}, u32[]{:S(2)}, u32[]{:S(2)}) %collective-permute-start.26) | collective-permute-done | bytes 40992 | tf_op jit(solution)/shard_map/ppermute | solution.py:191
  131.5 3.5 %collective-permute-done.27 = bf16[32,640]{1,0:T(8,128)(2,1)S(1)} collective-permute-done((bf16[32,640]{1,0:T(8,128)(2,1)S(1)}, bf16[32,640]{1,0:T(8,128)(2,1)S(1)}, u32[]{:S(2)}, u32[]{:S(2)}) %collective-permute-start.27) | collective-permute-done | bytes 40992 | tf_op jit(solution)/shard_map/ppermute | solution.py:191
  135.0 2.6 %collective-permute-start.28 = (bf16[32,640]{1,0:T(8,128)(2,1)S(1)}, bf16[32,640]{1,0:T(8,128)(2,1)S(1)}, u32[]{:S(2)}, u32[]{:S(2)}) collective-permute-start(bf16[32,640]{1,0:T(8,128)(2,1)S(1)} %convert_element_type.176), channel_id=1, source_target_pairs={{0,224},{1,225},{2,226},{3,227},{4,228},{5,229},{6,230},{7,231},{8... | collective-permute-start | bytes 122888 | tf_op jit(solution)/shard_map/ppermute | solution.py:191
  137.6 2.2 %collective-permute-done.28 = bf16[32,640]{1,0:T(8,128)(2,1)S(1)} collective-permute-done((bf16[32,640]{1,0:T(8,128)(2,1)S(1)}, bf16[32,640]{1,0:T(8,128)(2,1)S(1)}, u32[]{:S(2)}, u32[]{:S(2)}) %collective-permute-start.28) | collective-permute-done | bytes 40992 | tf_op jit(solution)/shard_map/ppermute | solution.py:191
  139.9 3.5 %collective-permute-done.29 = bf16[32,640]{1,0:T(8,128)(2,1)S(1)} collective-permute-done((bf16[32,640]{1,0:T(8,128)(2,1)S(1)}, bf16[32,640]{1,0:T(8,128)(2,1)S(1)}, u32[]{:S(2)}, u32[]{:S(2)}) %collective-permute-start.29) | collective-permute-done | bytes 40992 | tf_op jit(solution)/shard_map/ppermute | solution.py:191
  143.6 4.7 %collective-permute-done.30 = bf16[32,640]{1,0:T(8,128)(2,1)S(1)} collective-permute-done((bf16[32,640]{1,0:T(8,128)(2,1)S(1)}, bf16[32,640]{1,0:T(8,128)(2,1)S(1)}, u32[]{:S(2)}, u32[]{:S(2)}) %collective-permute-start.30) | collective-permute-done | bytes 40992 | tf_op jit(solution)/shard_map/ppermute | solution.py:191
  148.3 1.9 %collective-permute-start.31 = (bf16[32,640]{1,0:T(8,128)(2,1)S(1)}, bf16[32,640]{1,0:T(8,128)(2,1)S(1)}, u32[]{:S(2)}, u32[]{:S(2)}) collective-permute-start(bf16[32,640]{1,0:T(8,128)(2,1)S(1)} %convert_element_type.182), channel_id=1, source_target_pairs={{0,44},{1,45},{2,46},{3,47},{4,56},{5,57},{6,58},{7,59},{8,52},{9,... | collective-permute-start | bytes 122888 | tf_op jit(solution)/shard_map/ppermute | solution.py:191
  150.2 4.4 %collective-permute-done.31 = bf16[32,640]{1,0:T(8,128)(2,1)S(1)} collective-permute-done((bf16[32,640]{1,0:T(8,128)(2,1)S(1)}, bf16[32,640]{1,0:T(8,128)(2,1)S(1)}, u32[]{:S(2)}, u32[]{:S(2)}) %collective-permute-start.31) | collective-permute-done | bytes 40992 | tf_op jit(solution)/shard_map/ppermute | solution.py:191
  155.1 0.9 collective-permute-done.32.got_ref
  156.0 6.2 %shard_map.82 = bf16[2048,512]{1,0:T(8,128)(2,1)} custom-call(s32[5]{0:T(128)S(1)} %stack.39.flags_ref.half_ref, f32[32,640]{1,0:T(8,128)S(1)} %convert_add_fusion.own_ref, f32[32,640]{1,0:T(8,128)S(1)} %collective-permute-done.32.got_ref, f32[64,512]{1,0:T(8,128)S(1)} %get-tuple-element.41.basis_ref, bf16[2048,512]{1,0:T(8,128)(2,1)S(1)} %get-tuple-element.33.feature_ref, ...), custom_call_target="tpu_custom_call" | custom-call | tf_op jit(solution)/shard_map/pallas_call | solution.py:307
  (89 shorter events, 6.9 us)
Async XLA Ops:
  0.0 11.4 %copy-start = (bf16[64,32,512]{2,1,0:T(8,128)(2,1)S(1)}, bf16[64,32,512]{2,1,0:T(8,128)(2,1)}, u32[]{:S(2)}) copy-start(bf16[64,32,512]{2,1,0:T(8,128)(2,1)} %band_ref.7) | copy-start | bytes 6291460
  0.0 18.1 %copy-start.5 = (f32[21,512]{1,0:T(8,128)S(1)}, f32[21,512]{1,0:T(8,128)}, u32[]{:S(2)}) copy-start(f32[21,512]{1,0:T(8,128)} %taps_ref.7) | copy-start | bytes 129028
  2.8 24.2 %collective-permute-start.2 = (bf16[10,64,256]{2,1,0:T(8,128)(2,1)}, bf16[10,64,256]{2,1,0:T(8,128)(2,1)S(1)}, u32[]{:S(2)}, u32[]{:S(2)}) collective-permute-start(bf16[10,64,256]{2,1,0:T(8,128)(2,1)} %get-tuple-element.26), channel_id=1, source_target_pairs={{0,1},{1,2},{2,3},{3,4},{4,5},{5,6},{6,7},{7,8},{8,9},{9,10},{10,1... | collective-permute-start | bytes 983048 | tf_op jit(solution)/shard_map/ppermute | solution.py:363
  4.8 22.2 %collective-permute-start.3 = (bf16[10,64,256]{2,1,0:T(8,128)(2,1)}, bf16[10,64,256]{2,1,0:T(8,128)(2,1)S(1)}, u32[]{:S(2)}, u32[]{:S(2)}) collective-permute-start(bf16[10,64,256]{2,1,0:T(8,128)(2,1)} %get-tuple-element.27), channel_id=1, source_target_pairs={{0,31},{1,0},{2,1},{3,2},{4,3},{5,4},{6,5},{7,6},{8,7},{9,8},{10,9... | collective-permute-start | bytes 983048 | tf_op jit(solution)/shard_map/ppermute | solution.py:363
  13.2 16.5 %collective-permute-start = (bf16[10,64,256]{2,1,0:T(8,128)(2,1)}, bf16[10,64,256]{2,1,0:T(8,128)(2,1)S(1)}, u32[]{:S(2)}, u32[]{:S(2)}) collective-permute-start(bf16[10,64,256]{2,1,0:T(8,128)(2,1)} %get-tuple-element.24), channel_id=1, source_target_pairs={{0,1},{1,2},{2,3},{3,4},{4,5},{5,6},{6,7},{7,8},{8,9},{9,10},{10,1... | collective-permute-start | bytes 983048 | tf_op jit(solution)/shard_map/ppermute | solution.py:363
  13.2 16.5 %collective-permute-start.1 = (bf16[10,64,256]{2,1,0:T(8,128)(2,1)}, bf16[10,64,256]{2,1,0:T(8,128)(2,1)S(1)}, u32[]{:S(2)}, u32[]{:S(2)}) collective-permute-start(bf16[10,64,256]{2,1,0:T(8,128)(2,1)} %get-tuple-element.25), channel_id=1, source_target_pairs={{0,31},{1,0},{2,1},{3,2},{4,3},{5,4},{6,5},{7,6},{8,7},{9,8},{10,9... | collective-permute-start | bytes 983048 | tf_op jit(solution)/shard_map/ppermute | solution.py:363
  29.7 5.6 %copy-start.6 = (f32[21,512]{1,0:T(8,128)S(1)}, f32[21,512]{1,0:T(8,128)}, u32[]{:S(2)}) copy-start(f32[21,512]{1,0:T(8,128)} %taps_ref.9) | copy-start | bytes 129028
  32.5 10.4 %collective-permute-start.5 = (bf16[10,32,512]{2,1,0:T(8,128)(2,1)S(1)}, bf16[10,32,512]{2,1,0:T(8,128)(2,1)S(1)}, u32[]{:S(2)}, u32[]{:S(2)}) collective-permute-start(bf16[10,32,512]{2,1,0:T(8,128)(2,1)S(1)} %get-tuple-element.43), channel_id=1, source_target_pairs={{0,224},{32,0},{64,32},{96,64},{128,96},{160,128},{192,160},{224,1... | collective-permute-start | bytes 983048 | tf_op jit(solution)/shard_map/ppermute | solution.py:393
  34.1 8.9 %copy-start.1 = (bf16[512,512]{1,0:T(8,128)(2,1)S(1)}, bf16[512,512]{1,0:T(8,128)(2,1)}, u32[]{:S(2)}) copy-start(bf16[512,512]{1,0:T(8,128)(2,1)} %w_ref.1) | copy-start | bytes 1572868
  34.1 8.9 %copy-start.2 = (f32[512,64]{0,1:T(8,128)S(1)}, f32[512,64]{0,1:T(8,128)}, u32[]{:S(2)}) copy-start(f32[512,64]{0,1:T(8,128)} %param.11) | copy-start | bytes 393220
  34.1 8.9 %collective-permute-start.4 = (bf16[10,32,512]{2,1,0:T(8,128)(2,1)S(1)}, bf16[10,32,512]{2,1,0:T(8,128)(2,1)S(1)}, u32[]{:S(2)}, u32[]{:S(2)}) collective-permute-start(bf16[10,32,512]{2,1,0:T(8,128)(2,1)S(1)} %get-tuple-element.44), channel_id=1, source_target_pairs={{0,32},{32,64},{64,96},{96,128},{128,160},{160,192},{192,224},{224... | collective-permute-start | bytes 983048 | tf_op jit(solution)/shard_map/ppermute | solution.py:392
  47.7 1.4 collective-permute-start.6
  49.1 3.6 %collective-permute-start.7 = (bf16[32,640]{1,0:T(8,128)(2,1)S(1)}, bf16[32,640]{1,0:T(8,128)(2,1)S(1)}, u32[]{:S(2)}, u32[]{:S(2)}) collective-permute-start(bf16[32,640]{1,0:T(8,128)(2,1)S(1)} %convert_element_type.140), channel_id=1, source_target_pairs={{0,33},{1,32},{2,35},{3,34},{4,37},{5,36},{6,39},{7,38},{8,41},{9,... | collective-permute-start | bytes 122888 | tf_op jit(solution)/shard_map/ppermute | solution.py:191
  52.8 5.0 %collective-permute-start.8 = (bf16[32,640]{1,0:T(8,128)(2,1)S(1)}, bf16[32,640]{1,0:T(8,128)(2,1)S(1)}, u32[]{:S(2)}, u32[]{:S(2)}) collective-permute-start(bf16[32,640]{1,0:T(8,128)(2,1)S(1)} %convert_element_type.142), channel_id=1, source_target_pairs={{0,35},{1,34},{2,33},{3,32},{4,39},{5,38},{6,37},{7,36},{8,43},{9,... | collective-permute-start | bytes 122888 | tf_op jit(solution)/shard_map/ppermute | solution.py:191
  57.8 3.6 %collective-permute-start.9 = (bf16[32,640]{1,0:T(8,128)(2,1)S(1)}, bf16[32,640]{1,0:T(8,128)(2,1)S(1)}, u32[]{:S(2)}, u32[]{:S(2)}) collective-permute-start(bf16[32,640]{1,0:T(8,128)(2,1)S(1)} %convert_element_type.144), channel_id=1, source_target_pairs={{0,96},{1,97},{2,98},{3,99},{4,100},{5,101},{6,102},{7,103},{8,104... | collective-permute-start | bytes 122888 | tf_op jit(solution)/shard_map/ppermute | solution.py:191
  61.4 4.8 %collective-permute-start.10 = (bf16[32,640]{1,0:T(8,128)(2,1)S(1)}, bf16[32,640]{1,0:T(8,128)(2,1)S(1)}, u32[]{:S(2)}, u32[]{:S(2)}) collective-permute-start(bf16[32,640]{1,0:T(8,128)(2,1)S(1)} %convert_element_type.146), channel_id=1, source_target_pairs={{0,224},{1,225},{2,226},{3,227},{4,228},{5,229},{6,230},{7,231},{8... | collective-permute-start | bytes 122888 | tf_op jit(solution)/shard_map/ppermute | solution.py:191
  66.3 3.6 %collective-permute-start.11 = (bf16[32,640]{1,0:T(8,128)(2,1)S(1)}, bf16[32,640]{1,0:T(8,128)(2,1)S(1)}, u32[]{:S(2)}, u32[]{:S(2)}) collective-permute-start(bf16[32,640]{1,0:T(8,128)(2,1)S(1)} %convert_element_type.148), channel_id=1, source_target_pairs={{0,36},{1,37},{2,38},{3,39},{4,32},{5,33},{6,34},{7,35},{8,44},{9,... | collective-permute-start | bytes 122888 | tf_op jit(solution)/shard_map/ppermute | solution.py:191
  69.9 4.8 %collective-permute-start.12 = (bf16[32,640]{1,0:T(8,128)(2,1)S(1)}, bf16[32,640]{1,0:T(8,128)(2,1)S(1)}, u32[]{:S(2)}, u32[]{:S(2)}) collective-permute-start(bf16[32,640]{1,0:T(8,128)(2,1)S(1)} %convert_element_type.150), channel_id=1, source_target_pairs={{0,60},{1,61},{2,62},{3,63},{4,40},{5,41},{6,42},{7,43},{8,36},{9,... | collective-permute-start | bytes 122888 | tf_op jit(solution)/shard_map/ppermute | solution.py:191
  74.8 5.4 %collective-permute-start.13 = (bf16[32,640]{1,0:T(8,128)(2,1)S(1)}, bf16[32,640]{1,0:T(8,128)(2,1)S(1)}, u32[]{:S(2)}, u32[]{:S(2)}) collective-permute-start(bf16[32,640]{1,0:T(8,128)(2,1)S(1)} %convert_element_type.152), channel_id=1, source_target_pairs={{0,44},{1,45},{2,46},{3,47},{4,56},{5,57},{6,58},{7,59},{8,52},{9,... | collective-permute-start | bytes 122888 | tf_op jit(solution)/shard_map/ppermute | solution.py:191
  80.2 1.4 collective-permute-start.14
  84.1 1.3 collective-permute-start.15
  85.5 3.6 %collective-permute-start.16 = (bf16[32,640]{1,0:T(8,128)(2,1)S(1)}, bf16[32,640]{1,0:T(8,128)(2,1)S(1)}, u32[]{:S(2)}, u32[]{:S(2)}) collective-permute-start(bf16[32,640]{1,0:T(8,128)(2,1)S(1)} %convert_element_type.155), channel_id=1, source_target_pairs={{0,33},{1,32},{2,35},{3,34},{4,37},{5,36},{6,39},{7,38},{8,41},{9,... | collective-permute-start | bytes 122888 | tf_op jit(solution)/shard_map/ppermute | solution.py:191
  89.1 4.8 %collective-permute-start.17 = (bf16[32,640]{1,0:T(8,128)(2,1)S(1)}, bf16[32,640]{1,0:T(8,128)(2,1)S(1)}, u32[]{:S(2)}, u32[]{:S(2)}) collective-permute-start(bf16[32,640]{1,0:T(8,128)(2,1)S(1)} %convert_element_type.157), channel_id=1, source_target_pairs={{0,35},{1,34},{2,33},{3,32},{4,39},{5,38},{6,37},{7,36},{8,43},{9,... | collective-permute-start | bytes 122888 | tf_op jit(solution)/shard_map/ppermute | solution.py:191
  94.0 3.6 %collective-permute-start.18 = (bf16[32,640]{1,0:T(8,128)(2,1)S(1)}, bf16[32,640]{1,0:T(8,128)(2,1)S(1)}, u32[]{:S(2)}, u32[]{:S(2)}) collective-permute-start(bf16[32,640]{1,0:T(8,128)(2,1)S(1)} %convert_element_type.159), channel_id=1, source_target_pairs={{0,96},{1,97},{2,98},{3,99},{4,100},{5,101},{6,102},{7,103},{8,104... | collective-permute-start | bytes 122888 | tf_op jit(solution)/shard_map/ppermute | solution.py:191
  97.6 4.8 %collective-permute-start.19 = (bf16[32,640]{1,0:T(8,128)(2,1)S(1)}, bf16[32,640]{1,0:T(8,128)(2,1)S(1)}, u32[]{:S(2)}, u32[]{:S(2)}) collective-permute-start(bf16[32,640]{1,0:T(8,128)(2,1)S(1)} %convert_element_type.161), channel_id=1, source_target_pairs={{0,224},{1,225},{2,226},{3,227},{4,228},{5,229},{6,230},{7,231},{8... | collective-permute-start | bytes 122888 | tf_op jit(solution)/shard_map/ppermute | solution.py:191
  102.4 3.6 %collective-permute-start.20 = (bf16[32,640]{1,0:T(8,128)(2,1)S(1)}, bf16[32,640]{1,0:T(8,128)(2,1)S(1)}, u32[]{:S(2)}, u32[]{:S(2)}) collective-permute-start(bf16[32,640]{1,0:T(8,128)(2,1)S(1)} %convert_element_type.163), channel_id=1, source_target_pairs={{0,36},{1,37},{2,38},{3,39},{4,32},{5,33},{6,34},{7,35},{8,44},{9,... | collective-permute-start | bytes 122888 | tf_op jit(solution)/shard_map/ppermute | solution.py:191
  106.1 4.8 %collective-permute-start.21 = (bf16[32,640]{1,0:T(8,128)(2,1)S(1)}, bf16[32,640]{1,0:T(8,128)(2,1)S(1)}, u32[]{:S(2)}, u32[]{:S(2)}) collective-permute-start(bf16[32,640]{1,0:T(8,128)(2,1)S(1)} %convert_element_type.165), channel_id=1, source_target_pairs={{0,60},{1,61},{2,62},{3,63},{4,40},{5,41},{6,42},{7,43},{8,36},{9,... | collective-permute-start | bytes 122888 | tf_op jit(solution)/shard_map/ppermute | solution.py:191
  110.9 6.4 %collective-permute-start.22 = (bf16[32,640]{1,0:T(8,128)(2,1)S(1)}, bf16[32,640]{1,0:T(8,128)(2,1)S(1)}, u32[]{:S(2)}, u32[]{:S(2)}) collective-permute-start(bf16[32,640]{1,0:T(8,128)(2,1)S(1)} %convert_element_type.167), channel_id=1, source_target_pairs={{0,44},{1,45},{2,46},{3,47},{4,56},{5,57},{6,58},{7,59},{8,52},{9,... | collective-permute-start | bytes 122888 | tf_op jit(solution)/shard_map/ppermute | solution.py:191
  117.3 1.4 collective-permute-start.23
  121.3 34.8 %copy-start.3 = (bf16[512,512]{1,0:T(8,128)(2,1)S(1)}, bf16[512,512]{1,0:T(8,128)(2,1)}, u32[]{:S(2)}) copy-start(bf16[512,512]{1,0:T(8,128)(2,1)} %wham_ref.1) | copy-start | bytes 1572868
  121.3 34.7 %copy-start.4 = (bf16[512,512]{1,0:T(8,128)(2,1)S(1)}, bf16[512,512]{1,0:T(8,128)(2,1)}, u32[]{:S(2)}) copy-start(bf16[512,512]{1,0:T(8,128)(2,1)} %walign_ref.1) | copy-start | bytes 1572868
  121.3 1.5 collective-permute-start.24
  122.9 3.6 %collective-permute-start.25 = (bf16[32,640]{1,0:T(8,128)(2,1)S(1)}, bf16[32,640]{1,0:T(8,128)(2,1)S(1)}, u32[]{:S(2)}, u32[]{:S(2)}) collective-permute-start(bf16[32,640]{1,0:T(8,128)(2,1)S(1)} %convert_element_type.170), channel_id=1, source_target_pairs={{0,33},{1,32},{2,35},{3,34},{4,37},{5,36},{6,39},{7,38},{8,41},{9,... | collective-permute-start | bytes 122888 | tf_op jit(solution)/shard_map/ppermute | solution.py:191
  126.5 4.8 %collective-permute-start.26 = (bf16[32,640]{1,0:T(8,128)(2,1)S(1)}, bf16[32,640]{1,0:T(8,128)(2,1)S(1)}, u32[]{:S(2)}, u32[]{:S(2)}) collective-permute-start(bf16[32,640]{1,0:T(8,128)(2,1)S(1)} %convert_element_type.172), channel_id=1, source_target_pairs={{0,35},{1,34},{2,33},{3,32},{4,39},{5,38},{6,37},{7,36},{8,43},{9,... | collective-permute-start | bytes 122888 | tf_op jit(solution)/shard_map/ppermute | solution.py:191
  131.4 3.6 %collective-permute-start.27 = (bf16[32,640]{1,0:T(8,128)(2,1)S(1)}, bf16[32,640]{1,0:T(8,128)(2,1)S(1)}, u32[]{:S(2)}, u32[]{:S(2)}) collective-permute-start(bf16[32,640]{1,0:T(8,128)(2,1)S(1)} %convert_element_type.174), channel_id=1, source_target_pairs={{0,96},{1,97},{2,98},{3,99},{4,100},{5,101},{6,102},{7,103},{8,104... | collective-permute-start | bytes 122888 | tf_op jit(solution)/shard_map/ppermute | solution.py:191
  135.0 4.8 %collective-permute-start.28 = (bf16[32,640]{1,0:T(8,128)(2,1)S(1)}, bf16[32,640]{1,0:T(8,128)(2,1)S(1)}, u32[]{:S(2)}, u32[]{:S(2)}) collective-permute-start(bf16[32,640]{1,0:T(8,128)(2,1)S(1)} %convert_element_type.176), channel_id=1, source_target_pairs={{0,224},{1,225},{2,226},{3,227},{4,228},{5,229},{6,230},{7,231},{8... | collective-permute-start | bytes 122888 | tf_op jit(solution)/shard_map/ppermute | solution.py:191
  139.8 3.6 %collective-permute-start.29 = (bf16[32,640]{1,0:T(8,128)(2,1)S(1)}, bf16[32,640]{1,0:T(8,128)(2,1)S(1)}, u32[]{:S(2)}, u32[]{:S(2)}) collective-permute-start(bf16[32,640]{1,0:T(8,128)(2,1)S(1)} %convert_element_type.178), channel_id=1, source_target_pairs={{0,36},{1,37},{2,38},{3,39},{4,32},{5,33},{6,34},{7,35},{8,44},{9,... | collective-permute-start | bytes 122888 | tf_op jit(solution)/shard_map/ppermute | solution.py:191
  143.5 4.8 %collective-permute-start.30 = (bf16[32,640]{1,0:T(8,128)(2,1)S(1)}, bf16[32,640]{1,0:T(8,128)(2,1)S(1)}, u32[]{:S(2)}, u32[]{:S(2)}) collective-permute-start(bf16[32,640]{1,0:T(8,128)(2,1)S(1)} %convert_element_type.180), channel_id=1, source_target_pairs={{0,60},{1,61},{2,62},{3,63},{4,40},{5,41},{6,42},{7,43},{8,36},{9,... | collective-permute-start | bytes 122888 | tf_op jit(solution)/shard_map/ppermute | solution.py:191
  148.3 6.3 %collective-permute-start.31 = (bf16[32,640]{1,0:T(8,128)(2,1)S(1)}, bf16[32,640]{1,0:T(8,128)(2,1)S(1)}, u32[]{:S(2)}, u32[]{:S(2)}) collective-permute-start(bf16[32,640]{1,0:T(8,128)(2,1)S(1)} %convert_element_type.182), channel_id=1, source_target_pairs={{0,44},{1,45},{2,46},{3,47},{4,56},{5,57},{6,58},{7,59},{8,52},{9,... | collective-permute-start | bytes 122888 | tf_op jit(solution)/shard_map/ppermute | solution.py:191
  154.6 1.4 collective-permute-start.32

commit v9 on v4

--- a/solution.py
+++ b/solution.py
@@ -221,25 +221,32 @@
 
 
 def first_kernel(
-    flags_ref, mid_ref, top_ref, low_ref, above_ref, below_ref, taps_ref, w_ref, basis_ref,
+    flags_ref, mid_ref, top_ref, low_ref, near_ref, far_ref, taps_ref, w_ref, basis_ref,
     feature_ref, coeffs_ref, mine_ref, theirs_ref,
 ):
     rows, cols, channels = mid_ref.shape
     edge, mid = MARGIN * cols, rows * cols
     w = w_ref[...]
-    top = finished_edge(
-        top_ref, above_ref, taps_ref, flags_ref[3] == 1, lambda o: [(j - o, j) for j in range(o, MARGIN)]
-    )
-    low = finished_edge(
-        low_ref, below_ref, taps_ref, flags_ref[4] == 1, lambda o: [(2 * MARGIN + j - o, j) for j in range(o + 1)]
-    )
 
     def squeezed(mixed):
         return jnp.maximum(dot(mixed, w, NN), 0.0).astype(BF)
 
-    feature_ref[:edge] = squeezed(top)
+    for core, (above_ref, below_ref) in enumerate(((far_ref, near_ref), (near_ref, far_ref))):
+
+        @pl.when(flags_ref[5] == core)
+        def _(above_ref=above_ref, below_ref=below_ref):
+            top = finished_edge(
+                top_ref, above_ref, taps_ref, flags_ref[3] == 1,
+                lambda o: [(j - o, j) for j in range(o, MARGIN)],
+            )
+            low = finished_edge(
+                low_ref, below_ref, taps_ref, flags_ref[4] == 1,
+                lambda o: [(2 * MARGIN + j - o, j) for j in range(o + 1)],
+            )
+            feature_ref[:edge] = squeezed(top)
+            feature_ref[edge + mid :] = squeezed(low)
+
     feature_ref[edge : edge + mid] = squeezed(mid_ref[...].reshape(mid, channels))
-    feature_ref[edge + mid :] = squeezed(low)
     feature = feature_ref[...]
     basis = basis_ref[...]
     scores = dot(basis.astype(BF), feature, NT)
@@ -301,7 +308,7 @@
     index = {name: lax.axis_index(name) for name in ALL}
     half = sum(index.values()) % 2
     row, col = lax.axis_index(ROWS), lax.axis_index(COLS)
-    flags = [half, col > 0, col < Z * X - 1, row > 0, row < Y * CORE - 1]
+    flags = [half, col > 0, col < Z * X - 1, row > 0, row < Y * CORE - 1, index["core"]]
     flags = jnp.stack([f.astype(jnp.int32) for f in flags])
     sds = jax.ShapeDtypeStruct
 
@@ -344,8 +351,13 @@
         scratch_shapes=[pltpu.VMEM((margin, tile_rows, LANES), F32)] * 2 + [flat],
         compiler_params=params,
     )(flags, own, left, right, column_taps)
-    above = lax.ppermute(filtered[tile_rows - margin :], ROWS, ring(Y * CORE, 1))
-    below = lax.ppermute(filtered[:margin], ROWS, ring(Y * CORE, -1))
+    bottom = tile_rows - margin
+    even = index["core"] == 0
+    to_far = lax.dynamic_slice_in_dim(filtered, jnp.where(even, 0, bottom), margin)
+    to_near = lax.dynamic_slice_in_dim(filtered, jnp.where(even, bottom, 0), margin)
+    chips = [(i, (i + 1) % (Y * CORE)) for i in range(1, Y * CORE, 2)]
+    far = lax.ppermute(to_far, ROWS, chips + [(j, i) for i, j in chips])
+    near = lax.ppermute(to_near, "core", [(0, 1), (1, 0)])
     rest = tile_rows - 2 * margin
     mid, top, low = pl.pallas_call(
         rows_own_kernel,
@@ -372,7 +384,7 @@
     feature, coeffs, mine, theirs = call(
         first_kernel,
         [sds((n, channels), BF), sds((r, n), F32)] + sums,
-        flags, mid, top, low, above, below, row_taps, w_squeeze, basis,
+        flags, mid, top, low, near, far, row_taps, w_squeeze, basis,
     )
     for _ in range(STEPS - 1):
         own, got = summed_over_all(mine, theirs)

time: 161 us -> 163 us (1.012)
  waiting for transfers between devices: 64.8 us -> 72.4 us
  starting transfers between devices: 53.1 us -> 47.1 us
    ppermute x21, waiting for transfers between devices: 54.1 us -> 62.3 us  [summed_over_all(): got = lax.ppermute(total.astype(BF), ALL, round_pairs(axis, rule))]
    ppermute x21, starting transfers between devices: 39.6 us -> 31.5 us  [summed_over_all(): got = lax.ppermute(total.astype(BF), ALL, round_pairs(axis, rule))]
where the time goes in v9:
time: 163 us
  waiting for transfers between devices  72.4 us (44%)
  starting transfers between devices  47.1 us (29%)
  Pallas kernels  37.6 us (23%)
  local copies, waits for them, and re-layouts  4.56 us (3%)
    ppermute x21, waiting for transfers between devices, summed_over_all(): got = lax.ppermute(total.astype(BF), ALL, round_pairs(axis, rule))  62.3 us
    ppermute x21, starting transfers between devices, summed_over_all(): got = lax.ppermute(total.astype(BF), ALL, round_pairs(axis, rule))  31.5 us
    pallas_call x4, Pallas kernels, call(): pl.pallas_call(kernel, out_shape=outs, in_specs=specs, out_specs=jax.tree...  16 us
    pallas_call x1, Pallas kernels, on_device(): pl.pallas_call(columns_own_kernel, grid=grid, in_specs=[tile, taps], out_...  8.92 us
    pallas_call x1, Pallas kernels, on_device(): pl.pallas_call(rows_own_kernel, grid=grid, in_specs=[tile, tile, taps], o...  7.66 us
    ppermute x1, starting transfers between devices, on_device(): right = lax.ppermute(right, COLS, ring(Z * X, -1))  6.56 us
    pallas_call x1, Pallas kernels, on_device(): pl.pallas_call(columns_rest_kernel, grid=grid, in_specs=[scalar, turned,...  5.01 us
    ppermute x1, waiting for transfers between devices, on_device(): left = lax.ppermute(left, COLS, ring(Z * X, 1))  4.41 us
  transfers between devices with their start and end apart: 31, of which 29 were waited for; matrix products, arithmetic and copies ran while one was open for 1% of the time, Pallas kernels for 10%

profile of v9, /device:TPU:1, one launch (start us, length us, event | category | flops | bytes accessed | tf_op | source)
XLA Modules:
  0.0 162.5 jit_solution(1096780766047256902)
XLA Ops:
  0.0 2.0 %fusion = (bf16[64,10,512]{2,1,0:T(8,128)(2,1)S(1)}, bf16[64,10,512]{2,1,0:T(8,128)(2,1)S(1)}) fusion(bf16[64,32,512]{2,1,0:T(8,128)(2,1)} %band_ref.3), kind=kLoop, calls=%fused_computation.28 | loop fusion | bytes 2621440 | tf_op jit(solution)/shard_map/slice | solution.py:319
  2.0 1.2 copy.15
  3.2 2.0 %collective-permute-start = (bf16[10,64,512]{2,1,0:T(8,128)(2,1)}, bf16[10,64,512]{2,1,0:T(8,128)(2,1)S(1)}, u32[]{:S(2)}, u32[]{:S(2)}) collective-permute-start(bf16[10,64,512]{2,1,0:T(8,128)(2,1)} %bitcast.13), channel_id=1, source_target_pairs={{0,1},{1,2},{2,3},{3,4},{4,5},{5,6},{6,7},{7,8},{8,9},{9,10},{10,1... | collective-permute-start | bytes 1966088 | tf_op jit(solution)/shard_map/ppermute | solution.py:320
  5.3 1.2 copy.14
  6.5 6.6 %collective-permute-start.1 = (bf16[10,64,512]{2,1,0:T(8,128)(2,1)}, bf16[10,64,512]{2,1,0:T(8,128)(2,1)S(1)}, u32[]{:S(2)}, u32[]{:S(2)}) collective-permute-start(bf16[10,64,512]{2,1,0:T(8,128)(2,1)} %bitcast.12), channel_id=1, source_target_pairs={{0,31},{1,0},{2,1},{3,2},{4,3},{5,4},{6,5},{7,6},{8,7},{9,8},{10,9... | collective-permute-start | bytes 1966088 | tf_op jit(solution)/shard_map/ppermute | solution.py:321
  13.1 8.9 %shard_map.73.own_ref = f32[32,64,512]{2,1,0:T(8,128)S(1)} custom-call(bf16[64,32,512]{2,1,0:T(8,128)(2,1)S(1)} %copy-done, f32[21,512]{1,0:T(8,128)S(1)} %copy-done.5), custom_call_target="tpu_custom_call" | custom-call | flops 44040192 | bytes 6291456 | tf_op jit(solution)/shard_map/pallas_call | solution.py:335
  22.0 4.4 %collective-permute-done.left_ref = bf16[10,64,512]{2,1,0:T(8,128)(2,1)S(1)} collective-permute-done((bf16[10,64,512]{2,1,0:T(8,128)(2,1)}, bf16[10,64,512]{2,1,0:T(8,128)(2,1)S(1)}, u32[]{:S(2)}, u32[]{:S(2)}) %collective-permute-start) | collective-permute-done | bytes 655392 | tf_op jit(solution)/shard_map/ppermute | solution.py:320
  26.7 5.0 %shard_map.74.filtered_ref = bf16[64,32,512]{2,1,0:T(8,128)(2,1)S(1)} custom-call(s32[6]{0:T(128)S(1)} %stack.43.flags_ref.half_ref, f32[32,64,512]{2,1,0:T(8,128)S(1)} %shard_map.73.own_ref, bf16[10,64,512]{2,1,0:T(8,128)(2,1)S(1)} %collective-permute-done.left_ref, bf16[10,64,512]{2,1,0:T(8,128)(2,1)S(1)} %collective-permute-done.1.right_ref, ...), custom_call_target="tpu_custom_call" | custom-call | tf_op jit(solution)/shard_map/pallas_call | solution.py:345
  31.8 1.6 collective-permute-start.2
  33.5 1.3 collective-permute-start.3
  34.8 7.7 %shard_map.75 = (bf16[44,32,512]{2,1,0:T(8,128)(2,1)S(1)}, f32[10,32,512]{2,1,0:T(8,128)S(1)}, f32[10,32,512]{2,1,0:T(8,128)S(1)}) custom-call(bf16[64,32,512]{2,1,0:T(8,128)(2,1)S(1)} %shard_map.74.filtered_ref, bf16[64,32,512]{2,1,0:T(8,128)(2,1)S(1)} %copy-done, f32[21,512]{1,0:T(8,128)S(1)} %copy-done.6), custom_call_target="tpu_custom_call" | custom-call | flops 44040192 | bytes 6291456 | tf_op jit(solution)/shard_map/pallas_call | solution.py:362
  42.5 4.2 %shard_map.76 = (bf16[2048,512]{1,0:T(8,128)(2,1)S(1)}, f32[64,2048]{1,0:T(8,128)S(1)}, f32[32,640]{1,0:T(8,128)S(1)}, bf16[32,640]{1,0:T(8,128)(2,1)S(1)}) custom-call(s32[6]{0:T(128)S(1)} %stack.43.flags_ref.half_ref, bf16[44,32,512]{2,1,0:T(8,128)(2,1)S(1)} %get-tuple-element.20.mid_ref, f32[10,32,512]{2,1,0:T(8,128)S(1)} %get-tuple-element.21.top_ref, ...), custom_call_target="tpu_custom_call" | custom-call | tf_op jit(solution)/shard_map/pallas_call | solution.py:296
  46.7 1.9 %collective-permute-start.4 = (bf16[32,640]{1,0:T(8,128)(2,1)S(1)}, bf16[32,640]{1,0:T(8,128)(2,1)S(1)}, u32[]{:S(2)}, u32[]{:S(2)}) collective-permute-start(bf16[32,640]{1,0:T(8,128)(2,1)S(1)} %get-tuple-element.24), channel_id=1, source_target_pairs={{0,32},{32,0},{1,33},{33,1},{2,34},{34,2},{3,35},{35,3},{4,36},{36... | collective-permute-start | bytes 122888 | tf_op jit(solution)/shard_map/ppermute | solution.py:178
  49.6 3.5 %collective-permute-done.5 = bf16[32,640]{1,0:T(8,128)(2,1)S(1)} collective-permute-done((bf16[32,640]{1,0:T(8,128)(2,1)S(1)}, bf16[32,640]{1,0:T(8,128)(2,1)S(1)}, u32[]{:S(2)}, u32[]{:S(2)}) %collective-permute-start.5) | collective-permute-done | bytes 40992 | tf_op jit(solution)/shard_map/ppermute | solution.py:181
  53.9 4.0 %collective-permute-done.6 = bf16[32,640]{1,0:T(8,128)(2,1)S(1)} collective-permute-done((bf16[32,640]{1,0:T(8,128)(2,1)S(1)}, bf16[32,640]{1,0:T(8,128)(2,1)S(1)}, u32[]{:S(2)}, u32[]{:S(2)}) %collective-permute-start.6) | collective-permute-done | bytes 40992 | tf_op jit(solution)/shard_map/ppermute | solution.py:181
  58.2 3.5 %collective-permute-done.7 = bf16[32,640]{1,0:T(8,128)(2,1)S(1)} collective-permute-done((bf16[32,640]{1,0:T(8,128)(2,1)S(1)}, bf16[32,640]{1,0:T(8,128)(2,1)S(1)}, u32[]{:S(2)}, u32[]{:S(2)}) %collective-permute-start.7) | collective-permute-done | bytes 40992 | tf_op jit(solution)/shard_map/ppermute | solution.py:181
  62.5 4.0 %collective-permute-done.8 = bf16[32,640]{1,0:T(8,128)(2,1)S(1)} collective-permute-done((bf16[32,640]{1,0:T(8,128)(2,1)S(1)}, bf16[32,640]{1,0:T(8,128)(2,1)S(1)}, u32[]{:S(2)}, u32[]{:S(2)}) %collective-permute-start.8) | collective-permute-done | bytes 40992 | tf_op jit(solution)/shard_map/ppermute | solution.py:181
  66.7 3.5 %collective-permute-done.9 = bf16[32,640]{1,0:T(8,128)(2,1)S(1)} collective-permute-done((bf16[32,640]{1,0:T(8,128)(2,1)S(1)}, bf16[32,640]{1,0:T(8,128)(2,1)S(1)}, u32[]{:S(2)}, u32[]{:S(2)}) %collective-permute-start.9) | collective-permute-done | bytes 40992 | tf_op jit(solution)/shard_map/ppermute | solution.py:181
  70.3 2.7 %collective-permute-start.10 = (bf16[32,640]{1,0:T(8,128)(2,1)S(1)}, bf16[32,640]{1,0:T(8,128)(2,1)S(1)}, u32[]{:S(2)}, u32[]{:S(2)}) collective-permute-start(bf16[32,640]{1,0:T(8,128)(2,1)S(1)} %convert_element_type.150), channel_id=1, source_target_pairs={{0,60},{1,61},{2,62},{3,63},{4,40},{5,41},{6,42},{7,43},{8,36},{9,... | collective-permute-start | bytes 122888 | tf_op jit(solution)/shard_map/ppermute | solution.py:181
  73.0 2.1 %collective-permute-done.10 = bf16[32,640]{1,0:T(8,128)(2,1)S(1)} collective-permute-done((bf16[32,640]{1,0:T(8,128)(2,1)S(1)}, bf16[32,640]{1,0:T(8,128)(2,1)S(1)}, u32[]{:S(2)}, u32[]{:S(2)}) %collective-permute-start.10) | collective-permute-done | bytes 40992 | tf_op jit(solution)/shard_map/ppermute | solution.py:181
  75.1 4.2 %collective-permute-start.11 = (bf16[32,640]{1,0:T(8,128)(2,1)S(1)}, bf16[32,640]{1,0:T(8,128)(2,1)S(1)}, u32[]{:S(2)}, u32[]{:S(2)}) collective-permute-start(bf16[32,640]{1,0:T(8,128)(2,1)S(1)} %convert_element_type.152), channel_id=1, source_target_pairs={{0,44},{1,45},{2,46},{3,47},{4,56},{5,57},{6,58},{7,59},{8,52},{9,... | collective-permute-start | bytes 122888 | tf_op jit(solution)/shard_map/ppermute | solution.py:181
  79.3 1.8 %collective-permute-done.11 = bf16[32,640]{1,0:T(8,128)(2,1)S(1)} collective-permute-done((bf16[32,640]{1,0:T(8,128)(2,1)S(1)}, bf16[32,640]{1,0:T(8,128)(2,1)S(1)}, u32[]{:S(2)}, u32[]{:S(2)}) %collective-permute-start.11) | collective-permute-done | bytes 40992 | tf_op jit(solution)/shard_map/ppermute | solution.py:181
  81.5 0.9 collective-permute-done.12.got_ref
  82.4 2.7 %shard_map.77 = (f32[64,512]{1,0:T(8,128)S(1)}, f32[64,2048]{1,0:T(8,128)S(1)}, f32[32,640]{1,0:T(8,128)S(1)}, bf16[32,640]{1,0:T(8,128)(2,1)S(1)}) custom-call(s32[6]{0:T(128)S(1)} %stack.43.flags_ref.half_ref, f32[32,640]{1,0:T(8,128)S(1)} %convert_add_fusion.16.own_ref, f32[32,640]{1,0:T(8,128)S(1)} %collective-permute-done.12.got_ref, ...), custom_call_target="tpu_custom_call" | custom-call | tf_op jit(solution)/shard_map/pallas_call | solution.py:296
  86.6 3.5 %collective-permute-done.14 = bf16[32,640]{1,0:T(8,128)(2,1)S(1)} collective-permute-done((bf16[32,640]{1,0:T(8,128)(2,1)S(1)}, bf16[32,640]{1,0:T(8,128)(2,1)S(1)}, u32[]{:S(2)}, u32[]{:S(2)}) %collective-permute-start.14) | collective-permute-done | bytes 40992 | tf_op jit(solution)/shard_map/ppermute | solution.py:181
  90.1 3.3 %collective-permute-start.15 = (bf16[32,640]{1,0:T(8,128)(2,1)S(1)}, bf16[32,640]{1,0:T(8,128)(2,1)S(1)}, u32[]{:S(2)}, u32[]{:S(2)}) collective-permute-start(bf16[32,640]{1,0:T(8,128)(2,1)S(1)} %convert_element_type.157), channel_id=1, source_target_pairs={{0,35},{1,34},{2,33},{3,32},{4,39},{5,38},{6,37},{7,36},{8,43},{9,... | collective-permute-start | bytes 122888 | tf_op jit(solution)/shard_map/ppermute | solution.py:181
  93.5 1.8 %collective-permute-done.15 = bf16[32,640]{1,0:T(8,128)(2,1)S(1)} collective-permute-done((bf16[32,640]{1,0:T(8,128)(2,1)S(1)}, bf16[32,640]{1,0:T(8,128)(2,1)S(1)}, u32[]{:S(2)}, u32[]{:S(2)}) %collective-permute-start.15) | collective-permute-done | bytes 40992 | tf_op jit(solution)/shard_map/ppermute | solution.py:181
  95.4 3.5 %collective-permute-done.16 = bf16[32,640]{1,0:T(8,128)(2,1)S(1)} collective-permute-done((bf16[32,640]{1,0:T(8,128)(2,1)S(1)}, bf16[32,640]{1,0:T(8,128)(2,1)S(1)}, u32[]{:S(2)}, u32[]{:S(2)}) %collective-permute-start.16) | collective-permute-done | bytes 40992 | tf_op jit(solution)/shard_map/ppermute | solution.py:181
  99.7 4.0 %collective-permute-done.17 = bf16[32,640]{1,0:T(8,128)(2,1)S(1)} collective-permute-done((bf16[32,640]{1,0:T(8,128)(2,1)S(1)}, bf16[32,640]{1,0:T(8,128)(2,1)S(1)}, u32[]{:S(2)}, u32[]{:S(2)}) %collective-permute-start.17) | collective-permute-done | bytes 40992 | tf_op jit(solution)/shard_map/ppermute | solution.py:181
  104.6 2.8 %collective-permute-done.18 = bf16[32,640]{1,0:T(8,128)(2,1)S(1)} collective-permute-done((bf16[32,640]{1,0:T(8,128)(2,1)S(1)}, bf16[32,640]{1,0:T(8,128)(2,1)S(1)}, u32[]{:S(2)}, u32[]{:S(2)}) %collective-permute-start.18) | collective-permute-done | bytes 40992 | tf_op jit(solution)/shard_map/ppermute | solution.py:181
  107.4 2.8 %collective-permute-start.19 = (bf16[32,640]{1,0:T(8,128)(2,1)S(1)}, bf16[32,640]{1,0:T(8,128)(2,1)S(1)}, u32[]{:S(2)}, u32[]{:S(2)}) collective-permute-start(bf16[32,640]{1,0:T(8,128)(2,1)S(1)} %convert_element_type.165), channel_id=1, source_target_pairs={{0,60},{1,61},{2,62},{3,63},{4,40},{5,41},{6,42},{7,43},{8,36},{9,... | collective-permute-start | bytes 122888 | tf_op jit(solution)/shard_map/ppermute | solution.py:181
  110.2 2.0 %collective-permute-done.19 = bf16[32,640]{1,0:T(8,128)(2,1)S(1)} collective-permute-done((bf16[32,640]{1,0:T(8,128)(2,1)S(1)}, bf16[32,640]{1,0:T(8,128)(2,1)S(1)}, u32[]{:S(2)}, u32[]{:S(2)}) %collective-permute-start.19) | collective-permute-done | bytes 40992 | tf_op jit(solution)/shard_map/ppermute | solution.py:181
  112.2 3.3 %collective-permute-start.20 = (bf16[32,640]{1,0:T(8,128)(2,1)S(1)}, bf16[32,640]{1,0:T(8,128)(2,1)S(1)}, u32[]{:S(2)}, u32[]{:S(2)}) collective-permute-start(bf16[32,640]{1,0:T(8,128)(2,1)S(1)} %convert_element_type.167), channel_id=1, source_target_pairs={{0,44},{1,45},{2,46},{3,47},{4,56},{5,57},{6,58},{7,59},{8,52},{9,... | collective-permute-start | bytes 122888 | tf_op jit(solution)/shard_map/ppermute | solution.py:181
  115.6 2.1 %collective-permute-done.20 = bf16[32,640]{1,0:T(8,128)(2,1)S(1)} collective-permute-done((bf16[32,640]{1,0:T(8,128)(2,1)S(1)}, bf16[32,640]{1,0:T(8,128)(2,1)S(1)}, u32[]{:S(2)}, u32[]{:S(2)}) %collective-permute-start.20) | collective-permute-done | bytes 40992 | tf_op jit(solution)/shard_map/ppermute | solution.py:181
  118.1 0.9 collective-permute-done.21.got_ref
  119.0 2.7 %shard_map.78 = (f32[64,512]{1,0:T(8,128)S(1)}, f32[64,2048]{1,0:T(8,128)S(1)}, f32[32,640]{1,0:T(8,128)S(1)}, bf16[32,640]{1,0:T(8,128)(2,1)S(1)}) custom-call(s32[6]{0:T(128)S(1)} %stack.43.flags_ref.half_ref, f32[32,640]{1,0:T(8,128)S(1)} %convert_add_fusion.8.own_ref, f32[32,640]{1,0:T(8,128)S(1)} %collective-permute-done.21.got_ref, ...), custom_call_target="tpu_custom_call" | custom-call | tf_op jit(solution)/shard_map/pallas_call | solution.py:296
  123.2 3.5 %collective-permute-done.23 = bf16[32,640]{1,0:T(8,128)(2,1)S(1)} collective-permute-done((bf16[32,640]{1,0:T(8,128)(2,1)S(1)}, bf16[32,640]{1,0:T(8,128)(2,1)S(1)}, u32[]{:S(2)}, u32[]{:S(2)}) %collective-permute-start.23) | collective-permute-done | bytes 40992 | tf_op jit(solution)/shard_map/ppermute | solution.py:181
  126.8 3.0 %collective-permute-start.24 = (bf16[32,640]{1,0:T(8,128)(2,1)S(1)}, bf16[32,640]{1,0:T(8,128)(2,1)S(1)}, u32[]{:S(2)}, u32[]{:S(2)}) collective-permute-start(bf16[32,640]{1,0:T(8,128)(2,1)S(1)} %convert_element_type.172), channel_id=1, source_target_pairs={{0,35},{1,34},{2,33},{3,32},{4,39},{5,38},{6,37},{7,36},{8,43},{9,... | collective-permute-start | bytes 122888 | tf_op jit(solution)/shard_map/ppermute | solution.py:181
  129.8 1.8 %collective-permute-done.24 = bf16[32,640]{1,0:T(8,128)(2,1)S(1)} collective-permute-done((bf16[32,640]{1,0:T(8,128)(2,1)S(1)}, bf16[32,640]{1,0:T(8,128)(2,1)S(1)}, u32[]{:S(2)}, u32[]{:S(2)}) %collective-permute-start.24) | collective-permute-done | bytes 40992 | tf_op jit(solution)/shard_map/ppermute | solution.py:181
  131.9 3.5 %collective-permute-done.25 = bf16[32,640]{1,0:T(8,128)(2,1)S(1)} collective-permute-done((bf16[32,640]{1,0:T(8,128)(2,1)S(1)}, bf16[32,640]{1,0:T(8,128)(2,1)S(1)}, u32[]{:S(2)}, u32[]{:S(2)}) %collective-permute-start.25) | collective-permute-done | bytes 40992 | tf_op jit(solution)/shard_map/ppermute | solution.py:181
  136.2 4.0 %collective-permute-done.26 = bf16[32,640]{1,0:T(8,128)(2,1)S(1)} collective-permute-done((bf16[32,640]{1,0:T(8,128)(2,1)S(1)}, bf16[32,640]{1,0:T(8,128)(2,1)S(1)}, u32[]{:S(2)}, u32[]{:S(2)}) %collective-permute-start.26) | collective-permute-done | bytes 40992 | tf_op jit(solution)/shard_map/ppermute | solution.py:181
  141.1 2.8 %collective-permute-done.27 = bf16[32,640]{1,0:T(8,128)(2,1)S(1)} collective-permute-done((bf16[32,640]{1,0:T(8,128)(2,1)S(1)}, bf16[32,640]{1,0:T(8,128)(2,1)S(1)}, u32[]{:S(2)}, u32[]{:S(2)}) %collective-permute-start.27) | collective-permute-done | bytes 40992 | tf_op jit(solution)/shard_map/ppermute | solution.py:181
  143.9 3.5 %collective-permute-start.28 = (bf16[32,640]{1,0:T(8,128)(2,1)S(1)}, bf16[32,640]{1,0:T(8,128)(2,1)S(1)}, u32[]{:S(2)}, u32[]{:S(2)}) collective-permute-start(bf16[32,640]{1,0:T(8,128)(2,1)S(1)} %convert_element_type.180), channel_id=1, source_target_pairs={{0,60},{1,61},{2,62},{3,63},{4,40},{5,41},{6,42},{7,43},{8,36},{9,... | collective-permute-start | bytes 122888 | tf_op jit(solution)/shard_map/ppermute | solution.py:181
  147.5 1.8 %collective-permute-done.28 = bf16[32,640]{1,0:T(8,128)(2,1)S(1)} collective-permute-done((bf16[32,640]{1,0:T(8,128)(2,1)S(1)}, bf16[32,640]{1,0:T(8,128)(2,1)S(1)}, u32[]{:S(2)}, u32[]{:S(2)}) %collective-permute-start.28) | collective-permute-done | bytes 40992 | tf_op jit(solution)/shard_map/ppermute | solution.py:181
  149.3 2.9 %collective-permute-start.29 = (bf16[32,640]{1,0:T(8,128)(2,1)S(1)}, bf16[32,640]{1,0:T(8,128)(2,1)S(1)}, u32[]{:S(2)}, u32[]{:S(2)}) collective-permute-start(bf16[32,640]{1,0:T(8,128)(2,1)S(1)} %convert_element_type.182), channel_id=1, source_target_pairs={{0,44},{1,45},{2,46},{3,47},{4,56},{5,57},{6,58},{7,59},{8,52},{9,... | collective-permute-start | bytes 122888 | tf_op jit(solution)/shard_map/ppermute | solution.py:181
  152.1 2.6 %collective-permute-done.29 = bf16[32,640]{1,0:T(8,128)(2,1)S(1)} collective-permute-done((bf16[32,640]{1,0:T(8,128)(2,1)S(1)}, bf16[32,640]{1,0:T(8,128)(2,1)S(1)}, u32[]{:S(2)}, u32[]{:S(2)}) %collective-permute-start.29) | collective-permute-done | bytes 40992 | tf_op jit(solution)/shard_map/ppermute | solution.py:181
  155.2 0.9 collective-permute-done.30.got_ref
  156.1 6.4 %shard_map.79 = bf16[2048,512]{1,0:T(8,128)(2,1)} custom-call(s32[6]{0:T(128)S(1)} %stack.43.flags_ref.half_ref, f32[32,640]{1,0:T(8,128)S(1)} %convert_add_fusion.own_ref, f32[32,640]{1,0:T(8,128)S(1)} %collective-permute-done.30.got_ref, f32[64,512]{1,0:T(8,128)S(1)} %get-tuple-element.33.basis_ref, bf16[2048,512]{1,0:T(8,128)(2,1)S(1)} %get-tuple-element.25.feature_ref, ...), custom_call_target="tpu_custom_call" | custom-call | tf_op jit(solution)/shard_map/pallas_call | solution.py:296
  (85 shorter events, 11.4 us)
Async XLA Ops:
  2.0 11.1 %copy-start = (bf16[64,32,512]{2,1,0:T(8,128)(2,1)S(1)}, bf16[64,32,512]{2,1,0:T(8,128)(2,1)}, u32[]{:S(2)}) copy-start(bf16[64,32,512]{2,1,0:T(8,128)(2,1)} %band_ref.3) | copy-start | bytes 6291460
  2.0 11.1 %copy-start.5 = (f32[21,512]{1,0:T(8,128)S(1)}, f32[21,512]{1,0:T(8,128)}, u32[]{:S(2)}) copy-start(f32[21,512]{1,0:T(8,128)} %taps_ref.5) | copy-start | bytes 129028
  3.2 23.2 %collective-permute-start = (bf16[10,64,512]{2,1,0:T(8,128)(2,1)}, bf16[10,64,512]{2,1,0:T(8,128)(2,1)S(1)}, u32[]{:S(2)}, u32[]{:S(2)}) collective-permute-start(bf16[10,64,512]{2,1,0:T(8,128)(2,1)} %bitcast.13), channel_id=1, source_target_pairs={{0,1},{1,2},{2,3},{3,4},{4,5},{5,6},{6,7},{7,8},{8,9},{9,10},{10,1... | collective-permute-start | bytes 1966088 | tf_op jit(solution)/shard_map/ppermute | solution.py:320
  6.5 20.3 %collective-permute-start.1 = (bf16[10,64,512]{2,1,0:T(8,128)(2,1)}, bf16[10,64,512]{2,1,0:T(8,128)(2,1)S(1)}, u32[]{:S(2)}, u32[]{:S(2)}) collective-permute-start(bf16[10,64,512]{2,1,0:T(8,128)(2,1)} %bitcast.12), channel_id=1, source_target_pairs={{0,31},{1,0},{2,1},{3,2},{4,3},{5,4},{6,5},{7,6},{8,7},{9,8},{10,9... | collective-permute-start | bytes 1966088 | tf_op jit(solution)/shard_map/ppermute | solution.py:321
  22.0 12.7 %copy-start.6 = (f32[21,512]{1,0:T(8,128)S(1)}, f32[21,512]{1,0:T(8,128)}, u32[]{:S(2)}) copy-start(f32[21,512]{1,0:T(8,128)} %taps_ref.7) | copy-start | bytes 129028
  31.8 10.6 %collective-permute-start.2 = (bf16[10,32,512]{2,1,0:T(8,128)(2,1)S(1)}, bf16[10,32,512]{2,1,0:T(8,128)(2,1)S(1)}, u32[]{:S(2)}, u32[]{:S(2)}) collective-permute-start(bf16[10,32,512]{2,1,0:T(8,128)(2,1)S(1)} %get-tuple-element.36), channel_id=1, source_target_pairs={{0,32},{32,0},{1,33},{33,1},{2,34},{34,2},{3,35},{35,3},{4,36},{36... | collective-permute-start | bytes 983048 | tf_op jit(solution)/shard_map/ppermute | solution.py:360
  33.5 9.0 %copy-start.1 = (bf16[512,512]{1,0:T(8,128)(2,1)S(1)}, bf16[512,512]{1,0:T(8,128)(2,1)}, u32[]{:S(2)}) copy-start(bf16[512,512]{1,0:T(8,128)(2,1)} %w_ref.1) | copy-start | bytes 1572868
  33.5 9.0 %copy-start.4 = (f32[512,64]{0,1:T(8,128)S(1)}, f32[512,64]{0,1:T(8,128)}, u32[]{:S(2)}) copy-start(f32[512,64]{0,1:T(8,128)} %param.11) | copy-start | bytes 393220
  33.5 9.0 %collective-permute-start.3 = (bf16[10,32,512]{2,1,0:T(8,128)(2,1)S(1)}, bf16[10,32,512]{2,1,0:T(8,128)(2,1)S(1)}, u32[]{:S(2)}, u32[]{:S(2)}) collective-permute-start(bf16[10,32,512]{2,1,0:T(8,128)(2,1)S(1)} %get-tuple-element.35), channel_id=1, source_target_pairs={{32,64},{96,128},{160,192},{224,0},{64,32},{128,96},{192,160},{0,2... | collective-permute-start | bytes 983048 | tf_op jit(solution)/shard_map/ppermute | solution.py:359
  46.7 2.8 %collective-permute-start.4 = (bf16[32,640]{1,0:T(8,128)(2,1)S(1)}, bf16[32,640]{1,0:T(8,128)(2,1)S(1)}, u32[]{:S(2)}, u32[]{:S(2)}) collective-permute-start(bf16[32,640]{1,0:T(8,128)(2,1)S(1)} %get-tuple-element.24), channel_id=1, source_target_pairs={{0,32},{32,0},{1,33},{33,1},{2,34},{34,2},{3,35},{35,3},{4,36},{36... | collective-permute-start | bytes 122888 | tf_op jit(solution)/shard_map/ppermute | solution.py:178
  49.5 3.6 %collective-permute-start.5 = (bf16[32,640]{1,0:T(8,128)(2,1)S(1)}, bf16[32,640]{1,0:T(8,128)(2,1)S(1)}, u32[]{:S(2)}, u32[]{:S(2)}) collective-permute-start(bf16[32,640]{1,0:T(8,128)(2,1)S(1)} %convert_element_type.140), channel_id=1, source_target_pairs={{0,33},{1,32},{2,35},{3,34},{4,37},{5,36},{6,39},{7,38},{8,41},{9,... | collective-permute-start | bytes 122888 | tf_op jit(solution)/shard_map/ppermute | solution.py:181
  53.1 4.8 %collective-permute-start.6 = (bf16[32,640]{1,0:T(8,128)(2,1)S(1)}, bf16[32,640]{1,0:T(8,128)(2,1)S(1)}, u32[]{:S(2)}, u32[]{:S(2)}) collective-permute-start(bf16[32,640]{1,0:T(8,128)(2,1)S(1)} %convert_element_type.142), channel_id=1, source_target_pairs={{0,35},{1,34},{2,33},{3,32},{4,39},{5,38},{6,37},{7,36},{8,43},{9,... | collective-permute-start | bytes 122888 | tf_op jit(solution)/shard_map/ppermute | solution.py:181
  58.0 3.8 %collective-permute-start.7 = (bf16[32,640]{1,0:T(8,128)(2,1)S(1)}, bf16[32,640]{1,0:T(8,128)(2,1)S(1)}, u32[]{:S(2)}, u32[]{:S(2)}) collective-permute-start(bf16[32,640]{1,0:T(8,128)(2,1)S(1)} %convert_element_type.144), channel_id=1, source_target_pairs={{0,96},{1,97},{2,98},{3,99},{4,100},{5,101},{6,102},{7,103},{8,104... | collective-permute-start | bytes 122888 | tf_op jit(solution)/shard_map/ppermute | solution.py:181
  61.8 4.8 %collective-permute-start.8 = (bf16[32,640]{1,0:T(8,128)(2,1)S(1)}, bf16[32,640]{1,0:T(8,128)(2,1)S(1)}, u32[]{:S(2)}, u32[]{:S(2)}) collective-permute-start(bf16[32,640]{1,0:T(8,128)(2,1)S(1)} %convert_element_type.146), channel_id=1, source_target_pairs={{0,224},{1,225},{2,226},{3,227},{4,228},{5,229},{6,230},{7,231},{8... | collective-permute-start | bytes 122888 | tf_op jit(solution)/shard_map/ppermute | solution.py:181
  66.6 3.6 %collective-permute-start.9 = (bf16[32,640]{1,0:T(8,128)(2,1)S(1)}, bf16[32,640]{1,0:T(8,128)(2,1)S(1)}, u32[]{:S(2)}, u32[]{:S(2)}) collective-permute-start(bf16[32,640]{1,0:T(8,128)(2,1)S(1)} %convert_element_type.148), channel_id=1, source_target_pairs={{0,36},{1,37},{2,38},{3,39},{4,32},{5,33},{6,34},{7,35},{8,44},{9,... | collective-permute-start | bytes 122888 | tf_op jit(solution)/shard_map/ppermute | solution.py:181
  70.3 4.8 %collective-permute-start.10 = (bf16[32,640]{1,0:T(8,128)(2,1)S(1)}, bf16[32,640]{1,0:T(8,128)(2,1)S(1)}, u32[]{:S(2)}, u32[]{:S(2)}) collective-permute-start(bf16[32,640]{1,0:T(8,128)(2,1)S(1)} %convert_element_type.150), channel_id=1, source_target_pairs={{0,60},{1,61},{2,62},{3,63},{4,40},{5,41},{6,42},{7,43},{8,36},{9,... | collective-permute-start | bytes 122888 | tf_op jit(solution)/shard_map/ppermute | solution.py:181
  75.1 6.0 %collective-permute-start.11 = (bf16[32,640]{1,0:T(8,128)(2,1)S(1)}, bf16[32,640]{1,0:T(8,128)(2,1)S(1)}, u32[]{:S(2)}, u32[]{:S(2)}) collective-permute-start(bf16[32,640]{1,0:T(8,128)(2,1)S(1)} %convert_element_type.152), channel_id=1, source_target_pairs={{0,44},{1,45},{2,46},{3,47},{4,56},{5,57},{6,58},{7,59},{8,52},{9,... | collective-permute-start | bytes 122888 | tf_op jit(solution)/shard_map/ppermute | solution.py:181
  81.1 1.4 collective-permute-start.12
  85.2 1.3 collective-permute-start.13
  86.5 3.6 %collective-permute-start.14 = (bf16[32,640]{1,0:T(8,128)(2,1)S(1)}, bf16[32,640]{1,0:T(8,128)(2,1)S(1)}, u32[]{:S(2)}, u32[]{:S(2)}) collective-permute-start(bf16[32,640]{1,0:T(8,128)(2,1)S(1)} %convert_element_type.155), channel_id=1, source_target_pairs={{0,33},{1,32},{2,35},{3,34},{4,37},{5,36},{6,39},{7,38},{8,41},{9,... | collective-permute-start | bytes 122888 | tf_op jit(solution)/shard_map/ppermute | solution.py:181
  90.1 5.1 %collective-permute-start.15 = (bf16[32,640]{1,0:T(8,128)(2,1)S(1)}, bf16[32,640]{1,0:T(8,128)(2,1)S(1)}, u32[]{:S(2)}, u32[]{:S(2)}) collective-permute-start(bf16[32,640]{1,0:T(8,128)(2,1)S(1)} %convert_element_type.157), channel_id=1, source_target_pairs={{0,35},{1,34},{2,33},{3,32},{4,39},{5,38},{6,37},{7,36},{8,43},{9,... | collective-permute-start | bytes 122888 | tf_op jit(solution)/shard_map/ppermute | solution.py:181
  95.3 3.6 %collective-permute-start.16 = (bf16[32,640]{1,0:T(8,128)(2,1)S(1)}, bf16[32,640]{1,0:T(8,128)(2,1)S(1)}, u32[]{:S(2)}, u32[]{:S(2)}) collective-permute-start(bf16[32,640]{1,0:T(8,128)(2,1)S(1)} %convert_element_type.159), channel_id=1, source_target_pairs={{0,96},{1,97},{2,98},{3,99},{4,100},{5,101},{6,102},{7,103},{8,104... | collective-permute-start | bytes 122888 | tf_op jit(solution)/shard_map/ppermute | solution.py:181
  98.9 4.8 %collective-permute-start.17 = (bf16[32,640]{1,0:T(8,128)(2,1)S(1)}, bf16[32,640]{1,0:T(8,128)(2,1)S(1)}, u32[]{:S(2)}, u32[]{:S(2)}) collective-permute-start(bf16[32,640]{1,0:T(8,128)(2,1)S(1)} %convert_element_type.161), channel_id=1, source_target_pairs={{0,224},{1,225},{2,226},{3,227},{4,228},{5,229},{6,230},{7,231},{8... | collective-permute-start | bytes 122888 | tf_op jit(solution)/shard_map/ppermute | solution.py:181
  103.8 3.6 %collective-permute-start.18 = (bf16[32,640]{1,0:T(8,128)(2,1)S(1)}, bf16[32,640]{1,0:T(8,128)(2,1)S(1)}, u32[]{:S(2)}, u32[]{:S(2)}) collective-permute-start(bf16[32,640]{1,0:T(8,128)(2,1)S(1)} %convert_element_type.163), channel_id=1, source_target_pairs={{0,36},{1,37},{2,38},{3,39},{4,32},{5,33},{6,34},{7,35},{8,44},{9,... | collective-permute-start | bytes 122888 | tf_op jit(solution)/shard_map/ppermute | solution.py:181
  107.4 4.8 %collective-permute-start.19 = (bf16[32,640]{1,0:T(8,128)(2,1)S(1)}, bf16[32,640]{1,0:T(8,128)(2,1)S(1)}, u32[]{:S(2)}, u32[]{:S(2)}) collective-permute-start(bf16[32,640]{1,0:T(8,128)(2,1)S(1)} %convert_element_type.165), channel_id=1, source_target_pairs={{0,60},{1,61},{2,62},{3,63},{4,40},{5,41},{6,42},{7,43},{8,36},{9,... | collective-permute-start | bytes 122888 | tf_op jit(solution)/shard_map/ppermute | solution.py:181
  112.2 5.4 %collective-permute-start.20 = (bf16[32,640]{1,0:T(8,128)(2,1)S(1)}, bf16[32,640]{1,0:T(8,128)(2,1)S(1)}, u32[]{:S(2)}, u32[]{:S(2)}) collective-permute-start(bf16[32,640]{1,0:T(8,128)(2,1)S(1)} %convert_element_type.167), channel_id=1, source_target_pairs={{0,44},{1,45},{2,46},{3,47},{4,56},{5,57},{6,58},{7,59},{8,52},{9,... | collective-permute-start | bytes 122888 | tf_op jit(solution)/shard_map/ppermute | solution.py:181
  117.7 1.4 collective-permute-start.21
  119.0 37.1 %copy-start.2 = (bf16[512,512]{1,0:T(8,128)(2,1)S(1)}, bf16[512,512]{1,0:T(8,128)(2,1)}, u32[]{:S(2)}) copy-start(bf16[512,512]{1,0:T(8,128)(2,1)} %wham_ref.1) | copy-start | bytes 1572868
  119.0 37.1 %copy-start.3 = (bf16[512,512]{1,0:T(8,128)(2,1)S(1)}, bf16[512,512]{1,0:T(8,128)(2,1)}, u32[]{:S(2)}) copy-start(bf16[512,512]{1,0:T(8,128)(2,1)} %walign_ref.1) | copy-start | bytes 1572868
  121.8 1.3 collective-permute-start.22
  123.1 3.6 %collective-permute-start.23 = (bf16[32,640]{1,0:T(8,128)(2,1)S(1)}, bf16[32,640]{1,0:T(8,128)(2,1)S(1)}, u32[]{:S(2)}, u32[]{:S(2)}) collective-permute-start(bf16[32,640]{1,0:T(8,128)(2,1)S(1)} %convert_element_type.170), channel_id=1, source_target_pairs={{0,33},{1,32},{2,35},{3,34},{4,37},{5,36},{6,39},{7,38},{8,41},{9,... | collective-permute-start | bytes 122888 | tf_op jit(solution)/shard_map/ppermute | solution.py:181
  126.8 4.8 %collective-permute-start.24 = (bf16[32,640]{1,0:T(8,128)(2,1)S(1)}, bf16[32,640]{1,0:T(8,128)(2,1)S(1)}, u32[]{:S(2)}, u32[]{:S(2)}) collective-permute-start(bf16[32,640]{1,0:T(8,128)(2,1)S(1)} %convert_element_type.172), channel_id=1, source_target_pairs={{0,35},{1,34},{2,33},{3,32},{4,39},{5,38},{6,37},{7,36},{8,43},{9,... | collective-permute-start | bytes 122888 | tf_op jit(solution)/shard_map/ppermute | solution.py:181
  131.6 3.8 %collective-permute-start.25 = (bf16[32,640]{1,0:T(8,128)(2,1)S(1)}, bf16[32,640]{1,0:T(8,128)(2,1)S(1)}, u32[]{:S(2)}, u32[]{:S(2)}) collective-permute-start(bf16[32,640]{1,0:T(8,128)(2,1)S(1)} %convert_element_type.174), channel_id=1, source_target_pairs={{0,96},{1,97},{2,98},{3,99},{4,100},{5,101},{6,102},{7,103},{8,104... | collective-permute-start | bytes 122888 | tf_op jit(solution)/shard_map/ppermute | solution.py:181
  135.5 4.8 %collective-permute-start.26 = (bf16[32,640]{1,0:T(8,128)(2,1)S(1)}, bf16[32,640]{1,0:T(8,128)(2,1)S(1)}, u32[]{:S(2)}, u32[]{:S(2)}) collective-permute-start(bf16[32,640]{1,0:T(8,128)(2,1)S(1)} %convert_element_type.176), channel_id=1, source_target_pairs={{0,224},{1,225},{2,226},{3,227},{4,228},{5,229},{6,230},{7,231},{8... | collective-permute-start | bytes 122888 | tf_op jit(solution)/shard_map/ppermute | solution.py:181
  140.3 3.6 %collective-permute-start.27 = (bf16[32,640]{1,0:T(8,128)(2,1)S(1)}, bf16[32,640]{1,0:T(8,128)(2,1)S(1)}, u32[]{:S(2)}, u32[]{:S(2)}) collective-permute-start(bf16[32,640]{1,0:T(8,128)(2,1)S(1)} %convert_element_type.178), channel_id=1, source_target_pairs={{0,36},{1,37},{2,38},{3,39},{4,32},{5,33},{6,34},{7,35},{8,44},{9,... | collective-permute-start | bytes 122888 | tf_op jit(solution)/shard_map/ppermute | solution.py:181
  143.9 5.3 %collective-permute-start.28 = (bf16[32,640]{1,0:T(8,128)(2,1)S(1)}, bf16[32,640]{1,0:T(8,128)(2,1)S(1)}, u32[]{:S(2)}, u32[]{:S(2)}) collective-permute-start(bf16[32,640]{1,0:T(8,128)(2,1)S(1)} %convert_element_type.180), channel_id=1, source_target_pairs={{0,60},{1,61},{2,62},{3,63},{4,40},{5,41},{6,42},{7,43},{8,36},{9,... | collective-permute-start | bytes 122888 | tf_op jit(solution)/shard_map/ppermute | solution.py:181
  149.3 5.5 %collective-permute-start.29 = (bf16[32,640]{1,0:T(8,128)(2,1)S(1)}, bf16[32,640]{1,0:T(8,128)(2,1)S(1)}, u32[]{:S(2)}, u32[]{:S(2)}) collective-permute-start(bf16[32,640]{1,0:T(8,128)(2,1)S(1)} %convert_element_type.182), channel_id=1, source_target_pairs={{0,44},{1,45},{2,46},{3,47},{4,56},{5,57},{6,58},{7,59},{8,52},{9,... | collective-permute-start | bytes 122888 | tf_op jit(solution)/shard_map/ppermute | solution.py:181
  154.8 1.4 collective-permute-start.30

commit v10 on v4

--- a/solution.py
+++ b/solution.py
@@ -56,18 +56,23 @@
         rows = pl.ds(pl.multiple_of(i * 8, 8), 8)
 
         def emit(o, value):
-            out_ref[o, rows, :] = value
+            flat[pl.ds(i * (8 * w) + o, 8, stride=w), :] = value
 
         own_sums(taps_ref, lambda j: turned[j, rows, :], w, 8, emit)
         return carry
 
     lax.fori_loop(0, h // 8, body, 0)
+    out_ref[...] = flat[...].reshape(h, w, lanes)
 
 
 def columns_rest_kernel(flags_ref, own_ref, left_ref, right_ref, taps_ref, out_ref, lefts, rights, flat):
-    w, h, lanes = own_ref.shape
+    h, w, lanes = own_ref.shape
     lefts[...] = jnp.where(flags_ref[1] == 1, left_ref[...].astype(F32), 0.0)
     rights[...] = jnp.where(flags_ref[2] == 1, right_ref[...].astype(F32), 0.0)
+
+    @pl.when(pl.program_id(0) == 0)
+    def _():
+        flat[...] = jnp.zeros_like(flat)
 
     def body(i, carry):
         rows = pl.ds(pl.multiple_of(i * 8, 8), 8)
@@ -78,17 +83,15 @@
         before = [lefts[j, rows, :] for j in range(MARGIN)]
         items = [{j - o: before[j] for j in range(o, MARGIN)} for o in range(MARGIN)]
         for o, value in enumerate(weighted(taps_ref, items, 8)):
-            put(o, own_ref[o, rows, :] + value)
-        for o in range(MARGIN, w - MARGIN):
-            put(o, own_ref[o, rows, :])
+            put(o, value)
         after = [rights[j, rows, :] for j in range(MARGIN)]
         items = [{2 * MARGIN + j - o: after[j] for j in range(o + 1)} for o in range(MARGIN)]
         for o, value in enumerate(weighted(taps_ref, items, 8)):
-            put(w - MARGIN + o, own_ref[w - MARGIN + o, rows, :] + value)
+            put(w - MARGIN + o, value)
         return carry
 
     lax.fori_loop(0, h // 8, body, 0)
-    out_ref[...] = flat[...].reshape(h, w, lanes).astype(BF)
+    out_ref[...] = (own_ref[...] + flat[...].reshape(h, w, lanes)).astype(BF)
 
 
 def rows_own_kernel(filtered_ref, band_ref, taps_ref, mid_ref, top_ref, low_ref, source, residual, mixed):
@@ -317,7 +320,7 @@
         return pl.BlockSpec((*dims, LANES), lambda i: (*(0 for _ in dims), i))
 
     scalar = pl.BlockSpec(memory_space=pltpu.SMEM)
-    tile, turned = blocks(tile_rows, tile_cols), blocks(tile_cols, tile_rows)
+    tile = blocks(tile_rows, tile_cols)
     side, edge = blocks(margin, tile_rows), blocks(margin, tile_cols)
     taps = blocks(TAPS)
     grid = (channels // LANES,)
@@ -329,8 +332,8 @@
         columns_own_kernel,
         grid=grid,
         in_specs=[tile, taps],
-        out_specs=turned,
-        out_shape=sds((tile_cols, tile_rows, channels), F32),
+        out_specs=tile,
+        out_shape=sds(band_input.shape, F32),
         scratch_shapes=[flat, pltpu.VMEM((tile_cols, tile_rows, LANES), F32)],
         compiler_params=params,
         cost_estimate=cost,
@@ -338,7 +341,7 @@
     filtered = pl.pallas_call(
         columns_rest_kernel,
         grid=grid,
-        in_specs=[scalar, turned, side, side, taps],
+        in_specs=[scalar, tile, side, side, taps],
         out_specs=tile,
         out_shape=sds(band_input.shape, BF),
         scratch_shapes=[pltpu.VMEM((margin, tile_rows, LANES), F32)] * 2 + [flat],

time: 161 us -> 160 us (level)
  transfers between devices with their start and end apart: 31 -> 31, of which waited for: 29 -> 29; matrix products, arithmetic and copies ran while one was open for 1% -> 1% of each run, Pallas kernels for 10% -> 11%
where the time goes in v10:
time: 160 us
  waiting for transfers between devices  63.9 us (40%)
  starting transfers between devices  53 us (33%)
  Pallas kernels  37.5 us (23%)
  local copies, waits for them, and re-layouts  4.55 us (3%)
    ppermute x21, waiting for transfers between devices, summed_over_all(): got = lax.ppermute(total.astype(BF), ALL, round_pairs(axis, rule))  54.1 us
    ppermute x21, starting transfers between devices, summed_over_all(): got = lax.ppermute(total.astype(BF), ALL, round_pairs(axis, rule))  39.6 us
    pallas_call x4, Pallas kernels, call(): pl.pallas_call(kernel, out_shape=outs, in_specs=specs, out_specs=jax.tree...  15.8 us
    pallas_call x1, Pallas kernels, on_device(): pl.pallas_call(columns_own_kernel, grid=grid, in_specs=[tile, taps], out_...  9.81 us
    pallas_call x1, Pallas kernels, on_device(): pl.pallas_call(rows_own_kernel, grid=grid, in_specs=[tile, tile, taps], o...  7.66 us
    ppermute x1, starting transfers between devices, on_device(): right = lax.ppermute(right, COLS, ring(Z * X, -1))  6.56 us
    pallas_call x1, Pallas kernels, on_device(): pl.pallas_call(columns_rest_kernel, grid=grid, in_specs=[scalar, tile, si...  4.18 us
    ppermute x1, waiting for transfers between devices, on_device(): left = lax.ppermute(left, COLS, ring(Z * X, 1))  3.52 us
  transfers between devices with their start and end apart: 31, of which 29 were waited for; matrix products, arithmetic and copies ran while one was open for 1% of the time, Pallas kernels for 11%

profile of v10, /device:TPU:1, one launch (start us, length us, event | category | flops | bytes accessed | tf_op | source)
XLA Modules:
  0.0 159.8 jit_solution(17657015819084322463)
XLA Ops:
  0.0 2.0 %fusion.1 = (bf16[64,10,512]{2,1,0:T(8,128)(2,1)S(1)}, bf16[64,10,512]{2,1,0:T(8,128)(2,1)S(1)}) fusion(bf16[64,32,512]{2,1,0:T(8,128)(2,1)} %band_ref.3), kind=kLoop, calls=%fused_computation.27 | loop fusion | bytes 2621440 | tf_op jit(solution)/shard_map/slice | solution.py:315
  2.0 1.2 copy.15
  3.2 2.0 %collective-permute-start = (bf16[10,64,512]{2,1,0:T(8,128)(2,1)}, bf16[10,64,512]{2,1,0:T(8,128)(2,1)S(1)}, u32[]{:S(2)}, u32[]{:S(2)}) collective-permute-start(bf16[10,64,512]{2,1,0:T(8,128)(2,1)} %bitcast.12), channel_id=1, source_target_pairs={{0,1},{1,2},{2,3},{3,4},{4,5},{5,6},{6,7},{7,8},{8,9},{9,10},{10,1... | collective-permute-start | bytes 1966088 | tf_op jit(solution)/shard_map/ppermute | solution.py:316
  5.3 1.2 copy.14
  6.5 6.6 %collective-permute-start.1 = (bf16[10,64,512]{2,1,0:T(8,128)(2,1)}, bf16[10,64,512]{2,1,0:T(8,128)(2,1)S(1)}, u32[]{:S(2)}, u32[]{:S(2)}) collective-permute-start(bf16[10,64,512]{2,1,0:T(8,128)(2,1)} %bitcast.11), channel_id=1, source_target_pairs={{0,31},{1,0},{2,1},{3,2},{4,3},{5,4},{6,5},{7,6},{8,7},{9,8},{10,9... | collective-permute-start | bytes 1966088 | tf_op jit(solution)/shard_map/ppermute | solution.py:317
  13.1 9.8 %shard_map.73.own_ref = f32[64,32,512]{2,1,0:T(8,128)S(1)} custom-call(bf16[64,32,512]{2,1,0:T(8,128)(2,1)S(1)} %copy-done, f32[21,512]{1,0:T(8,128)S(1)} %copy-done.5), custom_call_target="tpu_custom_call" | custom-call | flops 44040192 | bytes 6291456 | tf_op jit(solution)/shard_map/pallas_call | solution.py:331
  22.9 3.5 %collective-permute-done.left_ref = bf16[10,64,512]{2,1,0:T(8,128)(2,1)S(1)} collective-permute-done((bf16[10,64,512]{2,1,0:T(8,128)(2,1)}, bf16[10,64,512]{2,1,0:T(8,128)(2,1)S(1)}, u32[]{:S(2)}, u32[]{:S(2)}) %collective-permute-start) | collective-permute-done | bytes 655392 | tf_op jit(solution)/shard_map/ppermute | solution.py:316
  26.7 4.2 %shard_map.74.filtered_ref = bf16[64,32,512]{2,1,0:T(8,128)(2,1)S(1)} custom-call(s32[5]{0:T(128)S(1)} %stack.39.flags_ref.half_ref, f32[64,32,512]{2,1,0:T(8,128)S(1)} %shard_map.73.own_ref, bf16[10,64,512]{2,1,0:T(8,128)(2,1)S(1)} %collective-permute-done.left_ref, bf16[10,64,512]{2,1,0:T(8,128)(2,1)S(1)} %collective-permute-done.1.right_ref, ...), custom_call_target="tpu_custom_call" | custom-call | tf_op jit(solution)/shard_map/pallas_call | solution.py:341
  31.0 1.5 collective-permute-start.3
  32.5 1.2 collective-permute-start.2
  33.8 7.7 %shard_map.75 = (bf16[44,32,512]{2,1,0:T(8,128)(2,1)S(1)}, f32[10,32,512]{2,1,0:T(8,128)S(1)}, f32[10,32,512]{2,1,0:T(8,128)S(1)}) custom-call(bf16[64,32,512]{2,1,0:T(8,128)(2,1)S(1)} %shard_map.74.filtered_ref, bf16[64,32,512]{2,1,0:T(8,128)(2,1)S(1)} %copy-done, f32[21,512]{1,0:T(8,128)S(1)} %copy-done.6), custom_call_target="tpu_custom_call" | custom-call | flops 44040192 | bytes 6291456 | tf_op jit(solution)/shard_map/pallas_call | solution.py:353
  41.5 4.0 %shard_map.76 = (bf16[2048,512]{1,0:T(8,128)(2,1)S(1)}, f32[64,2048]{1,0:T(8,128)S(1)}, f32[32,640]{1,0:T(8,128)S(1)}, bf16[32,640]{1,0:T(8,128)(2,1)S(1)}) custom-call(s32[5]{0:T(128)S(1)} %stack.39.flags_ref.half_ref, bf16[44,32,512]{2,1,0:T(8,128)(2,1)S(1)} %get-tuple-element.20.mid_ref, f32[10,32,512]{2,1,0:T(8,128)S(1)} %get-tuple-element.21.top_ref, ...), custom_call_target="tpu_custom_call" | custom-call | tf_op jit(solution)/shard_map/pallas_call | solution.py:292
  46.9 3.5 %collective-permute-done.5 = bf16[32,640]{1,0:T(8,128)(2,1)S(1)} collective-permute-done((bf16[32,640]{1,0:T(8,128)(2,1)S(1)}, bf16[32,640]{1,0:T(8,128)(2,1)S(1)}, u32[]{:S(2)}, u32[]{:S(2)}) %collective-permute-start.5) | collective-permute-done | bytes 40992 | tf_op jit(solution)/shard_map/ppermute | solution.py:184
  50.9 4.4 %collective-permute-done.6 = bf16[32,640]{1,0:T(8,128)(2,1)S(1)} collective-permute-done((bf16[32,640]{1,0:T(8,128)(2,1)S(1)}, bf16[32,640]{1,0:T(8,128)(2,1)S(1)}, u32[]{:S(2)}, u32[]{:S(2)}) %collective-permute-start.6) | collective-permute-done | bytes 40992 | tf_op jit(solution)/shard_map/ppermute | solution.py:184
  56.5 2.4 %collective-permute-done.7 = bf16[32,640]{1,0:T(8,128)(2,1)S(1)} collective-permute-done((bf16[32,640]{1,0:T(8,128)(2,1)S(1)}, bf16[32,640]{1,0:T(8,128)(2,1)S(1)}, u32[]{:S(2)}, u32[]{:S(2)}) %collective-permute-start.7) | collective-permute-done | bytes 40992 | tf_op jit(solution)/shard_map/ppermute | solution.py:184
  58.9 2.7 %collective-permute-start.8 = (bf16[32,640]{1,0:T(8,128)(2,1)S(1)}, bf16[32,640]{1,0:T(8,128)(2,1)S(1)}, u32[]{:S(2)}, u32[]{:S(2)}) collective-permute-start(bf16[32,640]{1,0:T(8,128)(2,1)S(1)} %convert_element_type.146), channel_id=1, source_target_pairs={{0,224},{1,225},{2,226},{3,227},{4,228},{5,229},{6,230},{7,231},{8... | collective-permute-start | bytes 122888 | tf_op jit(solution)/shard_map/ppermute | solution.py:184
  61.7 2.1 %collective-permute-done.8 = bf16[32,640]{1,0:T(8,128)(2,1)S(1)} collective-permute-done((bf16[32,640]{1,0:T(8,128)(2,1)S(1)}, bf16[32,640]{1,0:T(8,128)(2,1)S(1)}, u32[]{:S(2)}, u32[]{:S(2)}) %collective-permute-start.8) | collective-permute-done | bytes 40992 | tf_op jit(solution)/shard_map/ppermute | solution.py:184
  63.9 3.5 %collective-permute-done.9 = bf16[32,640]{1,0:T(8,128)(2,1)S(1)} collective-permute-done((bf16[32,640]{1,0:T(8,128)(2,1)S(1)}, bf16[32,640]{1,0:T(8,128)(2,1)S(1)}, u32[]{:S(2)}, u32[]{:S(2)}) %collective-permute-start.9) | collective-permute-done | bytes 40992 | tf_op jit(solution)/shard_map/ppermute | solution.py:184
  67.4 3.0 %collective-permute-start.10 = (bf16[32,640]{1,0:T(8,128)(2,1)S(1)}, bf16[32,640]{1,0:T(8,128)(2,1)S(1)}, u32[]{:S(2)}, u32[]{:S(2)}) collective-permute-start(bf16[32,640]{1,0:T(8,128)(2,1)S(1)} %convert_element_type.150), channel_id=1, source_target_pairs={{0,60},{1,61},{2,62},{3,63},{4,40},{5,41},{6,42},{7,43},{8,36},{9,... | collective-permute-start | bytes 122888 | tf_op jit(solution)/shard_map/ppermute | solution.py:184
  70.4 2.0 %collective-permute-done.10 = bf16[32,640]{1,0:T(8,128)(2,1)S(1)} collective-permute-done((bf16[32,640]{1,0:T(8,128)(2,1)S(1)}, bf16[32,640]{1,0:T(8,128)(2,1)S(1)}, u32[]{:S(2)}, u32[]{:S(2)}) %collective-permute-start.10) | collective-permute-done | bytes 40992 | tf_op jit(solution)/shard_map/ppermute | solution.py:184
  72.5 4.5 %collective-permute-start.11 = (bf16[32,640]{1,0:T(8,128)(2,1)S(1)}, bf16[32,640]{1,0:T(8,128)(2,1)S(1)}, u32[]{:S(2)}, u32[]{:S(2)}) collective-permute-start(bf16[32,640]{1,0:T(8,128)(2,1)S(1)} %convert_element_type.152), channel_id=1, source_target_pairs={{0,44},{1,45},{2,46},{3,47},{4,56},{5,57},{6,58},{7,59},{8,52},{9,... | collective-permute-start | bytes 122888 | tf_op jit(solution)/shard_map/ppermute | solution.py:184
  76.9 1.7 %collective-permute-done.11 = bf16[32,640]{1,0:T(8,128)(2,1)S(1)} collective-permute-done((bf16[32,640]{1,0:T(8,128)(2,1)S(1)}, bf16[32,640]{1,0:T(8,128)(2,1)S(1)}, u32[]{:S(2)}, u32[]{:S(2)}) %collective-permute-start.11) | collective-permute-done | bytes 40992 | tf_op jit(solution)/shard_map/ppermute | solution.py:184
  80.0 2.7 %shard_map.77 = (f32[64,512]{1,0:T(8,128)S(1)}, f32[64,2048]{1,0:T(8,128)S(1)}, f32[32,640]{1,0:T(8,128)S(1)}, bf16[32,640]{1,0:T(8,128)(2,1)S(1)}) custom-call(s32[5]{0:T(128)S(1)} %stack.39.flags_ref.half_ref, f32[32,640]{1,0:T(8,128)S(1)} %convert_add_fusion.16.own_ref, f32[32,640]{1,0:T(8,128)S(1)} %collective-permute-done.12.got_ref, ...), custom_call_target="tpu_custom_call" | custom-call | tf_op jit(solution)/shard_map/pallas_call | solution.py:292
  84.2 3.4 %collective-permute-done.14 = bf16[32,640]{1,0:T(8,128)(2,1)S(1)} collective-permute-done((bf16[32,640]{1,0:T(8,128)(2,1)S(1)}, bf16[32,640]{1,0:T(8,128)(2,1)S(1)}, u32[]{:S(2)}, u32[]{:S(2)}) %collective-permute-start.14) | collective-permute-done | bytes 40992 | tf_op jit(solution)/shard_map/ppermute | solution.py:184
  87.6 2.8 %collective-permute-start.15 = (bf16[32,640]{1,0:T(8,128)(2,1)S(1)}, bf16[32,640]{1,0:T(8,128)(2,1)S(1)}, u32[]{:S(2)}, u32[]{:S(2)}) collective-permute-start(bf16[32,640]{1,0:T(8,128)(2,1)S(1)} %convert_element_type.157), channel_id=1, source_target_pairs={{0,35},{1,34},{2,33},{3,32},{4,39},{5,38},{6,37},{7,36},{8,43},{9,... | collective-permute-start | bytes 122888 | tf_op jit(solution)/shard_map/ppermute | solution.py:184
  90.4 2.0 %collective-permute-done.15 = bf16[32,640]{1,0:T(8,128)(2,1)S(1)} collective-permute-done((bf16[32,640]{1,0:T(8,128)(2,1)S(1)}, bf16[32,640]{1,0:T(8,128)(2,1)S(1)}, u32[]{:S(2)}, u32[]{:S(2)}) %collective-permute-start.15) | collective-permute-done | bytes 40992 | tf_op jit(solution)/shard_map/ppermute | solution.py:184
  92.6 3.3 %collective-permute-done.16 = bf16[32,640]{1,0:T(8,128)(2,1)S(1)} collective-permute-done((bf16[32,640]{1,0:T(8,128)(2,1)S(1)}, bf16[32,640]{1,0:T(8,128)(2,1)S(1)}, u32[]{:S(2)}, u32[]{:S(2)}) %collective-permute-start.16) | collective-permute-done | bytes 40992 | tf_op jit(solution)/shard_map/ppermute | solution.py:184
  95.9 2.8 %collective-permute-start.17 = (bf16[32,640]{1,0:T(8,128)(2,1)S(1)}, bf16[32,640]{1,0:T(8,128)(2,1)S(1)}, u32[]{:S(2)}, u32[]{:S(2)}) collective-permute-start(bf16[32,640]{1,0:T(8,128)(2,1)S(1)} %convert_element_type.161), channel_id=1, source_target_pairs={{0,224},{1,225},{2,226},{3,227},{4,228},{5,229},{6,230},{7,231},{8... | collective-permute-start | bytes 122888 | tf_op jit(solution)/shard_map/ppermute | solution.py:184
  98.7 1.9 %collective-permute-done.17 = bf16[32,640]{1,0:T(8,128)(2,1)S(1)} collective-permute-done((bf16[32,640]{1,0:T(8,128)(2,1)S(1)}, bf16[32,640]{1,0:T(8,128)(2,1)S(1)}, u32[]{:S(2)}, u32[]{:S(2)}) %collective-permute-start.17) | collective-permute-done | bytes 40992 | tf_op jit(solution)/shard_map/ppermute | solution.py:184
  100.7 1.3 collective-permute-start.18
  102.0 2.2 %collective-permute-done.18 = bf16[32,640]{1,0:T(8,128)(2,1)S(1)} collective-permute-done((bf16[32,640]{1,0:T(8,128)(2,1)S(1)}, bf16[32,640]{1,0:T(8,128)(2,1)S(1)}, u32[]{:S(2)}, u32[]{:S(2)}) %collective-permute-start.18) | collective-permute-done | bytes 40992 | tf_op jit(solution)/shard_map/ppermute | solution.py:184
  104.2 3.6 %collective-permute-start.19 = (bf16[32,640]{1,0:T(8,128)(2,1)S(1)}, bf16[32,640]{1,0:T(8,128)(2,1)S(1)}, u32[]{:S(2)}, u32[]{:S(2)}) collective-permute-start(bf16[32,640]{1,0:T(8,128)(2,1)S(1)} %convert_element_type.165), channel_id=1, source_target_pairs={{0,60},{1,61},{2,62},{3,63},{4,40},{5,41},{6,42},{7,43},{8,36},{9,... | collective-permute-start | bytes 122888 | tf_op jit(solution)/shard_map/ppermute | solution.py:184
  107.8 1.8 %collective-permute-done.19 = bf16[32,640]{1,0:T(8,128)(2,1)S(1)} collective-permute-done((bf16[32,640]{1,0:T(8,128)(2,1)S(1)}, bf16[32,640]{1,0:T(8,128)(2,1)S(1)}, u32[]{:S(2)}, u32[]{:S(2)}) %collective-permute-start.19) | collective-permute-done | bytes 40992 | tf_op jit(solution)/shard_map/ppermute | solution.py:184
  109.6 3.6 %collective-permute-start.20 = (bf16[32,640]{1,0:T(8,128)(2,1)S(1)}, bf16[32,640]{1,0:T(8,128)(2,1)S(1)}, u32[]{:S(2)}, u32[]{:S(2)}) collective-permute-start(bf16[32,640]{1,0:T(8,128)(2,1)S(1)} %convert_element_type.167), channel_id=1, source_target_pairs={{0,44},{1,45},{2,46},{3,47},{4,56},{5,57},{6,58},{7,59},{8,52},{9,... | collective-permute-start | bytes 122888 | tf_op jit(solution)/shard_map/ppermute | solution.py:184
  113.2 1.9 %collective-permute-done.20 = bf16[32,640]{1,0:T(8,128)(2,1)S(1)} collective-permute-done((bf16[32,640]{1,0:T(8,128)(2,1)S(1)}, bf16[32,640]{1,0:T(8,128)(2,1)S(1)}, u32[]{:S(2)}, u32[]{:S(2)}) %collective-permute-start.20) | collective-permute-done | bytes 40992 | tf_op jit(solution)/shard_map/ppermute | solution.py:184
  116.5 2.7 %shard_map.78 = (f32[64,512]{1,0:T(8,128)S(1)}, f32[64,2048]{1,0:T(8,128)S(1)}, f32[32,640]{1,0:T(8,128)S(1)}, bf16[32,640]{1,0:T(8,128)(2,1)S(1)}) custom-call(s32[5]{0:T(128)S(1)} %stack.39.flags_ref.half_ref, f32[32,640]{1,0:T(8,128)S(1)} %convert_add_fusion.8.own_ref, f32[32,640]{1,0:T(8,128)S(1)} %collective-permute-done.21.got_ref, ...), custom_call_target="tpu_custom_call" | custom-call | tf_op jit(solution)/shard_map/pallas_call | solution.py:292
  120.7 3.5 %collective-permute-done.23 = bf16[32,640]{1,0:T(8,128)(2,1)S(1)} collective-permute-done((bf16[32,640]{1,0:T(8,128)(2,1)S(1)}, bf16[32,640]{1,0:T(8,128)(2,1)S(1)}, u32[]{:S(2)}, u32[]{:S(2)}) %collective-permute-start.23) | collective-permute-done | bytes 40992 | tf_op jit(solution)/shard_map/ppermute | solution.py:184
  124.2 2.5 %collective-permute-start.24 = (bf16[32,640]{1,0:T(8,128)(2,1)S(1)}, bf16[32,640]{1,0:T(8,128)(2,1)S(1)}, u32[]{:S(2)}, u32[]{:S(2)}) collective-permute-start(bf16[32,640]{1,0:T(8,128)(2,1)S(1)} %convert_element_type.172), channel_id=1, source_target_pairs={{0,35},{1,34},{2,33},{3,32},{4,39},{5,38},{6,37},{7,36},{8,43},{9,... | collective-permute-start | bytes 122888 | tf_op jit(solution)/shard_map/ppermute | solution.py:184
  126.7 2.3 %collective-permute-done.24 = bf16[32,640]{1,0:T(8,128)(2,1)S(1)} collective-permute-done((bf16[32,640]{1,0:T(8,128)(2,1)S(1)}, bf16[32,640]{1,0:T(8,128)(2,1)S(1)}, u32[]{:S(2)}, u32[]{:S(2)}) %collective-permute-start.24) | collective-permute-done | bytes 40992 | tf_op jit(solution)/shard_map/ppermute | solution.py:184
  129.1 3.5 %collective-permute-done.25 = bf16[32,640]{1,0:T(8,128)(2,1)S(1)} collective-permute-done((bf16[32,640]{1,0:T(8,128)(2,1)S(1)}, bf16[32,640]{1,0:T(8,128)(2,1)S(1)}, u32[]{:S(2)}, u32[]{:S(2)}) %collective-permute-start.25) | collective-permute-done | bytes 40992 | tf_op jit(solution)/shard_map/ppermute | solution.py:184
  132.6 2.7 %collective-permute-start.26 = (bf16[32,640]{1,0:T(8,128)(2,1)S(1)}, bf16[32,640]{1,0:T(8,128)(2,1)S(1)}, u32[]{:S(2)}, u32[]{:S(2)}) collective-permute-start(bf16[32,640]{1,0:T(8,128)(2,1)S(1)} %convert_element_type.176), channel_id=1, source_target_pairs={{0,224},{1,225},{2,226},{3,227},{4,228},{5,229},{6,230},{7,231},{8... | collective-permute-start | bytes 122888 | tf_op jit(solution)/shard_map/ppermute | solution.py:184
  135.4 2.1 %collective-permute-done.26 = bf16[32,640]{1,0:T(8,128)(2,1)S(1)} collective-permute-done((bf16[32,640]{1,0:T(8,128)(2,1)S(1)}, bf16[32,640]{1,0:T(8,128)(2,1)S(1)}, u32[]{:S(2)}, u32[]{:S(2)}) %collective-permute-start.26) | collective-permute-done | bytes 40992 | tf_op jit(solution)/shard_map/ppermute | solution.py:184
  138.3 2.8 %collective-permute-done.27 = bf16[32,640]{1,0:T(8,128)(2,1)S(1)} collective-permute-done((bf16[32,640]{1,0:T(8,128)(2,1)S(1)}, bf16[32,640]{1,0:T(8,128)(2,1)S(1)}, u32[]{:S(2)}, u32[]{:S(2)}) %collective-permute-start.27) | collective-permute-done | bytes 40992 | tf_op jit(solution)/shard_map/ppermute | solution.py:184
  141.1 3.9 %collective-permute-start.28 = (bf16[32,640]{1,0:T(8,128)(2,1)S(1)}, bf16[32,640]{1,0:T(8,128)(2,1)S(1)}, u32[]{:S(2)}, u32[]{:S(2)}) collective-permute-start(bf16[32,640]{1,0:T(8,128)(2,1)S(1)} %convert_element_type.180), channel_id=1, source_target_pairs={{0,60},{1,61},{2,62},{3,63},{4,40},{5,41},{6,42},{7,43},{8,36},{9,... | collective-permute-start | bytes 122888 | tf_op jit(solution)/shard_map/ppermute | solution.py:184
  145.0 1.7 %collective-permute-done.28 = bf16[32,640]{1,0:T(8,128)(2,1)S(1)} collective-permute-done((bf16[32,640]{1,0:T(8,128)(2,1)S(1)}, bf16[32,640]{1,0:T(8,128)(2,1)S(1)}, u32[]{:S(2)}, u32[]{:S(2)}) %collective-permute-start.28) | collective-permute-done | bytes 40992 | tf_op jit(solution)/shard_map/ppermute | solution.py:184
  146.7 3.0 %collective-permute-start.29 = (bf16[32,640]{1,0:T(8,128)(2,1)S(1)}, bf16[32,640]{1,0:T(8,128)(2,1)S(1)}, u32[]{:S(2)}, u32[]{:S(2)}) collective-permute-start(bf16[32,640]{1,0:T(8,128)(2,1)S(1)} %convert_element_type.182), channel_id=1, source_target_pairs={{0,44},{1,45},{2,46},{3,47},{4,56},{5,57},{6,58},{7,59},{8,52},{9,... | collective-permute-start | bytes 122888 | tf_op jit(solution)/shard_map/ppermute | solution.py:184
  149.7 2.3 %collective-permute-done.29 = bf16[32,640]{1,0:T(8,128)(2,1)S(1)} collective-permute-done((bf16[32,640]{1,0:T(8,128)(2,1)S(1)}, bf16[32,640]{1,0:T(8,128)(2,1)S(1)}, u32[]{:S(2)}, u32[]{:S(2)}) %collective-permute-start.29) | collective-permute-done | bytes 40992 | tf_op jit(solution)/shard_map/ppermute | solution.py:184
  153.4 6.4 %shard_map.79 = bf16[2048,512]{1,0:T(8,128)(2,1)} custom-call(s32[5]{0:T(128)S(1)} %stack.39.flags_ref.half_ref, f32[32,640]{1,0:T(8,128)S(1)} %convert_add_fusion.own_ref, f32[32,640]{1,0:T(8,128)S(1)} %collective-permute-done.30.got_ref, f32[64,512]{1,0:T(8,128)S(1)} %get-tuple-element.33.basis_ref, bf16[2048,512]{1,0:T(8,128)(2,1)S(1)} %get-tuple-element.25.feature_ref, ...), custom_call_target="tpu_custom_call" | custom-call | tf_op jit(solution)/shard_map/pallas_call | solution.py:292
  (85 shorter events, 12.1 us)
Async XLA Ops:
  2.0 11.1 %copy-start = (bf16[64,32,512]{2,1,0:T(8,128)(2,1)S(1)}, bf16[64,32,512]{2,1,0:T(8,128)(2,1)}, u32[]{:S(2)}) copy-start(bf16[64,32,512]{2,1,0:T(8,128)(2,1)} %band_ref.3) | copy-start | bytes 6291460
  2.0 11.1 %copy-start.5 = (f32[21,512]{1,0:T(8,128)S(1)}, f32[21,512]{1,0:T(8,128)}, u32[]{:S(2)}) copy-start(f32[21,512]{1,0:T(8,128)} %taps_ref.5) | copy-start | bytes 129028
  3.2 23.2 %collective-permute-start = (bf16[10,64,512]{2,1,0:T(8,128)(2,1)}, bf16[10,64,512]{2,1,0:T(8,128)(2,1)S(1)}, u32[]{:S(2)}, u32[]{:S(2)}) collective-permute-start(bf16[10,64,512]{2,1,0:T(8,128)(2,1)} %bitcast.12), channel_id=1, source_target_pairs={{0,1},{1,2},{2,3},{3,4},{4,5},{5,6},{6,7},{7,8},{8,9},{9,10},{10,1... | collective-permute-start | bytes 1966088 | tf_op jit(solution)/shard_map/ppermute | solution.py:316
  6.5 20.3 %collective-permute-start.1 = (bf16[10,64,512]{2,1,0:T(8,128)(2,1)}, bf16[10,64,512]{2,1,0:T(8,128)(2,1)S(1)}, u32[]{:S(2)}, u32[]{:S(2)}) collective-permute-start(bf16[10,64,512]{2,1,0:T(8,128)(2,1)} %bitcast.11), channel_id=1, source_target_pairs={{0,31},{1,0},{2,1},{3,2},{4,3},{5,4},{6,5},{7,6},{8,7},{9,8},{10,9... | collective-permute-start | bytes 1966088 | tf_op jit(solution)/shard_map/ppermute | solution.py:317
  22.9 10.8 %copy-start.6 = (f32[21,512]{1,0:T(8,128)S(1)}, f32[21,512]{1,0:T(8,128)}, u32[]{:S(2)}) copy-start(f32[21,512]{1,0:T(8,128)} %taps_ref.7) | copy-start | bytes 129028
  31.0 10.4 %collective-permute-start.3 = (bf16[10,32,512]{2,1,0:T(8,128)(2,1)S(1)}, bf16[10,32,512]{2,1,0:T(8,128)(2,1)S(1)}, u32[]{:S(2)}, u32[]{:S(2)}) collective-permute-start(bf16[10,32,512]{2,1,0:T(8,128)(2,1)S(1)} %get-tuple-element.35), channel_id=1, source_target_pairs={{0,224},{32,0},{64,32},{96,64},{128,96},{160,128},{192,160},{224,1... | collective-permute-start | bytes 983048 | tf_op jit(solution)/shard_map/ppermute | solution.py:351
  32.5 8.9 %copy-start.1 = (bf16[512,512]{1,0:T(8,128)(2,1)S(1)}, bf16[512,512]{1,0:T(8,128)(2,1)}, u32[]{:S(2)}) copy-start(bf16[512,512]{1,0:T(8,128)(2,1)} %w_ref.1) | copy-start | bytes 1572868
  32.5 8.9 %copy-start.4 = (f32[512,64]{0,1:T(8,128)S(1)}, f32[512,64]{0,1:T(8,128)}, u32[]{:S(2)}) copy-start(f32[512,64]{0,1:T(8,128)} %param.11) | copy-start | bytes 393220
  32.5 8.9 %collective-permute-start.2 = (bf16[10,32,512]{2,1,0:T(8,128)(2,1)S(1)}, bf16[10,32,512]{2,1,0:T(8,128)(2,1)S(1)}, u32[]{:S(2)}, u32[]{:S(2)}) collective-permute-start(bf16[10,32,512]{2,1,0:T(8,128)(2,1)S(1)} %get-tuple-element.36), channel_id=1, source_target_pairs={{0,32},{32,64},{64,96},{96,128},{128,160},{160,192},{192,224},{224... | collective-permute-start | bytes 983048 | tf_op jit(solution)/shard_map/ppermute | solution.py:350
  45.4 1.4 collective-permute-start.4
  46.8 3.6 %collective-permute-start.5 = (bf16[32,640]{1,0:T(8,128)(2,1)S(1)}, bf16[32,640]{1,0:T(8,128)(2,1)S(1)}, u32[]{:S(2)}, u32[]{:S(2)}) collective-permute-start(bf16[32,640]{1,0:T(8,128)(2,1)S(1)} %convert_element_type.140), channel_id=1, source_target_pairs={{0,33},{1,32},{2,35},{3,34},{4,37},{5,36},{6,39},{7,38},{8,41},{9,... | collective-permute-start | bytes 122888 | tf_op jit(solution)/shard_map/ppermute | solution.py:184
  50.5 4.8 %collective-permute-start.6 = (bf16[32,640]{1,0:T(8,128)(2,1)S(1)}, bf16[32,640]{1,0:T(8,128)(2,1)S(1)}, u32[]{:S(2)}, u32[]{:S(2)}) collective-permute-start(bf16[32,640]{1,0:T(8,128)(2,1)S(1)} %convert_element_type.142), channel_id=1, source_target_pairs={{0,35},{1,34},{2,33},{3,32},{4,39},{5,38},{6,37},{7,36},{8,43},{9,... | collective-permute-start | bytes 122888 | tf_op jit(solution)/shard_map/ppermute | solution.py:184
  55.3 3.6 %collective-permute-start.7 = (bf16[32,640]{1,0:T(8,128)(2,1)S(1)}, bf16[32,640]{1,0:T(8,128)(2,1)S(1)}, u32[]{:S(2)}, u32[]{:S(2)}) collective-permute-start(bf16[32,640]{1,0:T(8,128)(2,1)S(1)} %convert_element_type.144), channel_id=1, source_target_pairs={{0,96},{1,97},{2,98},{3,99},{4,100},{5,101},{6,102},{7,103},{8,104... | collective-permute-start | bytes 122888 | tf_op jit(solution)/shard_map/ppermute | solution.py:184
  58.9 4.8 %collective-permute-start.8 = (bf16[32,640]{1,0:T(8,128)(2,1)S(1)}, bf16[32,640]{1,0:T(8,128)(2,1)S(1)}, u32[]{:S(2)}, u32[]{:S(2)}) collective-permute-start(bf16[32,640]{1,0:T(8,128)(2,1)S(1)} %convert_element_type.146), channel_id=1, source_target_pairs={{0,224},{1,225},{2,226},{3,227},{4,228},{5,229},{6,230},{7,231},{8... | collective-permute-start | bytes 122888 | tf_op jit(solution)/shard_map/ppermute | solution.py:184
  63.8 3.6 %collective-permute-start.9 = (bf16[32,640]{1,0:T(8,128)(2,1)S(1)}, bf16[32,640]{1,0:T(8,128)(2,1)S(1)}, u32[]{:S(2)}, u32[]{:S(2)}) collective-permute-start(bf16[32,640]{1,0:T(8,128)(2,1)S(1)} %convert_element_type.148), channel_id=1, source_target_pairs={{0,36},{1,37},{2,38},{3,39},{4,32},{5,33},{6,34},{7,35},{8,44},{9,... | collective-permute-start | bytes 122888 | tf_op jit(solution)/shard_map/ppermute | solution.py:184
  67.4 5.0 %collective-permute-start.10 = (bf16[32,640]{1,0:T(8,128)(2,1)S(1)}, bf16[32,640]{1,0:T(8,128)(2,1)S(1)}, u32[]{:S(2)}, u32[]{:S(2)}) collective-permute-start(bf16[32,640]{1,0:T(8,128)(2,1)S(1)} %convert_element_type.150), channel_id=1, source_target_pairs={{0,60},{1,61},{2,62},{3,63},{4,40},{5,41},{6,42},{7,43},{8,36},{9,... | collective-permute-start | bytes 122888 | tf_op jit(solution)/shard_map/ppermute | solution.py:184
  72.5 6.2 %collective-permute-start.11 = (bf16[32,640]{1,0:T(8,128)(2,1)S(1)}, bf16[32,640]{1,0:T(8,128)(2,1)S(1)}, u32[]{:S(2)}, u32[]{:S(2)}) collective-permute-start(bf16[32,640]{1,0:T(8,128)(2,1)S(1)} %convert_element_type.152), channel_id=1, source_target_pairs={{0,44},{1,45},{2,46},{3,47},{4,56},{5,57},{6,58},{7,59},{8,52},{9,... | collective-permute-start | bytes 122888 | tf_op jit(solution)/shard_map/ppermute | solution.py:184
  78.6 1.4 collective-permute-start.12
  82.8 1.3 collective-permute-start.13
  84.1 3.5 %collective-permute-start.14 = (bf16[32,640]{1,0:T(8,128)(2,1)S(1)}, bf16[32,640]{1,0:T(8,128)(2,1)S(1)}, u32[]{:S(2)}, u32[]{:S(2)}) collective-permute-start(bf16[32,640]{1,0:T(8,128)(2,1)S(1)} %convert_element_type.155), channel_id=1, source_target_pairs={{0,33},{1,32},{2,35},{3,34},{4,37},{5,36},{6,39},{7,38},{8,41},{9,... | collective-permute-start | bytes 122888 | tf_op jit(solution)/shard_map/ppermute | solution.py:184
  87.6 4.7 %collective-permute-start.15 = (bf16[32,640]{1,0:T(8,128)(2,1)S(1)}, bf16[32,640]{1,0:T(8,128)(2,1)S(1)}, u32[]{:S(2)}, u32[]{:S(2)}) collective-permute-start(bf16[32,640]{1,0:T(8,128)(2,1)S(1)} %convert_element_type.157), channel_id=1, source_target_pairs={{0,35},{1,34},{2,33},{3,32},{4,39},{5,38},{6,37},{7,36},{8,43},{9,... | collective-permute-start | bytes 122888 | tf_op jit(solution)/shard_map/ppermute | solution.py:184
  92.4 3.5 %collective-permute-start.16 = (bf16[32,640]{1,0:T(8,128)(2,1)S(1)}, bf16[32,640]{1,0:T(8,128)(2,1)S(1)}, u32[]{:S(2)}, u32[]{:S(2)}) collective-permute-start(bf16[32,640]{1,0:T(8,128)(2,1)S(1)} %convert_element_type.159), channel_id=1, source_target_pairs={{0,96},{1,97},{2,98},{3,99},{4,100},{5,101},{6,102},{7,103},{8,104... | collective-permute-start | bytes 122888 | tf_op jit(solution)/shard_map/ppermute | solution.py:184
  95.9 4.7 %collective-permute-start.17 = (bf16[32,640]{1,0:T(8,128)(2,1)S(1)}, bf16[32,640]{1,0:T(8,128)(2,1)S(1)}, u32[]{:S(2)}, u32[]{:S(2)}) collective-permute-start(bf16[32,640]{1,0:T(8,128)(2,1)S(1)} %convert_element_type.161), channel_id=1, source_target_pairs={{0,224},{1,225},{2,226},{3,227},{4,228},{5,229},{6,230},{7,231},{8... | collective-permute-start | bytes 122888 | tf_op jit(solution)/shard_map/ppermute | solution.py:184
  100.7 3.5 %collective-permute-start.18 = (bf16[32,640]{1,0:T(8,128)(2,1)S(1)}, bf16[32,640]{1,0:T(8,128)(2,1)S(1)}, u32[]{:S(2)}, u32[]{:S(2)}) collective-permute-start(bf16[32,640]{1,0:T(8,128)(2,1)S(1)} %convert_element_type.163), channel_id=1, source_target_pairs={{0,36},{1,37},{2,38},{3,39},{4,32},{5,33},{6,34},{7,35},{8,44},{9,... | collective-permute-start | bytes 122888 | tf_op jit(solution)/shard_map/ppermute | solution.py:184
  104.2 5.4 %collective-permute-start.19 = (bf16[32,640]{1,0:T(8,128)(2,1)S(1)}, bf16[32,640]{1,0:T(8,128)(2,1)S(1)}, u32[]{:S(2)}, u32[]{:S(2)}) collective-permute-start(bf16[32,640]{1,0:T(8,128)(2,1)S(1)} %convert_element_type.165), channel_id=1, source_target_pairs={{0,60},{1,61},{2,62},{3,63},{4,40},{5,41},{6,42},{7,43},{8,36},{9,... | collective-permute-start | bytes 122888 | tf_op jit(solution)/shard_map/ppermute | solution.py:184
  109.6 5.5 %collective-permute-start.20 = (bf16[32,640]{1,0:T(8,128)(2,1)S(1)}, bf16[32,640]{1,0:T(8,128)(2,1)S(1)}, u32[]{:S(2)}, u32[]{:S(2)}) collective-permute-start(bf16[32,640]{1,0:T(8,128)(2,1)S(1)} %convert_element_type.167), channel_id=1, source_target_pairs={{0,44},{1,45},{2,46},{3,47},{4,56},{5,57},{6,58},{7,59},{8,52},{9,... | collective-permute-start | bytes 122888 | tf_op jit(solution)/shard_map/ppermute | solution.py:184
  115.1 1.4 collective-permute-start.21
  116.5 36.9 %copy-start.2 = (bf16[512,512]{1,0:T(8,128)(2,1)S(1)}, bf16[512,512]{1,0:T(8,128)(2,1)}, u32[]{:S(2)}) copy-start(bf16[512,512]{1,0:T(8,128)(2,1)} %wham_ref.1) | copy-start | bytes 1572868
  116.5 36.9 %copy-start.3 = (bf16[512,512]{1,0:T(8,128)(2,1)S(1)}, bf16[512,512]{1,0:T(8,128)(2,1)}, u32[]{:S(2)}) copy-start(bf16[512,512]{1,0:T(8,128)(2,1)} %walign_ref.1) | copy-start | bytes 1572868
  119.2 1.3 collective-permute-start.22
  120.6 3.6 %collective-permute-start.23 = (bf16[32,640]{1,0:T(8,128)(2,1)S(1)}, bf16[32,640]{1,0:T(8,128)(2,1)S(1)}, u32[]{:S(2)}, u32[]{:S(2)}) collective-permute-start(bf16[32,640]{1,0:T(8,128)(2,1)S(1)} %convert_element_type.170), channel_id=1, source_target_pairs={{0,33},{1,32},{2,35},{3,34},{4,37},{5,36},{6,39},{7,38},{8,41},{9,... | collective-permute-start | bytes 122888 | tf_op jit(solution)/shard_map/ppermute | solution.py:184
  124.2 4.8 %collective-permute-start.24 = (bf16[32,640]{1,0:T(8,128)(2,1)S(1)}, bf16[32,640]{1,0:T(8,128)(2,1)S(1)}, u32[]{:S(2)}, u32[]{:S(2)}) collective-permute-start(bf16[32,640]{1,0:T(8,128)(2,1)S(1)} %convert_element_type.172), channel_id=1, source_target_pairs={{0,35},{1,34},{2,33},{3,32},{4,39},{5,38},{6,37},{7,36},{8,43},{9,... | collective-permute-start | bytes 122888 | tf_op jit(solution)/shard_map/ppermute | solution.py:184
  129.0 3.6 %collective-permute-start.25 = (bf16[32,640]{1,0:T(8,128)(2,1)S(1)}, bf16[32,640]{1,0:T(8,128)(2,1)S(1)}, u32[]{:S(2)}, u32[]{:S(2)}) collective-permute-start(bf16[32,640]{1,0:T(8,128)(2,1)S(1)} %convert_element_type.174), channel_id=1, source_target_pairs={{0,96},{1,97},{2,98},{3,99},{4,100},{5,101},{6,102},{7,103},{8,104... | collective-permute-start | bytes 122888 | tf_op jit(solution)/shard_map/ppermute | solution.py:184
  132.6 4.8 %collective-permute-start.26 = (bf16[32,640]{1,0:T(8,128)(2,1)S(1)}, bf16[32,640]{1,0:T(8,128)(2,1)S(1)}, u32[]{:S(2)}, u32[]{:S(2)}) collective-permute-start(bf16[32,640]{1,0:T(8,128)(2,1)S(1)} %convert_element_type.176), channel_id=1, source_target_pairs={{0,224},{1,225},{2,226},{3,227},{4,228},{5,229},{6,230},{7,231},{8... | collective-permute-start | bytes 122888 | tf_op jit(solution)/shard_map/ppermute | solution.py:184
  137.5 3.6 %collective-permute-start.27 = (bf16[32,640]{1,0:T(8,128)(2,1)S(1)}, bf16[32,640]{1,0:T(8,128)(2,1)S(1)}, u32[]{:S(2)}, u32[]{:S(2)}) collective-permute-start(bf16[32,640]{1,0:T(8,128)(2,1)S(1)} %convert_element_type.178), channel_id=1, source_target_pairs={{0,36},{1,37},{2,38},{3,39},{4,32},{5,33},{6,34},{7,35},{8,44},{9,... | collective-permute-start | bytes 122888 | tf_op jit(solution)/shard_map/ppermute | solution.py:184
  141.1 5.5 %collective-permute-start.28 = (bf16[32,640]{1,0:T(8,128)(2,1)S(1)}, bf16[32,640]{1,0:T(8,128)(2,1)S(1)}, u32[]{:S(2)}, u32[]{:S(2)}) collective-permute-start(bf16[32,640]{1,0:T(8,128)(2,1)S(1)} %convert_element_type.180), channel_id=1, source_target_pairs={{0,60},{1,61},{2,62},{3,63},{4,40},{5,41},{6,42},{7,43},{8,36},{9,... | collective-permute-start | bytes 122888 | tf_op jit(solution)/shard_map/ppermute | solution.py:184
  146.7 5.3 %collective-permute-start.29 = (bf16[32,640]{1,0:T(8,128)(2,1)S(1)}, bf16[32,640]{1,0:T(8,128)(2,1)S(1)}, u32[]{:S(2)}, u32[]{:S(2)}) collective-permute-start(bf16[32,640]{1,0:T(8,128)(2,1)S(1)} %convert_element_type.182), channel_id=1, source_target_pairs={{0,44},{1,45},{2,46},{3,47},{4,56},{5,57},{6,58},{7,59},{8,52},{9,... | collective-permute-start | bytes 122888 | tf_op jit(solution)/shard_map/ppermute | solution.py:184
  152.0 1.4 collective-permute-start.30

commit v11 on v10

--- a/solution.py
+++ b/solution.py
@@ -44,6 +44,16 @@
         ]
         for i, value in enumerate(weighted(taps_ref, items, 8)):
             emit(start + i, value)
+
+
+def pack_kernel(band_ref, first_ref, last_ref, flat):
+    h, w, channels = band_ref.shape
+    for t in range(channels // LANES):
+        lanes = slice(t * LANES, (t + 1) * LANES)
+        flat[t] = band_ref[:, :, lanes].astype(F32).reshape(h * w, LANES)
+        for j in range(MARGIN):
+            first_ref[j, :, lanes] = flat[t, pl.ds(j, h, stride=w), :].astype(BF)
+            last_ref[j, :, lanes] = flat[t, pl.ds(w - MARGIN + j, h, stride=w), :].astype(BF)
 
 
 def columns_own_kernel(band_ref, taps_ref, out_ref, flat, turned):
@@ -311,8 +321,17 @@
     def ring(count, by):
         return [(i, (i + by) % count) for i in range(count)]
 
-    left = band_input[:, tile_cols - margin :].transpose(1, 0, 2)
-    right = band_input[:, :margin].transpose(1, 0, 2)
+    rows_at_once = 16
+    sent = pl.BlockSpec((margin, rows_at_once, channels), lambda i: (0, i, 0))
+    right, left = pl.pallas_call(
+        pack_kernel,
+        grid=(tile_rows // rows_at_once,),
+        in_specs=[pl.BlockSpec((rows_at_once, tile_cols, channels), lambda i: (i, 0, 0))],
+        out_specs=[sent, sent],
+        out_shape=[sds((margin, tile_rows, channels), BF)] * 2,
+        scratch_shapes=[pltpu.VMEM((channels // LANES, rows_at_once * tile_cols, LANES), F32)],
+        compiler_params=pltpu.CompilerParams(vmem_limit_bytes=58 * 2**20),
+    )(band_input)
     left = lax.ppermute(left, COLS, ring(Z * X, 1))
     right = lax.ppermute(right, COLS, ring(Z * X, -1))
 

time: 160 us -> 161 us (level)
  waiting for transfers between devices: 63.9 us -> 69 us
  Pallas kernels: 37.5 us -> 42.1 us
  local copies, waits for them, and re-layouts: 4.55 us -> 0.16 us
  starting transfers between devices: 53 us -> 49 us
    pallas_call x0 -> x1, Pallas kernels: none -> 4.66 us  [on_device(): pl.pallas_call(pack_kernel, grid=(tile_rows // rows_at_once,), in_specs=[...]
    ppermute x21, waiting for transfers between devices: 54.1 us -> 58.6 us  [summed_over_all(): got = lax.ppermute(total.astype(BF), ALL, round_pairs(axis, rule))]
    ppermute x21, starting transfers between devices: 39.6 us -> 35.2 us  [summed_over_all(): got = lax.ppermute(total.astype(BF), ALL, round_pairs(axis, rule))]
    unnamed x16 -> x14, local copies, waits for them, and re-layouts: 2.43 us -> 0.03 us
    slice x1 -> x0, local copies, waits for them, and re-layouts: 1.99 us -> none  [on_device(): right = band_input[:, :margin].transpose(1, 0, 2)]
  transfers between devices with their start and end apart: 31 -> 31, of which waited for: 29 -> 28; matrix products, arithmetic and copies ran while one was open for 1% -> 0% of each run, Pallas kernels for 11% -> 11%
where the time goes in v11:
time: 161 us
  waiting for transfers between devices  69 us (43%)
  starting transfers between devices  49 us (30%)
  Pallas kernels  42.1 us (26%)
    ppermute x21, waiting for transfers between devices, summed_over_all(): got = lax.ppermute(total.astype(BF), ALL, round_pairs(axis, rule))  58.6 us
    ppermute x21, starting transfers between devices, summed_over_all(): got = lax.ppermute(total.astype(BF), ALL, round_pairs(axis, rule))  35.2 us
    pallas_call x4, Pallas kernels, call(): pl.pallas_call(kernel, out_shape=outs, in_specs=specs, out_specs=jax.tree...  15.8 us
    pallas_call x1, Pallas kernels, on_device(): pl.pallas_call(columns_own_kernel, grid=grid, in_specs=[tile, taps], out_...  9.81 us
    pallas_call x1, Pallas kernels, on_device(): pl.pallas_call(rows_own_kernel, grid=grid, in_specs=[tile, tile, taps], o...  7.66 us
    ppermute x1, starting transfers between devices, on_device(): right = lax.ppermute(right, COLS, ring(Z * X, -1))  6.56 us
    ppermute x1, waiting for transfers between devices, on_device(): left = lax.ppermute(left, COLS, ring(Z * X, 1))  4.72 us
    pallas_call x1, Pallas kernels, on_device(): pl.pallas_call(pack_kernel, grid=(tile_rows // rows_at_once,), in_specs=[...  4.66 us
  transfers between devices with their start and end apart: 31, of which 28 were waited for; matrix products, arithmetic and copies ran while one was open for 0% of the time, Pallas kernels for 11%

profile of v11, /device:TPU:1, one launch (start us, length us, event | category | flops | bytes accessed | tf_op | source)
XLA Modules:
  0.0 161.2 jit_solution(17464469983497255291)
XLA Ops:
  0.0 4.7 %shard_map.74 = (bf16[10,64,512]{2,1,0:T(8,128)(2,1)}, bf16[10,64,512]{2,1,0:T(8,128)(2,1)}) custom-call(bf16[64,32,512]{2,1,0:T(8,128)(2,1)} %band_ref.5), custom_call_target="tpu_custom_call" | custom-call | tf_op jit(solution)/shard_map/pallas_call | solution.py:326
  4.7 2.0 %collective-permute-start = (bf16[10,64,512]{2,1,0:T(8,128)(2,1)}, bf16[10,64,512]{2,1,0:T(8,128)(2,1)S(1)}, u32[]{:S(2)}, u32[]{:S(2)}) collective-permute-start(bf16[10,64,512]{2,1,0:T(8,128)(2,1)} %get-tuple-element.22), channel_id=1, source_target_pairs={{0,1},{1,2},{2,3},{3,4},{4,5},{5,6},{6,7},{7,8},{8,9},{9,10},{10,1... | collective-permute-start | bytes 1966088 | tf_op jit(solution)/shard_map/ppermute | solution.py:335
  6.7 6.6 %collective-permute-start.1 = (bf16[10,64,512]{2,1,0:T(8,128)(2,1)}, bf16[10,64,512]{2,1,0:T(8,128)(2,1)S(1)}, u32[]{:S(2)}, u32[]{:S(2)}) collective-permute-start(bf16[10,64,512]{2,1,0:T(8,128)(2,1)} %get-tuple-element.23), channel_id=1, source_target_pairs={{0,31},{1,0},{2,1},{3,2},{4,3},{5,4},{6,5},{7,6},{8,7},{9,8},{10,9... | collective-permute-start | bytes 1966088 | tf_op jit(solution)/shard_map/ppermute | solution.py:336
  13.3 9.8 %shard_map.73.own_ref = f32[64,32,512]{2,1,0:T(8,128)S(1)} custom-call(bf16[64,32,512]{2,1,0:T(8,128)(2,1)S(1)} %copy-done, f32[21,512]{1,0:T(8,128)S(1)} %copy-done.5), custom_call_target="tpu_custom_call" | custom-call | flops 44040192 | bytes 6291456 | tf_op jit(solution)/shard_map/pallas_call | solution.py:350
  23.2 4.7 %collective-permute-done.left_ref = bf16[10,64,512]{2,1,0:T(8,128)(2,1)S(1)} collective-permute-done((bf16[10,64,512]{2,1,0:T(8,128)(2,1)}, bf16[10,64,512]{2,1,0:T(8,128)(2,1)S(1)}, u32[]{:S(2)}, u32[]{:S(2)}) %collective-permute-start) | collective-permute-done | bytes 655392 | tf_op jit(solution)/shard_map/ppermute | solution.py:335
  27.9 4.2 %shard_map.75.filtered_ref = bf16[64,32,512]{2,1,0:T(8,128)(2,1)S(1)} custom-call(s32[5]{0:T(128)S(1)} %stack.39.flags_ref.half_ref, f32[64,32,512]{2,1,0:T(8,128)S(1)} %shard_map.73.own_ref, bf16[10,64,512]{2,1,0:T(8,128)(2,1)S(1)} %collective-permute-done.left_ref, bf16[10,64,512]{2,1,0:T(8,128)(2,1)S(1)} %collective-permute-done.1.right_ref, ...), custom_call_target="tpu_custom_call" | custom-call | tf_op jit(solution)/shard_map/pallas_call | solution.py:360
  32.1 1.3 collective-permute-start.3
  33.4 1.2 collective-permute-start.2
  34.6 7.7 %shard_map.76 = (bf16[44,32,512]{2,1,0:T(8,128)(2,1)S(1)}, f32[10,32,512]{2,1,0:T(8,128)S(1)}, f32[10,32,512]{2,1,0:T(8,128)S(1)}) custom-call(bf16[64,32,512]{2,1,0:T(8,128)(2,1)S(1)} %shard_map.75.filtered_ref, bf16[64,32,512]{2,1,0:T(8,128)(2,1)S(1)} %copy-done, f32[21,512]{1,0:T(8,128)S(1)} %copy-done.6), custom_call_target="tpu_custom_call" | custom-call | flops 44040192 | bytes 6291456 | tf_op jit(solution)/shard_map/pallas_call | solution.py:372
  42.4 3.9 %shard_map.77 = (bf16[2048,512]{1,0:T(8,128)(2,1)S(1)}, f32[64,2048]{1,0:T(8,128)S(1)}, f32[32,640]{1,0:T(8,128)S(1)}, bf16[32,640]{1,0:T(8,128)(2,1)S(1)}) custom-call(s32[5]{0:T(128)S(1)} %stack.39.flags_ref.half_ref, bf16[44,32,512]{2,1,0:T(8,128)(2,1)S(1)} %get-tuple-element.24.mid_ref, f32[10,32,512]{2,1,0:T(8,128)S(1)} %get-tuple-element.25.top_ref, ...), custom_call_target="tpu_custom_call" | custom-call | tf_op jit(solution)/shard_map/pallas_call | solution.py:302
  48.1 3.5 %collective-permute-done.5 = bf16[32,640]{1,0:T(8,128)(2,1)S(1)} collective-permute-done((bf16[32,640]{1,0:T(8,128)(2,1)S(1)}, bf16[32,640]{1,0:T(8,128)(2,1)S(1)}, u32[]{:S(2)}, u32[]{:S(2)}) %collective-permute-start.5) | collective-permute-done | bytes 40992 | tf_op jit(solution)/shard_map/ppermute | solution.py:194
  51.7 4.7 %collective-permute-done.6 = bf16[32,640]{1,0:T(8,128)(2,1)S(1)} collective-permute-done((bf16[32,640]{1,0:T(8,128)(2,1)S(1)}, bf16[32,640]{1,0:T(8,128)(2,1)S(1)}, u32[]{:S(2)}, u32[]{:S(2)}) %collective-permute-start.6) | collective-permute-done | bytes 40992 | tf_op jit(solution)/shard_map/ppermute | solution.py:194
  57.4 2.7 %collective-permute-done.7 = bf16[32,640]{1,0:T(8,128)(2,1)S(1)} collective-permute-done((bf16[32,640]{1,0:T(8,128)(2,1)S(1)}, bf16[32,640]{1,0:T(8,128)(2,1)S(1)}, u32[]{:S(2)}, u32[]{:S(2)}) %collective-permute-start.7) | collective-permute-done | bytes 40992 | tf_op jit(solution)/shard_map/ppermute | solution.py:194
  60.1 2.7 %collective-permute-start.8 = (bf16[32,640]{1,0:T(8,128)(2,1)S(1)}, bf16[32,640]{1,0:T(8,128)(2,1)S(1)}, u32[]{:S(2)}, u32[]{:S(2)}) collective-permute-start(bf16[32,640]{1,0:T(8,128)(2,1)S(1)} %convert_element_type.146), channel_id=1, source_target_pairs={{0,224},{1,225},{2,226},{3,227},{4,228},{5,229},{6,230},{7,231},{8... | collective-permute-start | bytes 122888 | tf_op jit(solution)/shard_map/ppermute | solution.py:194
  62.8 2.1 %collective-permute-done.8 = bf16[32,640]{1,0:T(8,128)(2,1)S(1)} collective-permute-done((bf16[32,640]{1,0:T(8,128)(2,1)S(1)}, bf16[32,640]{1,0:T(8,128)(2,1)S(1)}, u32[]{:S(2)}, u32[]{:S(2)}) %collective-permute-start.8) | collective-permute-done | bytes 40992 | tf_op jit(solution)/shard_map/ppermute | solution.py:194
  65.0 3.5 %collective-permute-done.9 = bf16[32,640]{1,0:T(8,128)(2,1)S(1)} collective-permute-done((bf16[32,640]{1,0:T(8,128)(2,1)S(1)}, bf16[32,640]{1,0:T(8,128)(2,1)S(1)}, u32[]{:S(2)}, u32[]{:S(2)}) %collective-permute-start.9) | collective-permute-done | bytes 40992 | tf_op jit(solution)/shard_map/ppermute | solution.py:194
  68.6 1.9 %collective-permute-start.10 = (bf16[32,640]{1,0:T(8,128)(2,1)S(1)}, bf16[32,640]{1,0:T(8,128)(2,1)S(1)}, u32[]{:S(2)}, u32[]{:S(2)}) collective-permute-start(bf16[32,640]{1,0:T(8,128)(2,1)S(1)} %convert_element_type.150), channel_id=1, source_target_pairs={{0,60},{1,61},{2,62},{3,63},{4,40},{5,41},{6,42},{7,43},{8,36},{9,... | collective-permute-start | bytes 122888 | tf_op jit(solution)/shard_map/ppermute | solution.py:194
  70.5 2.9 %collective-permute-done.10 = bf16[32,640]{1,0:T(8,128)(2,1)S(1)} collective-permute-done((bf16[32,640]{1,0:T(8,128)(2,1)S(1)}, bf16[32,640]{1,0:T(8,128)(2,1)S(1)}, u32[]{:S(2)}, u32[]{:S(2)}) %collective-permute-start.10) | collective-permute-done | bytes 40992 | tf_op jit(solution)/shard_map/ppermute | solution.py:194
  73.4 3.6 %collective-permute-start.11 = (bf16[32,640]{1,0:T(8,128)(2,1)S(1)}, bf16[32,640]{1,0:T(8,128)(2,1)S(1)}, u32[]{:S(2)}, u32[]{:S(2)}) collective-permute-start(bf16[32,640]{1,0:T(8,128)(2,1)S(1)} %convert_element_type.152), channel_id=1, source_target_pairs={{0,44},{1,45},{2,46},{3,47},{4,56},{5,57},{6,58},{7,59},{8,52},{9,... | collective-permute-start | bytes 122888 | tf_op jit(solution)/shard_map/ppermute | solution.py:194
  77.0 1.8 %collective-permute-done.11 = bf16[32,640]{1,0:T(8,128)(2,1)S(1)} collective-permute-done((bf16[32,640]{1,0:T(8,128)(2,1)S(1)}, bf16[32,640]{1,0:T(8,128)(2,1)S(1)}, u32[]{:S(2)}, u32[]{:S(2)}) %collective-permute-start.11) | collective-permute-done | bytes 40992 | tf_op jit(solution)/shard_map/ppermute | solution.py:194
  79.5 0.9 collective-permute-done.12.got_ref
  80.4 2.7 %shard_map.78 = (f32[64,512]{1,0:T(8,128)S(1)}, f32[64,2048]{1,0:T(8,128)S(1)}, f32[32,640]{1,0:T(8,128)S(1)}, bf16[32,640]{1,0:T(8,128)(2,1)S(1)}) custom-call(s32[5]{0:T(128)S(1)} %stack.39.flags_ref.half_ref, f32[32,640]{1,0:T(8,128)S(1)} %convert_add_fusion.16.own_ref, f32[32,640]{1,0:T(8,128)S(1)} %collective-permute-done.12.got_ref, ...), custom_call_target="tpu_custom_call" | custom-call | tf_op jit(solution)/shard_map/pallas_call | solution.py:302
  84.6 3.5 %collective-permute-done.14 = bf16[32,640]{1,0:T(8,128)(2,1)S(1)} collective-permute-done((bf16[32,640]{1,0:T(8,128)(2,1)S(1)}, bf16[32,640]{1,0:T(8,128)(2,1)S(1)}, u32[]{:S(2)}, u32[]{:S(2)}) %collective-permute-start.14) | collective-permute-done | bytes 40992 | tf_op jit(solution)/shard_map/ppermute | solution.py:194
  88.1 2.5 %collective-permute-start.15 = (bf16[32,640]{1,0:T(8,128)(2,1)S(1)}, bf16[32,640]{1,0:T(8,128)(2,1)S(1)}, u32[]{:S(2)}, u32[]{:S(2)}) collective-permute-start(bf16[32,640]{1,0:T(8,128)(2,1)S(1)} %convert_element_type.157), channel_id=1, source_target_pairs={{0,35},{1,34},{2,33},{3,32},{4,39},{5,38},{6,37},{7,36},{8,43},{9,... | collective-permute-start | bytes 122888 | tf_op jit(solution)/shard_map/ppermute | solution.py:194
  90.6 2.3 %collective-permute-done.15 = bf16[32,640]{1,0:T(8,128)(2,1)S(1)} collective-permute-done((bf16[32,640]{1,0:T(8,128)(2,1)S(1)}, bf16[32,640]{1,0:T(8,128)(2,1)S(1)}, u32[]{:S(2)}, u32[]{:S(2)}) %collective-permute-start.15) | collective-permute-done | bytes 40992 | tf_op jit(solution)/shard_map/ppermute | solution.py:194
  93.0 3.5 %collective-permute-done.16 = bf16[32,640]{1,0:T(8,128)(2,1)S(1)} collective-permute-done((bf16[32,640]{1,0:T(8,128)(2,1)S(1)}, bf16[32,640]{1,0:T(8,128)(2,1)S(1)}, u32[]{:S(2)}, u32[]{:S(2)}) %collective-permute-start.16) | collective-permute-done | bytes 40992 | tf_op jit(solution)/shard_map/ppermute | solution.py:194
  96.6 2.4 %collective-permute-start.17 = (bf16[32,640]{1,0:T(8,128)(2,1)S(1)}, bf16[32,640]{1,0:T(8,128)(2,1)S(1)}, u32[]{:S(2)}, u32[]{:S(2)}) collective-permute-start(bf16[32,640]{1,0:T(8,128)(2,1)S(1)} %convert_element_type.161), channel_id=1, source_target_pairs={{0,224},{1,225},{2,226},{3,227},{4,228},{5,229},{6,230},{7,231},{8... | collective-permute-start | bytes 122888 | tf_op jit(solution)/shard_map/ppermute | solution.py:194
  99.0 2.4 %collective-permute-done.17 = bf16[32,640]{1,0:T(8,128)(2,1)S(1)} collective-permute-done((bf16[32,640]{1,0:T(8,128)(2,1)S(1)}, bf16[32,640]{1,0:T(8,128)(2,1)S(1)}, u32[]{:S(2)}, u32[]{:S(2)}) %collective-permute-start.17) | collective-permute-done | bytes 40992 | tf_op jit(solution)/shard_map/ppermute | solution.py:194
  102.3 2.7 %collective-permute-done.18 = bf16[32,640]{1,0:T(8,128)(2,1)S(1)} collective-permute-done((bf16[32,640]{1,0:T(8,128)(2,1)S(1)}, bf16[32,640]{1,0:T(8,128)(2,1)S(1)}, u32[]{:S(2)}, u32[]{:S(2)}) %collective-permute-start.18) | collective-permute-done | bytes 40992 | tf_op jit(solution)/shard_map/ppermute | solution.py:194
  105.1 3.0 %collective-permute-start.19 = (bf16[32,640]{1,0:T(8,128)(2,1)S(1)}, bf16[32,640]{1,0:T(8,128)(2,1)S(1)}, u32[]{:S(2)}, u32[]{:S(2)}) collective-permute-start(bf16[32,640]{1,0:T(8,128)(2,1)S(1)} %convert_element_type.165), channel_id=1, source_target_pairs={{0,60},{1,61},{2,62},{3,63},{4,40},{5,41},{6,42},{7,43},{8,36},{9,... | collective-permute-start | bytes 122888 | tf_op jit(solution)/shard_map/ppermute | solution.py:194
  108.0 1.9 %collective-permute-done.19 = bf16[32,640]{1,0:T(8,128)(2,1)S(1)} collective-permute-done((bf16[32,640]{1,0:T(8,128)(2,1)S(1)}, bf16[32,640]{1,0:T(8,128)(2,1)S(1)}, u32[]{:S(2)}, u32[]{:S(2)}) %collective-permute-start.19) | collective-permute-done | bytes 40992 | tf_op jit(solution)/shard_map/ppermute | solution.py:194
  109.9 3.5 %collective-permute-start.20 = (bf16[32,640]{1,0:T(8,128)(2,1)S(1)}, bf16[32,640]{1,0:T(8,128)(2,1)S(1)}, u32[]{:S(2)}, u32[]{:S(2)}) collective-permute-start(bf16[32,640]{1,0:T(8,128)(2,1)S(1)} %convert_element_type.167), channel_id=1, source_target_pairs={{0,44},{1,45},{2,46},{3,47},{4,56},{5,57},{6,58},{7,59},{8,52},{9,... | collective-permute-start | bytes 122888 | tf_op jit(solution)/shard_map/ppermute | solution.py:194
  113.4 1.9 %collective-permute-done.20 = bf16[32,640]{1,0:T(8,128)(2,1)S(1)} collective-permute-done((bf16[32,640]{1,0:T(8,128)(2,1)S(1)}, bf16[32,640]{1,0:T(8,128)(2,1)S(1)}, u32[]{:S(2)}, u32[]{:S(2)}) %collective-permute-start.20) | collective-permute-done | bytes 40992 | tf_op jit(solution)/shard_map/ppermute | solution.py:194
  115.7 0.9 collective-permute-done.21.got_ref
  116.7 2.7 %shard_map.79 = (f32[64,512]{1,0:T(8,128)S(1)}, f32[64,2048]{1,0:T(8,128)S(1)}, f32[32,640]{1,0:T(8,128)S(1)}, bf16[32,640]{1,0:T(8,128)(2,1)S(1)}) custom-call(s32[5]{0:T(128)S(1)} %stack.39.flags_ref.half_ref, f32[32,640]{1,0:T(8,128)S(1)} %convert_add_fusion.8.own_ref, f32[32,640]{1,0:T(8,128)S(1)} %collective-permute-done.21.got_ref, ...), custom_call_target="tpu_custom_call" | custom-call | tf_op jit(solution)/shard_map/pallas_call | solution.py:302
  120.9 3.5 %collective-permute-done.23 = bf16[32,640]{1,0:T(8,128)(2,1)S(1)} collective-permute-done((bf16[32,640]{1,0:T(8,128)(2,1)S(1)}, bf16[32,640]{1,0:T(8,128)(2,1)S(1)}, u32[]{:S(2)}, u32[]{:S(2)}) %collective-permute-start.23) | collective-permute-done | bytes 40992 | tf_op jit(solution)/shard_map/ppermute | solution.py:194
  124.4 2.6 %collective-permute-start.24 = (bf16[32,640]{1,0:T(8,128)(2,1)S(1)}, bf16[32,640]{1,0:T(8,128)(2,1)S(1)}, u32[]{:S(2)}, u32[]{:S(2)}) collective-permute-start(bf16[32,640]{1,0:T(8,128)(2,1)S(1)} %convert_element_type.172), channel_id=1, source_target_pairs={{0,35},{1,34},{2,33},{3,32},{4,39},{5,38},{6,37},{7,36},{8,43},{9,... | collective-permute-start | bytes 122888 | tf_op jit(solution)/shard_map/ppermute | solution.py:194
  127.0 2.2 %collective-permute-done.24 = bf16[32,640]{1,0:T(8,128)(2,1)S(1)} collective-permute-done((bf16[32,640]{1,0:T(8,128)(2,1)S(1)}, bf16[32,640]{1,0:T(8,128)(2,1)S(1)}, u32[]{:S(2)}, u32[]{:S(2)}) %collective-permute-start.24) | collective-permute-done | bytes 40992 | tf_op jit(solution)/shard_map/ppermute | solution.py:194
  129.3 3.5 %collective-permute-done.25 = bf16[32,640]{1,0:T(8,128)(2,1)S(1)} collective-permute-done((bf16[32,640]{1,0:T(8,128)(2,1)S(1)}, bf16[32,640]{1,0:T(8,128)(2,1)S(1)}, u32[]{:S(2)}, u32[]{:S(2)}) %collective-permute-start.25) | collective-permute-done | bytes 40992 | tf_op jit(solution)/shard_map/ppermute | solution.py:194
  132.9 2.7 %collective-permute-start.26 = (bf16[32,640]{1,0:T(8,128)(2,1)S(1)}, bf16[32,640]{1,0:T(8,128)(2,1)S(1)}, u32[]{:S(2)}, u32[]{:S(2)}) collective-permute-start(bf16[32,640]{1,0:T(8,128)(2,1)S(1)} %convert_element_type.176), channel_id=1, source_target_pairs={{0,224},{1,225},{2,226},{3,227},{4,228},{5,229},{6,230},{7,231},{8... | collective-permute-start | bytes 122888 | tf_op jit(solution)/shard_map/ppermute | solution.py:194
  135.6 2.1 %collective-permute-done.26 = bf16[32,640]{1,0:T(8,128)(2,1)S(1)} collective-permute-done((bf16[32,640]{1,0:T(8,128)(2,1)S(1)}, bf16[32,640]{1,0:T(8,128)(2,1)S(1)}, u32[]{:S(2)}, u32[]{:S(2)}) %collective-permute-start.26) | collective-permute-done | bytes 40992 | tf_op jit(solution)/shard_map/ppermute | solution.py:194
  138.6 2.7 %collective-permute-done.27 = bf16[32,640]{1,0:T(8,128)(2,1)S(1)} collective-permute-done((bf16[32,640]{1,0:T(8,128)(2,1)S(1)}, bf16[32,640]{1,0:T(8,128)(2,1)S(1)}, u32[]{:S(2)}, u32[]{:S(2)}) %collective-permute-start.27) | collective-permute-done | bytes 40992 | tf_op jit(solution)/shard_map/ppermute | solution.py:194
  141.3 3.8 %collective-permute-start.28 = (bf16[32,640]{1,0:T(8,128)(2,1)S(1)}, bf16[32,640]{1,0:T(8,128)(2,1)S(1)}, u32[]{:S(2)}, u32[]{:S(2)}) collective-permute-start(bf16[32,640]{1,0:T(8,128)(2,1)S(1)} %convert_element_type.180), channel_id=1, source_target_pairs={{0,60},{1,61},{2,62},{3,63},{4,40},{5,41},{6,42},{7,43},{8,36},{9,... | collective-permute-start | bytes 122888 | tf_op jit(solution)/shard_map/ppermute | solution.py:194
  145.1 1.8 %collective-permute-done.28 = bf16[32,640]{1,0:T(8,128)(2,1)S(1)} collective-permute-done((bf16[32,640]{1,0:T(8,128)(2,1)S(1)}, bf16[32,640]{1,0:T(8,128)(2,1)S(1)}, u32[]{:S(2)}, u32[]{:S(2)}) %collective-permute-start.28) | collective-permute-done | bytes 40992 | tf_op jit(solution)/shard_map/ppermute | solution.py:194
  146.9 3.1 %collective-permute-start.29 = (bf16[32,640]{1,0:T(8,128)(2,1)S(1)}, bf16[32,640]{1,0:T(8,128)(2,1)S(1)}, u32[]{:S(2)}, u32[]{:S(2)}) collective-permute-start(bf16[32,640]{1,0:T(8,128)(2,1)S(1)} %convert_element_type.182), channel_id=1, source_target_pairs={{0,44},{1,45},{2,46},{3,47},{4,56},{5,57},{6,58},{7,59},{8,52},{9,... | collective-permute-start | bytes 122888 | tf_op jit(solution)/shard_map/ppermute | solution.py:194
  150.0 3.4 %collective-permute-done.29 = bf16[32,640]{1,0:T(8,128)(2,1)S(1)} collective-permute-done((bf16[32,640]{1,0:T(8,128)(2,1)S(1)}, bf16[32,640]{1,0:T(8,128)(2,1)S(1)}, u32[]{:S(2)}, u32[]{:S(2)}) %collective-permute-start.29) | collective-permute-done | bytes 40992 | tf_op jit(solution)/shard_map/ppermute | solution.py:194
  153.5 1.3 collective-permute-done.30.got_ref
  154.8 6.4 %shard_map.80 = bf16[2048,512]{1,0:T(8,128)(2,1)} custom-call(s32[5]{0:T(128)S(1)} %stack.39.flags_ref.half_ref, f32[32,640]{1,0:T(8,128)S(1)} %convert_add_fusion.own_ref, f32[32,640]{1,0:T(8,128)S(1)} %collective-permute-done.30.got_ref, f32[64,512]{1,0:T(8,128)S(1)} %get-tuple-element.37.basis_ref, bf16[2048,512]{1,0:T(8,128)(2,1)S(1)} %get-tuple-element.29.feature_ref, ...), custom_call_target="tpu_custom_call" | custom-call | tf_op jit(solution)/shard_map/pallas_call | solution.py:302
  (83 shorter events, 9.3 us)
Async XLA Ops:
  0.0 13.3 %copy-start = (bf16[64,32,512]{2,1,0:T(8,128)(2,1)S(1)}, bf16[64,32,512]{2,1,0:T(8,128)(2,1)}, u32[]{:S(2)}) copy-start(bf16[64,32,512]{2,1,0:T(8,128)(2,1)} %band_ref.5) | copy-start | bytes 6291460
  0.0 13.3 %copy-start.5 = (f32[21,512]{1,0:T(8,128)S(1)}, f32[21,512]{1,0:T(8,128)}, u32[]{:S(2)}) copy-start(f32[21,512]{1,0:T(8,128)} %taps_ref.5) | copy-start | bytes 129028
  4.7 23.2 %collective-permute-start = (bf16[10,64,512]{2,1,0:T(8,128)(2,1)}, bf16[10,64,512]{2,1,0:T(8,128)(2,1)S(1)}, u32[]{:S(2)}, u32[]{:S(2)}) collective-permute-start(bf16[10,64,512]{2,1,0:T(8,128)(2,1)} %get-tuple-element.22), channel_id=1, source_target_pairs={{0,1},{1,2},{2,3},{3,4},{4,5},{5,6},{6,7},{7,8},{8,9},{9,10},{10,1... | collective-permute-start | bytes 1966088 | tf_op jit(solution)/shard_map/ppermute | solution.py:335
  6.7 21.2 %collective-permute-start.1 = (bf16[10,64,512]{2,1,0:T(8,128)(2,1)}, bf16[10,64,512]{2,1,0:T(8,128)(2,1)S(1)}, u32[]{:S(2)}, u32[]{:S(2)}) collective-permute-start(bf16[10,64,512]{2,1,0:T(8,128)(2,1)} %get-tuple-element.23), channel_id=1, source_target_pairs={{0,31},{1,0},{2,1},{3,2},{4,3},{5,4},{6,5},{7,6},{8,7},{9,8},{10,9... | collective-permute-start | bytes 1966088 | tf_op jit(solution)/shard_map/ppermute | solution.py:336
  23.2 11.5 %copy-start.6 = (f32[21,512]{1,0:T(8,128)S(1)}, f32[21,512]{1,0:T(8,128)}, u32[]{:S(2)}) copy-start(f32[21,512]{1,0:T(8,128)} %taps_ref.7) | copy-start | bytes 129028
  32.1 10.2 %collective-permute-start.3 = (bf16[10,32,512]{2,1,0:T(8,128)(2,1)S(1)}, bf16[10,32,512]{2,1,0:T(8,128)(2,1)S(1)}, u32[]{:S(2)}, u32[]{:S(2)}) collective-permute-start(bf16[10,32,512]{2,1,0:T(8,128)(2,1)S(1)} %get-tuple-element.39), channel_id=1, source_target_pairs={{0,224},{32,0},{64,32},{96,64},{128,96},{160,128},{192,160},{224,1... | collective-permute-start | bytes 983048 | tf_op jit(solution)/shard_map/ppermute | solution.py:370
  33.4 8.9 %copy-start.1 = (bf16[512,512]{1,0:T(8,128)(2,1)S(1)}, bf16[512,512]{1,0:T(8,128)(2,1)}, u32[]{:S(2)}) copy-start(bf16[512,512]{1,0:T(8,128)(2,1)} %w_ref.1) | copy-start | bytes 1572868
  33.4 8.9 %copy-start.4 = (f32[512,64]{0,1:T(8,128)S(1)}, f32[512,64]{0,1:T(8,128)}, u32[]{:S(2)}) copy-start(f32[512,64]{0,1:T(8,128)} %param.11) | copy-start | bytes 393220
  33.4 8.9 %collective-permute-start.2 = (bf16[10,32,512]{2,1,0:T(8,128)(2,1)S(1)}, bf16[10,32,512]{2,1,0:T(8,128)(2,1)S(1)}, u32[]{:S(2)}, u32[]{:S(2)}) collective-permute-start(bf16[10,32,512]{2,1,0:T(8,128)(2,1)S(1)} %get-tuple-element.40), channel_id=1, source_target_pairs={{0,32},{32,64},{64,96},{96,128},{128,160},{160,192},{192,224},{224... | collective-permute-start | bytes 983048 | tf_op jit(solution)/shard_map/ppermute | solution.py:369
  46.3 1.6 %collective-permute-start.4 = (bf16[32,640]{1,0:T(8,128)(2,1)S(1)}, bf16[32,640]{1,0:T(8,128)(2,1)S(1)}, u32[]{:S(2)}, u32[]{:S(2)}) collective-permute-start(bf16[32,640]{1,0:T(8,128)(2,1)S(1)} %get-tuple-element.28), channel_id=1, source_target_pairs={{0,32},{32,0},{1,33},{33,1},{2,34},{34,2},{3,35},{35,3},{4,36},{36... | collective-permute-start | bytes 122888 | tf_op jit(solution)/shard_map/ppermute | solution.py:191
  48.0 3.6 %collective-permute-start.5 = (bf16[32,640]{1,0:T(8,128)(2,1)S(1)}, bf16[32,640]{1,0:T(8,128)(2,1)S(1)}, u32[]{:S(2)}, u32[]{:S(2)}) collective-permute-start(bf16[32,640]{1,0:T(8,128)(2,1)S(1)} %convert_element_type.140), channel_id=1, source_target_pairs={{0,33},{1,32},{2,35},{3,34},{4,37},{5,36},{6,39},{7,38},{8,41},{9,... | collective-permute-start | bytes 122888 | tf_op jit(solution)/shard_map/ppermute | solution.py:194
  51.6 4.8 %collective-permute-start.6 = (bf16[32,640]{1,0:T(8,128)(2,1)S(1)}, bf16[32,640]{1,0:T(8,128)(2,1)S(1)}, u32[]{:S(2)}, u32[]{:S(2)}) collective-permute-start(bf16[32,640]{1,0:T(8,128)(2,1)S(1)} %convert_element_type.142), channel_id=1, source_target_pairs={{0,35},{1,34},{2,33},{3,32},{4,39},{5,38},{6,37},{7,36},{8,43},{9,... | collective-permute-start | bytes 122888 | tf_op jit(solution)/shard_map/ppermute | solution.py:194
  56.5 3.6 %collective-permute-start.7 = (bf16[32,640]{1,0:T(8,128)(2,1)S(1)}, bf16[32,640]{1,0:T(8,128)(2,1)S(1)}, u32[]{:S(2)}, u32[]{:S(2)}) collective-permute-start(bf16[32,640]{1,0:T(8,128)(2,1)S(1)} %convert_element_type.144), channel_id=1, source_target_pairs={{0,96},{1,97},{2,98},{3,99},{4,100},{5,101},{6,102},{7,103},{8,104... | collective-permute-start | bytes 122888 | tf_op jit(solution)/shard_map/ppermute | solution.py:194
  60.1 4.8 %collective-permute-start.8 = (bf16[32,640]{1,0:T(8,128)(2,1)S(1)}, bf16[32,640]{1,0:T(8,128)(2,1)S(1)}, u32[]{:S(2)}, u32[]{:S(2)}) collective-permute-start(bf16[32,640]{1,0:T(8,128)(2,1)S(1)} %convert_element_type.146), channel_id=1, source_target_pairs={{0,224},{1,225},{2,226},{3,227},{4,228},{5,229},{6,230},{7,231},{8... | collective-permute-start | bytes 122888 | tf_op jit(solution)/shard_map/ppermute | solution.py:194
  64.9 3.6 %collective-permute-start.9 = (bf16[32,640]{1,0:T(8,128)(2,1)S(1)}, bf16[32,640]{1,0:T(8,128)(2,1)S(1)}, u32[]{:S(2)}, u32[]{:S(2)}) collective-permute-start(bf16[32,640]{1,0:T(8,128)(2,1)S(1)} %convert_element_type.148), channel_id=1, source_target_pairs={{0,36},{1,37},{2,38},{3,39},{4,32},{5,33},{6,34},{7,35},{8,44},{9,... | collective-permute-start | bytes 122888 | tf_op jit(solution)/shard_map/ppermute | solution.py:194
  68.6 4.8 %collective-permute-start.10 = (bf16[32,640]{1,0:T(8,128)(2,1)S(1)}, bf16[32,640]{1,0:T(8,128)(2,1)S(1)}, u32[]{:S(2)}, u32[]{:S(2)}) collective-permute-start(bf16[32,640]{1,0:T(8,128)(2,1)S(1)} %convert_element_type.150), channel_id=1, source_target_pairs={{0,60},{1,61},{2,62},{3,63},{4,40},{5,41},{6,42},{7,43},{8,36},{9,... | collective-permute-start | bytes 122888 | tf_op jit(solution)/shard_map/ppermute | solution.py:194
  73.4 5.4 %collective-permute-start.11 = (bf16[32,640]{1,0:T(8,128)(2,1)S(1)}, bf16[32,640]{1,0:T(8,128)(2,1)S(1)}, u32[]{:S(2)}, u32[]{:S(2)}) collective-permute-start(bf16[32,640]{1,0:T(8,128)(2,1)S(1)} %convert_element_type.152), channel_id=1, source_target_pairs={{0,44},{1,45},{2,46},{3,47},{4,56},{5,57},{6,58},{7,59},{8,52},{9,... | collective-permute-start | bytes 122888 | tf_op jit(solution)/shard_map/ppermute | solution.py:194
  78.8 1.5 collective-permute-start.12
  83.1 1.3 collective-permute-start.13
  84.5 3.6 %collective-permute-start.14 = (bf16[32,640]{1,0:T(8,128)(2,1)S(1)}, bf16[32,640]{1,0:T(8,128)(2,1)S(1)}, u32[]{:S(2)}, u32[]{:S(2)}) collective-permute-start(bf16[32,640]{1,0:T(8,128)(2,1)S(1)} %convert_element_type.155), channel_id=1, source_target_pairs={{0,33},{1,32},{2,35},{3,34},{4,37},{5,36},{6,39},{7,38},{8,41},{9,... | collective-permute-start | bytes 122888 | tf_op jit(solution)/shard_map/ppermute | solution.py:194
  88.1 4.8 %collective-permute-start.15 = (bf16[32,640]{1,0:T(8,128)(2,1)S(1)}, bf16[32,640]{1,0:T(8,128)(2,1)S(1)}, u32[]{:S(2)}, u32[]{:S(2)}) collective-permute-start(bf16[32,640]{1,0:T(8,128)(2,1)S(1)} %convert_element_type.157), channel_id=1, source_target_pairs={{0,35},{1,34},{2,33},{3,32},{4,39},{5,38},{6,37},{7,36},{8,43},{9,... | collective-permute-start | bytes 122888 | tf_op jit(solution)/shard_map/ppermute | solution.py:194
  92.9 3.6 %collective-permute-start.16 = (bf16[32,640]{1,0:T(8,128)(2,1)S(1)}, bf16[32,640]{1,0:T(8,128)(2,1)S(1)}, u32[]{:S(2)}, u32[]{:S(2)}) collective-permute-start(bf16[32,640]{1,0:T(8,128)(2,1)S(1)} %convert_element_type.159), channel_id=1, source_target_pairs={{0,96},{1,97},{2,98},{3,99},{4,100},{5,101},{6,102},{7,103},{8,104... | collective-permute-start | bytes 122888 | tf_op jit(solution)/shard_map/ppermute | solution.py:194
  96.6 4.8 %collective-permute-start.17 = (bf16[32,640]{1,0:T(8,128)(2,1)S(1)}, bf16[32,640]{1,0:T(8,128)(2,1)S(1)}, u32[]{:S(2)}, u32[]{:S(2)}) collective-permute-start(bf16[32,640]{1,0:T(8,128)(2,1)S(1)} %convert_element_type.161), channel_id=1, source_target_pairs={{0,224},{1,225},{2,226},{3,227},{4,228},{5,229},{6,230},{7,231},{8... | collective-permute-start | bytes 122888 | tf_op jit(solution)/shard_map/ppermute | solution.py:194
  101.4 3.6 %collective-permute-start.18 = (bf16[32,640]{1,0:T(8,128)(2,1)S(1)}, bf16[32,640]{1,0:T(8,128)(2,1)S(1)}, u32[]{:S(2)}, u32[]{:S(2)}) collective-permute-start(bf16[32,640]{1,0:T(8,128)(2,1)S(1)} %convert_element_type.163), channel_id=1, source_target_pairs={{0,36},{1,37},{2,38},{3,39},{4,32},{5,33},{6,34},{7,35},{8,44},{9,... | collective-permute-start | bytes 122888 | tf_op jit(solution)/shard_map/ppermute | solution.py:194
  105.1 4.8 %collective-permute-start.19 = (bf16[32,640]{1,0:T(8,128)(2,1)S(1)}, bf16[32,640]{1,0:T(8,128)(2,1)S(1)}, u32[]{:S(2)}, u32[]{:S(2)}) collective-permute-start(bf16[32,640]{1,0:T(8,128)(2,1)S(1)} %convert_element_type.165), channel_id=1, source_target_pairs={{0,60},{1,61},{2,62},{3,63},{4,40},{5,41},{6,42},{7,43},{8,36},{9,... | collective-permute-start | bytes 122888 | tf_op jit(solution)/shard_map/ppermute | solution.py:194
  109.9 5.4 %collective-permute-start.20 = (bf16[32,640]{1,0:T(8,128)(2,1)S(1)}, bf16[32,640]{1,0:T(8,128)(2,1)S(1)}, u32[]{:S(2)}, u32[]{:S(2)}) collective-permute-start(bf16[32,640]{1,0:T(8,128)(2,1)S(1)} %convert_element_type.167), channel_id=1, source_target_pairs={{0,44},{1,45},{2,46},{3,47},{4,56},{5,57},{6,58},{7,59},{8,52},{9,... | collective-permute-start | bytes 122888 | tf_op jit(solution)/shard_map/ppermute | solution.py:194
  115.3 1.4 collective-permute-start.21
  116.7 38.1 %copy-start.2 = (bf16[512,512]{1,0:T(8,128)(2,1)S(1)}, bf16[512,512]{1,0:T(8,128)(2,1)}, u32[]{:S(2)}) copy-start(bf16[512,512]{1,0:T(8,128)(2,1)} %wham_ref.1) | copy-start | bytes 1572868
  116.7 38.1 %copy-start.3 = (bf16[512,512]{1,0:T(8,128)(2,1)S(1)}, bf16[512,512]{1,0:T(8,128)(2,1)}, u32[]{:S(2)}) copy-start(bf16[512,512]{1,0:T(8,128)(2,1)} %walign_ref.1) | copy-start | bytes 1572868
  119.4 1.3 collective-permute-start.22
  120.8 3.6 %collective-permute-start.23 = (bf16[32,640]{1,0:T(8,128)(2,1)S(1)}, bf16[32,640]{1,0:T(8,128)(2,1)S(1)}, u32[]{:S(2)}, u32[]{:S(2)}) collective-permute-start(bf16[32,640]{1,0:T(8,128)(2,1)S(1)} %convert_element_type.170), channel_id=1, source_target_pairs={{0,33},{1,32},{2,35},{3,34},{4,37},{5,36},{6,39},{7,38},{8,41},{9,... | collective-permute-start | bytes 122888 | tf_op jit(solution)/shard_map/ppermute | solution.py:194
  124.4 4.8 %collective-permute-start.24 = (bf16[32,640]{1,0:T(8,128)(2,1)S(1)}, bf16[32,640]{1,0:T(8,128)(2,1)S(1)}, u32[]{:S(2)}, u32[]{:S(2)}) collective-permute-start(bf16[32,640]{1,0:T(8,128)(2,1)S(1)} %convert_element_type.172), channel_id=1, source_target_pairs={{0,35},{1,34},{2,33},{3,32},{4,39},{5,38},{6,37},{7,36},{8,43},{9,... | collective-permute-start | bytes 122888 | tf_op jit(solution)/shard_map/ppermute | solution.py:194
  129.2 3.6 %collective-permute-start.25 = (bf16[32,640]{1,0:T(8,128)(2,1)S(1)}, bf16[32,640]{1,0:T(8,128)(2,1)S(1)}, u32[]{:S(2)}, u32[]{:S(2)}) collective-permute-start(bf16[32,640]{1,0:T(8,128)(2,1)S(1)} %convert_element_type.174), channel_id=1, source_target_pairs={{0,96},{1,97},{2,98},{3,99},{4,100},{5,101},{6,102},{7,103},{8,104... | collective-permute-start | bytes 122888 | tf_op jit(solution)/shard_map/ppermute | solution.py:194
  132.9 4.8 %collective-permute-start.26 = (bf16[32,640]{1,0:T(8,128)(2,1)S(1)}, bf16[32,640]{1,0:T(8,128)(2,1)S(1)}, u32[]{:S(2)}, u32[]{:S(2)}) collective-permute-start(bf16[32,640]{1,0:T(8,128)(2,1)S(1)} %convert_element_type.176), channel_id=1, source_target_pairs={{0,224},{1,225},{2,226},{3,227},{4,228},{5,229},{6,230},{7,231},{8... | collective-permute-start | bytes 122888 | tf_op jit(solution)/shard_map/ppermute | solution.py:194
  137.7 3.6 %collective-permute-start.27 = (bf16[32,640]{1,0:T(8,128)(2,1)S(1)}, bf16[32,640]{1,0:T(8,128)(2,1)S(1)}, u32[]{:S(2)}, u32[]{:S(2)}) collective-permute-start(bf16[32,640]{1,0:T(8,128)(2,1)S(1)} %convert_element_type.178), channel_id=1, source_target_pairs={{0,36},{1,37},{2,38},{3,39},{4,32},{5,33},{6,34},{7,35},{8,44},{9,... | collective-permute-start | bytes 122888 | tf_op jit(solution)/shard_map/ppermute | solution.py:194
  141.3 5.5 %collective-permute-start.28 = (bf16[32,640]{1,0:T(8,128)(2,1)S(1)}, bf16[32,640]{1,0:T(8,128)(2,1)S(1)}, u32[]{:S(2)}, u32[]{:S(2)}) collective-permute-start(bf16[32,640]{1,0:T(8,128)(2,1)S(1)} %convert_element_type.180), channel_id=1, source_target_pairs={{0,60},{1,61},{2,62},{3,63},{4,40},{5,41},{6,42},{7,43},{8,36},{9,... | collective-permute-start | bytes 122888 | tf_op jit(solution)/shard_map/ppermute | solution.py:194
  146.9 6.5 %collective-permute-start.29 = (bf16[32,640]{1,0:T(8,128)(2,1)S(1)}, bf16[32,640]{1,0:T(8,128)(2,1)S(1)}, u32[]{:S(2)}, u32[]{:S(2)}) collective-permute-start(bf16[32,640]{1,0:T(8,128)(2,1)S(1)} %convert_element_type.182), channel_id=1, source_target_pairs={{0,44},{1,45},{2,46},{3,47},{4,56},{5,57},{6,58},{7,59},{8,52},{9,... | collective-permute-start | bytes 122888 | tf_op jit(solution)/shard_map/ppermute | solution.py:194
  153.4 1.4 collective-permute-start.30

commit v12 on v10

--- a/solution.py
+++ b/solution.py
@@ -156,8 +156,8 @@
 
 
 ROUNDS = [
-    ("x", pair_4a), ("x", pair_4b), ("y", pair_4a), ("y", pair_4b),
     ("z", pair_8a), ("z", pair_8b), ("z", pair_8c),
+    ("y", pair_4b), ("y", pair_4a), ("x", pair_4b), ("x", pair_4a),
 ]
 
 

time: 160 us -> 160 us (level)
  starting transfers between devices: 53 us -> 50.8 us
  waiting for transfers between devices: 63.9 us -> 65.9 us
    ppermute x21, starting transfers between devices: 39.6 us -> 37.3 us  [summed_over_all(): got = lax.ppermute(total.astype(BF), ALL, round_pairs(axis, rule))]
    ppermute x21, waiting for transfers between devices: 54.1 us -> 56.1 us  [summed_over_all(): got = lax.ppermute(total.astype(BF), ALL, round_pairs(axis, rule))]
where the time goes in v12:
time: 160 us
  waiting for transfers between devices  65.9 us (41%)
  starting transfers between devices  50.8 us (32%)
  Pallas kernels  37.5 us (23%)
  local copies, waits for them, and re-layouts  4.55 us (3%)
    ppermute x21, waiting for transfers between devices, summed_over_all(): got = lax.ppermute(total.astype(BF), ALL, round_pairs(axis, rule))  56.1 us
    ppermute x21, starting transfers between devices, summed_over_all(): got = lax.ppermute(total.astype(BF), ALL, round_pairs(axis, rule))  37.3 us
    pallas_call x4, Pallas kernels, call(): pl.pallas_call(kernel, out_shape=outs, in_specs=specs, out_specs=jax.tree...  15.8 us
    pallas_call x1, Pallas kernels, on_device(): pl.pallas_call(columns_own_kernel, grid=grid, in_specs=[tile, taps], out_...  9.81 us
    pallas_call x1, Pallas kernels, on_device(): pl.pallas_call(rows_own_kernel, grid=grid, in_specs=[tile, tile, taps], o...  7.66 us
    ppermute x1, starting transfers between devices, on_device(): right = lax.ppermute(right, COLS, ring(Z * X, -1))  6.56 us
    pallas_call x1, Pallas kernels, on_device(): pl.pallas_call(columns_rest_kernel, grid=grid, in_specs=[scalar, tile, si...  4.18 us
    ppermute x1, waiting for transfers between devices, on_device(): left = lax.ppermute(left, COLS, ring(Z * X, 1))  3.52 us
  transfers between devices with their start and end apart: 31, of which 29 were waited for; matrix products, arithmetic and copies ran while one was open for 1% of the time, Pallas kernels for 11%

profile of v12, /device:TPU:1, one launch (start us, length us, event | category | flops | bytes accessed | tf_op | source)
XLA Modules:
  0.0 159.5 jit_solution(6469742491602662627)
XLA Ops:
  0.0 2.0 %fusion.1 = (bf16[64,10,512]{2,1,0:T(8,128)(2,1)S(1)}, bf16[64,10,512]{2,1,0:T(8,128)(2,1)S(1)}) fusion(bf16[64,32,512]{2,1,0:T(8,128)(2,1)} %band_ref.3), kind=kLoop, calls=%fused_computation.27 | loop fusion | bytes 2621440 | tf_op jit(solution)/shard_map/slice | solution.py:315
  2.0 1.2 copy.15
  3.2 2.0 %collective-permute-start = (bf16[10,64,512]{2,1,0:T(8,128)(2,1)}, bf16[10,64,512]{2,1,0:T(8,128)(2,1)S(1)}, u32[]{:S(2)}, u32[]{:S(2)}) collective-permute-start(bf16[10,64,512]{2,1,0:T(8,128)(2,1)} %bitcast.12), channel_id=1, source_target_pairs={{0,1},{1,2},{2,3},{3,4},{4,5},{5,6},{6,7},{7,8},{8,9},{9,10},{10,1... | collective-permute-start | bytes 1966088 | tf_op jit(solution)/shard_map/ppermute | solution.py:316
  5.3 1.2 copy.14
  6.5 6.6 %collective-permute-start.1 = (bf16[10,64,512]{2,1,0:T(8,128)(2,1)}, bf16[10,64,512]{2,1,0:T(8,128)(2,1)S(1)}, u32[]{:S(2)}, u32[]{:S(2)}) collective-permute-start(bf16[10,64,512]{2,1,0:T(8,128)(2,1)} %bitcast.11), channel_id=1, source_target_pairs={{0,31},{1,0},{2,1},{3,2},{4,3},{5,4},{6,5},{7,6},{8,7},{9,8},{10,9... | collective-permute-start | bytes 1966088 | tf_op jit(solution)/shard_map/ppermute | solution.py:317
  13.1 9.8 %shard_map.73.own_ref = f32[64,32,512]{2,1,0:T(8,128)S(1)} custom-call(bf16[64,32,512]{2,1,0:T(8,128)(2,1)S(1)} %copy-done, f32[21,512]{1,0:T(8,128)S(1)} %copy-done.5), custom_call_target="tpu_custom_call" | custom-call | flops 44040192 | bytes 6291456 | tf_op jit(solution)/shard_map/pallas_call | solution.py:331
  22.9 3.5 %collective-permute-done.left_ref = bf16[10,64,512]{2,1,0:T(8,128)(2,1)S(1)} collective-permute-done((bf16[10,64,512]{2,1,0:T(8,128)(2,1)}, bf16[10,64,512]{2,1,0:T(8,128)(2,1)S(1)}, u32[]{:S(2)}, u32[]{:S(2)}) %collective-permute-start) | collective-permute-done | bytes 655392 | tf_op jit(solution)/shard_map/ppermute | solution.py:316
  26.7 4.2 %shard_map.74.filtered_ref = bf16[64,32,512]{2,1,0:T(8,128)(2,1)S(1)} custom-call(s32[5]{0:T(128)S(1)} %stack.39.flags_ref.half_ref, f32[64,32,512]{2,1,0:T(8,128)S(1)} %shard_map.73.own_ref, bf16[10,64,512]{2,1,0:T(8,128)(2,1)S(1)} %collective-permute-done.left_ref, bf16[10,64,512]{2,1,0:T(8,128)(2,1)S(1)} %collective-permute-done.1.right_ref, ...), custom_call_target="tpu_custom_call" | custom-call | tf_op jit(solution)/shard_map/pallas_call | solution.py:341
  31.0 1.5 collective-permute-start.3
  32.5 1.2 collective-permute-start.2
  33.8 7.7 %shard_map.75 = (bf16[44,32,512]{2,1,0:T(8,128)(2,1)S(1)}, f32[10,32,512]{2,1,0:T(8,128)S(1)}, f32[10,32,512]{2,1,0:T(8,128)S(1)}) custom-call(bf16[64,32,512]{2,1,0:T(8,128)(2,1)S(1)} %shard_map.74.filtered_ref, bf16[64,32,512]{2,1,0:T(8,128)(2,1)S(1)} %copy-done, f32[21,512]{1,0:T(8,128)S(1)} %copy-done.6), custom_call_target="tpu_custom_call" | custom-call | flops 44040192 | bytes 6291456 | tf_op jit(solution)/shard_map/pallas_call | solution.py:353
  41.5 4.0 %shard_map.76 = (bf16[2048,512]{1,0:T(8,128)(2,1)S(1)}, f32[64,2048]{1,0:T(8,128)S(1)}, f32[32,640]{1,0:T(8,128)S(1)}, bf16[32,640]{1,0:T(8,128)(2,1)S(1)}) custom-call(s32[5]{0:T(128)S(1)} %stack.39.flags_ref.half_ref, bf16[44,32,512]{2,1,0:T(8,128)(2,1)S(1)} %get-tuple-element.20.mid_ref, f32[10,32,512]{2,1,0:T(8,128)S(1)} %get-tuple-element.21.top_ref, ...), custom_call_target="tpu_custom_call" | custom-call | tf_op jit(solution)/shard_map/pallas_call | solution.py:292
  46.9 3.5 %collective-permute-done.5 = bf16[32,640]{1,0:T(8,128)(2,1)S(1)} collective-permute-done((bf16[32,640]{1,0:T(8,128)(2,1)S(1)}, bf16[32,640]{1,0:T(8,128)(2,1)S(1)}, u32[]{:S(2)}, u32[]{:S(2)}) %collective-permute-start.5) | collective-permute-done | bytes 40992 | tf_op jit(solution)/shard_map/ppermute | solution.py:184
  50.5 1.4 collective-permute-start.6
  51.8 3.5 %collective-permute-done.6 = bf16[32,640]{1,0:T(8,128)(2,1)S(1)} collective-permute-done((bf16[32,640]{1,0:T(8,128)(2,1)S(1)}, bf16[32,640]{1,0:T(8,128)(2,1)S(1)}, u32[]{:S(2)}, u32[]{:S(2)}) %collective-permute-start.6) | collective-permute-done | bytes 40992 | tf_op jit(solution)/shard_map/ppermute | solution.py:184
  55.3 1.5 collective-permute-start.7
  56.8 3.9 %collective-permute-done.7 = bf16[32,640]{1,0:T(8,128)(2,1)S(1)} collective-permute-done((bf16[32,640]{1,0:T(8,128)(2,1)S(1)}, bf16[32,640]{1,0:T(8,128)(2,1)S(1)}, u32[]{:S(2)}, u32[]{:S(2)}) %collective-permute-start.7) | collective-permute-done | bytes 40992 | tf_op jit(solution)/shard_map/ppermute | solution.py:184
  60.7 3.1 %collective-permute-start.8 = (bf16[32,640]{1,0:T(8,128)(2,1)S(1)}, bf16[32,640]{1,0:T(8,128)(2,1)S(1)}, u32[]{:S(2)}, u32[]{:S(2)}) collective-permute-start(bf16[32,640]{1,0:T(8,128)(2,1)S(1)} %convert_element_type.146), channel_id=1, source_target_pairs={{0,224},{1,225},{2,226},{3,227},{4,228},{5,229},{6,230},{7,231},{8... | collective-permute-start | bytes 122888 | tf_op jit(solution)/shard_map/ppermute | solution.py:184
  63.8 1.7 %collective-permute-done.8 = bf16[32,640]{1,0:T(8,128)(2,1)S(1)} collective-permute-done((bf16[32,640]{1,0:T(8,128)(2,1)S(1)}, bf16[32,640]{1,0:T(8,128)(2,1)S(1)}, u32[]{:S(2)}, u32[]{:S(2)}) %collective-permute-start.8) | collective-permute-done | bytes 40992 | tf_op jit(solution)/shard_map/ppermute | solution.py:184
  65.9 3.3 %collective-permute-done.9 = bf16[32,640]{1,0:T(8,128)(2,1)S(1)} collective-permute-done((bf16[32,640]{1,0:T(8,128)(2,1)S(1)}, bf16[32,640]{1,0:T(8,128)(2,1)S(1)}, u32[]{:S(2)}, u32[]{:S(2)}) %collective-permute-start.9) | collective-permute-done | bytes 40992 | tf_op jit(solution)/shard_map/ppermute | solution.py:184
  69.2 4.1 %collective-permute-start.10 = (bf16[32,640]{1,0:T(8,128)(2,1)S(1)}, bf16[32,640]{1,0:T(8,128)(2,1)S(1)}, u32[]{:S(2)}, u32[]{:S(2)}) collective-permute-start(bf16[32,640]{1,0:T(8,128)(2,1)S(1)} %convert_element_type.150), channel_id=1, source_target_pairs={{0,35},{1,34},{2,33},{3,32},{4,39},{5,38},{6,37},{7,36},{8,43},{9,... | collective-permute-start | bytes 122888 | tf_op jit(solution)/shard_map/ppermute | solution.py:184
  73.2 1.7 %collective-permute-done.10 = bf16[32,640]{1,0:T(8,128)(2,1)S(1)} collective-permute-done((bf16[32,640]{1,0:T(8,128)(2,1)S(1)}, bf16[32,640]{1,0:T(8,128)(2,1)S(1)}, u32[]{:S(2)}, u32[]{:S(2)}) %collective-permute-start.10) | collective-permute-done | bytes 40992 | tf_op jit(solution)/shard_map/ppermute | solution.py:184
  75.0 3.4 %collective-permute-done.11 = bf16[32,640]{1,0:T(8,128)(2,1)S(1)} collective-permute-done((bf16[32,640]{1,0:T(8,128)(2,1)S(1)}, bf16[32,640]{1,0:T(8,128)(2,1)S(1)}, u32[]{:S(2)}, u32[]{:S(2)}) %collective-permute-start.11) | collective-permute-done | bytes 40992 | tf_op jit(solution)/shard_map/ppermute | solution.py:184
  79.8 2.7 %shard_map.77 = (f32[64,512]{1,0:T(8,128)S(1)}, f32[64,2048]{1,0:T(8,128)S(1)}, f32[32,640]{1,0:T(8,128)S(1)}, bf16[32,640]{1,0:T(8,128)(2,1)S(1)}) custom-call(s32[5]{0:T(128)S(1)} %stack.39.flags_ref.half_ref, f32[32,640]{1,0:T(8,128)S(1)} %convert_add_fusion.16.own_ref, f32[32,640]{1,0:T(8,128)S(1)} %collective-permute-done.12.got_ref, ...), custom_call_target="tpu_custom_call" | custom-call | tf_op jit(solution)/shard_map/pallas_call | solution.py:292
  85.0 2.5 %collective-permute-done.14 = bf16[32,640]{1,0:T(8,128)(2,1)S(1)} collective-permute-done((bf16[32,640]{1,0:T(8,128)(2,1)S(1)}, bf16[32,640]{1,0:T(8,128)(2,1)S(1)}, u32[]{:S(2)}, u32[]{:S(2)}) %collective-permute-start.14) | collective-permute-done | bytes 40992 | tf_op jit(solution)/shard_map/ppermute | solution.py:184
  87.5 3.5 %collective-permute-start.15 = (bf16[32,640]{1,0:T(8,128)(2,1)S(1)}, bf16[32,640]{1,0:T(8,128)(2,1)S(1)}, u32[]{:S(2)}, u32[]{:S(2)}) collective-permute-start(bf16[32,640]{1,0:T(8,128)(2,1)S(1)} %convert_element_type.157), channel_id=1, source_target_pairs={{0,60},{1,61},{2,62},{3,63},{4,40},{5,41},{6,42},{7,43},{8,36},{9,... | collective-permute-start | bytes 122888 | tf_op jit(solution)/shard_map/ppermute | solution.py:184
  91.0 1.8 %collective-permute-done.15 = bf16[32,640]{1,0:T(8,128)(2,1)S(1)} collective-permute-done((bf16[32,640]{1,0:T(8,128)(2,1)S(1)}, bf16[32,640]{1,0:T(8,128)(2,1)S(1)}, u32[]{:S(2)}, u32[]{:S(2)}) %collective-permute-start.15) | collective-permute-done | bytes 40992 | tf_op jit(solution)/shard_map/ppermute | solution.py:184
  92.8 3.2 %collective-permute-start.16 = (bf16[32,640]{1,0:T(8,128)(2,1)S(1)}, bf16[32,640]{1,0:T(8,128)(2,1)S(1)}, u32[]{:S(2)}, u32[]{:S(2)}) collective-permute-start(bf16[32,640]{1,0:T(8,128)(2,1)S(1)} %convert_element_type.159), channel_id=1, source_target_pairs={{0,44},{1,45},{2,46},{3,47},{4,56},{5,57},{6,58},{7,59},{8,52},{9,... | collective-permute-start | bytes 122888 | tf_op jit(solution)/shard_map/ppermute | solution.py:184
  96.0 2.3 %collective-permute-done.16 = bf16[32,640]{1,0:T(8,128)(2,1)S(1)} collective-permute-done((bf16[32,640]{1,0:T(8,128)(2,1)S(1)}, bf16[32,640]{1,0:T(8,128)(2,1)S(1)}, u32[]{:S(2)}, u32[]{:S(2)}) %collective-permute-start.16) | collective-permute-done | bytes 40992 | tf_op jit(solution)/shard_map/ppermute | solution.py:184
  98.3 2.8 %collective-permute-start.17 = (bf16[32,640]{1,0:T(8,128)(2,1)S(1)}, bf16[32,640]{1,0:T(8,128)(2,1)S(1)}, u32[]{:S(2)}, u32[]{:S(2)}) collective-permute-start(bf16[32,640]{1,0:T(8,128)(2,1)S(1)} %convert_element_type.161), channel_id=1, source_target_pairs={{0,224},{1,225},{2,226},{3,227},{4,228},{5,229},{6,230},{7,231},{8... | collective-permute-start | bytes 122888 | tf_op jit(solution)/shard_map/ppermute | solution.py:184
  101.1 2.0 %collective-permute-done.17 = bf16[32,640]{1,0:T(8,128)(2,1)S(1)} collective-permute-done((bf16[32,640]{1,0:T(8,128)(2,1)S(1)}, bf16[32,640]{1,0:T(8,128)(2,1)S(1)}, u32[]{:S(2)}, u32[]{:S(2)}) %collective-permute-start.17) | collective-permute-done | bytes 40992 | tf_op jit(solution)/shard_map/ppermute | solution.py:184
  103.2 3.5 %collective-permute-done.18 = bf16[32,640]{1,0:T(8,128)(2,1)S(1)} collective-permute-done((bf16[32,640]{1,0:T(8,128)(2,1)S(1)}, bf16[32,640]{1,0:T(8,128)(2,1)S(1)}, u32[]{:S(2)}, u32[]{:S(2)}) %collective-permute-start.18) | collective-permute-done | bytes 40992 | tf_op jit(solution)/shard_map/ppermute | solution.py:184
  106.8 3.0 %collective-permute-start.19 = (bf16[32,640]{1,0:T(8,128)(2,1)S(1)}, bf16[32,640]{1,0:T(8,128)(2,1)S(1)}, u32[]{:S(2)}, u32[]{:S(2)}) collective-permute-start(bf16[32,640]{1,0:T(8,128)(2,1)S(1)} %convert_element_type.165), channel_id=1, source_target_pairs={{0,35},{1,34},{2,33},{3,32},{4,39},{5,38},{6,37},{7,36},{8,43},{9,... | collective-permute-start | bytes 122888 | tf_op jit(solution)/shard_map/ppermute | solution.py:184
  109.7 1.8 %collective-permute-done.19 = bf16[32,640]{1,0:T(8,128)(2,1)S(1)} collective-permute-done((bf16[32,640]{1,0:T(8,128)(2,1)S(1)}, bf16[32,640]{1,0:T(8,128)(2,1)S(1)}, u32[]{:S(2)}, u32[]{:S(2)}) %collective-permute-start.19) | collective-permute-done | bytes 40992 | tf_op jit(solution)/shard_map/ppermute | solution.py:184
  111.7 3.5 %collective-permute-done.20 = bf16[32,640]{1,0:T(8,128)(2,1)S(1)} collective-permute-done((bf16[32,640]{1,0:T(8,128)(2,1)S(1)}, bf16[32,640]{1,0:T(8,128)(2,1)S(1)}, u32[]{:S(2)}, u32[]{:S(2)}) %collective-permute-start.20) | collective-permute-done | bytes 40992 | tf_op jit(solution)/shard_map/ppermute | solution.py:184
  116.6 2.7 %shard_map.78 = (f32[64,512]{1,0:T(8,128)S(1)}, f32[64,2048]{1,0:T(8,128)S(1)}, f32[32,640]{1,0:T(8,128)S(1)}, bf16[32,640]{1,0:T(8,128)(2,1)S(1)}) custom-call(s32[5]{0:T(128)S(1)} %stack.39.flags_ref.half_ref, f32[32,640]{1,0:T(8,128)S(1)} %convert_add_fusion.8.own_ref, f32[32,640]{1,0:T(8,128)S(1)} %collective-permute-done.21.got_ref, ...), custom_call_target="tpu_custom_call" | custom-call | tf_op jit(solution)/shard_map/pallas_call | solution.py:292
  121.4 2.9 %collective-permute-done.23 = bf16[32,640]{1,0:T(8,128)(2,1)S(1)} collective-permute-done((bf16[32,640]{1,0:T(8,128)(2,1)S(1)}, bf16[32,640]{1,0:T(8,128)(2,1)S(1)}, u32[]{:S(2)}, u32[]{:S(2)}) %collective-permute-start.23) | collective-permute-done | bytes 40992 | tf_op jit(solution)/shard_map/ppermute | solution.py:184
  124.3 3.6 %collective-permute-start.24 = (bf16[32,640]{1,0:T(8,128)(2,1)S(1)}, bf16[32,640]{1,0:T(8,128)(2,1)S(1)}, u32[]{:S(2)}, u32[]{:S(2)}) collective-permute-start(bf16[32,640]{1,0:T(8,128)(2,1)S(1)} %convert_element_type.172), channel_id=1, source_target_pairs={{0,60},{1,61},{2,62},{3,63},{4,40},{5,41},{6,42},{7,43},{8,36},{9,... | collective-permute-start | bytes 122888 | tf_op jit(solution)/shard_map/ppermute | solution.py:184
  127.9 1.7 %collective-permute-done.24 = bf16[32,640]{1,0:T(8,128)(2,1)S(1)} collective-permute-done((bf16[32,640]{1,0:T(8,128)(2,1)S(1)}, bf16[32,640]{1,0:T(8,128)(2,1)S(1)}, u32[]{:S(2)}, u32[]{:S(2)}) %collective-permute-start.24) | collective-permute-done | bytes 40992 | tf_op jit(solution)/shard_map/ppermute | solution.py:184
  129.6 2.8 %collective-permute-start.25 = (bf16[32,640]{1,0:T(8,128)(2,1)S(1)}, bf16[32,640]{1,0:T(8,128)(2,1)S(1)}, u32[]{:S(2)}, u32[]{:S(2)}) collective-permute-start(bf16[32,640]{1,0:T(8,128)(2,1)S(1)} %convert_element_type.174), channel_id=1, source_target_pairs={{0,44},{1,45},{2,46},{3,47},{4,56},{5,57},{6,58},{7,59},{8,52},{9,... | collective-permute-start | bytes 122888 | tf_op jit(solution)/shard_map/ppermute | solution.py:184
  132.4 2.5 %collective-permute-done.25 = bf16[32,640]{1,0:T(8,128)(2,1)S(1)} collective-permute-done((bf16[32,640]{1,0:T(8,128)(2,1)S(1)}, bf16[32,640]{1,0:T(8,128)(2,1)S(1)}, u32[]{:S(2)}, u32[]{:S(2)}) %collective-permute-start.25) | collective-permute-done | bytes 40992 | tf_op jit(solution)/shard_map/ppermute | solution.py:184
  135.0 2.8 %collective-permute-start.26 = (bf16[32,640]{1,0:T(8,128)(2,1)S(1)}, bf16[32,640]{1,0:T(8,128)(2,1)S(1)}, u32[]{:S(2)}, u32[]{:S(2)}) collective-permute-start(bf16[32,640]{1,0:T(8,128)(2,1)S(1)} %convert_element_type.176), channel_id=1, source_target_pairs={{0,224},{1,225},{2,226},{3,227},{4,228},{5,229},{6,230},{7,231},{8... | collective-permute-start | bytes 122888 | tf_op jit(solution)/shard_map/ppermute | solution.py:184
  137.7 1.9 %collective-permute-done.26 = bf16[32,640]{1,0:T(8,128)(2,1)S(1)} collective-permute-done((bf16[32,640]{1,0:T(8,128)(2,1)S(1)}, bf16[32,640]{1,0:T(8,128)(2,1)S(1)}, u32[]{:S(2)}, u32[]{:S(2)}) %collective-permute-start.26) | collective-permute-done | bytes 40992 | tf_op jit(solution)/shard_map/ppermute | solution.py:184
  139.8 3.4 %collective-permute-done.27 = bf16[32,640]{1,0:T(8,128)(2,1)S(1)} collective-permute-done((bf16[32,640]{1,0:T(8,128)(2,1)S(1)}, bf16[32,640]{1,0:T(8,128)(2,1)S(1)}, u32[]{:S(2)}, u32[]{:S(2)}) %collective-permute-start.27) | collective-permute-done | bytes 40992 | tf_op jit(solution)/shard_map/ppermute | solution.py:184
  143.2 3.0 %collective-permute-start.28 = (bf16[32,640]{1,0:T(8,128)(2,1)S(1)}, bf16[32,640]{1,0:T(8,128)(2,1)S(1)}, u32[]{:S(2)}, u32[]{:S(2)}) collective-permute-start(bf16[32,640]{1,0:T(8,128)(2,1)S(1)} %convert_element_type.180), channel_id=1, source_target_pairs={{0,35},{1,34},{2,33},{3,32},{4,39},{5,38},{6,37},{7,36},{8,43},{9,... | collective-permute-start | bytes 122888 | tf_op jit(solution)/shard_map/ppermute | solution.py:184
  146.3 1.9 %collective-permute-done.28 = bf16[32,640]{1,0:T(8,128)(2,1)S(1)} collective-permute-done((bf16[32,640]{1,0:T(8,128)(2,1)S(1)}, bf16[32,640]{1,0:T(8,128)(2,1)S(1)}, u32[]{:S(2)}, u32[]{:S(2)}) %collective-permute-start.28) | collective-permute-done | bytes 40992 | tf_op jit(solution)/shard_map/ppermute | solution.py:184
  148.3 3.4 %collective-permute-done.29 = bf16[32,640]{1,0:T(8,128)(2,1)S(1)} collective-permute-done((bf16[32,640]{1,0:T(8,128)(2,1)S(1)}, bf16[32,640]{1,0:T(8,128)(2,1)S(1)}, u32[]{:S(2)}, u32[]{:S(2)}) %collective-permute-start.29) | collective-permute-done | bytes 40992 | tf_op jit(solution)/shard_map/ppermute | solution.py:184
  153.1 6.4 %shard_map.79 = bf16[2048,512]{1,0:T(8,128)(2,1)} custom-call(s32[5]{0:T(128)S(1)} %stack.39.flags_ref.half_ref, f32[32,640]{1,0:T(8,128)S(1)} %convert_add_fusion.own_ref, f32[32,640]{1,0:T(8,128)S(1)} %collective-permute-done.30.got_ref, f32[64,512]{1,0:T(8,128)S(1)} %get-tuple-element.33.basis_ref, bf16[2048,512]{1,0:T(8,128)(2,1)S(1)} %get-tuple-element.25.feature_ref, ...), custom_call_target="tpu_custom_call" | custom-call | tf_op jit(solution)/shard_map/pallas_call | solution.py:292
  (85 shorter events, 11.5 us)
Async XLA Ops:
  2.0 11.1 %copy-start = (bf16[64,32,512]{2,1,0:T(8,128)(2,1)S(1)}, bf16[64,32,512]{2,1,0:T(8,128)(2,1)}, u32[]{:S(2)}) copy-start(bf16[64,32,512]{2,1,0:T(8,128)(2,1)} %band_ref.3) | copy-start | bytes 6291460
  2.0 11.1 %copy-start.5 = (f32[21,512]{1,0:T(8,128)S(1)}, f32[21,512]{1,0:T(8,128)}, u32[]{:S(2)}) copy-start(f32[21,512]{1,0:T(8,128)} %taps_ref.5) | copy-start | bytes 129028
  3.2 23.2 %collective-permute-start = (bf16[10,64,512]{2,1,0:T(8,128)(2,1)}, bf16[10,64,512]{2,1,0:T(8,128)(2,1)S(1)}, u32[]{:S(2)}, u32[]{:S(2)}) collective-permute-start(bf16[10,64,512]{2,1,0:T(8,128)(2,1)} %bitcast.12), channel_id=1, source_target_pairs={{0,1},{1,2},{2,3},{3,4},{4,5},{5,6},{6,7},{7,8},{8,9},{9,10},{10,1... | collective-permute-start | bytes 1966088 | tf_op jit(solution)/shard_map/ppermute | solution.py:316
  6.5 20.3 %collective-permute-start.1 = (bf16[10,64,512]{2,1,0:T(8,128)(2,1)}, bf16[10,64,512]{2,1,0:T(8,128)(2,1)S(1)}, u32[]{:S(2)}, u32[]{:S(2)}) collective-permute-start(bf16[10,64,512]{2,1,0:T(8,128)(2,1)} %bitcast.11), channel_id=1, source_target_pairs={{0,31},{1,0},{2,1},{3,2},{4,3},{5,4},{6,5},{7,6},{8,7},{9,8},{10,9... | collective-permute-start | bytes 1966088 | tf_op jit(solution)/shard_map/ppermute | solution.py:317
  22.9 10.8 %copy-start.6 = (f32[21,512]{1,0:T(8,128)S(1)}, f32[21,512]{1,0:T(8,128)}, u32[]{:S(2)}) copy-start(f32[21,512]{1,0:T(8,128)} %taps_ref.7) | copy-start | bytes 129028
  31.0 10.4 %collective-permute-start.3 = (bf16[10,32,512]{2,1,0:T(8,128)(2,1)S(1)}, bf16[10,32,512]{2,1,0:T(8,128)(2,1)S(1)}, u32[]{:S(2)}, u32[]{:S(2)}) collective-permute-start(bf16[10,32,512]{2,1,0:T(8,128)(2,1)S(1)} %get-tuple-element.35), channel_id=1, source_target_pairs={{0,224},{32,0},{64,32},{96,64},{128,96},{160,128},{192,160},{224,1... | collective-permute-start | bytes 983048 | tf_op jit(solution)/shard_map/ppermute | solution.py:351
  32.5 8.9 %copy-start.1 = (bf16[512,512]{1,0:T(8,128)(2,1)S(1)}, bf16[512,512]{1,0:T(8,128)(2,1)}, u32[]{:S(2)}) copy-start(bf16[512,512]{1,0:T(8,128)(2,1)} %w_ref.1) | copy-start | bytes 1572868
  32.5 8.9 %copy-start.4 = (f32[512,64]{0,1:T(8,128)S(1)}, f32[512,64]{0,1:T(8,128)}, u32[]{:S(2)}) copy-start(f32[512,64]{0,1:T(8,128)} %param.11) | copy-start | bytes 393220
  32.5 8.9 %collective-permute-start.2 = (bf16[10,32,512]{2,1,0:T(8,128)(2,1)S(1)}, bf16[10,32,512]{2,1,0:T(8,128)(2,1)S(1)}, u32[]{:S(2)}, u32[]{:S(2)}) collective-permute-start(bf16[10,32,512]{2,1,0:T(8,128)(2,1)S(1)} %get-tuple-element.36), channel_id=1, source_target_pairs={{0,32},{32,64},{64,96},{96,128},{128,160},{160,192},{192,224},{224... | collective-permute-start | bytes 983048 | tf_op jit(solution)/shard_map/ppermute | solution.py:350
  45.4 1.4 collective-permute-start.4
  46.8 3.6 %collective-permute-start.5 = (bf16[32,640]{1,0:T(8,128)(2,1)S(1)}, bf16[32,640]{1,0:T(8,128)(2,1)S(1)}, u32[]{:S(2)}, u32[]{:S(2)}) collective-permute-start(bf16[32,640]{1,0:T(8,128)(2,1)S(1)} %convert_element_type.140), channel_id=1, source_target_pairs={{0,36},{1,37},{2,38},{3,39},{4,32},{5,33},{6,34},{7,35},{8,44},{9,... | collective-permute-start | bytes 122888 | tf_op jit(solution)/shard_map/ppermute | solution.py:184
  50.5 4.8 %collective-permute-start.6 = (bf16[32,640]{1,0:T(8,128)(2,1)S(1)}, bf16[32,640]{1,0:T(8,128)(2,1)S(1)}, u32[]{:S(2)}, u32[]{:S(2)}) collective-permute-start(bf16[32,640]{1,0:T(8,128)(2,1)S(1)} %convert_element_type.142), channel_id=1, source_target_pairs={{0,60},{1,61},{2,62},{3,63},{4,40},{5,41},{6,42},{7,43},{8,36},{9,... | collective-permute-start | bytes 122888 | tf_op jit(solution)/shard_map/ppermute | solution.py:184
  55.3 5.4 %collective-permute-start.7 = (bf16[32,640]{1,0:T(8,128)(2,1)S(1)}, bf16[32,640]{1,0:T(8,128)(2,1)S(1)}, u32[]{:S(2)}, u32[]{:S(2)}) collective-permute-start(bf16[32,640]{1,0:T(8,128)(2,1)S(1)} %convert_element_type.144), channel_id=1, source_target_pairs={{0,44},{1,45},{2,46},{3,47},{4,56},{5,57},{6,58},{7,59},{8,52},{9,... | collective-permute-start | bytes 122888 | tf_op jit(solution)/shard_map/ppermute | solution.py:184
  60.7 4.8 %collective-permute-start.8 = (bf16[32,640]{1,0:T(8,128)(2,1)S(1)}, bf16[32,640]{1,0:T(8,128)(2,1)S(1)}, u32[]{:S(2)}, u32[]{:S(2)}) collective-permute-start(bf16[32,640]{1,0:T(8,128)(2,1)S(1)} %convert_element_type.146), channel_id=1, source_target_pairs={{0,224},{1,225},{2,226},{3,227},{4,228},{5,229},{6,230},{7,231},{8... | collective-permute-start | bytes 122888 | tf_op jit(solution)/shard_map/ppermute | solution.py:184
  65.6 3.5 %collective-permute-start.9 = (bf16[32,640]{1,0:T(8,128)(2,1)S(1)}, bf16[32,640]{1,0:T(8,128)(2,1)S(1)}, u32[]{:S(2)}, u32[]{:S(2)}) collective-permute-start(bf16[32,640]{1,0:T(8,128)(2,1)S(1)} %convert_element_type.148), channel_id=1, source_target_pairs={{0,96},{1,97},{2,98},{3,99},{4,100},{5,101},{6,102},{7,103},{8,104... | collective-permute-start | bytes 122888 | tf_op jit(solution)/shard_map/ppermute | solution.py:184
  69.2 5.7 %collective-permute-start.10 = (bf16[32,640]{1,0:T(8,128)(2,1)S(1)}, bf16[32,640]{1,0:T(8,128)(2,1)S(1)}, u32[]{:S(2)}, u32[]{:S(2)}) collective-permute-start(bf16[32,640]{1,0:T(8,128)(2,1)S(1)} %convert_element_type.150), channel_id=1, source_target_pairs={{0,35},{1,34},{2,33},{3,32},{4,39},{5,38},{6,37},{7,36},{8,43},{9,... | collective-permute-start | bytes 122888 | tf_op jit(solution)/shard_map/ppermute | solution.py:184
  74.9 3.5 %collective-permute-start.11 = (bf16[32,640]{1,0:T(8,128)(2,1)S(1)}, bf16[32,640]{1,0:T(8,128)(2,1)S(1)}, u32[]{:S(2)}, u32[]{:S(2)}) collective-permute-start(bf16[32,640]{1,0:T(8,128)(2,1)S(1)} %convert_element_type.152), channel_id=1, source_target_pairs={{0,33},{1,32},{2,35},{3,34},{4,37},{5,36},{6,39},{7,38},{8,41},{9,... | collective-permute-start | bytes 122888 | tf_op jit(solution)/shard_map/ppermute | solution.py:184
  78.5 1.4 collective-permute-start.12
  82.6 1.3 collective-permute-start.13
  83.9 3.5 %collective-permute-start.14 = (bf16[32,640]{1,0:T(8,128)(2,1)S(1)}, bf16[32,640]{1,0:T(8,128)(2,1)S(1)}, u32[]{:S(2)}, u32[]{:S(2)}) collective-permute-start(bf16[32,640]{1,0:T(8,128)(2,1)S(1)} %convert_element_type.155), channel_id=1, source_target_pairs={{0,36},{1,37},{2,38},{3,39},{4,32},{5,33},{6,34},{7,35},{8,44},{9,... | collective-permute-start | bytes 122888 | tf_op jit(solution)/shard_map/ppermute | solution.py:184
  87.5 5.3 %collective-permute-start.15 = (bf16[32,640]{1,0:T(8,128)(2,1)S(1)}, bf16[32,640]{1,0:T(8,128)(2,1)S(1)}, u32[]{:S(2)}, u32[]{:S(2)}) collective-permute-start(bf16[32,640]{1,0:T(8,128)(2,1)S(1)} %convert_element_type.157), channel_id=1, source_target_pairs={{0,60},{1,61},{2,62},{3,63},{4,40},{5,41},{6,42},{7,43},{8,36},{9,... | collective-permute-start | bytes 122888 | tf_op jit(solution)/shard_map/ppermute | solution.py:184
  92.8 5.5 %collective-permute-start.16 = (bf16[32,640]{1,0:T(8,128)(2,1)S(1)}, bf16[32,640]{1,0:T(8,128)(2,1)S(1)}, u32[]{:S(2)}, u32[]{:S(2)}) collective-permute-start(bf16[32,640]{1,0:T(8,128)(2,1)S(1)} %convert_element_type.159), channel_id=1, source_target_pairs={{0,44},{1,45},{2,46},{3,47},{4,56},{5,57},{6,58},{7,59},{8,52},{9,... | collective-permute-start | bytes 122888 | tf_op jit(solution)/shard_map/ppermute | solution.py:184
  98.3 4.8 %collective-permute-start.17 = (bf16[32,640]{1,0:T(8,128)(2,1)S(1)}, bf16[32,640]{1,0:T(8,128)(2,1)S(1)}, u32[]{:S(2)}, u32[]{:S(2)}) collective-permute-start(bf16[32,640]{1,0:T(8,128)(2,1)S(1)} %convert_element_type.161), channel_id=1, source_target_pairs={{0,224},{1,225},{2,226},{3,227},{4,228},{5,229},{6,230},{7,231},{8... | collective-permute-start | bytes 122888 | tf_op jit(solution)/shard_map/ppermute | solution.py:184
  103.1 3.6 %collective-permute-start.18 = (bf16[32,640]{1,0:T(8,128)(2,1)S(1)}, bf16[32,640]{1,0:T(8,128)(2,1)S(1)}, u32[]{:S(2)}, u32[]{:S(2)}) collective-permute-start(bf16[32,640]{1,0:T(8,128)(2,1)S(1)} %convert_element_type.163), channel_id=1, source_target_pairs={{0,96},{1,97},{2,98},{3,99},{4,100},{5,101},{6,102},{7,103},{8,104... | collective-permute-start | bytes 122888 | tf_op jit(solution)/shard_map/ppermute | solution.py:184
  106.8 4.8 %collective-permute-start.19 = (bf16[32,640]{1,0:T(8,128)(2,1)S(1)}, bf16[32,640]{1,0:T(8,128)(2,1)S(1)}, u32[]{:S(2)}, u32[]{:S(2)}) collective-permute-start(bf16[32,640]{1,0:T(8,128)(2,1)S(1)} %convert_element_type.165), channel_id=1, source_target_pairs={{0,35},{1,34},{2,33},{3,32},{4,39},{5,38},{6,37},{7,36},{8,43},{9,... | collective-permute-start | bytes 122888 | tf_op jit(solution)/shard_map/ppermute | solution.py:184
  111.6 3.6 %collective-permute-start.20 = (bf16[32,640]{1,0:T(8,128)(2,1)S(1)}, bf16[32,640]{1,0:T(8,128)(2,1)S(1)}, u32[]{:S(2)}, u32[]{:S(2)}) collective-permute-start(bf16[32,640]{1,0:T(8,128)(2,1)S(1)} %convert_element_type.167), channel_id=1, source_target_pairs={{0,33},{1,32},{2,35},{3,34},{4,37},{5,36},{6,39},{7,38},{8,41},{9,... | collective-permute-start | bytes 122888 | tf_op jit(solution)/shard_map/ppermute | solution.py:184
  115.2 1.4 collective-permute-start.21
  116.6 36.5 %copy-start.2 = (bf16[512,512]{1,0:T(8,128)(2,1)S(1)}, bf16[512,512]{1,0:T(8,128)(2,1)}, u32[]{:S(2)}) copy-start(bf16[512,512]{1,0:T(8,128)(2,1)} %wham_ref.1) | copy-start | bytes 1572868
  116.6 36.5 %copy-start.3 = (bf16[512,512]{1,0:T(8,128)(2,1)S(1)}, bf16[512,512]{1,0:T(8,128)(2,1)}, u32[]{:S(2)}) copy-start(bf16[512,512]{1,0:T(8,128)(2,1)} %walign_ref.1) | copy-start | bytes 1572868
  119.3 1.3 collective-permute-start.22
  120.7 3.6 %collective-permute-start.23 = (bf16[32,640]{1,0:T(8,128)(2,1)S(1)}, bf16[32,640]{1,0:T(8,128)(2,1)S(1)}, u32[]{:S(2)}, u32[]{:S(2)}) collective-permute-start(bf16[32,640]{1,0:T(8,128)(2,1)S(1)} %convert_element_type.170), channel_id=1, source_target_pairs={{0,36},{1,37},{2,38},{3,39},{4,32},{5,33},{6,34},{7,35},{8,44},{9,... | collective-permute-start | bytes 122888 | tf_op jit(solution)/shard_map/ppermute | solution.py:184
  124.3 5.3 %collective-permute-start.24 = (bf16[32,640]{1,0:T(8,128)(2,1)S(1)}, bf16[32,640]{1,0:T(8,128)(2,1)S(1)}, u32[]{:S(2)}, u32[]{:S(2)}) collective-permute-start(bf16[32,640]{1,0:T(8,128)(2,1)S(1)} %convert_element_type.172), channel_id=1, source_target_pairs={{0,60},{1,61},{2,62},{3,63},{4,40},{5,41},{6,42},{7,43},{8,36},{9,... | collective-permute-start | bytes 122888 | tf_op jit(solution)/shard_map/ppermute | solution.py:184
  129.6 5.3 %collective-permute-start.25 = (bf16[32,640]{1,0:T(8,128)(2,1)S(1)}, bf16[32,640]{1,0:T(8,128)(2,1)S(1)}, u32[]{:S(2)}, u32[]{:S(2)}) collective-permute-start(bf16[32,640]{1,0:T(8,128)(2,1)S(1)} %convert_element_type.174), channel_id=1, source_target_pairs={{0,44},{1,45},{2,46},{3,47},{4,56},{5,57},{6,58},{7,59},{8,52},{9,... | collective-permute-start | bytes 122888 | tf_op jit(solution)/shard_map/ppermute | solution.py:184
  135.0 4.7 %collective-permute-start.26 = (bf16[32,640]{1,0:T(8,128)(2,1)S(1)}, bf16[32,640]{1,0:T(8,128)(2,1)S(1)}, u32[]{:S(2)}, u32[]{:S(2)}) collective-permute-start(bf16[32,640]{1,0:T(8,128)(2,1)S(1)} %convert_element_type.176), channel_id=1, source_target_pairs={{0,224},{1,225},{2,226},{3,227},{4,228},{5,229},{6,230},{7,231},{8... | collective-permute-start | bytes 122888 | tf_op jit(solution)/shard_map/ppermute | solution.py:184
  139.7 3.5 %collective-permute-start.27 = (bf16[32,640]{1,0:T(8,128)(2,1)S(1)}, bf16[32,640]{1,0:T(8,128)(2,1)S(1)}, u32[]{:S(2)}, u32[]{:S(2)}) collective-permute-start(bf16[32,640]{1,0:T(8,128)(2,1)S(1)} %convert_element_type.178), channel_id=1, source_target_pairs={{0,96},{1,97},{2,98},{3,99},{4,100},{5,101},{6,102},{7,103},{8,104... | collective-permute-start | bytes 122888 | tf_op jit(solution)/shard_map/ppermute | solution.py:184
  143.2 4.9 %collective-permute-start.28 = (bf16[32,640]{1,0:T(8,128)(2,1)S(1)}, bf16[32,640]{1,0:T(8,128)(2,1)S(1)}, u32[]{:S(2)}, u32[]{:S(2)}) collective-permute-start(bf16[32,640]{1,0:T(8,128)(2,1)S(1)} %convert_element_type.180), channel_id=1, source_target_pairs={{0,35},{1,34},{2,33},{3,32},{4,39},{5,38},{6,37},{7,36},{8,43},{9,... | collective-permute-start | bytes 122888 | tf_op jit(solution)/shard_map/ppermute | solution.py:184
  148.2 3.5 %collective-permute-start.29 = (bf16[32,640]{1,0:T(8,128)(2,1)S(1)}, bf16[32,640]{1,0:T(8,128)(2,1)S(1)}, u32[]{:S(2)}, u32[]{:S(2)}) collective-permute-start(bf16[32,640]{1,0:T(8,128)(2,1)S(1)} %convert_element_type.182), channel_id=1, source_target_pairs={{0,33},{1,32},{2,35},{3,34},{4,37},{5,36},{6,39},{7,38},{8,41},{9,... | collective-permute-start | bytes 122888 | tf_op jit(solution)/shard_map/ppermute | solution.py:184
  151.7 1.4 collective-permute-start.30
